TPU v7x, 32 devices: a whole 2x2x4 slice. The times are simulated.
32 devices in a mesh: groups: 2 (over x), day: 16 (over z, y, core).
Axes of the slice: x: 2, y: 2, z: 4, core: 2. Of those that a mesh axis runs over, the one named last changes fastest.
Arguments:
- couplings: float32 [6, 128, 32, 512], P(None, ('groups', 'day')), parts along dimension 1, may hold values from 0.01 to 2.7, as said below
- probe_bits: int32 [16, 128, 32, 512], P(None, ('groups', 'day')), parts along dimension 1, may hold values 0 or 1
- land_mask: int32 [64, 512], P('groups'), parts along dimension 0, may hold values 0 or 1
Outputs:
- variance: float32 [128, 32, 512], P(('groups', 'day')), parts along dimension 0
There are 2 independent parts, one for each index of `groups`. A program takes and returns all parts, laid end to end along the dimension named above; each array names one. Nothing has to cross between parts.
Inputs may be any that keep to these rules, and one draw needn't show every extreme that they name: `couplings`: all weights positive.
All inputs are finite; a program needn't handle non-finite values. No bound on the sum of `probe_bits` on one device may be relied on, other than what follows from the above.
Results may differ from a plain program's by a relative error of at most 0.0003.
Values sent between devices are 32-bit elements; how exact they have to be, the bound alone decides.
No kernel may reach another device: no remote copies, remote signals or barrier semaphores. Data moves between devices by JAX's collectives and lax.ppermute only.
A program may use at most 64 MiB of HBM per device.

v0:
```python
import jax
import jax.numpy as jnp
from jax import lax
from jax.sharding import PartitionSpec as P

ITERS = 3


LINK_OFFSETS = ((0, 1), (1, 0), (1, 1), (1, -1))
COASTAL_FACTOR = 0.2


def passed_along(value, axis, steps):
    count = lax.axis_size(axis)
    pairs = [(source, (source + steps) % count) for source in range(count)]
    return lax.ppermute(value, axis, pairs)


def extended(block, sides, width):
    for axis, dim in sides:
        count = lax.axis_size(axis)
        forward = [(i, i + 1) for i in range(count - 1)]
        forward.append((count - 1, 0))
        backward = [(target, source) for source, target in forward]
        low = lax.ppermute(
            lax.slice_in_dim(block, block.shape[dim] - width, None, axis=dim), axis, forward
        )
        high = lax.ppermute(lax.slice_in_dim(block, 0, width, axis=dim), axis, backward)
        block = jnp.concatenate([low, block, high], axis=dim)
    return block


def shift_plane(values, step_row, step_col):
    lat_size, lon_size = (values.shape[-2], values.shape[-1])
    margins = [(0, 0)] * (values.ndim - 2) + [
        (max(step_row, 0), max(-step_row, 0)),
        (max(step_col, 0), max(-step_col, 0)),
    ]
    padded = jnp.pad(values, margins)
    row_start = max(-step_row, 0)
    col_start = max(-step_col, 0)
    return padded[..., row_start : row_start + lat_size, col_start : col_start + lon_size]


def prepare(couplings, land_mask):
    ones_field = jnp.ones(land_mask.shape, jnp.float32)
    result = [couplings[0]]
    for slot_n, (step_row, step_col) in enumerate(LINK_OFFSETS):
        target = shift_plane(land_mask, -step_row, -step_col)
        inside = shift_plane(ones_field, -step_row, -step_col)
        factor = (
            jnp.where(land_mask == target, jnp.float32(1.0), jnp.float32(COASTAL_FACTOR)) * inside
        )
        result.append(couplings[slot_n + 1] * factor)
    result.append(couplings[5])
    return jnp.stack(result)


def stencil(padded, coef_block, link_prev):
    field = padded[..., 1:-1, :, :]
    next_day = padded[..., 2:, :, :]
    prev_day = padded[..., :-2, :, :]
    result = (
        coef_block[0] * field + coef_block[5] * (field - next_day) + link_prev * (field - prev_day)
    )
    for slot_n, (step_row, step_col) in enumerate(LINK_OFFSETS):
        link_coef = coef_block[slot_n + 1]
        link_back = shift_plane(link_coef, step_row, step_col)
        result = result + link_coef * (field - shift_plane(field, -step_row, -step_col))
        result = result + link_back * (field - shift_plane(field, step_row, step_col))
    return result


def diagonal(coef_block, link_prev):
    result = coef_block[0] + coef_block[5] + link_prev
    for slot_n, (step_row, step_col) in enumerate(LINK_OFFSETS):
        link_coef = coef_block[slot_n + 1]
        result = result + link_coef + shift_plane(link_coef, step_row, step_col)
    return result


def spread(vector):
    return vector[:, None, None, None]


def summed(first, second):
    return jnp.sum(first * second, axis=(1, 2, 3))


def norm_sum(residual, scaled):
    return lax.psum(summed(residual, scaled), "day")


def body(couplings, probe_bits, land_mask):
    probes_n, days_n = (probe_bits.shape[0], probe_bits.shape[1])
    links_eff = prepare(couplings, land_mask)
    signs = (2 * probe_bits - 1).astype(jnp.float32)
    prev_plane = passed_along(links_eff[5, days_n - 1 : days_n], "day", 1)
    link_prev = jnp.concatenate([prev_plane, links_eff[5, : days_n - 1]], axis=0)
    diag_own = diagonal(links_eff, link_prev)
    residual = signs
    scaled = signs / diag_own
    estimate = jnp.zeros_like(signs)
    norm_now = norm_sum(residual, scaled)
    direction = scaled
    for turn in range(ITERS):
        padded = extended(direction, (("day", 1),), 1)
        image = stencil(padded, links_eff, link_prev)
        step_len = norm_now / lax.psum(summed(direction, image), "day")
        estimate = estimate + spread(step_len) * direction
        if turn + 1 < ITERS:
            residual = residual - spread(step_len) * image
            scaled = residual / diag_own
            norm_next = norm_sum(residual, scaled)
            direction = scaled + spread(norm_next / norm_now) * direction
            norm_now = norm_next
    return jnp.sum(signs * estimate, axis=0) / probes_n


def solution(mesh):
    return jax.shard_map(
        body,
        mesh=mesh,
        in_specs=(
            P(None, ("groups", "day"), None, None),
            P(None, ("groups", "day"), None, None),
            P("groups", None),
        ),
        out_specs=P(("groups", "day"), None, None),
        check_vma=False,
    )
```

profile of v0, /device:TPU:0, one launch (start us, length us, event | category | flops | bytes accessed | tf_op | source)
XLA Modules:
  0.0 300.4 jit_solution(4284825563196142856)
XLA Ops:
  0.0 0.0 copy-start
  0.0 1.0 slice_bitcast_fusion.3
  1.0 0.5 collective-permute-start
  1.5 1.2 fusion.93
  2.7 1.3 bitcast_multiply_fusion.3
  4.0 0.9 slice_bitcast_fusion.2
  4.9 3.5 %collective-permute-done = f32[1,32,512]{2,1,0:T(8,128)S(1)} collective-permute-done((f32[1,32,512]{2,1,0:T(8,128)S(1)}, f32[1,32,512]{2,1,0:T(8,128)S(1)}, u32[]{:S(2)}, u32[]{:S(2)}) %collective-permute-start) | collective-permute-done | bytes 65568 | tf_op jit(solution)/shard_map/ppermute | solution.py:16
  8.4 1.5 pad_maximum_fusion.6
  9.9 0.0 copy-done
  9.9 0.9 convert_divide_fusion
  10.8 0.0 copy-start.3
  10.9 0.2 fusion.104
  11.0 1.8 collective-permute-start.1
  12.9 0.0 collective-permute-start.2
  12.9 0.0 copy-done.3
  12.9 0.2 slice_bitcast_fusion.1
  13.1 12.1 %collective-permute-done.1 = f32[16,1,32,512]{3,2,1,0:T(8,128)S(1)} collective-permute-done((f32[16,1,32,512]{3,2,1,0:T(8,128)S(1)}, f32[16,1,32,512]{3,2,1,0:T(8,128)S(1)}, u32[]{:S(2)}, u32[]{:S(2)}) %collective-permute-start.1) | collective-permute-done | bytes 1048608 | tf_op jit(solution)/shard_map/ppermute | solution.py:28
  25.2 4.7 %collective-permute-done.2 = f32[16,1,32,512]{3,2,1,0:T(8,128)S(1)} collective-permute-done((f32[16,1,32,512]{3,2,1,0:T(8,128)S(1)}, f32[16,1,32,512]{3,2,1,0:T(8,128)S(1)}, u32[]{:S(2)}, u32[]{:S(2)}) %collective-permute-start.2) | collective-permute-done | bytes 1048608 | tf_op jit(solution)/shard_map/ppermute | solution.py:25
  29.9 12.8 %multiply_reduce_fusion.4 = (f32[16]{0:T(128)S(1)}, f32[16]{0:T(128)S(1)}, f32[16,4,32,512]{3,2,1,0:T(8,128)}) fusion(f32[4,32,512]{2,1,0:T(8,128)S(1)} %get-tuple-element.31, s32[16,4,32,512]{3,2,1,0:T(8,128)S(1)} %copy-done, f32[16,4,32,512]{3,2,1,0:T(8,128)S(1)} %convert_divide_fusion, f32[4,32,512]{2,1,0:T(8,128)S(1)} %get-tuple-element.35, ...), kind=kLoop, calls=%fused_computation.129 | loop fusion | flops 42991584 | bytes 17825920 | tf_op jit(solution)/shard_map/reduce_sum | solution.py:87
  42.7 35.4 %all-reduce.36 = (f32[16]{0:T(128)S(1)}, f32[16]{0:T(128)S(1)}) all-reduce(f32[16]{0:T(128)S(1)} %get-tuple-element.6, f32[16]{0:T(128)S(1)} %get-tuple-element.5), channel_id=1, replica_groups=mesh['groups'=2,'day'=16] {'day'}, use_global_device_ids=true, to_apply=%region_1.2 | all-reduce | flops 32 | bytes 256 | tf_op jit(solution)/shard_map/psum | solution.py:91
  78.1 6.6 %multiply_reduce_fusion.3 = (f32[16]{0:T(128)S(1)}, f32[16,4,32,512]{3,2,1,0:T(8,128)}) fusion(f32[4,32,512]{2,1,0:T(8,128)S(1)} %get-tuple-element.31, f32[16,4,32,512]{3,2,1,0:T(8,128)} %get-tuple-element.13, f32[16]{0:T(128)S(1)} %div.43, s32[16,4,32,512]{3,2,1,0:T(8,128)} %param.4), kind=kLoop, calls=%fused_computation.127 | loop fusion | flops 8388592 | bytes 12845184 | tf_op jit(solution)/shard_map/reduce_sum | solution.py:87
  84.7 29.6 %psum.44 = f32[16]{0:T(128)S(1)} all-reduce(f32[16]{0:T(128)S(1)} %get-tuple-element.11), channel_id=1, replica_groups=mesh['groups'=2,'day'=16] {'day'}, use_global_device_ids=true, to_apply=%region_5.6 | all-reduce | flops 16 | bytes 128 | tf_op jit(solution)/shard_map/psum | solution.py:91
  114.4 4.6 %multiply_add_fusion.1 = f32[16,4,32,512]{3,2,1,0:T(8,128)S(1)} fusion(f32[16,4,32,512]{3,2,1,0:T(8,128)} %get-tuple-element.12, f32[16]{0:T(128)S(1)} %div.45, f32[4,32,512]{2,1,0:T(8,128)S(1)} %get-tuple-element.31, s32[16,4,32,512]{3,2,1,0:T(8,128)} %param.4), kind=kLoop, calls=%fused_computation.126 | loop fusion | flops 7340032 | bytes 12845120 | tf_op jit(solution)/shard_map/add | solution.py:115
  119.0 0.0 copy-start.1
  119.0 0.3 fusion.103
  119.3 0.1 collective-permute-start.3
  119.4 0.5 collective-permute-start.4
  119.9 11.8 %collective-permute-done.3 = f32[16,1,32,512]{3,2,1,0:T(8,128)S(1)} collective-permute-done((f32[16,1,32,512]{3,2,1,0:T(8,128)S(1)}, f32[16,1,32,512]{3,2,1,0:T(8,128)S(1)}, u32[]{:S(2)}, u32[]{:S(2)}) %collective-permute-start.3) | collective-permute-done | bytes 1048608 | tf_op jit(solution)/shard_map/ppermute | solution.py:28
  131.7 4.8 %collective-permute-done.4 = f32[16,1,32,512]{3,2,1,0:T(8,128)S(1)} collective-permute-done((f32[16,1,32,512]{3,2,1,0:T(8,128)S(1)}, f32[16,1,32,512]{3,2,1,0:T(8,128)S(1)}, u32[]{:S(2)}, u32[]{:S(2)}) %collective-permute-start.4) | collective-permute-done | bytes 1048608 | tf_op jit(solution)/shard_map/ppermute | solution.py:25
  136.5 12.2 %multiply_reduce_fusion.2 = (f32[16]{0:T(128)S(1)}, f32[16,4,32,512]{3,2,1,0:T(8,128)}) fusion(f32[16,4,32,512]{3,2,1,0:T(8,128)S(1)} %multiply_add_fusion.1, f32[4,32,512]{2,1,0:T(8,128)S(1)} %get-tuple-element.35, f32[4,32,512]{2,1,0:T(8,128)S(1)} %get-tuple-element.24, f32[4,32,512]{2,1,0:T(8,128)S(1)} %get-tuple-element.34, ...), kind=kLoop, calls=%fused_computation.125 | loop fusion | flops 36700144 | bytes 13369408 | tf_op jit(solution)/shard_map/reduce_sum | solution.py:87
  148.7 0.0 copy-done.1
  148.7 37.5 %psum.45 = f32[16]{0:T(128)S(1)} all-reduce(f32[16]{0:T(128)S(1)} %get-tuple-element.9), channel_id=1, replica_groups=mesh['groups'=2,'day'=16] {'day'}, use_global_device_ids=true, to_apply=%region_7.8 | all-reduce | flops 16 | bytes 128 | tf_op jit(solution)/shard_map/psum | solution.py:109
  186.3 4.4 %multiply_reduce_fusion.1 = f32[16]{0:T(128)S(1)} fusion(f32[4,32,512]{2,1,0:T(8,128)S(1)} %get-tuple-element.31, f32[16,4,32,512]{3,2,1,0:T(8,128)} %get-tuple-element.12, f32[16,4,32,512]{3,2,1,0:T(8,128)} %get-tuple-element.10, f32[16]{0:T(128)S(1)} %div.46), kind=kLoop, calls=%fused_computation.123 | loop fusion | flops 5242864 | bytes 8650880 | tf_op jit(solution)/shard_map/reduce_sum | solution.py:87
  190.7 29.5 %psum.46 = f32[16]{0:T(128)S(1)} all-reduce(f32[16]{0:T(128)S(1)} %multiply_reduce_fusion.1), channel_id=1, replica_groups=mesh['groups'=2,'day'=16] {'day'}, use_global_device_ids=true, to_apply=%region_9.10 | all-reduce | flops 16 | bytes 128 | tf_op jit(solution)/shard_map/psum | solution.py:91
  220.2 6.4 %multiply_add_fusion = f32[16,4,32,512]{3,2,1,0:T(8,128)S(1)} fusion(f32[16,4,32,512]{3,2,1,0:T(8,128)} %copy-done.1, f32[16]{0:T(128)S(1)} %div.48, f32[4,32,512]{2,1,0:T(8,128)S(1)} %get-tuple-element.31, f32[16,4,32,512]{3,2,1,0:T(8,128)} %get-tuple-element.12, f32[16,4,32,512]{3,2,1,0:T(8,128)} %get-tuple-element.10, f32[16]{0:T(128)S(1)} %div.46), kind=kLoop, calls=%fused_computation.122 | loop fusion | flops 5242880 | bytes 17039488 | tf_op jit(solution)/shard_map/add | solution.py:115
  226.6 0.0 copy-start.2
  226.6 0.3 fusion.102
  226.9 0.1 collective-permute-start.5
  227.0 0.5 collective-permute-start.6
  227.5 11.8 %collective-permute-done.5 = f32[16,1,32,512]{3,2,1,0:T(8,128)S(1)} collective-permute-done((f32[16,1,32,512]{3,2,1,0:T(8,128)S(1)}, f32[16,1,32,512]{3,2,1,0:T(8,128)S(1)}, u32[]{:S(2)}, u32[]{:S(2)}) %collective-permute-start.5) | collective-permute-done | bytes 1048608 | tf_op jit(solution)/shard_map/ppermute | solution.py:28
  239.3 4.9 %collective-permute-done.6 = f32[16,1,32,512]{3,2,1,0:T(8,128)S(1)} collective-permute-done((f32[16,1,32,512]{3,2,1,0:T(8,128)S(1)}, f32[16,1,32,512]{3,2,1,0:T(8,128)S(1)}, u32[]{:S(2)}, u32[]{:S(2)}) %collective-permute-start.6) | collective-permute-done | bytes 1048608 | tf_op jit(solution)/shard_map/ppermute | solution.py:25
  244.2 0.0 copy-done.2
  244.2 11.4 %fusion.91 = f32[16]{0:T(128)S(1)} fusion(f32[16,4,32,512]{3,2,1,0:T(8,128)S(1)} %multiply_add_fusion, f32[16,1,32,512]{3,2,1,0:T(8,128)S(1)} %collective-permute-done.6, f32[16,1,32,512]{3,2,1,0:T(8,128)S(1)} %collective-permute-done.5, f32[4,32,512]{2,1,0:T(8,128)S(1)} %get-tuple-element.35, f32[4,32,512]{2,1,0:T(8,128)S(1)} %get-tuple-element.24, ...), kind=kLoop, calls=%fused_computation.133 | loop fusion | flops 36700144 | bytes 9175104 | tf_op jit(solution)/shard_map/reduce_sum | solution.py:87
  255.7 37.5 %psum.47 = f32[16]{0:T(128)S(1)} all-reduce(f32[16]{0:T(128)S(1)} %fusion.91), channel_id=1, replica_groups=mesh['groups'=2,'day'=16] {'day'}, use_global_device_ids=true, to_apply=%region_11.12 | all-reduce | flops 16 | bytes 128 | tf_op jit(solution)/shard_map/psum | solution.py:109
  293.2 6.5 %multiply_reduce_fusion = f32[4,32,512]{2,1,0:T(8,128)S(1)} fusion(f32[16,4,32,512]{3,2,1,0:T(8,128)} %copy-done.2, f32[16,4,32,512]{3,2,1,0:T(8,128)} %copy-done.1, s32[16,4,32,512]{3,2,1,0:T(8,128)} %param.4, f32[16]{0:T(128)S(1)} %div.49, f32[16]{0:T(128)S(1)} %div.46, f32[16]{0:T(128)S(1)} %div.43, f32[4,32,512]{2,1,0:T(8,128)S(1)} %get-tuple-element.31), kind=kLoop, calls=%fused_computation.121 | loop fusion | flops 11468800 | bytes 13107392 | tf_op jit(solution)/shard_map/reduce_sum | solution.py:117
  299.7 0.7 broadcast_multiply_fusion
  (6 shorter events, 0.0 us)
Async XLA Ops:
  0.0 9.9 %copy-start = (s32[16,4,32,512]{3,2,1,0:T(8,128)S(1)}, s32[16,4,32,512]{3,2,1,0:T(8,128)}, u32[]{:S(2)}) copy-start(s32[16,4,32,512]{3,2,1,0:T(8,128)} %param.4) | copy-start | bytes 12582916
  1.0 7.4 %collective-permute-start = (f32[1,32,512]{2,1,0:T(8,128)S(1)}, f32[1,32,512]{2,1,0:T(8,128)S(1)}, u32[]{:S(2)}, u32[]{:S(2)}) collective-permute-start(f32[1,32,512]{2,1,0:T(8,128)S(1)} %slice_bitcast_fusion.3), channel_id=1, source_target_pairs={{0,1},{1,2},{2,3},{3,4},{4,5},{5,6},{6,7},{7,8},{8,9},{9,10},{10,1... | collective-permute-start | bytes 196616 | tf_op jit(solution)/shard_map/ppermute | solution.py:16
  10.8 2.0 copy-start.3
  11.0 14.1 %collective-permute-start.1 = (f32[16,1,32,512]{3,2,1,0:T(8,128)S(1)}, f32[16,1,32,512]{3,2,1,0:T(8,128)S(1)}, u32[]{:S(2)}, u32[]{:S(2)}) collective-permute-start(f32[16,1,32,512]{3,2,1,0:T(8,128)S(1)} %get-tuple-element.18), channel_id=1, source_target_pairs={{1,0},{2,1},{3,2},{4,3},{5,4},{6,5},{7,6},{8,7},{9,8},{10,9},{11,1... | collective-permute-start | bytes 3145736 | tf_op jit(solution)/shard_map/ppermute | solution.py:28
  12.9 17.0 %collective-permute-start.2 = (f32[16,1,32,512]{3,2,1,0:T(8,128)S(1)}, f32[16,1,32,512]{3,2,1,0:T(8,128)S(1)}, u32[]{:S(2)}, u32[]{:S(2)}) collective-permute-start(f32[16,1,32,512]{3,2,1,0:T(8,128)S(1)} %get-tuple-element.19), channel_id=1, source_target_pairs={{0,1},{1,2},{2,3},{3,4},{4,5},{5,6},{6,7},{7,8},{8,9},{9,10},{10,1... | collective-permute-start | bytes 3145736 | tf_op jit(solution)/shard_map/ppermute | solution.py:25
  119.0 29.7 %copy-start.1 = (f32[16,4,32,512]{3,2,1,0:T(8,128)}, f32[16,4,32,512]{3,2,1,0:T(8,128)S(1)}, u32[]{:S(2)}) copy-start(f32[16,4,32,512]{3,2,1,0:T(8,128)S(1)} %multiply_add_fusion.1) | copy-start | bytes 12582916
  119.3 12.4 %collective-permute-start.3 = (f32[16,1,32,512]{3,2,1,0:T(8,128)S(1)}, f32[16,1,32,512]{3,2,1,0:T(8,128)S(1)}, u32[]{:S(2)}, u32[]{:S(2)}) collective-permute-start(f32[16,1,32,512]{3,2,1,0:T(8,128)S(1)} %get-tuple-element.16), channel_id=1, source_target_pairs={{1,0},{2,1},{3,2},{4,3},{5,4},{6,5},{7,6},{8,7},{9,8},{10,9},{11,1... | collective-permute-start | bytes 3145736 | tf_op jit(solution)/shard_map/ppermute | solution.py:28
  119.4 17.1 %collective-permute-start.4 = (f32[16,1,32,512]{3,2,1,0:T(8,128)S(1)}, f32[16,1,32,512]{3,2,1,0:T(8,128)S(1)}, u32[]{:S(2)}, u32[]{:S(2)}) collective-permute-start(f32[16,1,32,512]{3,2,1,0:T(8,128)S(1)} %get-tuple-element.17), channel_id=1, source_target_pairs={{0,1},{1,2},{2,3},{3,4},{4,5},{5,6},{6,7},{7,8},{8,9},{9,10},{10,1... | collective-permute-start | bytes 3145736 | tf_op jit(solution)/shard_map/ppermute | solution.py:25
  226.6 17.6 %copy-start.2 = (f32[16,4,32,512]{3,2,1,0:T(8,128)}, f32[16,4,32,512]{3,2,1,0:T(8,128)S(1)}, u32[]{:S(2)}) copy-start(f32[16,4,32,512]{3,2,1,0:T(8,128)S(1)} %multiply_add_fusion) | copy-start | bytes 12582916
  226.9 12.4 %collective-permute-start.5 = (f32[16,1,32,512]{3,2,1,0:T(8,128)S(1)}, f32[16,1,32,512]{3,2,1,0:T(8,128)S(1)}, u32[]{:S(2)}, u32[]{:S(2)}) collective-permute-start(f32[16,1,32,512]{3,2,1,0:T(8,128)S(1)} %get-tuple-element.14), channel_id=1, source_target_pairs={{1,0},{2,1},{3,2},{4,3},{5,4},{6,5},{7,6},{8,7},{9,8},{10,9},{11,1... | collective-permute-start | bytes 3145736 | tf_op jit(solution)/shard_map/ppermute | solution.py:28
  227.0 17.3 %collective-permute-start.6 = (f32[16,1,32,512]{3,2,1,0:T(8,128)S(1)}, f32[16,1,32,512]{3,2,1,0:T(8,128)S(1)}, u32[]{:S(2)}, u32[]{:S(2)}) collective-permute-start(f32[16,1,32,512]{3,2,1,0:T(8,128)S(1)} %get-tuple-element.15), channel_id=1, source_target_pairs={{0,1},{1,2},{2,3},{3,4},{4,5},{5,6},{6,7},{7,8},{8,9},{9,10},{10,1... | collective-permute-start | bytes 3145736 | tf_op jit(solution)/shard_map/ppermute | solution.py:25
where the time goes:
time: 301 us; the launch traced here: 300 us
  blocking collectives  170 us (56%)
  other arithmetic  71.1 us (24%)
  waiting for transfers between devices  53.6 us (18%)
  starting transfers between devices  3.38 us (1%)
    psum x3, blocking collectives, norm_sum(): return lax.psum(summed(residual, scaled), 'day')  94.5 us
    psum x2, blocking collectives, body(): step_len = norm_now / lax.psum(summed(direction, image), 'day')  75.1 us
    reduce_sum x5, other arithmetic, summed(): return jnp.sum(first * second, axis=(1, 2, 3))  47.6 us
    ppermute x3, waiting for transfers between devices, extended(): lax.ppermute(lax.slice_in_dim(block, 0, width, axis=dim), axis, backward)  35.7 us
    ppermute x3, waiting for transfers between devices, extended(): lax.ppermute(lax.slice_in_dim(block, block.shape[dim] - width, None, axis...  14.4 us
    add x2, other arithmetic, body(): direction = scaled + spread(norm_next / norm_now) * direction  11.1 us
    reduce_sum x1, other arithmetic, body(): return jnp.sum(signs * estimate, axis=0) / probes_n  6.5 us
  transfers between devices with their start and end apart: 7, of which 7 were waited for; matrix products, arithmetic and copies ran while one was open for 1% of the time, Pallas kernels for 0%

commit v1 on v0

v1 whole, which is shorter than its diff:
```python
import functools

import jax
import jax.numpy as jnp
from jax import lax
from jax.experimental import pallas as pl
from jax.experimental.pallas import tpu as pltpu
from jax.sharding import PartitionSpec as P

LINK_OFFSETS = ((0, 1), (1, 0), (1, 1), (1, -1))
COASTAL_FACTOR = 0.2
F32 = jnp.float32


def passed_along(value, steps):
    count = lax.axis_size("day")
    return lax.ppermute(value, "day", [(i, (i + steps) % count) for i in range(count)])


def turned(value, step_row, step_col):
    rows, cols = value.shape
    if step_col:
        value = pltpu.roll(value, step_col % cols, 1)
    if step_row:
        value = pltpu.roll(value, step_row % rows, 0)
    return value


PLANES = 8


def planes_kernel(coup_ref, mask_ref, planes_ref, part_ref):
    days, rows, cols = coup_ref.shape[1:]
    mask = mask_ref[...]
    row = lax.broadcasted_iota(jnp.int32, (rows, cols), 0)
    col = lax.broadcasted_iota(jnp.int32, (rows, cols), 1)
    factors = []
    for step_row, step_col in LINK_OFFSETS:
        same = mask == turned(mask, -step_row, -step_col)
        inside = (row + step_row < rows) & (col + step_col < cols) & (col + step_col >= 0)
        factors.append(jnp.where(inside, jnp.where(same, 1.0, COASTAL_FACTOR), 0.0))
    for d in range(days):
        east, south, se, sw = (coup_ref[n + 1, d] * factors[n] for n in range(4))
        west = turned(east, 0, 1)
        se_w = turned(se, 0, 1)
        sw_e = turned(sw, 0, -1)
        above = turned(south, 1, 0)
        part = coup_ref[0, d] + coup_ref[5, d]
        if d:
            part = part + coup_ref[5, d - 1]
        part = part + east + west + south + above
        part = part + se + turned(se_w, 1, 0) + sw + turned(sw_e, 1, 0)
        part_ref[d] = part
        for n, plane in enumerate(
            (east, west, south, se_w, sw_e, above, turned(se, 1, 0), turned(sw, 1, 0))
        ):
            planes_ref[n, d] = plane


def lower_half(v, v_east, v_west, planes_ref, d):
    down = planes_ref[2, d] * v + planes_ref[3, d] * v_west + planes_ref[4, d] * v_east
    return planes_ref[0, d] * v_east + turned(down, 1, 0)


def upper_half(v, v_east, v_west, planes_ref, d):
    up = planes_ref[5, d] * v + planes_ref[6, d] * v_east + planes_ref[7, d] * v_west
    return planes_ref[1, d] * v_west + turned(up, -1, 0)


def coupled(v, planes_ref, d):
    v_east, v_west = turned(v, 0, -1), turned(v, 0, 1)
    return lower_half(v, v_east, v_west, planes_ref, d) + upper_half(v, v_east, v_west, planes_ref, d)


def local_apply(field, ahead, dinv, planes_ref, d):
    days = planes_ref.shape[1]
    result = coupled(field(d), planes_ref, d)
    if d + 1 < days:
        result = result + ahead(d) * field(d + 1)
    if d:
        result = result + ahead(d - 1) * field(d - 1)
    return result * dinv(d)


def first_kernel(bits_ref, planes_ref, ahead_ref, before_ref, part_ref,
                 w1_ref, low_ref, high_ref, diag_ref, dinv_ref, w0_ref):
    per, days = bits_ref.shape[:2]

    @pl.when(pl.program_id(0) == 0)
    def _():
        for d in range(days):
            diag = part_ref[d]
            if d == 0:
                diag = diag + before_ref[...]
            diag_ref[d] = diag
            dinv_ref[d] = 1.0 / diag

    def probe(k, carry):
        for d in range(days):
            w0_ref[d] = jnp.where(bits_ref[k, d] == 1, dinv_ref[d], -dinv_ref[d])
        for d in range(days):
            w1 = local_apply(lambda t: w0_ref[t], lambda t: ahead_ref[t],
                             lambda t: dinv_ref[t], planes_ref, d)
            w1_ref[k, d] = w1
            if d == 0:
                low_ref[k] = w1
            if d == days - 1:
                high_ref[k] = w1
        return carry

    lax.fori_loop(0, per, probe, 0)


def second_kernel(w1_ref, prev_ref, next_ref, planes_ref, ahead_ref, before_ref, dinv_ref,
                  dprev_ref, dnext_ref, w1c_ref, w2_ref, high_ref):
    per, days = w1_ref.shape[:2]
    last = days - 1

    def probe(k, carry):
        for d in range(days):
            w1 = w1_ref[k, d]
            if d == 0:
                scale = before_ref[...] * dinv_ref[0] * dprev_ref[...]
                w1 = w1 + jnp.where(prev_ref[k] == 1, scale, -scale)
            if d == last:
                scale = ahead_ref[last] * dinv_ref[last] * dnext_ref[...]
                w1 = w1 + jnp.where(next_ref[k] == 1, scale, -scale)
            w1c_ref[k, d] = w1
        for d in range(days):
            w2 = local_apply(lambda t: w1c_ref[k, t], lambda t: ahead_ref[t],
                             lambda t: dinv_ref[t], planes_ref, d)
            w2_ref[k, d] = w2
            if d == last:
                high_ref[k] = w2
        return carry

    lax.fori_loop(0, per, probe, 0)


def folded(value):
    cols = value.shape[1]
    total = value[:, :128]
    for start in range(128, cols, 128):
        total = total + value[:, start : start + 128]
    return jnp.sum(total, axis=0, keepdims=True)


def third_kernel(bits_ref, w1_ref, w2_ref, low_ref, high_ref, planes_ref, ahead_ref, before_ref,
                 diag_ref, dinv_ref, dprev_ref, dnext_ref, p1_ref, p2_ref, cross_ref, sums_ref,
                 w2c_ref):
    per, days = bits_ref.shape[:2]
    last = days - 1

    def probe(k, carry):
        n1 = n2 = n3 = n4 = n5 = 0.0
        for d in range(days):
            sign = (2 * bits_ref[k, d] - 1).astype(F32)
            w1 = w1_ref[k, d]
            w2 = w2_ref[k, d]
            if d == 0:
                w1_prev = low_ref[k] + dprev_ref[...] * before_ref[...] * (sign * dinv_ref[0])
                w2 = w2 + dinv_ref[0] * before_ref[...] * w1_prev
                cross = before_ref[...] * w2
                cross_ref[k] = cross
                n5 = n5 + 2.0 * (cross * (dprev_ref[...] * before_ref[...] * w1))
            if d == last:
                w1_next = high_ref[k] + dnext_ref[...] * ahead_ref[last] * (sign * dinv_ref[last])
                w2 = w2 + dinv_ref[last] * ahead_ref[last] * w1_next
            w2c_ref[d] = w2
            p1 = sign * w1
            p1_ref[k, d] = p1
            p2_ref[k, d] = sign * w2
            scaled = diag_ref[d] * w2
            n1 = n1 + p1
            n2 = n2 + diag_ref[d] * w1 * w1
            n3 = n3 + scaled * w1
            n4 = n4 + scaled * w2
            if d:
                n5 = n5 + 2.0 * (ahead_ref[d - 1] * w2c_ref[d - 1] * w2)
            v_east, v_west = turned(w2, 0, -1), turned(w2, 0, 1)
            n5 = n5 + 2.0 * (w2 * lower_half(w2, v_east, v_west, planes_ref, d))
        n0 = dinv_ref[0]
        for d in range(1, days):
            n0 = n0 + dinv_ref[d]
        zero = jnp.zeros((1, 128), F32)
        rows = [folded(n) for n in (n0, n1, n2, n3, n4, n5)] + [zero, zero]
        sums_ref[k] = jnp.concatenate(rows, axis=0)
        return carry

    lax.fori_loop(0, per, probe, 0)


def fourth_kernel(cross_ref, high_ref, sums_ref, moments_ref):
    probes = cross_ref.shape[0]
    lane = lax.broadcasted_iota(jnp.int32, (8, 128), 1)
    row = lax.broadcasted_iota(jnp.int32, (8, 128), 0)
    result = jnp.zeros((8, 128), F32)
    for k in range(probes):
        extra = 2.0 * folded(cross_ref[k] * high_ref[k])
        sums = sums_ref[k] + jnp.where(row == 5, extra, 0.0)
        result = jnp.where(lane == k, jnp.sum(sums, axis=1, keepdims=True), result)
    moments_ref[...] = result


def coefficients(moments, probes):
    lane = lax.broadcasted_iota(jnp.int32, (1, 128), 1)
    live = lane < probes
    n0, n1, n2, n3, n4, n5 = (jnp.where(live, moments[j : j + 1], 1.0) for j in range(6))
    a0 = n1 / n0
    s11 = jnp.maximum(n2 - a0 * n1, 1e-7 * n2 + 1e-30)
    s12 = n3 - a0 * n2
    s13 = n4 - a0 * n3
    s14 = n5 - a0 * n4
    a1 = jnp.clip(s12 / s11 - a0, -1.0, 0.999)
    b1 = s11 / n0
    s22 = jnp.maximum(s13 - a1 * s12 - b1 * n2, 1e-7 * n4 + 1e-30)
    s23 = s14 - a1 * s13 - b1 * n3
    a2 = jnp.clip(s23 / s22 - s12 / s11, -1.0, 0.999)
    b2 = s22 / s11
    e2 = 1.0 - a2
    e1 = (1.0 - a1) - b2 / e2
    e0 = (1.0 - a0) - b1 / e1
    y0 = 1.0 / e0
    y1 = y0 / e1
    y2 = y1 / e2
    scale = jnp.where(live, 1.0 / probes, 0.0)
    return (
        scale * (y0 - a0 * y1 + (a0 * a1 - b1) * y2),
        scale * (y1 - (a0 + a1) * y2),
        scale * y2,
    )


def last_kernel(moments_ref, p1_ref, p2_ref, dinv_ref, out_ref):
    probes, days = p1_ref.shape[:2]
    c0, c1, c2 = coefficients(moments_ref[...], probes)
    c0 = jnp.sum(c0, axis=1, keepdims=True)
    for d in range(days):
        total = c0 * dinv_ref[d]
        for k in range(probes):
            total = total + (c1[:, k : k + 1] * p1_ref[k, d] + c2[:, k : k + 1] * p2_ref[k, d])
        out_ref[d] = total


def call(kernel, grid, ins, outs, scratch=(), cost=None, limit=None):
    in_specs = [spec for _, spec in ins]
    return pl.pallas_call(
        kernel,
        grid=grid,
        in_specs=in_specs,
        out_specs=[spec for _, spec in outs],
        out_shape=[jax.ShapeDtypeStruct(shape, F32) for shape, _ in outs],
        scratch_shapes=list(scratch),
        cost_estimate=cost,
        compiler_params=pltpu.CompilerParams(vmem_limit_bytes=limit),
    )(*[value for value, _ in ins])


def split(shape, per):
    return pl.BlockSpec((per,) + tuple(shape[1:]), lambda i: (i,) + (0,) * (len(shape) - 1))


def whole(shape):
    return pl.BlockSpec(tuple(shape), lambda i: (0,) * len(shape))


def body(couplings, probe_bits, land_mask):
    probes, days, rows, cols = probe_bits.shape
    count = lax.axis_size("day")
    plane = (rows, cols)
    field = (probes, days, rows, cols)
    edge = (probes, rows, cols)
    per = 2
    grid = (probes // per,)
    limit = 40 << 20
    mib = field[0] * field[1] * field[2] * field[3] * 4

    def cost(stencils, fields):
        return pl.CostEstimate(flops=stencils * mib * 6, bytes_accessed=fields * mib, transcendentals=0)

    before = passed_along(couplings[5, days - 1], 1)
    bits_next = passed_along(probe_bits[:, 0], -1)
    bits_prev = passed_along(probe_bits[:, days - 1], 1)

    shape8 = (PLANES, days) + plane
    planes, part = call(
        planes_kernel, (1,),
        [(couplings, whole(couplings.shape)), (land_mask, whole(plane))],
        [(shape8, whole(shape8)), ((days,) + plane, whole((days,) + plane))],
        cost=cost(1, 1), limit=limit,
    )
    ahead = couplings[5]
    dplanes = (days,) + plane
    w1, low, high, diag, dinv = call(
        first_kernel, grid,
        [(probe_bits, split(field, per)), (planes, whole(shape8)), (ahead, whole(dplanes)),
         (before, whole(plane)), (part, whole(dplanes))],
        [(field, split(field, per)), (edge, split(edge, per)), (edge, split(edge, per)),
         (dplanes, whole(dplanes)), (dplanes, whole(dplanes))],
        scratch=[pltpu.VMEM(dplanes, F32)], cost=cost(1, 2), limit=limit,
    )
    dprev = passed_along(dinv[days - 1], 1)
    dnext = passed_along(dinv[0], -1)
    high_prev = passed_along(high, 1)
    low_next = passed_along(low, -1)

    w1c, w2, high2 = call(
        second_kernel, grid,
        [(w1, split(field, per)), (bits_prev, split(edge, per)), (bits_next, split(edge, per)),
         (planes, whole(shape8)), (ahead, whole(dplanes)), (before, whole(plane)),
         (dinv, whole(dplanes)), (dprev, whole(plane)), (dnext, whole(plane))],
        [(field, split(field, per)), (field, split(field, per)), (edge, split(edge, per))],
        cost=cost(1, 3), limit=limit,
    )
    high2_prev = passed_along(high2, 1)

    sums_shape = (probes, 8, 128)
    p1, p2, cross, sums = call(
        third_kernel, grid,
        [(probe_bits, split(field, per)), (w1c, split(field, per)), (w2, split(field, per)),
         (high_prev, split(edge, per)), (low_next, split(edge, per)), (planes, whole(shape8)),
         (ahead, whole(dplanes)), (before, whole(plane)), (diag, whole(dplanes)),
         (dinv, whole(dplanes)), (dprev, whole(plane)), (dnext, whole(plane))],
        [(field, split(field, per)), (field, split(field, per)), (edge, split(edge, per)),
         (sums_shape, split(sums_shape, per))],
        scratch=[pltpu.VMEM(dplanes, F32)], cost=cost(1, 5), limit=limit,
    )
    (moments,) = call(
        fourth_kernel, (1,),
        [(cross, whole(edge)), (high2_prev, whole(edge)), (sums, whole(sums_shape))],
        [((8, 128), whole((8, 128)))],
        cost=pl.CostEstimate(flops=mib, bytes_accessed=mib // 2, transcendentals=0), limit=limit,
    )
    step = 1
    while step < count:
        moments = moments + lax.ppermute(moments, "day", [(i, i ^ step) for i in range(count)])
        step *= 2

    (out,) = call(
        last_kernel, (1,),
        [(moments, whole((8, 128))), (p1, whole(field)), (p2, whole(field)), (dinv, whole(dplanes))],
        [(dplanes, whole(dplanes))],
        cost=cost(1, 2), limit=limit,
    )
    return out


def solution(mesh):
    assert mesh.shape["day"] & (mesh.shape["day"] - 1) == 0
    return jax.shard_map(
        body,
        mesh=mesh,
        in_specs=(
            P(None, ("groups", "day"), None, None),
            P(None, ("groups", "day"), None, None),
            P("groups", None),
        ),
        out_specs=P(("groups", "day"), None, None),
        check_vma=False,
    )
```

time: 301 us -> 105 us (0.35)
  blocking collectives: 170 us -> 0 us
  other arithmetic: 71.1 us -> 0.01 us
  starting transfers between devices: 3.38 us -> 29.3 us
  Pallas kernels: 0 us -> 25.8 us
  waiting for transfers between devices: 53.6 us -> 36.1 us
  local copies, waits for them, and re-layouts: 2.67 us -> 13.3 us
    psum x5 -> x0, blocking collectives: 170 us -> none  [the longest x3 94.5 us: norm_sum(): return lax.psum(summed(residual, scaled), 'day')]
    reduce_sum x6 -> x0, other arithmetic: 54.1 us -> none  [the longest x5 47.6 us: summed(): return jnp.sum(first * second, axis=(1, 2, 3))]
    ppermute x7 -> x12, starting transfers between devices: 3.38 us -> 29.3 us  [the longest x8 15.6 us: passed_along(): lax.ppermute(value, 'day', [(i, (i + steps) % count) for i in range(count)])]
    pallas_call x0 -> x6, Pallas kernels: none -> 25.8 us  [call(): pl.pallas_call(kernel, grid=grid, in_specs=in_specs, out_specs=[spec for...]
    ppermute x7 -> x12, waiting for transfers between devices: 53.6 us -> 36.1 us  [the longest x8 28.1 us: passed_along(): lax.ppermute(value, 'day', [(i, (i + steps) % count) for i in range(count)])]
    add x2 -> x4, other arithmetic: 11.1 us -> 0.01 us  [body(): moments + lax.ppermute(moments, 'day', [(i, i ^ step) for i in range(coun...]
    unnamed x8 -> x14, local copies, waits for them, and re-layouts: 0.02 us -> 9.47 us
  transfers between devices with their start and end apart: 7 -> 12, of which waited for: 7 -> 7; matrix products, arithmetic and copies ran while one was open for 1% -> 2% of each run, Pallas kernels for 0% -> 23%
where the time goes in v1:
time: 105 us
  waiting for transfers between devices  36.1 us (34%)
  starting transfers between devices  29.3 us (28%)
  Pallas kernels  25.8 us (25%)
  local copies, waits for them, and re-layouts  13.3 us (13%)
    ppermute x8, waiting for transfers between devices, passed_along(): lax.ppermute(value, 'day', [(i, (i + steps) % count) for i in range(count)])  28.1 us
    pallas_call x6, Pallas kernels, call(): pl.pallas_call(kernel, grid=grid, in_specs=in_specs, out_specs=[spec for...  25.8 us
    ppermute x8, starting transfers between devices, passed_along(): lax.ppermute(value, 'day', [(i, (i + steps) % count) for i in range(count)])  15.6 us
    ppermute x4, starting transfers between devices, body(): lax.ppermute(moments, 'day', [(i, i ^ step) for i in range(count)])  13.7 us
    unnamed x14, local copies, waits for them, and re-layouts  9.47 us
    ppermute x4, waiting for transfers between devices, body(): lax.ppermute(moments, 'day', [(i, i ^ step) for i in range(count)])  7.93 us
  transfers between devices with their start and end apart: 12, of which 7 were waited for; matrix products, arithmetic and copies ran while one was open for 2% of the time, Pallas kernels for 23%

profile of v1, /device:TPU:0, one launch (start us, length us, event | category | flops | bytes accessed | tf_op | source)
XLA Modules:
  0.0 104.6 jit_solution(3681260441289305577)
XLA Ops:
  0.0 0.0 copy-start
  0.0 0.0 copy-start.6
  0.0 2.0 %slice_bitcast_fusion = (s32[16,32,512]{2,1,0:T(8,128)S(1)}, s32[16,32,512]{2,1,0:T(8,128)S(1)}) fusion(s32[16,4,32,512]{3,2,1,0:T(8,128)} %bits_ref.3), kind=kLoop, calls=%fused_computation | loop fusion | bytes 4194304 | tf_op jit(solution)/shard_map/squeeze | solution.py:282
  2.0 5.5 %collective-permute-start.2 = (s32[16,32,512]{2,1,0:T(8,128)S(1)}, s32[16,32,512]{2,1,0:T(8,128)S(1)}, u32[]{:S(2)}, u32[]{:S(2)}) collective-permute-start(s32[16,32,512]{2,1,0:T(8,128)S(1)} %get-tuple-element.33), channel_id=1, source_target_pairs={{0,15},{1,0},{2,1},{3,2},{4,3},{5,4},{6,5},{7,6},{8,7},{9,8},{10,9... | collective-permute-start | bytes 3145736 | tf_op jit(solution)/shard_map/ppermute | solution.py:17
  7.5 0.0 collective-permute-start.1
  7.5 0.8 slice_bitcast_fusion.5
  8.3 0.0 collective-permute-start
  8.3 1.0 slice_bitcast_fusion.2.ahead_ref
  9.3 0.0 copy-done.6
  9.3 0.0 copy-start.5
  9.3 1.4 %copy-done.5 = f32[6,4,32,512]{3,2,1,0:T(8,128)S(1)} copy-done((f32[6,4,32,512]{3,2,1,0:T(8,128)S(1)}, f32[6,4,32,512]{3,2,1,0:T(8,128)}, u32[]{:S(2)}) %copy-start.5) | copy-done | bytes 1572888
  10.7 0.4 shard_map.37
  11.1 14.1 %collective-permute-done.before_ref = f32[32,512]{1,0:T(8,128)S(1)} collective-permute-done((f32[32,512]{1,0:T(8,128)S(1)}, f32[32,512]{1,0:T(8,128)S(1)}, u32[]{:S(2)}, u32[]{:S(2)}) %collective-permute-start) | collective-permute-done | bytes 65568 | tf_op jit(solution)/shard_map/ppermute | solution.py:17
  25.2 0.0 copy-done
  25.2 5.0 %shard_map.38 = (f32[16,4,32,512]{3,2,1,0:T(8,128)S(1)}, f32[16,32,512]{2,1,0:T(8,128)S(1)}, f32[16,32,512]{2,1,0:T(8,128)S(1)}, f32[4,32,512]{2,1,0:T(8,128)S(1)}, f32[4,32,512]{2,1,0:T(8,128)S(1)}) custom-call(s32[16,4,32,512]{3,2,1,0:T(8,128)S(1)} %copy-done, f32[8,4,32,512]{3,2,1,0:T(8,128)S(1)} %get-tuple-element.19.planes_ref, ...), custom_call_target="tpu_custom_call" | custom-call | flops 25165824 | bytes 8388608 | tf_op jit(solution)/shard_map/pallas_call | solution.py:247
  30.3 0.0 copy-start.2
  30.3 1.9 %copy-done.2 = f32[16,4,32,512]{3,2,1,0:T(8,128)} copy-done((f32[16,4,32,512]{3,2,1,0:T(8,128)}, f32[16,4,32,512]{3,2,1,0:T(8,128)S(1)}, u32[]{:S(2)}) %copy-start.2) | copy-done | bytes 4194328
  32.2 0.1 collective-permute-start.4
  32.3 3.7 %collective-permute-start.3 = (f32[32,512]{1,0:T(8,128)S(1)}, f32[32,512]{1,0:T(8,128)S(1)}, u32[]{:S(2)}, u32[]{:S(2)}) collective-permute-start(f32[32,512]{1,0:T(8,128)S(1)} %get-tuple-element.36), channel_id=1, source_target_pairs={{0,1},{1,2},{2,3},{3,4},{4,5},{5,6},{6,7},{7,8},{8,9},{9,10},{10,1... | collective-permute-start | bytes 196616 | tf_op jit(solution)/shard_map/ppermute | solution.py:17
  36.0 2.5 %collective-permute-start.5 = (f32[16,32,512]{2,1,0:T(8,128)S(1)}, f32[16,32,512]{2,1,0:T(8,128)S(1)}, u32[]{:S(2)}, u32[]{:S(2)}) collective-permute-start(f32[16,32,512]{2,1,0:T(8,128)S(1)} %get-tuple-element.25), channel_id=1, source_target_pairs={{0,1},{1,2},{2,3},{3,4},{4,5},{5,6},{6,7},{7,8},{8,9},{9,10},{10,1... | collective-permute-start | bytes 3145736 | tf_op jit(solution)/shard_map/ppermute | solution.py:17
  38.5 0.0 collective-permute-done.4.dnext_ref
  38.5 3.9 %collective-permute-start.6 = (f32[16,32,512]{2,1,0:T(8,128)S(1)}, f32[16,32,512]{2,1,0:T(8,128)S(1)}, u32[]{:S(2)}, u32[]{:S(2)}) collective-permute-start(f32[16,32,512]{2,1,0:T(8,128)S(1)} %get-tuple-element.26), channel_id=1, source_target_pairs={{0,15},{1,0},{2,1},{3,2},{4,3},{5,4},{6,5},{7,6},{8,7},{9,8},{10,9... | collective-permute-start | bytes 3145736 | tf_op jit(solution)/shard_map/ppermute | solution.py:17
  42.3 1.0 collective-permute-done.3.dprev_ref
  43.4 0.0 collective-permute-done.2.next_ref
  43.4 0.0 collective-permute-done.1.prev_ref
  43.4 7.7 %shard_map.39 = (f32[16,4,32,512]{3,2,1,0:T(8,128)S(1)}, f32[16,4,32,512]{3,2,1,0:T(8,128)S(1)}, f32[16,32,512]{2,1,0:T(8,128)S(1)}) custom-call(f32[16,4,32,512]{3,2,1,0:T(8,128)} %copy-done.2, s32[16,32,512]{2,1,0:T(8,128)S(1)} %collective-permute-done.1.prev_ref, s32[16,32,512]{2,1,0:T(8,128)S(1)} %collective-permute-done.2.next_ref, ...), custom_call_target="tpu_custom_call" | custom-call | flops 25165824 | bytes 12582912 | tf_op jit(solution)/shard_map/pallas_call | solution.py:247
  51.1 0.0 copy-start.3
  51.1 1.9 %copy-done.3 = f32[16,4,32,512]{3,2,1,0:T(8,128)} copy-done((f32[16,4,32,512]{3,2,1,0:T(8,128)}, f32[16,4,32,512]{3,2,1,0:T(8,128)S(1)}, u32[]{:S(2)}) %copy-start.3) | copy-done | bytes 4194328
  53.0 0.0 copy-start.4
  53.0 2.0 %copy-done.4 = f32[16,4,32,512]{3,2,1,0:T(8,128)} copy-done((f32[16,4,32,512]{3,2,1,0:T(8,128)}, f32[16,4,32,512]{3,2,1,0:T(8,128)S(1)}, u32[]{:S(2)}) %copy-start.4) | copy-done | bytes 4194328
  55.0 0.0 collective-permute-start.7
  55.0 0.0 collective-permute-done.5.low_ref
  55.0 0.0 collective-permute-done.6.high_ref
  55.0 11.0 %shard_map.40 = (f32[16,4,32,512]{3,2,1,0:T(8,128)S(1)}, f32[16,4,32,512]{3,2,1,0:T(8,128)}, f32[16,32,512]{2,1,0:T(8,128)S(1)}, f32[16,8,128]{2,1,0:T(8,128)S(1)}) custom-call(s32[16,4,32,512]{3,2,1,0:T(8,128)} %bits_ref.3, f32[16,4,32,512]{3,2,1,0:T(8,128)} %copy-done.3, f32[16,4,32,512]{3,2,1,0:T(8,128)} %copy-done.4, ...), custom_call_target="tpu_custom_call" | custom-call | flops 25165824 | bytes 20971520 | tf_op jit(solution)/shard_map/pallas_call | solution.py:247
  66.0 13.0 %collective-permute-done.7.high_ref = f32[16,32,512]{2,1,0:T(8,128)S(1)} collective-permute-done((f32[16,32,512]{2,1,0:T(8,128)S(1)}, f32[16,32,512]{2,1,0:T(8,128)S(1)}, u32[]{:S(2)}, u32[]{:S(2)}) %collective-permute-start.7) | collective-permute-done | bytes 1048608 | tf_op jit(solution)/shard_map/ppermute | solution.py:17
  79.0 0.2 shard_map.41
  79.2 0.0 collective-permute-start.8
  79.3 1.2 %collective-permute-done.8 = f32[8,128]{1,0:T(8,128)S(1)} collective-permute-done((f32[8,128]{1,0:T(8,128)S(1)}, f32[8,128]{1,0:T(8,128)S(1)}, u32[]{:S(2)}, u32[]{:S(2)}) %collective-permute-start.8) | collective-permute-done | bytes 4128 | tf_op jit(solution)/shard_map/ppermute | solution.py:336
  80.4 0.0 collective-permute-start.9
  80.4 3.6 %collective-permute-done.9 = f32[8,128]{1,0:T(8,128)S(1)} collective-permute-done((f32[8,128]{1,0:T(8,128)S(1)}, f32[8,128]{1,0:T(8,128)S(1)}, u32[]{:S(2)}, u32[]{:S(2)}) %collective-permute-start.9) | collective-permute-done | bytes 4128 | tf_op jit(solution)/shard_map/ppermute | solution.py:336
  84.0 10.6 %collective-permute-start.10 = (f32[8,128]{1,0:T(8,128)S(1)}, f32[8,128]{1,0:T(8,128)S(1)}, u32[]{:S(2)}, u32[]{:S(2)}) collective-permute-start(f32[8,128]{1,0:T(8,128)S(1)} %add.13), channel_id=1, source_target_pairs={{0,4},{1,5},{2,6},{3,7},{4,0},{5,1},{6,2},{7,3},{8,12},{9,13},{10,... | collective-permute-start | bytes 12296 | tf_op jit(solution)/shard_map/ppermute | solution.py:336
  94.7 1.6 %collective-permute-done.10 = f32[8,128]{1,0:T(8,128)S(1)} collective-permute-done((f32[8,128]{1,0:T(8,128)S(1)}, f32[8,128]{1,0:T(8,128)S(1)}, u32[]{:S(2)}, u32[]{:S(2)}) %collective-permute-start.10) | collective-permute-done | bytes 4128 | tf_op jit(solution)/shard_map/ppermute | solution.py:336
  96.2 3.0 %collective-permute-start.11 = (f32[8,128]{1,0:T(8,128)S(1)}, f32[8,128]{1,0:T(8,128)S(1)}, u32[]{:S(2)}, u32[]{:S(2)}) collective-permute-start(f32[8,128]{1,0:T(8,128)S(1)} %add.14), channel_id=1, source_target_pairs={{0,8},{1,9},{2,10},{3,11},{4,12},{5,13},{6,14},{7,15},{8,0},{9,1},... | collective-permute-start | bytes 12296 | tf_op jit(solution)/shard_map/ppermute | solution.py:336
  99.3 1.6 %collective-permute-done.11 = f32[8,128]{1,0:T(8,128)S(1)} collective-permute-done((f32[8,128]{1,0:T(8,128)S(1)}, f32[8,128]{1,0:T(8,128)S(1)}, u32[]{:S(2)}, u32[]{:S(2)}) %collective-permute-start.11) | collective-permute-done | bytes 4128 | tf_op jit(solution)/shard_map/ppermute | solution.py:336
  100.9 0.0 copy-start.1
  100.9 2.2 %copy-done.1 = f32[16,4,32,512]{3,2,1,0:T(8,128)S(1)} copy-done((f32[16,4,32,512]{3,2,1,0:T(8,128)S(1)}, f32[16,4,32,512]{3,2,1,0:T(8,128)}, u32[]{:S(2)}) %copy-start.1) | copy-done | bytes 4194328
  103.1 1.5 %shard_map.42 = f32[4,32,512]{2,1,0:T(8,128)} custom-call(f32[8,128]{1,0:T(8,128)S(1)} %add.15.moments_ref, f32[16,4,32,512]{3,2,1,0:T(8,128)S(1)} %get-tuple-element.31.p1_ref, f32[16,4,32,512]{3,2,1,0:T(8,128)S(1)} %copy-done.1, f32[4,32,512]{2,1,0:T(8,128)S(1)} %get-tuple-element.22.dinv_ref), custom_call_target="tpu_custom_call" | custom-call | flops 25165824 | bytes 8388608 | tf_op jit(solution)/shard_map/pallas_call | solution.py:247
  (5 shorter events, 0.0 us)
Async XLA Ops:
  0.0 25.2 %copy-start = (s32[16,4,32,512]{3,2,1,0:T(8,128)S(1)}, s32[16,4,32,512]{3,2,1,0:T(8,128)}, u32[]{:S(2)}) copy-start(s32[16,4,32,512]{3,2,1,0:T(8,128)} %bits_ref.3) | copy-start | bytes 12582916
  0.0 9.3 %copy-start.6 = (s32[32,512]{1,0:T(8,128)S(1)}, s32[32,512]{1,0:T(8,128)}, u32[]{:S(2)}) copy-start(s32[32,512]{1,0:T(8,128)} %mask_ref.1) | copy-start | bytes 196612
  2.0 41.4 %collective-permute-start.2 = (s32[16,32,512]{2,1,0:T(8,128)S(1)}, s32[16,32,512]{2,1,0:T(8,128)S(1)}, u32[]{:S(2)}, u32[]{:S(2)}) collective-permute-start(s32[16,32,512]{2,1,0:T(8,128)S(1)} %get-tuple-element.33), channel_id=1, source_target_pairs={{0,15},{1,0},{2,1},{3,2},{4,3},{5,4},{6,5},{7,6},{8,7},{9,8},{10,9... | collective-permute-start | bytes 3145736 | tf_op jit(solution)/shard_map/ppermute | solution.py:17
  7.5 35.9 %collective-permute-start.1 = (s32[16,32,512]{2,1,0:T(8,128)S(1)}, s32[16,32,512]{2,1,0:T(8,128)S(1)}, u32[]{:S(2)}, u32[]{:S(2)}) collective-permute-start(s32[16,32,512]{2,1,0:T(8,128)S(1)} %get-tuple-element.34), channel_id=1, source_target_pairs={{0,1},{1,2},{2,3},{3,4},{4,5},{5,6},{6,7},{7,8},{8,9},{9,10},{10,1... | collective-permute-start | bytes 3145736 | tf_op jit(solution)/shard_map/ppermute | solution.py:17
  8.3 16.9 %collective-permute-start = (f32[32,512]{1,0:T(8,128)S(1)}, f32[32,512]{1,0:T(8,128)S(1)}, u32[]{:S(2)}, u32[]{:S(2)}) collective-permute-start(f32[32,512]{1,0:T(8,128)S(1)} %slice_bitcast_fusion.5), channel_id=1, source_target_pairs={{0,1},{1,2},{2,3},{3,4},{4,5},{5,6},{6,7},{7,8},{8,9},{9,10},{10,1... | collective-permute-start | bytes 196616 | tf_op jit(solution)/shard_map/ppermute | solution.py:17
  9.3 1.4 %copy-start.5 = (f32[6,4,32,512]{3,2,1,0:T(8,128)S(1)}, f32[6,4,32,512]{3,2,1,0:T(8,128)}, u32[]{:S(2)}) copy-start(f32[6,4,32,512]{3,2,1,0:T(8,128)} %coup_ref.1) | copy-start | bytes 4718596
  30.3 1.9 %copy-start.2 = (f32[16,4,32,512]{3,2,1,0:T(8,128)}, f32[16,4,32,512]{3,2,1,0:T(8,128)S(1)}, u32[]{:S(2)}) copy-start(f32[16,4,32,512]{3,2,1,0:T(8,128)S(1)} %get-tuple-element.21.w1_ref) | copy-start | bytes 12582916
  32.2 6.3 %collective-permute-start.4 = (f32[32,512]{1,0:T(8,128)S(1)}, f32[32,512]{1,0:T(8,128)S(1)}, u32[]{:S(2)}, u32[]{:S(2)}) collective-permute-start(f32[32,512]{1,0:T(8,128)S(1)} %get-tuple-element.35), channel_id=1, source_target_pairs={{0,15},{1,0},{2,1},{3,2},{4,3},{5,4},{6,5},{7,6},{8,7},{9,8},{10,9... | collective-permute-start | bytes 196616 | tf_op jit(solution)/shard_map/ppermute | solution.py:17
  32.3 11.1 %collective-permute-start.3 = (f32[32,512]{1,0:T(8,128)S(1)}, f32[32,512]{1,0:T(8,128)S(1)}, u32[]{:S(2)}, u32[]{:S(2)}) collective-permute-start(f32[32,512]{1,0:T(8,128)S(1)} %get-tuple-element.36), channel_id=1, source_target_pairs={{0,1},{1,2},{2,3},{3,4},{4,5},{5,6},{6,7},{7,8},{8,9},{9,10},{10,1... | collective-permute-start | bytes 196616 | tf_op jit(solution)/shard_map/ppermute | solution.py:17
  36.0 19.0 %collective-permute-start.5 = (f32[16,32,512]{2,1,0:T(8,128)S(1)}, f32[16,32,512]{2,1,0:T(8,128)S(1)}, u32[]{:S(2)}, u32[]{:S(2)}) collective-permute-start(f32[16,32,512]{2,1,0:T(8,128)S(1)} %get-tuple-element.25), channel_id=1, source_target_pairs={{0,1},{1,2},{2,3},{3,4},{4,5},{5,6},{6,7},{7,8},{8,9},{9,10},{10,1... | collective-permute-start | bytes 3145736 | tf_op jit(solution)/shard_map/ppermute | solution.py:17
  38.5 16.6 %collective-permute-start.6 = (f32[16,32,512]{2,1,0:T(8,128)S(1)}, f32[16,32,512]{2,1,0:T(8,128)S(1)}, u32[]{:S(2)}, u32[]{:S(2)}) collective-permute-start(f32[16,32,512]{2,1,0:T(8,128)S(1)} %get-tuple-element.26), channel_id=1, source_target_pairs={{0,15},{1,0},{2,1},{3,2},{4,3},{5,4},{6,5},{7,6},{8,7},{9,8},{10,9... | collective-permute-start | bytes 3145736 | tf_op jit(solution)/shard_map/ppermute | solution.py:17
  51.1 1.9 %copy-start.3 = (f32[16,4,32,512]{3,2,1,0:T(8,128)}, f32[16,4,32,512]{3,2,1,0:T(8,128)S(1)}, u32[]{:S(2)}) copy-start(f32[16,4,32,512]{3,2,1,0:T(8,128)S(1)} %get-tuple-element.23.w1_ref) | copy-start | bytes 12582916
  53.0 2.0 %copy-start.4 = (f32[16,4,32,512]{3,2,1,0:T(8,128)}, f32[16,4,32,512]{3,2,1,0:T(8,128)S(1)}, u32[]{:S(2)}) copy-start(f32[16,4,32,512]{3,2,1,0:T(8,128)S(1)} %get-tuple-element.24.w2_ref) | copy-start | bytes 12582916
  55.0 24.0 %collective-permute-start.7 = (f32[16,32,512]{2,1,0:T(8,128)S(1)}, f32[16,32,512]{2,1,0:T(8,128)S(1)}, u32[]{:S(2)}, u32[]{:S(2)}) collective-permute-start(f32[16,32,512]{2,1,0:T(8,128)S(1)} %get-tuple-element.29), channel_id=1, source_target_pairs={{0,1},{1,2},{2,3},{3,4},{4,5},{5,6},{6,7},{7,8},{8,9},{9,10},{10,1... | collective-permute-start | bytes 3145736 | tf_op jit(solution)/shard_map/ppermute | solution.py:17
  79.2 1.2 %collective-permute-start.8 = (f32[8,128]{1,0:T(8,128)S(1)}, f32[8,128]{1,0:T(8,128)S(1)}, u32[]{:S(2)}, u32[]{:S(2)}) collective-permute-start(f32[8,128]{1,0:T(8,128)S(1)} %shard_map.41), channel_id=1, source_target_pairs={{0,1},{1,0},{2,3},{3,2},{4,5},{5,4},{6,7},{7,6},{8,9},{9,8},{10,11... | collective-permute-start | bytes 12296 | tf_op jit(solution)/shard_map/ppermute | solution.py:336
  80.4 3.6 %collective-permute-start.9 = (f32[8,128]{1,0:T(8,128)S(1)}, f32[8,128]{1,0:T(8,128)S(1)}, u32[]{:S(2)}, u32[]{:S(2)}) collective-permute-start(f32[8,128]{1,0:T(8,128)S(1)} %add.12), channel_id=1, source_target_pairs={{0,2},{1,3},{2,0},{3,1},{4,6},{5,7},{6,4},{7,5},{8,10},{9,11},{10,... | collective-permute-start | bytes 12296 | tf_op jit(solution)/shard_map/ppermute | solution.py:336
  84.0 12.2 %collective-permute-start.10 = (f32[8,128]{1,0:T(8,128)S(1)}, f32[8,128]{1,0:T(8,128)S(1)}, u32[]{:S(2)}, u32[]{:S(2)}) collective-permute-start(f32[8,128]{1,0:T(8,128)S(1)} %add.13), channel_id=1, source_target_pairs={{0,4},{1,5},{2,6},{3,7},{4,0},{5,1},{6,2},{7,3},{8,12},{9,13},{10,... | collective-permute-start | bytes 12296 | tf_op jit(solution)/shard_map/ppermute | solution.py:336
  96.2 4.6 %collective-permute-start.11 = (f32[8,128]{1,0:T(8,128)S(1)}, f32[8,128]{1,0:T(8,128)S(1)}, u32[]{:S(2)}, u32[]{:S(2)}) collective-permute-start(f32[8,128]{1,0:T(8,128)S(1)} %add.14), channel_id=1, source_target_pairs={{0,8},{1,9},{2,10},{3,11},{4,12},{5,13},{6,14},{7,15},{8,0},{9,1},... | collective-permute-start | bytes 12296 | tf_op jit(solution)/shard_map/ppermute | solution.py:336
  100.9 2.2 %copy-start.1 = (f32[16,4,32,512]{3,2,1,0:T(8,128)S(1)}, f32[16,4,32,512]{3,2,1,0:T(8,128)}, u32[]{:S(2)}) copy-start(f32[16,4,32,512]{3,2,1,0:T(8,128)} %get-tuple-element.32.p2_ref) | copy-start | bytes 12582916

commit v2 on v1

v2 whole, which is shorter than its diff:
```python
import functools

import jax
import jax.numpy as jnp
from jax import lax
from jax.experimental import pallas as pl
from jax.experimental.pallas import tpu as pltpu
from jax.sharding import PartitionSpec as P

LINK_OFFSETS = ((0, 1), (1, 0), (1, 1), (1, -1))
COASTAL_FACTOR = 0.2
F32 = jnp.float32


def passed_along(value, steps):
    count = lax.axis_size("day")
    return lax.ppermute(value, "day", [(i, (i + steps) % count) for i in range(count)])


def turned(value, step_row, step_col):
    rows, cols = value.shape
    if step_col:
        value = pltpu.roll(value, step_col % cols, 1)
    if step_row:
        value = pltpu.roll(value, step_row % rows, 0)
    return value


PLANES = 8


def planes_kernel(coup_hbm, bits_hbm, mask_ref, planes_ref, part_ref, ahead_ref,
                  up_ref, down_ref, low_ref, high_ref, coup_ref, sems):
    days, rows, cols = coup_ref.shape[1:]
    last = days - 1
    coup_copy = pltpu.make_async_copy(coup_hbm, coup_ref, sems.at[0])
    low_copy = pltpu.make_async_copy(bits_hbm.at[:, 0], low_ref, sems.at[1])
    high_copy = pltpu.make_async_copy(bits_hbm.at[:, last], high_ref, sems.at[2])
    coup_copy.start()
    low_copy.start()
    high_copy.start()
    mask = mask_ref[...]
    row = lax.broadcasted_iota(jnp.int32, (rows, cols), 0)
    col = lax.broadcasted_iota(jnp.int32, (rows, cols), 1)
    factors = []
    for step_row, step_col in LINK_OFFSETS:
        same = mask == turned(mask, -step_row, -step_col)
        inside = (row + step_row < rows) & (col + step_col < cols) & (col + step_col >= 0)
        factors.append(jnp.where(inside, jnp.where(same, 1.0, COASTAL_FACTOR), 0.0))
    coup_copy.wait()
    for d in range(days):
        east, south, se, sw = (coup_ref[n + 1, d] * factors[n] for n in range(4))
        west = turned(east, 0, 1)
        se_w = turned(se, 0, 1)
        sw_e = turned(sw, 0, -1)
        above = turned(south, 1, 0)
        ahead = coup_ref[5, d]
        part = coup_ref[0, d] + ahead
        if d:
            part = part + coup_ref[5, d - 1]
        part = part + east + west + south + above
        part = part + se + turned(se_w, 1, 0) + sw + turned(sw_e, 1, 0)
        part_ref[d] = part
        ahead_ref[d] = ahead
        if d == 0:
            down_ref[...] = part
        if d == last:
            up_ref[0] = ahead
            up_ref[1] = part
        for n, plane in enumerate(
            (east, west, south, se_w, sw_e, above, turned(se, 1, 0), turned(sw, 1, 0))
        ):
            planes_ref[n, d] = plane
    low_copy.wait()
    high_copy.wait()


def lower_half(v, v_east, v_west, planes_ref, d):
    down = planes_ref[2, d] * v + planes_ref[3, d] * v_west + planes_ref[4, d] * v_east
    return planes_ref[0, d] * v_east + turned(down, 1, 0)


def upper_half(v, v_east, v_west, planes_ref, d):
    up = planes_ref[5, d] * v + planes_ref[6, d] * v_east + planes_ref[7, d] * v_west
    return planes_ref[1, d] * v_west + turned(up, -1, 0)


def local_apply(field, ahead_ref, dinv_ref, planes_ref, d):
    days = planes_ref.shape[1]
    v = field(d)
    v_east, v_west = turned(v, 0, -1), turned(v, 0, 1)
    result = lower_half(v, v_east, v_west, planes_ref, d)
    result = result + upper_half(v, v_east, v_west, planes_ref, d)
    if d + 1 < days:
        result = result + ahead_ref[d] * field(d + 1)
    if d:
        result = result + ahead_ref[d - 1] * field(d - 1)
    return result * dinv_ref[d]


def half_product(v, planes_ref, d):
    return v * lower_half(v, turned(v, 0, -1), turned(v, 0, 1), planes_ref, d)


def signed(bits, value):
    return jnp.where(bits == 1, value, -value)


def folded(value):
    total = None
    for r in range(0, value.shape[0], 8):
        for c in range(0, value.shape[1], 128):
            tile = value[r : r + 8, c : c + 128]
            total = tile if total is None else total + tile
    return total


def stacked(tiles):
    rows = [jnp.sum(tile, axis=0, keepdims=True) for tile in tiles]
    rows += [jnp.zeros((1, 128), F32)] * (8 - len(rows))
    return jnp.concatenate(rows, axis=0)


def first_kernel(bits_ref, planes_ref, ahead_ref, before_ref, part_ref,
                 w1_ref, low_ref, high_ref, diag_ref, dinv_ref, w0_ref):
    per, days = bits_ref.shape[:2]

    @pl.when(pl.program_id(0) == 0)
    def _():
        for d in range(days):
            diag = part_ref[d]
            if d == 0:
                diag = diag + before_ref[0]
            diag_ref[d] = diag
            dinv_ref[d] = 1.0 / diag

    def probe(k, carry):
        for d in range(days):
            w0_ref[d] = signed(bits_ref[k, d], dinv_ref[d])
        for d in range(days):
            w1 = local_apply(lambda t: w0_ref[t], ahead_ref, dinv_ref, planes_ref, d)
            w1_ref[k, d] = w1
            if d == 0:
                low_ref[k] = w1
            if d == days - 1:
                high_ref[k] = w1
        return carry

    lax.fori_loop(0, per, probe, 0)


def second_kernel(bits_ref, w1_ref, prev_ref, next_ref, planes_ref, ahead_ref, before_ref,
                  after_ref, diag_ref, dinv_ref,
                  p1_ref, p2_ref, w1e_ref, w2e_ref, high_ref, sums_ref, scale_ref, w1c_ref):
    per, days = w1_ref.shape[:2]
    last = days - 1

    @pl.when(pl.program_id(0) == 0)
    def _():
        scale_ref[0] = before_ref[0] * dinv_ref[0] / before_ref[1]
        scale_ref[1] = ahead_ref[last] * dinv_ref[last] / (after_ref[...] + ahead_ref[last])

    def probe(k, carry):
        for d in range(days):
            w1 = w1_ref[k, d]
            if d == 0:
                w1 = w1 + signed(prev_ref[k], scale_ref[0])
            if d == last:
                w1 = w1 + signed(next_ref[k], scale_ref[1])
            w1c_ref[d] = w1
        w1e_ref[k, 0] = w1c_ref[0]
        w1e_ref[k, 1] = w1c_ref[last]
        zero = jnp.zeros((8, 128), F32)
        n0 = n1 = n2 = n3 = n4 = n5 = zero
        for d in range(days):
            w2 = local_apply(lambda t: w1c_ref[t], ahead_ref, dinv_ref, planes_ref, d)
            n0 = n0 + folded(dinv_ref[d])
            if d == 0:
                w2e_ref[k, 0] = w2
                continue
            if d == last:
                w2e_ref[k, 1] = w2
                high_ref[k] = w2
                continue
            w1 = w1c_ref[d]
            bits = bits_ref[k, d]
            p1 = signed(bits, w1)
            p1_ref[k, d - 1] = p1
            p2_ref[k, d - 1] = signed(bits, w2)
            scaled = diag_ref[d] * w2
            n1 = n1 + folded(p1)
            n2 = n2 + folded(diag_ref[d] * w1 * w1)
            n3 = n3 + folded(scaled * w1)
            n4 = n4 + folded(scaled * w2)
            product = half_product(w2, planes_ref, d)
            if d > 1:
                product = product + ahead_ref[d - 1] * w2_before * w2
            n5 = n5 + folded(product)
            w2_before = w2
        sums_ref[k] = stacked([n0, n1, n2, n3, n4, 2.0 * n5])
        return carry

    lax.fori_loop(0, per, probe, 0)


def third_kernel(bits_ref, p2m_ref, w1e_ref, w2e_ref, low_ref, high_ref, sums_in_ref, planes_ref,
                 ahead_ref, before_ref, after_ref, diag_ref, dinv_ref,
                 p1_ref, p2_ref, cross_ref, sums_ref, scale_ref):
    per, days = bits_ref.shape[:2]
    last = days - 1

    @pl.when(pl.program_id(0) == 0)
    def _():
        before, ahead = before_ref[0], ahead_ref[last]
        scale_ref[0] = before / before_ref[1]
        scale_ref[1] = ahead / (after_ref[...] + ahead)
        scale_ref[2] = before * dinv_ref[0]
        scale_ref[3] = ahead * dinv_ref[last]

    def probe(k, carry):
        zero = jnp.zeros((8, 128), F32)
        n1 = n2 = n3 = n4 = n5 = zero
        for side, (d, inner) in enumerate(((0, 1), (last, last - 1))):
            bits = bits_ref[k, d]
            w1 = w1e_ref[k, side]
            arrived = (low_ref if side == 0 else high_ref)[k]
            neighbour = arrived + scale_ref[side] * signed(bits, dinv_ref[d])
            w2 = w2e_ref[k, side] + scale_ref[2 + side] * neighbour
            p1 = signed(bits, w1)
            p1_ref[k, side] = p1
            p2_ref[k, side] = signed(bits, w2)
            scaled = diag_ref[d] * w2
            n1 = n1 + folded(p1)
            n2 = n2 + folded(diag_ref[d] * w1 * w1)
            n3 = n3 + folded(scaled * w1)
            n4 = n4 + folded(scaled * w2)
            inner_w2 = signed(bits_ref[k, inner], p2m_ref[k, inner - 1])
            product = half_product(w2, planes_ref, d)
            product = product + ahead_ref[min(d, inner)] * w2 * inner_w2
            if side == 0:
                cross = before_ref[0] * w2
                cross_ref[k] = cross
                product = product + cross * (scale_ref[0] * w1)
            n5 = n5 + folded(product)
        sums_ref[k] = sums_in_ref[k] + stacked([zero, n1, n2, n3, n4, 2.0 * n5])
        return carry

    lax.fori_loop(0, per, probe, 0)


def fourth_kernel(cross_ref, high_ref, sums_ref, moments_ref):
    probes = cross_ref.shape[0]
    lane = lax.broadcasted_iota(jnp.int32, (8, 128), 1)
    row = lax.broadcasted_iota(jnp.int32, (8, 128), 0)
    result = jnp.zeros((8, 128), F32)
    for k in range(probes):
        extra = jnp.sum(2.0 * folded(cross_ref[k] * high_ref[k]), axis=0, keepdims=True)
        sums = sums_ref[k] + jnp.where(row == 5, extra, 0.0)
        result = jnp.where(lane == k, jnp.sum(sums, axis=1, keepdims=True), result)
    moments_ref[...] = result


def coefficients(moments, probes):
    lane = lax.broadcasted_iota(jnp.int32, (1, 128), 1)
    live = lane < probes
    n0, n1, n2, n3, n4, n5 = (jnp.where(live, moments[j : j + 1], 1.0) for j in range(6))
    a0 = n1 / n0
    s11 = jnp.maximum(n2 - a0 * n1, 1e-7 * n2 + 1e-30)
    s12 = n3 - a0 * n2
    s13 = n4 - a0 * n3
    s14 = n5 - a0 * n4
    a1 = jnp.clip(s12 / s11 - a0, -1.0, 0.999)
    b1 = s11 / n0
    s22 = jnp.maximum(s13 - a1 * s12 - b1 * n2, 1e-7 * n4 + 1e-30)
    s23 = s14 - a1 * s13 - b1 * n3
    a2 = jnp.clip(s23 / s22 - s12 / s11, -1.0, 0.999)
    b2 = s22 / s11
    e2 = 1.0 - a2
    e1 = (1.0 - a1) - b2 / e2
    e0 = (1.0 - a0) - b1 / e1
    y0 = 1.0 / e0
    y1 = y0 / e1
    y2 = y1 / e2
    scale = jnp.where(live, 1.0 / probes, 0.0)
    return (
        scale * (y0 - a0 * y1 + (a0 * a1 - b1) * y2),
        scale * (y1 - (a0 + a1) * y2),
        scale * y2,
    )


def last_kernel(moments_ref, p1m_ref, p2m_ref, p1e_ref, p2e_ref, dinv_ref, out_ref):
    probes, inner = p1m_ref.shape[:2]
    days = inner + 2
    c0, c1, c2 = coefficients(moments_ref[...], probes)
    c0 = jnp.sum(c0, axis=1, keepdims=True)
    for d in range(days):
        edge = d in (0, days - 1)
        p1_ref, p2_ref = (p1e_ref, p2e_ref) if edge else (p1m_ref, p2m_ref)
        spot = (1 if d else 0) if edge else d - 1
        total = c0 * dinv_ref[d]
        for k in range(probes):
            total = total + (c1[:, k : k + 1] * p1_ref[k, spot] + c2[:, k : k + 1] * p2_ref[k, spot])
        out_ref[d] = total


def split(shape, per):
    return pl.BlockSpec((per,) + tuple(shape[1:]), lambda i: (i,) + (0,) * (len(shape) - 1))


def whole(shape):
    return pl.BlockSpec(tuple(shape), lambda i: (0,) * len(shape))


def body(couplings, probe_bits, land_mask):
    probes, days, rows, cols = probe_bits.shape
    count = lax.axis_size("day")
    plane = (rows, cols)
    field = (probes, days, rows, cols)
    edge = (probes, rows, cols)
    pair = (probes, 2, rows, cols)
    middle = (probes, days - 2, rows, cols)
    dplanes = (days,) + plane
    sums_shape = (probes, 8, 128)
    tile = (8, 128)
    weights = (PLANES,) + dplanes
    per = 2
    grid = (probes // per,)
    size = probes * days * rows * cols

    def call(kernel, grid, ins, outs, scratch=(), cost=(1, 1), mib=16):
        def spec(shape, kind):
            if kind == "hbm":
                return pl.BlockSpec(memory_space=pltpu.HBM)
            return split(shape, per) if kind == "split" else whole(shape)

        return pl.pallas_call(
            kernel,
            grid=grid,
            in_specs=[spec(value.shape, kind) for value, kind in ins],
            out_specs=[spec(shape, kind) for shape, kind, _ in outs],
            out_shape=[jax.ShapeDtypeStruct(shape, dtype) for shape, _, dtype in outs],
            scratch_shapes=list(scratch),
            cost_estimate=pl.CostEstimate(
                flops=int(cost[0] * size * 24), bytes_accessed=int(cost[1] * size * 4), transcendentals=0
            ),
            compiler_params=pltpu.CompilerParams(vmem_limit_bytes=mib << 20),
        )(*[value for value, _ in ins])

    planes, part, ahead, up, down, low_bits, high_bits = call(
        planes_kernel, (1,),
        [(couplings, "hbm"), (probe_bits, "hbm"), (land_mask, "whole")],
        [(weights, "whole", F32), (dplanes, "whole", F32), (dplanes, "whole", F32),
         ((2,) + plane, "whole", F32), (plane, "whole", F32),
         (edge, "whole", jnp.int32), (edge, "whole", jnp.int32)],
        scratch=[pltpu.VMEM(couplings.shape, F32), pltpu.SemaphoreType.DMA((3,))],
        cost=(0.5, 1), mib=56,
    )
    before = passed_along(up, 1)
    after = passed_along(down, -1)
    high_bits, low_bits, before, after = lax.optimization_barrier((high_bits, low_bits, before, after))
    bits_prev = passed_along(high_bits, 1)
    bits_next = passed_along(low_bits, -1)

    w1, low, high, diag, dinv = call(
        first_kernel, grid,
        [(probe_bits, "split"), (planes, "whole"), (ahead, "whole"), (before, "whole"),
         (part, "whole")],
        [(field, "split", F32), (edge, "split", F32), (edge, "split", F32),
         (dplanes, "whole", F32), (dplanes, "whole", F32)],
        scratch=[pltpu.VMEM(dplanes, F32)], cost=(1, 2),
    )
    high_prev = passed_along(high, 1)
    low_next = passed_along(low, -1)

    p1m, p2m, w1e, w2e, high2, sums = call(
        second_kernel, grid,
        [(probe_bits, "split"), (w1, "split"), (bits_prev, "split"), (bits_next, "split"),
         (planes, "whole"), (ahead, "whole"), (before, "whole"), (after, "whole"),
         (diag, "whole"), (dinv, "whole")],
        [(middle, "split", F32), (middle, "split", F32), (pair, "split", F32),
         (pair, "split", F32), (edge, "split", F32), (sums_shape, "split", F32)],
        scratch=[pltpu.VMEM((2,) + plane, F32), pltpu.VMEM(dplanes, F32)], cost=(1.5, 4), mib=20,
    )
    high2_prev = passed_along(high2, 1)

    p1e, p2e, cross, sums = call(
        third_kernel, grid,
        [(probe_bits, "split"), (p2m, "split"), (w1e, "split"), (w2e, "split"),
         (high_prev, "split"), (low_next, "split"), (sums, "split"), (planes, "whole"),
         (ahead, "whole"), (before, "whole"), (after, "whole"), (diag, "whole"), (dinv, "whole")],
        [(pair, "split", F32), (pair, "split", F32), (edge, "split", F32),
         (sums_shape, "split", F32)],
        scratch=[pltpu.VMEM((4,) + plane, F32)], cost=(0.7, 4), mib=20,
    )
    (moments,) = call(
        fourth_kernel, (1,),
        [(cross, "whole"), (high2_prev, "whole"), (sums, "whole")],
        [(tile, "whole", F32)], cost=(0.1, 0.5), mib=8,
    )
    step = 1
    while step < count:
        moments = moments + lax.ppermute(moments, "day", [(i, i ^ step) for i in range(count)])
        step *= 2

    (out,) = call(
        last_kernel, (1,),
        [(moments, "whole"), (p1m, "whole"), (p2m, "whole"), (p1e, "whole"), (p2e, "whole"),
         (dinv, "whole")],
        [(dplanes, "whole", F32)], cost=(0.2, 2), mib=24,
    )
    return out


def solution(mesh):
    assert mesh.shape["day"] & (mesh.shape["day"] - 1) == 0
    return jax.shard_map(
        body,
        mesh=mesh,
        in_specs=(
            P(None, ("groups", "day"), None, None),
            P(None, ("groups", "day"), None, None),
            P("groups", None),
        ),
        out_specs=P(("groups", "day"), None, None),
        check_vma=False,
    )
```

time: 105 us -> 98 us (0.933)
  starting transfers between devices: 29.3 us -> 59 us
  waiting for transfers between devices: 36.1 us -> 10.7 us
  local copies, waits for them, and re-layouts: 13.3 us -> 3.5 us
  Pallas kernels: 25.8 us -> 24.5 us
    ppermute x8 -> x7, starting transfers between devices: 15.6 us -> 45.2 us  [passed_along(): lax.ppermute(value, 'day', [(i, (i + steps) % count) for i in range(count)])]
    ppermute x8 -> x7, waiting for transfers between devices: 28.1 us -> 2.92 us  [passed_along(): lax.ppermute(value, 'day', [(i, (i + steps) % count) for i in range(count)])]
    unnamed x14 -> x10, local copies, waits for them, and re-layouts: 9.47 us -> 3.5 us
    squeeze x4 -> x0, local copies, waits for them, and re-layouts: 3.79 us -> none  [the longest x1 1.96 us: body(): bits_next = passed_along(probe_bits[:, 0], -1)]
    pallas_call x6, Pallas kernels: 25.8 us -> 24.5 us  [call(): pl.pallas_call(kernel, grid=grid, in_specs=[spec(value.shape, kind) for v...]
  transfers between devices with their start and end apart: 12 -> 11, of which waited for: 7 -> 6; matrix products, arithmetic and copies ran while one was open for 2% -> 0% of each run, Pallas kernels for 23% -> 18%
where the time goes in v2:
time: 98 us; the launch traced here: 97.8 us
  starting transfers between devices  59 us (60%)
  Pallas kernels  24.5 us (25%)
  waiting for transfers between devices  10.7 us (11%)
  local copies, waits for them, and re-layouts  3.5 us (4%)
    ppermute x7, starting transfers between devices, passed_along(): lax.ppermute(value, 'day', [(i, (i + steps) % count) for i in range(count)])  45.2 us
    pallas_call x6, Pallas kernels, call(): pl.pallas_call(kernel, grid=grid, in_specs=[spec(value.shape, kind) for v...  24.5 us
    ppermute x4, starting transfers between devices, body(): lax.ppermute(moments, 'day', [(i, i ^ step) for i in range(count)])  13.8 us
    ppermute x4, waiting for transfers between devices, body(): lax.ppermute(moments, 'day', [(i, i ^ step) for i in range(count)])  7.78 us
    unnamed x10, local copies, waits for them, and re-layouts  3.5 us
    ppermute x7, waiting for transfers between devices, passed_along(): lax.ppermute(value, 'day', [(i, (i + steps) % count) for i in range(count)])  2.92 us
  transfers between devices with their start and end apart: 11, of which 6 were waited for; matrix products, arithmetic and copies ran while one was open for 0% of the time, Pallas kernels for 18%

profile of v2, /device:TPU:0, one launch (start us, length us, event | category | flops | bytes accessed | tf_op | source)
XLA Modules:
  0.0 97.8 jit_solution(3532420981420789297)
XLA Ops:
  0.0 0.0 copy-start
  0.0 5.5 %shard_map.37 = (f32[8,4,32,512]{3,2,1,0:T(8,128)}, f32[4,32,512]{2,1,0:T(8,128)}, f32[4,32,512]{2,1,0:T(8,128)}, f32[2,32,512]{2,1,0:T(8,128)}, f32[32,512]{1,0...) custom-call(f32[6,4,32,512]{3,2,1,0:T(8,128)} %coup_hbm.1, s32[16,4,32,512]{3,2,1,0:T(8,128)} %bits_ref.5, ...), custom_call_target="tpu_custom_call" | custom-call | flops 12582912 | bytes 4194304 | tf_op jit(solution)/shard_map/pallas_call | solution.py:337
  5.6 0.5 collective-permute-start
  6.1 5.1 %collective-permute-start.1 = (f32[32,512]{1,0:T(8,128)}, f32[32,512]{1,0:T(8,128)S(1)}, u32[]{:S(2)}, u32[]{:S(2)}) collective-permute-start(f32[32,512]{1,0:T(8,128)} %get-tuple-element.36), channel_id=1, source_target_pairs={{0,15},{1,0},{2,1},{3,2},{4,3},{5,4},{6,5},{7,6},{8,7},{9,8},{10,9... | collective-permute-start | bytes 196616 | tf_op jit(solution)/shard_map/ppermute | solution.py:17
  11.1 2.2 %collective-permute-done.1.after_ref = f32[32,512]{1,0:T(8,128)S(1)} collective-permute-done((f32[32,512]{1,0:T(8,128)}, f32[32,512]{1,0:T(8,128)S(1)}, u32[]{:S(2)}, u32[]{:S(2)}) %collective-permute-start.1) | collective-permute-done | bytes 65568 | tf_op jit(solution)/shard_map/ppermute | solution.py:17
  13.3 0.7 collective-permute-done.before_ref
  14.0 0.0 collective-permute-start.2
  14.0 4.4 %collective-permute-start.3 = (s32[16,32,512]{2,1,0:T(8,128)}, s32[16,32,512]{2,1,0:T(8,128)S(1)}, u32[]{:S(2)}, u32[]{:S(2)}) collective-permute-start(s32[16,32,512]{2,1,0:T(8,128)} %get-tuple-element.41), channel_id=1, source_target_pairs={{0,15},{1,0},{2,1},{3,2},{4,3},{5,4},{6,5},{7,6},{8,7},{9,8},{10,9... | collective-permute-start | bytes 3145736 | tf_op jit(solution)/shard_map/ppermute | solution.py:17
  18.5 0.0 copy-done
  18.5 0.0 copy-start.1
  18.5 1.6 %copy-done.1 = f32[8,4,32,512]{3,2,1,0:T(8,128)S(1)} copy-done((f32[8,4,32,512]{3,2,1,0:T(8,128)S(1)}, f32[8,4,32,512]{3,2,1,0:T(8,128)}, u32[]{:S(2)}) %copy-start.1) | copy-done | bytes 2097176
  20.1 0.0 copy-start.3
  20.1 0.9 copy-done.3
  21.0 0.0 copy-start.4
  21.0 0.9 copy-done.4
  22.0 0.0 copy-start.2
  22.0 5.0 %shard_map.38 = (f32[16,4,32,512]{3,2,1,0:T(8,128)S(1)}, f32[16,32,512]{2,1,0:T(8,128)S(1)}, f32[16,32,512]{2,1,0:T(8,128)S(1)}, f32[4,32,512]{2,1,0:T(8,128)S(1)}, f32[4,32,512]{2,1,0:T(8,128)S(1)}) custom-call(s32[16,4,32,512]{3,2,1,0:T(8,128)S(1)} %copy-done, f32[8,4,32,512]{3,2,1,0:T(8,128)S(1)} %copy-done.1, f32[4,32,512]{2,1,0:T(8,128)S(1)} %copy-done.3, ...), custom_call_target="tpu_custom_call" | custom-call | flops 25165824 | bytes 8388608 | tf_op jit(solution)/shard_map/pallas_call | solution.py:337
  27.0 0.1 collective-permute-start.4
  27.1 4.4 %collective-permute-start.5 = (f32[16,32,512]{2,1,0:T(8,128)S(1)}, f32[16,32,512]{2,1,0:T(8,128)S(1)}, u32[]{:S(2)}, u32[]{:S(2)}) collective-permute-start(f32[16,32,512]{2,1,0:T(8,128)S(1)} %get-tuple-element.49), channel_id=1, source_target_pairs={{0,15},{1,0},{2,1},{3,2},{4,3},{5,4},{6,5},{7,6},{8,7},{9,8},{10,9... | collective-permute-start | bytes 3145736 | tf_op jit(solution)/shard_map/ppermute | solution.py:17
  31.5 0.0 collective-permute-done.2.prev_ref
  31.5 0.0 collective-permute-done.3.next_ref
  31.5 0.0 copy-done.2
  31.5 8.8 %shard_map.39 = (f32[16,2,32,512]{3,2,1,0:T(8,128)S(1)}, f32[16,2,32,512]{3,2,1,0:T(8,128)S(1)}, f32[16,2,32,512]{3,2,1,0:T(8,128)S(1)}, f32[16,2,32,512]{3,2,1,...) custom-call(s32[16,4,32,512]{3,2,1,0:T(8,128)S(1)} %copy-done, ...), custom_call_target="tpu_custom_call" | custom-call | flops 37748736 | bytes 16777216 | tf_op jit(solution)/shard_map/pallas_call | solution.py:337
  40.4 30.7 %collective-permute-start.6 = (f32[16,32,512]{2,1,0:T(8,128)S(1)}, f32[16,32,512]{2,1,0:T(8,128)S(1)}, u32[]{:S(2)}, u32[]{:S(2)}) collective-permute-start(f32[16,32,512]{2,1,0:T(8,128)S(1)} %get-tuple-element.52), channel_id=1, source_target_pairs={{0,1},{1,2},{2,3},{3,4},{4,5},{5,6},{6,7},{7,8},{8,9},{9,10},{10,1... | collective-permute-start | bytes 3145736 | tf_op jit(solution)/shard_map/ppermute | solution.py:17
  71.0 0.0 collective-permute-done.4.low_ref
  71.0 0.0 collective-permute-done.5.high_ref
  71.0 3.4 %shard_map.40 = (f32[16,2,32,512]{3,2,1,0:T(8,128)S(1)}, f32[16,2,32,512]{3,2,1,0:T(8,128)S(1)}, f32[16,32,512]{2,1,0:T(8,128)S(1)}, f32[16,8,128]{2,1,0:T(8,128)S(1)}) custom-call(s32[16,4,32,512]{3,2,1,0:T(8,128)S(1)} %copy-done, f32[16,2,32,512]{3,2,1,0:T(8,128)S(1)} %get-tuple-element.45.p2m_ref, f32[16,2,32,512]{3,2,1,0:T(8,128)S(1)} %get-tuple-element.46.w1e_ref, ...), custom_call_target="tpu_custom_call" | custom-call | flops 17616076 | bytes 16777216 | tf_op jit(solution)/shard_map/pallas_call | solution.py:337
  74.4 0.0 collective-permute-done.6.high_ref
  74.4 0.2 shard_map.41
  74.6 8.4 %collective-permute-start.7 = (f32[8,128]{1,0:T(8,128)S(1)}, f32[8,128]{1,0:T(8,128)S(1)}, u32[]{:S(2)}, u32[]{:S(2)}) collective-permute-start(f32[8,128]{1,0:T(8,128)S(1)} %shard_map.41), channel_id=1, source_target_pairs={{0,1},{1,0},{2,3},{3,2},{4,5},{5,4},{6,7},{7,6},{8,9},{9,8},{10,11... | collective-permute-start | bytes 12296 | tf_op jit(solution)/shard_map/ppermute | solution.py:403
  83.0 0.8 collective-permute-done.7
  83.8 2.7 %collective-permute-start.8 = (f32[8,128]{1,0:T(8,128)S(1)}, f32[8,128]{1,0:T(8,128)S(1)}, u32[]{:S(2)}, u32[]{:S(2)}) collective-permute-start(f32[8,128]{1,0:T(8,128)S(1)} %add.12), channel_id=1, source_target_pairs={{0,2},{1,3},{2,0},{3,1},{4,6},{5,7},{6,4},{7,5},{8,10},{9,11},{10,... | collective-permute-start | bytes 12296 | tf_op jit(solution)/shard_map/ppermute | solution.py:403
  86.5 1.6 %collective-permute-done.8 = f32[8,128]{1,0:T(8,128)S(1)} collective-permute-done((f32[8,128]{1,0:T(8,128)S(1)}, f32[8,128]{1,0:T(8,128)S(1)}, u32[]{:S(2)}, u32[]{:S(2)}) %collective-permute-start.8) | collective-permute-done | bytes 4128 | tf_op jit(solution)/shard_map/ppermute | solution.py:403
  88.1 0.9 collective-permute-start.9
  89.0 2.7 %collective-permute-done.9 = f32[8,128]{1,0:T(8,128)S(1)} collective-permute-done((f32[8,128]{1,0:T(8,128)S(1)}, f32[8,128]{1,0:T(8,128)S(1)}, u32[]{:S(2)}, u32[]{:S(2)}) %collective-permute-start.9) | collective-permute-done | bytes 4128 | tf_op jit(solution)/shard_map/ppermute | solution.py:403
  91.7 1.9 %collective-permute-start.10 = (f32[8,128]{1,0:T(8,128)S(1)}, f32[8,128]{1,0:T(8,128)S(1)}, u32[]{:S(2)}, u32[]{:S(2)}) collective-permute-start(f32[8,128]{1,0:T(8,128)S(1)} %add.14), channel_id=1, source_target_pairs={{0,8},{1,9},{2,10},{3,11},{4,12},{5,13},{6,14},{7,15},{8,0},{9,1},... | collective-permute-start | bytes 12296 | tf_op jit(solution)/shard_map/ppermute | solution.py:403
  93.6 2.6 %collective-permute-done.10 = f32[8,128]{1,0:T(8,128)S(1)} collective-permute-done((f32[8,128]{1,0:T(8,128)S(1)}, f32[8,128]{1,0:T(8,128)S(1)}, u32[]{:S(2)}, u32[]{:S(2)}) %collective-permute-start.10) | collective-permute-done | bytes 4128 | tf_op jit(solution)/shard_map/ppermute | solution.py:403
  96.2 1.5 %shard_map.42 = f32[4,32,512]{2,1,0:T(8,128)} custom-call(f32[8,128]{1,0:T(8,128)S(1)} %add.15.moments_ref, f32[16,2,32,512]{3,2,1,0:T(8,128)S(1)} %get-tuple-element.54.p1m_ref, f32[16,2,32,512]{3,2,1,0:T(8,128)S(1)} %get-tuple-element.45.p2m_ref, f32[16,2,32,512]{3,2,1,0:T(8,128)S(1)} %get-tuple-element.55.p1e_ref, ...), custom_call_target="tpu_custom_call" | custom-call | flops 5033164 | bytes 8388608 | tf_op jit(solution)/shard_map/pallas_call | solution.py:337
  (4 shorter events, 0.0 us)
Async XLA Ops:
  0.0 18.5 %copy-start = (s32[16,4,32,512]{3,2,1,0:T(8,128)S(1)}, s32[16,4,32,512]{3,2,1,0:T(8,128)}, u32[]{:S(2)}) copy-start(s32[16,4,32,512]{3,2,1,0:T(8,128)} %bits_ref.5) | copy-start | bytes 12582916
  5.6 8.5 %collective-permute-start = (f32[2,32,512]{2,1,0:T(8,128)}, f32[2,32,512]{2,1,0:T(8,128)S(1)}, u32[]{:S(2)}, u32[]{:S(2)}) collective-permute-start(f32[2,32,512]{2,1,0:T(8,128)} %get-tuple-element.35), channel_id=1, source_target_pairs={{0,1},{1,2},{2,3},{3,4},{4,5},{5,6},{6,7},{7,8},{8,9},{9,10},{10,1... | collective-permute-start | bytes 393224 | tf_op jit(solution)/shard_map/ppermute | solution.py:17
  6.1 7.3 %collective-permute-start.1 = (f32[32,512]{1,0:T(8,128)}, f32[32,512]{1,0:T(8,128)S(1)}, u32[]{:S(2)}, u32[]{:S(2)}) collective-permute-start(f32[32,512]{1,0:T(8,128)} %get-tuple-element.36), channel_id=1, source_target_pairs={{0,15},{1,0},{2,1},{3,2},{4,3},{5,4},{6,5},{7,6},{8,7},{9,8},{10,9... | collective-permute-start | bytes 196616 | tf_op jit(solution)/shard_map/ppermute | solution.py:17
  14.0 17.5 %collective-permute-start.2 = (s32[16,32,512]{2,1,0:T(8,128)}, s32[16,32,512]{2,1,0:T(8,128)S(1)}, u32[]{:S(2)}, u32[]{:S(2)}) collective-permute-start(s32[16,32,512]{2,1,0:T(8,128)} %get-tuple-element.40), channel_id=1, source_target_pairs={{0,1},{1,2},{2,3},{3,4},{4,5},{5,6},{6,7},{7,8},{8,9},{9,10},{10,1... | collective-permute-start | bytes 3145736 | tf_op jit(solution)/shard_map/ppermute | solution.py:17
  14.0 17.5 %collective-permute-start.3 = (s32[16,32,512]{2,1,0:T(8,128)}, s32[16,32,512]{2,1,0:T(8,128)S(1)}, u32[]{:S(2)}, u32[]{:S(2)}) collective-permute-start(s32[16,32,512]{2,1,0:T(8,128)} %get-tuple-element.41), channel_id=1, source_target_pairs={{0,15},{1,0},{2,1},{3,2},{4,3},{5,4},{6,5},{7,6},{8,7},{9,8},{10,9... | collective-permute-start | bytes 3145736 | tf_op jit(solution)/shard_map/ppermute | solution.py:17
  18.5 1.6 %copy-start.1 = (f32[8,4,32,512]{3,2,1,0:T(8,128)S(1)}, f32[8,4,32,512]{3,2,1,0:T(8,128)}, u32[]{:S(2)}) copy-start(f32[8,4,32,512]{3,2,1,0:T(8,128)} %get-tuple-element.31.planes_ref) | copy-start | bytes 6291460
  20.1 0.9 copy-start.3
  21.0 0.9 copy-start.4
  22.0 9.6 %copy-start.2 = (f32[8,4,32,512]{3,2,1,0:T(8,128)S(1)}, f32[8,4,32,512]{3,2,1,0:T(8,128)}, u32[]{:S(2)}) copy-start(f32[8,4,32,512]{3,2,1,0:T(8,128)} %get-tuple-element.31.planes_ref) | copy-start | bytes 6291460
  27.0 44.0 %collective-permute-start.4 = (f32[16,32,512]{2,1,0:T(8,128)S(1)}, f32[16,32,512]{2,1,0:T(8,128)S(1)}, u32[]{:S(2)}, u32[]{:S(2)}) collective-permute-start(f32[16,32,512]{2,1,0:T(8,128)S(1)} %get-tuple-element.48), channel_id=1, source_target_pairs={{0,1},{1,2},{2,3},{3,4},{4,5},{5,6},{6,7},{7,8},{8,9},{9,10},{10,1... | collective-permute-start | bytes 3145736 | tf_op jit(solution)/shard_map/ppermute | solution.py:17
  27.1 44.0 %collective-permute-start.5 = (f32[16,32,512]{2,1,0:T(8,128)S(1)}, f32[16,32,512]{2,1,0:T(8,128)S(1)}, u32[]{:S(2)}, u32[]{:S(2)}) collective-permute-start(f32[16,32,512]{2,1,0:T(8,128)S(1)} %get-tuple-element.49), channel_id=1, source_target_pairs={{0,15},{1,0},{2,1},{3,2},{4,3},{5,4},{6,5},{7,6},{8,7},{9,8},{10,9... | collective-permute-start | bytes 3145736 | tf_op jit(solution)/shard_map/ppermute | solution.py:17
  40.4 34.1 %collective-permute-start.6 = (f32[16,32,512]{2,1,0:T(8,128)S(1)}, f32[16,32,512]{2,1,0:T(8,128)S(1)}, u32[]{:S(2)}, u32[]{:S(2)}) collective-permute-start(f32[16,32,512]{2,1,0:T(8,128)S(1)} %get-tuple-element.52), channel_id=1, source_target_pairs={{0,1},{1,2},{2,3},{3,4},{4,5},{5,6},{6,7},{7,8},{8,9},{9,10},{10,1... | collective-permute-start | bytes 3145736 | tf_op jit(solution)/shard_map/ppermute | solution.py:17
  74.6 9.2 %collective-permute-start.7 = (f32[8,128]{1,0:T(8,128)S(1)}, f32[8,128]{1,0:T(8,128)S(1)}, u32[]{:S(2)}, u32[]{:S(2)}) collective-permute-start(f32[8,128]{1,0:T(8,128)S(1)} %shard_map.41), channel_id=1, source_target_pairs={{0,1},{1,0},{2,3},{3,2},{4,5},{5,4},{6,7},{7,6},{8,9},{9,8},{10,11... | collective-permute-start | bytes 12296 | tf_op jit(solution)/shard_map/ppermute | solution.py:403
  83.8 4.3 %collective-permute-start.8 = (f32[8,128]{1,0:T(8,128)S(1)}, f32[8,128]{1,0:T(8,128)S(1)}, u32[]{:S(2)}, u32[]{:S(2)}) collective-permute-start(f32[8,128]{1,0:T(8,128)S(1)} %add.12), channel_id=1, source_target_pairs={{0,2},{1,3},{2,0},{3,1},{4,6},{5,7},{6,4},{7,5},{8,10},{9,11},{10,... | collective-permute-start | bytes 12296 | tf_op jit(solution)/shard_map/ppermute | solution.py:403
  88.1 3.6 %collective-permute-start.9 = (f32[8,128]{1,0:T(8,128)S(1)}, f32[8,128]{1,0:T(8,128)S(1)}, u32[]{:S(2)}, u32[]{:S(2)}) collective-permute-start(f32[8,128]{1,0:T(8,128)S(1)} %add.13), channel_id=1, source_target_pairs={{0,4},{1,5},{2,6},{3,7},{4,0},{5,1},{6,2},{7,3},{8,12},{9,13},{10,... | collective-permute-start | bytes 12296 | tf_op jit(solution)/shard_map/ppermute | solution.py:403
  91.7 4.5 %collective-permute-start.10 = (f32[8,128]{1,0:T(8,128)S(1)}, f32[8,128]{1,0:T(8,128)S(1)}, u32[]{:S(2)}, u32[]{:S(2)}) collective-permute-start(f32[8,128]{1,0:T(8,128)S(1)} %add.14), channel_id=1, source_target_pairs={{0,8},{1,9},{2,10},{3,11},{4,12},{5,13},{6,14},{7,15},{8,0},{9,1},... | collective-permute-start | bytes 12296 | tf_op jit(solution)/shard_map/ppermute | solution.py:403

commit v3 on v2

--- a/solution.py
+++ b/solution.py
@@ -12,9 +12,14 @@
 F32 = jnp.float32
 
 
-def passed_along(value, steps):
+def moved(value, kind):
     count = lax.axis_size("day")
-    return lax.ppermute(value, "day", [(i, (i + steps) % count) for i in range(count)])
+    target = {
+        "on": lambda i: i ^ 1,
+        "off": lambda i: (i + 1 if i % 2 else i - 1) % count,
+        "next": lambda i: (i + 1) % count,
+    }[kind]
+    return lax.ppermute(value, "day", [(i, target(i)) for i in range(count)])
 
 
 def turned(value, step_row, step_col):
@@ -29,16 +34,22 @@
 PLANES = 8
 
 
-def planes_kernel(coup_hbm, bits_hbm, mask_ref, planes_ref, part_ref, ahead_ref,
-                  up_ref, down_ref, low_ref, high_ref, coup_ref, sems):
+def edges_kernel(odd_ref, bits_hbm, off_ref, on_ref, sems):
+    last = bits_hbm.shape[1] - 1
+    off_day = odd_ref[0] * last
+    off_copy = pltpu.make_async_copy(bits_hbm.at[:, off_day], off_ref, sems.at[0])
+    on_copy = pltpu.make_async_copy(bits_hbm.at[:, last - off_day], on_ref, sems.at[1])
+    off_copy.start()
+    on_copy.start()
+    off_copy.wait()
+    on_copy.wait()
+
+
+def planes_kernel(odd_ref, coup_ref, mask_ref, planes_ref, part_ref, ahead_ref,
+                  off_ref, on_ref):
     days, rows, cols = coup_ref.shape[1:]
     last = days - 1
-    coup_copy = pltpu.make_async_copy(coup_hbm, coup_ref, sems.at[0])
-    low_copy = pltpu.make_async_copy(bits_hbm.at[:, 0], low_ref, sems.at[1])
-    high_copy = pltpu.make_async_copy(bits_hbm.at[:, last], high_ref, sems.at[2])
-    coup_copy.start()
-    low_copy.start()
-    high_copy.start()
+    odd = odd_ref[0]
     mask = mask_ref[...]
     row = lax.broadcasted_iota(jnp.int32, (rows, cols), 0)
     col = lax.broadcasted_iota(jnp.int32, (rows, cols), 1)
@@ -47,7 +58,6 @@
         same = mask == turned(mask, -step_row, -step_col)
         inside = (row + step_row < rows) & (col + step_col < cols) & (col + step_col >= 0)
         factors.append(jnp.where(inside, jnp.where(same, 1.0, COASTAL_FACTOR), 0.0))
-    coup_copy.wait()
     for d in range(days):
         east, south, se, sw = (coup_ref[n + 1, d] * factors[n] for n in range(4))
         west = turned(east, 0, 1)
@@ -62,17 +72,17 @@
         part = part + se + turned(se_w, 1, 0) + sw + turned(sw_e, 1, 0)
         part_ref[d] = part
         ahead_ref[d] = ahead
-        if d == 0:
-            down_ref[...] = part
-        if d == last:
-            up_ref[0] = ahead
-            up_ref[1] = part
         for n, plane in enumerate(
             (east, west, south, se_w, sw_e, above, turned(se, 1, 0), turned(sw, 1, 0))
         ):
             planes_ref[n, d] = plane
-    low_copy.wait()
-    high_copy.wait()
+    for out_ref, d in ((off_ref, odd * last), (on_ref, last - odd * last)):
+        out_ref[0] = coup_ref[5, last]
+        out_ref[1] = part_ref[d]
+
+
+def chosen(odd, even_value, odd_value):
+    return jnp.where(jnp.full(even_value.shape, odd, jnp.int32) == 1, odd_value, even_value)
 
 
 def lower_half(v, v_east, v_west, planes_ref, d):
@@ -121,16 +131,22 @@
     return jnp.concatenate(rows, axis=0)
 
 
-def first_kernel(bits_ref, planes_ref, ahead_ref, before_ref, part_ref,
-                 w1_ref, low_ref, high_ref, diag_ref, dinv_ref, w0_ref):
+def first_kernel(odd_ref, bits_ref, planes_ref, ahead_ref, soff_ref, son_ref, part_ref,
+                 w1_ref, off_ref, on_ref, diag_ref, dinv_ref, outside_ref, w0_ref):
     per, days = bits_ref.shape[:2]
+    last = days - 1
+    odd = odd_ref[0]
 
     @pl.when(pl.program_id(0) == 0)
     def _():
+        before = chosen(odd, soff_ref[0], son_ref[0])
+        outside_ref[0] = before
+        outside_ref[1] = chosen(odd, soff_ref[1], son_ref[1])
+        outside_ref[2] = chosen(odd, son_ref[1], soff_ref[1]) + ahead_ref[last]
         for d in range(days):
             diag = part_ref[d]
             if d == 0:
-                diag = diag + before_ref[0]
+                diag = diag + before
             diag_ref[d] = diag
             dinv_ref[d] = 1.0 / diag
 
@@ -141,32 +157,33 @@
             w1 = local_apply(lambda t: w0_ref[t], ahead_ref, dinv_ref, planes_ref, d)
             w1_ref[k, d] = w1
             if d == 0:
-                low_ref[k] = w1
-            if d == days - 1:
-                high_ref[k] = w1
+                w1_low = w1
+        off_ref[k] = chosen(odd, w1_low, w1)
+        on_ref[k] = chosen(odd, w1, w1_low)
         return carry
 
     lax.fori_loop(0, per, probe, 0)
 
 
-def second_kernel(bits_ref, w1_ref, prev_ref, next_ref, planes_ref, ahead_ref, before_ref,
-                  after_ref, diag_ref, dinv_ref,
+def second_kernel(odd_ref, token_ref, bits_ref, w1_ref, off_ref, on_ref, planes_ref, ahead_ref, outside_ref,
+                  diag_ref, dinv_ref,
                   p1_ref, p2_ref, w1e_ref, w2e_ref, high_ref, sums_ref, scale_ref, w1c_ref):
     per, days = w1_ref.shape[:2]
     last = days - 1
+    odd = odd_ref[0]
 
     @pl.when(pl.program_id(0) == 0)
     def _():
-        scale_ref[0] = before_ref[0] * dinv_ref[0] / before_ref[1]
-        scale_ref[1] = ahead_ref[last] * dinv_ref[last] / (after_ref[...] + ahead_ref[last])
+        scale_ref[0] = outside_ref[0] * dinv_ref[0] / outside_ref[1]
+        scale_ref[1] = ahead_ref[last] * dinv_ref[last] / outside_ref[2]
 
     def probe(k, carry):
         for d in range(days):
             w1 = w1_ref[k, d]
             if d == 0:
-                w1 = w1 + signed(prev_ref[k], scale_ref[0])
+                w1 = w1 + signed(chosen(odd, off_ref[k], on_ref[k]), scale_ref[0])
             if d == last:
-                w1 = w1 + signed(next_ref[k], scale_ref[1])
+                w1 = w1 + signed(chosen(odd, on_ref[k], off_ref[k]), scale_ref[1])
             w1c_ref[d] = w1
         w1e_ref[k, 0] = w1c_ref[0]
         w1e_ref[k, 1] = w1c_ref[last]
@@ -203,17 +220,18 @@
     lax.fori_loop(0, per, probe, 0)
 
 
-def third_kernel(bits_ref, p2m_ref, w1e_ref, w2e_ref, low_ref, high_ref, sums_in_ref, planes_ref,
-                 ahead_ref, before_ref, after_ref, diag_ref, dinv_ref,
+def third_kernel(odd_ref, token_ref, bits_ref, p2m_ref, w1e_ref, w2e_ref, off_ref, on_ref, sums_in_ref,
+                 planes_ref, ahead_ref, outside_ref, diag_ref, dinv_ref,
                  p1_ref, p2_ref, cross_ref, sums_ref, scale_ref):
     per, days = bits_ref.shape[:2]
     last = days - 1
+    odd = odd_ref[0]
 
     @pl.when(pl.program_id(0) == 0)
     def _():
-        before, ahead = before_ref[0], ahead_ref[last]
-        scale_ref[0] = before / before_ref[1]
-        scale_ref[1] = ahead / (after_ref[...] + ahead)
+        before, ahead = outside_ref[0], ahead_ref[last]
+        scale_ref[0] = before / outside_ref[1]
+        scale_ref[1] = ahead / outside_ref[2]
         scale_ref[2] = before * dinv_ref[0]
         scale_ref[3] = ahead * dinv_ref[last]
 
@@ -223,7 +241,7 @@
         for side, (d, inner) in enumerate(((0, 1), (last, last - 1))):
             bits = bits_ref[k, d]
             w1 = w1e_ref[k, side]
-            arrived = (low_ref if side == 0 else high_ref)[k]
+            arrived = chosen(odd, off_ref[k], on_ref[k]) if side == 0 else chosen(odd, on_ref[k], off_ref[k])
             neighbour = arrived + scale_ref[side] * signed(bits, dinv_ref[d])
             w2 = w2e_ref[k, side] + scale_ref[2 + side] * neighbour
             p1 = signed(bits, w1)
@@ -238,7 +256,7 @@
             product = half_product(w2, planes_ref, d)
             product = product + ahead_ref[min(d, inner)] * w2 * inner_w2
             if side == 0:
-                cross = before_ref[0] * w2
+                cross = outside_ref[0] * w2
                 cross_ref[k] = cross
                 product = product + cross * (scale_ref[0] * w1)
             n5 = n5 + folded(product)
@@ -332,6 +350,8 @@
         def spec(shape, kind):
             if kind == "hbm":
                 return pl.BlockSpec(memory_space=pltpu.HBM)
+            if kind == "smem":
+                return pl.BlockSpec(memory_space=pltpu.SMEM)
             return split(shape, per) if kind == "split" else whole(shape)
 
         return pl.pallas_call(
@@ -347,48 +367,61 @@
             compiler_params=pltpu.CompilerParams(vmem_limit_bytes=mib << 20),
         )(*[value for value, _ in ins])
 
-    planes, part, ahead, up, down, low_bits, high_bits = call(
+    odd = (lax.axis_index("day") % 2).astype(jnp.int32).reshape(1)
+    planes, part, ahead, small_off, small_on = call(
         planes_kernel, (1,),
-        [(couplings, "hbm"), (probe_bits, "hbm"), (land_mask, "whole")],
+        [(odd, "smem"), (couplings, "whole"), (land_mask, "whole")],
         [(weights, "whole", F32), (dplanes, "whole", F32), (dplanes, "whole", F32),
-         ((2,) + plane, "whole", F32), (plane, "whole", F32),
-         (edge, "whole", jnp.int32), (edge, "whole", jnp.int32)],
-        scratch=[pltpu.VMEM(couplings.shape, F32), pltpu.SemaphoreType.DMA((3,))],
-        cost=(0.5, 1), mib=56,
-    )
-    before = passed_along(up, 1)
-    after = passed_along(down, -1)
-    high_bits, low_bits, before, after = lax.optimization_barrier((high_bits, low_bits, before, after))
-    bits_prev = passed_along(high_bits, 1)
-    bits_next = passed_along(low_bits, -1)
-
-    w1, low, high, diag, dinv = call(
+         ((2,) + plane, "whole", F32), ((2,) + plane, "whole", F32)],
+        cost=(0.5, 1), mib=20,
+    )
+    small_off = moved(small_off, "off")
+    small_on = moved(small_on, "on")
+    off_bits, on_bits = call(
+        edges_kernel, (1,),
+        [(odd, "smem"), (probe_bits, "hbm")],
+        [(edge, "whole", jnp.int32), (edge, "whole", jnp.int32)],
+        scratch=[pltpu.SemaphoreType.DMA((2,))], cost=(0, 0.5), mib=4,
+    )
+    off_bits, on_bits, small_off, small_on = lax.optimization_barrier(
+        (off_bits, on_bits, small_off, small_on)
+    )
+    off_bits = moved(off_bits, "off")
+    on_bits = moved(on_bits, "on")
+
+    w1, off, on, diag, dinv, outside = call(
         first_kernel, grid,
-        [(probe_bits, "split"), (planes, "whole"), (ahead, "whole"), (before, "whole"),
-         (part, "whole")],
+        [(odd, "smem"), (probe_bits, "split"), (planes, "whole"), (ahead, "whole"),
+         (small_off, "whole"), (small_on, "whole"), (part, "whole")],
         [(field, "split", F32), (edge, "split", F32), (edge, "split", F32),
-         (dplanes, "whole", F32), (dplanes, "whole", F32)],
+         (dplanes, "whole", F32), (dplanes, "whole", F32), ((3,) + plane, "whole", F32)],
         scratch=[pltpu.VMEM(dplanes, F32)], cost=(1, 2),
     )
-    high_prev = passed_along(high, 1)
-    low_next = passed_along(low, -1)
+    on = moved(on, "on")
+    token, off_bits, on_bits = lax.optimization_barrier((dinv[0, :8, :128], off_bits, on_bits))
+    token = moved(token, "on")
+    off, outside, token = lax.optimization_barrier((off, outside, token))
+    off = moved(off, "off")
 
     p1m, p2m, w1e, w2e, high2, sums = call(
         second_kernel, grid,
-        [(probe_bits, "split"), (w1, "split"), (bits_prev, "split"), (bits_next, "split"),
-         (planes, "whole"), (ahead, "whole"), (before, "whole"), (after, "whole"),
+        [(odd, "smem"), (token, "whole"), (probe_bits, "split"), (w1, "split"), (off_bits, "split"),
+         (on_bits, "split"), (planes, "whole"), (ahead, "whole"), (outside, "whole"),
          (diag, "whole"), (dinv, "whole")],
         [(middle, "split", F32), (middle, "split", F32), (pair, "split", F32),
          (pair, "split", F32), (edge, "split", F32), (sums_shape, "split", F32)],
         scratch=[pltpu.VMEM((2,) + plane, F32), pltpu.VMEM(dplanes, F32)], cost=(1.5, 4), mib=20,
     )
-    high2_prev = passed_along(high2, 1)
+    token, off, high2 = lax.optimization_barrier((token, off, high2))
+    token = moved(token, "on")
+    high2, outside, token = lax.optimization_barrier((high2, outside, token))
+    high2_prev = moved(high2, "next")
 
     p1e, p2e, cross, sums = call(
         third_kernel, grid,
-        [(probe_bits, "split"), (p2m, "split"), (w1e, "split"), (w2e, "split"),
-         (high_prev, "split"), (low_next, "split"), (sums, "split"), (planes, "whole"),
-         (ahead, "whole"), (before, "whole"), (after, "whole"), (diag, "whole"), (dinv, "whole")],
+        [(odd, "smem"), (token, "whole"), (probe_bits, "split"), (p2m, "split"), (w1e, "split"), (w2e, "split"),
+         (off, "split"), (on, "split"), (sums, "split"), (planes, "whole"),
+         (ahead, "whole"), (outside, "whole"), (diag, "whole"), (dinv, "whole")],
         [(pair, "split", F32), (pair, "split", F32), (edge, "split", F32),
          (sums_shape, "split", F32)],
         scratch=[pltpu.VMEM((4,) + plane, F32)], cost=(0.7, 4), mib=20,
@@ -413,7 +446,7 @@
 
 
 def solution(mesh):
-    assert mesh.shape["day"] & (mesh.shape["day"] - 1) == 0
+    assert mesh.shape["day"] > 1 and mesh.shape["day"] & (mesh.shape["day"] - 1) == 0
     return jax.shard_map(
         body,
         mesh=mesh,

time: 98 us -> 96 us (0.980)
  starting transfers between devices: 59 us -> 30 us
  waiting for transfers between devices: 10.7 us -> 38.2 us
  Pallas kernels: 24.5 us -> 23.1 us
    ppermute x7 -> x9, waiting for transfers between devices: 2.92 us -> 25.4 us  [moved(): return lax.ppermute(value, 'day', [(i, target(i)) for i in range(count)])]
    ppermute x7 -> x9, starting transfers between devices: 45.2 us -> 29.9 us  [moved(): return lax.ppermute(value, 'day', [(i, target(i)) for i in range(count)])]
    ppermute x4, starting transfers between devices: 13.8 us -> 0.03 us  [body(): lax.ppermute(moments, 'day', [(i, i ^ step) for i in range(count)])]
    ppermute x4, waiting for transfers between devices: 7.78 us -> 12.9 us  [body(): lax.ppermute(moments, 'day', [(i, i ^ step) for i in range(count)])]
    pallas_call x6 -> x7, Pallas kernels: 24.5 us -> 23.1 us  [call(): pl.pallas_call(kernel, grid=grid, in_specs=[spec(value.shape, kind) for v...]
    unnamed x10 -> x8, local copies, waits for them, and re-layouts: 3.5 us -> 4.44 us
  transfers between devices with their start and end apart: 11 -> 13, of which waited for: 6 -> 11; matrix products, arithmetic and copies ran while one was open for 0% -> 0% of each run, Pallas kernels for 18% -> 22%
where the time goes in v3:
time: 96 us; the launch traced here: 95.8 us
  waiting for transfers between devices  38.2 us (40%)
  starting transfers between devices  30 us (31%)
  Pallas kernels  23.1 us (24%)
  local copies, waits for them, and re-layouts  4.44 us (5%)
    ppermute x9, starting transfers between devices, moved(): return lax.ppermute(value, 'day', [(i, target(i)) for i in range(count)])  29.9 us
    ppermute x9, waiting for transfers between devices, moved(): return lax.ppermute(value, 'day', [(i, target(i)) for i in range(count)])  25.4 us
    pallas_call x7, Pallas kernels, call(): pl.pallas_call(kernel, grid=grid, in_specs=[spec(value.shape, kind) for v...  23.1 us
    ppermute x4, waiting for transfers between devices, body(): lax.ppermute(moments, 'day', [(i, i ^ step) for i in range(count)])  12.9 us
    unnamed x8, local copies, waits for them, and re-layouts  4.44 us
  transfers between devices with their start and end apart: 13, of which 11 were waited for; matrix products, arithmetic and copies ran while one was open for 0% of the time, Pallas kernels for 22%

profile of v3, /device:TPU:0, one launch (start us, length us, event | category | flops | bytes accessed | tf_op | source)
XLA Modules:
  0.0 95.8 jit_solution(290150278028785594)
XLA Ops:
  0.0 0.0 copy-start.2
  0.0 1.4 %copy-done.2 = f32[6,4,32,512]{3,2,1,0:T(8,128)S(1)} copy-done((f32[6,4,32,512]{3,2,1,0:T(8,128)S(1)}, f32[6,4,32,512]{3,2,1,0:T(8,128)}, u32[]{:S(2)}) %copy-start.2) | copy-done | bytes 1572888
  1.4 0.0 copy-start.3
  1.4 0.8 copy-done.3
  2.2 0.5 shard_map.37
  2.7 5.5 %collective-permute-start = (f32[2,32,512]{2,1,0:T(8,128)S(1)}, f32[2,32,512]{2,1,0:T(8,128)S(1)}, u32[]{:S(2)}, u32[]{:S(2)}) collective-permute-start(f32[2,32,512]{2,1,0:T(8,128)S(1)} %get-tuple-element.48), channel_id=1, source_target_pairs={{0,15},{1,2},{2,1},{3,4},{4,3},{5,6},{6,5},{7,8},{8,7},{9,10},{10,... | collective-permute-start | bytes 393224 | tf_op jit(solution)/shard_map/ppermute | solution.py:22
  8.3 0.0 collective-permute-start.1
  8.3 0.0 copy-start
  8.3 2.2 %copy-done = s32[16,4,32,512]{3,2,1,0:T(8,128)S(1)} copy-done((s32[16,4,32,512]{3,2,1,0:T(8,128)S(1)}, s32[16,4,32,512]{3,2,1,0:T(8,128)}, u32[]{:S(2)}) %copy-start) | copy-done | bytes 4194328
  10.4 0.0 copy-start.1
  10.4 0.2 shard_map.38
  10.6 0.3 collective-permute-done.soff_ref
  10.9 0.0 collective-permute-done.1.son_ref
  10.9 4.4 %collective-permute-start.2 = (s32[16,32,512]{2,1,0:T(8,128)S(1)}, s32[16,32,512]{2,1,0:T(8,128)S(1)}, u32[]{:S(2)}, u32[]{:S(2)}) collective-permute-start(s32[16,32,512]{2,1,0:T(8,128)S(1)} %get-tuple-element.56), channel_id=1, source_target_pairs={{0,15},{1,2},{2,1},{3,4},{4,3},{5,6},{6,5},{7,8},{8,7},{9,10},{10,... | collective-permute-start | bytes 3145736 | tf_op jit(solution)/shard_map/ppermute | solution.py:22
  15.3 0.0 collective-permute-start.3
  15.4 0.0 copy-done.1
  15.4 6.1 %shard_map.39 = (f32[16,4,32,512]{3,2,1,0:T(8,128)S(1)}, f32[16,32,512]{2,1,0:T(8,128)S(1)}, f32[16,32,512]{2,1,0:T(8,128)S(1)}, f32[4,32,512]{2,1,0:T(8,128)S(1...) custom-call(s32[1]{0:T(128)} %bitcast.odd_ref, s32[16,4,32,512]{3,2,1,0:T(8,128)S(1)} %copy-done.1, ...), custom_call_target="tpu_custom_call" | custom-call | flops 25165824 | bytes 8388608 | tf_op jit(solution)/shard_map/pallas_call | solution.py:357
  21.4 6.5 %collective-permute-done.2.off_ref = s32[16,32,512]{2,1,0:T(8,128)S(1)} collective-permute-done((s32[16,32,512]{2,1,0:T(8,128)S(1)}, s32[16,32,512]{2,1,0:T(8,128)S(1)}, u32[]{:S(2)}, u32[]{:S(2)}) %collective-permute-start.2) | collective-permute-done | bytes 1048608 | tf_op jit(solution)/shard_map/ppermute | solution.py:22
  27.9 0.0 collective-permute-done.3.on_ref
  27.9 8.7 %collective-permute-start.4 = (f32[8,128]{1,0:T(8,128)S(1)}, f32[8,128]{1,0:T(8,128)S(1)}, u32[]{:S(2)}, u32[]{:S(2)}) collective-permute-start(f32[8,128]{1,0:T(8,128)S(1)} %slice_bitcast_fusion), channel_id=1, source_target_pairs={{0,1},{1,0},{2,3},{3,2},{4,5},{5,4},{6,7},{7,6},{8,9},{9,8},{10,11... | collective-permute-start | bytes 12296 | tf_op jit(solution)/shard_map/ppermute | solution.py:22
  36.7 0.8 collective-permute-done.4.token_ref
  37.5 2.1 %collective-permute-start.5 = (f32[16,32,512]{2,1,0:T(8,128)S(1)}, f32[16,32,512]{2,1,0:T(8,128)S(1)}, u32[]{:S(2)}, u32[]{:S(2)}) collective-permute-start(f32[16,32,512]{2,1,0:T(8,128)S(1)} %get-tuple-element.60), channel_id=1, source_target_pairs={{0,15},{1,2},{2,1},{3,4},{4,3},{5,6},{6,5},{7,8},{8,7},{9,10},{10,... | collective-permute-start | bytes 3145736 | tf_op jit(solution)/shard_map/ppermute | solution.py:22
  39.6 10.5 %shard_map.40 = (f32[16,2,32,512]{3,2,1,0:T(8,128)S(1)}, f32[16,2,32,512]{3,2,1,0:T(8,128)S(1)}, f32[16,2,32,512]{3,2,1,0:T(8,128)S(1)}, f32[16,2,32,512]{3,2,1,...) custom-call(s32[1]{0:T(128)} %bitcast.odd_ref, f32[8,128]{1,0:T(8,128)S(1)} %collective-permute-done.4.token_ref, ...), custom_call_target="tpu_custom_call" | custom-call | flops 37748736 | bytes 16777216 | tf_op jit(solution)/shard_map/pallas_call | solution.py:357
  50.1 4.4 %collective-permute-done.5.off_ref = f32[16,32,512]{2,1,0:T(8,128)S(1)} collective-permute-done((f32[16,32,512]{2,1,0:T(8,128)S(1)}, f32[16,32,512]{2,1,0:T(8,128)S(1)}, u32[]{:S(2)}, u32[]{:S(2)}) %collective-permute-start.5) | collective-permute-done | bytes 1048608 | tf_op jit(solution)/shard_map/ppermute | solution.py:22
  54.5 8.8 %collective-permute-start.6 = (f32[8,128]{1,0:T(8,128)S(1)}, f32[8,128]{1,0:T(8,128)S(1)}, u32[]{:S(2)}, u32[]{:S(2)}) collective-permute-start(f32[8,128]{1,0:T(8,128)S(1)} %collective-permute-done.4.token_ref), channel_id=1, source_target_pairs={{0,1},{1,0},{2,3},{3,2},{4,5},{5,4},{6,7},{7,6},{8,9},{9,8},{10,11... | collective-permute-start | bytes 12296 | tf_op jit(solution)/shard_map/ppermute | solution.py:22
  63.3 0.0 collective-permute-start.7
  63.3 0.8 collective-permute-done.6.token_ref
  64.1 0.3 collective-permute-start.8
  64.5 1.5 %collective-permute-done.7.on_ref = f32[16,32,512]{2,1,0:T(8,128)S(1)} collective-permute-done((f32[16,32,512]{2,1,0:T(8,128)S(1)}, f32[16,32,512]{2,1,0:T(8,128)S(1)}, u32[]{:S(2)}, u32[]{:S(2)}) %collective-permute-start.7) | collective-permute-done | bytes 1048608 | tf_op jit(solution)/shard_map/ppermute | solution.py:22
  66.0 4.0 %shard_map.41 = (f32[16,2,32,512]{3,2,1,0:T(8,128)S(1)}, f32[16,2,32,512]{3,2,1,0:T(8,128)S(1)}, f32[16,32,512]{2,1,0:T(8,128)S(1)}, f32[16,8,128]{2,1,0:T(8,128)S(1)}) custom-call(s32[1]{0:T(128)} %bitcast.odd_ref, f32[8,128]{1,0:T(8,128)S(1)} %collective-permute-done.6.token_ref, s32[16,4,32,512]{3,2,1,0:T(8,128)S(1)} %copy-done.1, ...), custom_call_target="tpu_custom_call" | custom-call | flops 17616076 | bytes 16777216 | tf_op jit(solution)/shard_map/pallas_call | solution.py:357
  70.0 11.0 %collective-permute-done.8.high_ref = f32[16,32,512]{2,1,0:T(8,128)S(1)} collective-permute-done((f32[16,32,512]{2,1,0:T(8,128)S(1)}, f32[16,32,512]{2,1,0:T(8,128)S(1)}, u32[]{:S(2)}, u32[]{:S(2)}) %collective-permute-start.8) | collective-permute-done | bytes 1048608 | tf_op jit(solution)/shard_map/ppermute | solution.py:22
  81.0 0.2 shard_map.42
  81.3 0.0 collective-permute-start.9
  81.3 1.2 %collective-permute-done.9 = f32[8,128]{1,0:T(8,128)S(1)} collective-permute-done((f32[8,128]{1,0:T(8,128)S(1)}, f32[8,128]{1,0:T(8,128)S(1)}, u32[]{:S(2)}, u32[]{:S(2)}) %collective-permute-start.9) | collective-permute-done | bytes 4128 | tf_op jit(solution)/shard_map/ppermute | solution.py:436
  82.5 0.0 collective-permute-start.10
  82.5 3.6 %collective-permute-done.10 = f32[8,128]{1,0:T(8,128)S(1)} collective-permute-done((f32[8,128]{1,0:T(8,128)S(1)}, f32[8,128]{1,0:T(8,128)S(1)}, u32[]{:S(2)}, u32[]{:S(2)}) %collective-permute-start.10) | collective-permute-done | bytes 4128 | tf_op jit(solution)/shard_map/ppermute | solution.py:436
  86.1 0.0 collective-permute-start.11
  86.1 3.6 %collective-permute-done.11 = f32[8,128]{1,0:T(8,128)S(1)} collective-permute-done((f32[8,128]{1,0:T(8,128)S(1)}, f32[8,128]{1,0:T(8,128)S(1)}, u32[]{:S(2)}, u32[]{:S(2)}) %collective-permute-start.11) | collective-permute-done | bytes 4128 | tf_op jit(solution)/shard_map/ppermute | solution.py:436
  89.7 0.0 collective-permute-start.12
  89.7 4.5 %collective-permute-done.12 = f32[8,128]{1,0:T(8,128)S(1)} collective-permute-done((f32[8,128]{1,0:T(8,128)S(1)}, f32[8,128]{1,0:T(8,128)S(1)}, u32[]{:S(2)}, u32[]{:S(2)}) %collective-permute-start.12) | collective-permute-done | bytes 4128 | tf_op jit(solution)/shard_map/ppermute | solution.py:436
  94.2 1.6 %shard_map.43 = f32[4,32,512]{2,1,0:T(8,128)} custom-call(f32[8,128]{1,0:T(8,128)S(1)} %add.20.moments_ref, f32[16,2,32,512]{3,2,1,0:T(8,128)S(1)} %get-tuple-element.80.p1m_ref, f32[16,2,32,512]{3,2,1,0:T(8,128)S(1)} %get-tuple-element.70.p2m_ref, f32[16,2,32,512]{3,2,1,0:T(8,128)S(1)} %get-tuple-element.81.p1e_ref, ...), custom_call_target="tpu_custom_call" | custom-call | flops 5033164 | bytes 8388608 | tf_op jit(solution)/shard_map/pallas_call | solution.py:357
  (5 shorter events, 0.0 us)
Async XLA Ops:
  0.0 1.4 %copy-start.2 = (f32[6,4,32,512]{3,2,1,0:T(8,128)S(1)}, f32[6,4,32,512]{3,2,1,0:T(8,128)}, u32[]{:S(2)}) copy-start(f32[6,4,32,512]{3,2,1,0:T(8,128)} %coup_ref.1) | copy-start | bytes 4718596
  1.4 0.8 copy-start.3
  2.7 8.2 %collective-permute-start = (f32[2,32,512]{2,1,0:T(8,128)S(1)}, f32[2,32,512]{2,1,0:T(8,128)S(1)}, u32[]{:S(2)}, u32[]{:S(2)}) collective-permute-start(f32[2,32,512]{2,1,0:T(8,128)S(1)} %get-tuple-element.48), channel_id=1, source_target_pairs={{0,15},{1,2},{2,1},{3,4},{4,3},{5,6},{6,5},{7,8},{8,7},{9,10},{10,... | collective-permute-start | bytes 393224 | tf_op jit(solution)/shard_map/ppermute | solution.py:22
  8.3 2.7 %collective-permute-start.1 = (f32[2,32,512]{2,1,0:T(8,128)S(1)}, f32[2,32,512]{2,1,0:T(8,128)S(1)}, u32[]{:S(2)}, u32[]{:S(2)}) collective-permute-start(f32[2,32,512]{2,1,0:T(8,128)S(1)} %get-tuple-element.49), channel_id=1, source_target_pairs={{0,1},{1,0},{2,3},{3,2},{4,5},{5,4},{6,7},{7,6},{8,9},{9,8},{10,11... | collective-permute-start | bytes 393224 | tf_op jit(solution)/shard_map/ppermute | solution.py:22
  8.3 2.2 %copy-start = (s32[16,4,32,512]{3,2,1,0:T(8,128)S(1)}, s32[16,4,32,512]{3,2,1,0:T(8,128)}, u32[]{:S(2)}) copy-start(s32[16,4,32,512]{3,2,1,0:T(8,128)} %bits_ref.5) | copy-start | bytes 12582916
  10.4 4.9 %copy-start.1 = (s32[16,4,32,512]{3,2,1,0:T(8,128)S(1)}, s32[16,4,32,512]{3,2,1,0:T(8,128)}, u32[]{:S(2)}) copy-start(s32[16,4,32,512]{3,2,1,0:T(8,128)} %bits_ref.5) | copy-start | bytes 12582916
  10.9 17.0 %collective-permute-start.2 = (s32[16,32,512]{2,1,0:T(8,128)S(1)}, s32[16,32,512]{2,1,0:T(8,128)S(1)}, u32[]{:S(2)}, u32[]{:S(2)}) collective-permute-start(s32[16,32,512]{2,1,0:T(8,128)S(1)} %get-tuple-element.56), channel_id=1, source_target_pairs={{0,15},{1,2},{2,1},{3,4},{4,3},{5,6},{6,5},{7,8},{8,7},{9,10},{10,... | collective-permute-start | bytes 3145736 | tf_op jit(solution)/shard_map/ppermute | solution.py:22
  15.3 12.6 %collective-permute-start.3 = (s32[16,32,512]{2,1,0:T(8,128)S(1)}, s32[16,32,512]{2,1,0:T(8,128)S(1)}, u32[]{:S(2)}, u32[]{:S(2)}) collective-permute-start(s32[16,32,512]{2,1,0:T(8,128)S(1)} %get-tuple-element.57), channel_id=1, source_target_pairs={{0,1},{1,0},{2,3},{3,2},{4,5},{5,4},{6,7},{7,6},{8,9},{9,8},{10,11... | collective-permute-start | bytes 3145736 | tf_op jit(solution)/shard_map/ppermute | solution.py:22
  27.9 9.6 %collective-permute-start.4 = (f32[8,128]{1,0:T(8,128)S(1)}, f32[8,128]{1,0:T(8,128)S(1)}, u32[]{:S(2)}, u32[]{:S(2)}) collective-permute-start(f32[8,128]{1,0:T(8,128)S(1)} %slice_bitcast_fusion), channel_id=1, source_target_pairs={{0,1},{1,0},{2,3},{3,2},{4,5},{5,4},{6,7},{7,6},{8,9},{9,8},{10,11... | collective-permute-start | bytes 12296 | tf_op jit(solution)/shard_map/ppermute | solution.py:22
  37.5 17.0 %collective-permute-start.5 = (f32[16,32,512]{2,1,0:T(8,128)S(1)}, f32[16,32,512]{2,1,0:T(8,128)S(1)}, u32[]{:S(2)}, u32[]{:S(2)}) collective-permute-start(f32[16,32,512]{2,1,0:T(8,128)S(1)} %get-tuple-element.60), channel_id=1, source_target_pairs={{0,15},{1,2},{2,1},{3,4},{4,3},{5,6},{6,5},{7,8},{8,7},{9,10},{10,... | collective-permute-start | bytes 3145736 | tf_op jit(solution)/shard_map/ppermute | solution.py:22
  54.5 9.6 %collective-permute-start.6 = (f32[8,128]{1,0:T(8,128)S(1)}, f32[8,128]{1,0:T(8,128)S(1)}, u32[]{:S(2)}, u32[]{:S(2)}) collective-permute-start(f32[8,128]{1,0:T(8,128)S(1)} %collective-permute-done.4.token_ref), channel_id=1, source_target_pairs={{0,1},{1,0},{2,3},{3,2},{4,5},{5,4},{6,7},{7,6},{8,9},{9,8},{10,11... | collective-permute-start | bytes 12296 | tf_op jit(solution)/shard_map/ppermute | solution.py:22
  63.3 2.7 %collective-permute-start.7 = (f32[16,32,512]{2,1,0:T(8,128)S(1)}, f32[16,32,512]{2,1,0:T(8,128)S(1)}, u32[]{:S(2)}, u32[]{:S(2)}) collective-permute-start(f32[16,32,512]{2,1,0:T(8,128)S(1)} %get-tuple-element.74), channel_id=1, source_target_pairs={{0,1},{1,0},{2,3},{3,2},{4,5},{5,4},{6,7},{7,6},{8,9},{9,8},{10,11... | collective-permute-start | bytes 3145736 | tf_op jit(solution)/shard_map/ppermute | solution.py:22
  64.1 16.9 %collective-permute-start.8 = (f32[16,32,512]{2,1,0:T(8,128)S(1)}, f32[16,32,512]{2,1,0:T(8,128)S(1)}, u32[]{:S(2)}, u32[]{:S(2)}) collective-permute-start(f32[16,32,512]{2,1,0:T(8,128)S(1)} %get-tuple-element.78), channel_id=1, source_target_pairs={{0,1},{1,2},{2,3},{3,4},{4,5},{5,6},{6,7},{7,8},{8,9},{9,10},{10,1... | collective-permute-start | bytes 3145736 | tf_op jit(solution)/shard_map/ppermute | solution.py:22
  81.3 1.2 %collective-permute-start.9 = (f32[8,128]{1,0:T(8,128)S(1)}, f32[8,128]{1,0:T(8,128)S(1)}, u32[]{:S(2)}, u32[]{:S(2)}) collective-permute-start(f32[8,128]{1,0:T(8,128)S(1)} %shard_map.42), channel_id=1, source_target_pairs={{0,1},{1,0},{2,3},{3,2},{4,5},{5,4},{6,7},{7,6},{8,9},{9,8},{10,11... | collective-permute-start | bytes 12296 | tf_op jit(solution)/shard_map/ppermute | solution.py:436
  82.5 3.6 %collective-permute-start.10 = (f32[8,128]{1,0:T(8,128)S(1)}, f32[8,128]{1,0:T(8,128)S(1)}, u32[]{:S(2)}, u32[]{:S(2)}) collective-permute-start(f32[8,128]{1,0:T(8,128)S(1)} %add.17), channel_id=1, source_target_pairs={{0,2},{1,3},{2,0},{3,1},{4,6},{5,7},{6,4},{7,5},{8,10},{9,11},{10,... | collective-permute-start | bytes 12296 | tf_op jit(solution)/shard_map/ppermute | solution.py:436
  86.1 3.6 %collective-permute-start.11 = (f32[8,128]{1,0:T(8,128)S(1)}, f32[8,128]{1,0:T(8,128)S(1)}, u32[]{:S(2)}, u32[]{:S(2)}) collective-permute-start(f32[8,128]{1,0:T(8,128)S(1)} %add.18), channel_id=1, source_target_pairs={{0,4},{1,5},{2,6},{3,7},{4,0},{5,1},{6,2},{7,3},{8,12},{9,13},{10,... | collective-permute-start | bytes 12296 | tf_op jit(solution)/shard_map/ppermute | solution.py:436
  89.7 4.5 %collective-permute-start.12 = (f32[8,128]{1,0:T(8,128)S(1)}, f32[8,128]{1,0:T(8,128)S(1)}, u32[]{:S(2)}, u32[]{:S(2)}) collective-permute-start(f32[8,128]{1,0:T(8,128)S(1)} %add.19), channel_id=1, source_target_pairs={{0,8},{1,9},{2,10},{3,11},{4,12},{5,13},{6,14},{7,15},{8,0},{9,1},... | collective-permute-start | bytes 12296 | tf_op jit(solution)/shard_map/ppermute | solution.py:436

commit v4 on v3

--- a/solution.py
+++ b/solution.py
@@ -34,22 +34,27 @@
 PLANES = 8
 
 
-def edges_kernel(odd_ref, bits_hbm, off_ref, on_ref, sems):
-    last = bits_hbm.shape[1] - 1
-    off_day = odd_ref[0] * last
-    off_copy = pltpu.make_async_copy(bits_hbm.at[:, off_day], off_ref, sems.at[0])
-    on_copy = pltpu.make_async_copy(bits_hbm.at[:, last - off_day], on_ref, sems.at[1])
-    off_copy.start()
-    on_copy.start()
-    off_copy.wait()
-    on_copy.wait()
-
-
-def planes_kernel(odd_ref, coup_ref, mask_ref, planes_ref, part_ref, ahead_ref,
-                  off_ref, on_ref):
+def planes_kernel(odd_ref, coup_hbm, bits_hbm, mask_hbm, own_ref, planes_ref, part_ref, ahead_ref,
+                  bits_ref, off_ref, on_ref, coup_ref, mask_ref, sems):
     days, rows, cols = coup_ref.shape[1:]
+    probes = bits_ref.shape[0]
     last = days - 1
     odd = odd_ref[0]
+    small = [
+        pltpu.make_async_copy(mask_hbm, mask_ref, sems.at[0]),
+        pltpu.make_async_copy(coup_hbm, coup_ref, sems.at[1]),
+    ]
+    chunk = probes // 4
+    large = [
+        pltpu.make_async_copy(
+            bits_hbm.at[pl.ds(n * chunk, chunk)], bits_ref.at[pl.ds(n * chunk, chunk)], sems.at[2 + n]
+        )
+        for n in range(4)
+    ]
+    for copy in small + large:
+        copy.start()
+    for copy in small:
+        copy.wait()
     mask = mask_ref[...]
     row = lax.broadcasted_iota(jnp.int32, (rows, cols), 0)
     col = lax.broadcasted_iota(jnp.int32, (rows, cols), 1)
@@ -76,9 +81,16 @@
             (east, west, south, se_w, sw_e, above, turned(se, 1, 0), turned(sw, 1, 0))
         ):
             planes_ref[n, d] = plane
+    for copy in large:
+        copy.wait()
     for out_ref, d in ((off_ref, odd * last), (on_ref, last - odd * last)):
-        out_ref[0] = coup_ref[5, last]
-        out_ref[1] = part_ref[d]
+        out_ref[probes] = part_ref[d]
+
+        def probe(k, carry):
+            out_ref[k] = jnp.where(bits_ref[k, d] == 1, 1.0, -1.0)
+            return carry
+
+        lax.fori_loop(0, probes, probe, 0)
 
 
 def chosen(odd, even_value, odd_value):
@@ -131,22 +143,17 @@
     return jnp.concatenate(rows, axis=0)
 
 
-def first_kernel(odd_ref, bits_ref, planes_ref, ahead_ref, soff_ref, son_ref, part_ref,
-                 w1_ref, off_ref, on_ref, diag_ref, dinv_ref, outside_ref, w0_ref):
+def first_kernel(odd_ref, bits_ref, planes_ref, ahead_ref, before_ref, part_ref,
+                 w1_ref, off_ref, on_ref, diag_ref, dinv_ref, w0_ref):
     per, days = bits_ref.shape[:2]
-    last = days - 1
     odd = odd_ref[0]
 
     @pl.when(pl.program_id(0) == 0)
     def _():
-        before = chosen(odd, soff_ref[0], son_ref[0])
-        outside_ref[0] = before
-        outside_ref[1] = chosen(odd, soff_ref[1], son_ref[1])
-        outside_ref[2] = chosen(odd, son_ref[1], soff_ref[1]) + ahead_ref[last]
         for d in range(days):
             diag = part_ref[d]
             if d == 0:
-                diag = diag + before
+                diag = diag + before_ref[...]
             diag_ref[d] = diag
             dinv_ref[d] = 1.0 / diag
 
@@ -165,25 +172,28 @@
     lax.fori_loop(0, per, probe, 0)
 
 
-def second_kernel(odd_ref, token_ref, bits_ref, w1_ref, off_ref, on_ref, planes_ref, ahead_ref, outside_ref,
-                  diag_ref, dinv_ref,
-                  p1_ref, p2_ref, w1e_ref, w2e_ref, high_ref, sums_ref, scale_ref, w1c_ref):
+def second_kernel(odd_ref, bits_ref, w1_ref, off_ref, on_ref, doff_ref, don_ref, planes_ref,
+                  ahead_ref, before_ref, diag_ref, dinv_ref,
+                  p1_ref, p2_ref, w1e_ref, w2e_ref, high_ref, sums_ref, ratio_ref, scale_ref, w1c_ref):
     per, days = w1_ref.shape[:2]
     last = days - 1
     odd = odd_ref[0]
 
     @pl.when(pl.program_id(0) == 0)
     def _():
-        scale_ref[0] = outside_ref[0] * dinv_ref[0] / outside_ref[1]
-        scale_ref[1] = ahead_ref[last] * dinv_ref[last] / outside_ref[2]
+        ahead = ahead_ref[last]
+        ratio_ref[0] = before_ref[...] / chosen(odd, doff_ref[0], don_ref[0])
+        ratio_ref[1] = ahead / (chosen(odd, don_ref[0], doff_ref[0]) + ahead)
+        scale_ref[0] = ratio_ref[0] * dinv_ref[0]
+        scale_ref[1] = ratio_ref[1] * dinv_ref[last]
 
     def probe(k, carry):
         for d in range(days):
             w1 = w1_ref[k, d]
             if d == 0:
-                w1 = w1 + signed(chosen(odd, off_ref[k], on_ref[k]), scale_ref[0])
+                w1 = w1 + chosen(odd, off_ref[k], on_ref[k]) * scale_ref[0]
             if d == last:
-                w1 = w1 + signed(chosen(odd, on_ref[k], off_ref[k]), scale_ref[1])
+                w1 = w1 + chosen(odd, on_ref[k], off_ref[k]) * scale_ref[1]
             w1c_ref[d] = w1
         w1e_ref[k, 0] = w1c_ref[0]
         w1e_ref[k, 1] = w1c_ref[last]
@@ -221,7 +231,7 @@
 
 
 def third_kernel(odd_ref, token_ref, bits_ref, p2m_ref, w1e_ref, w2e_ref, off_ref, on_ref, sums_in_ref,
-                 planes_ref, ahead_ref, outside_ref, diag_ref, dinv_ref,
+                 planes_ref, ahead_ref, before_ref, ratio_ref, diag_ref, dinv_ref,
                  p1_ref, p2_ref, cross_ref, sums_ref, scale_ref):
     per, days = bits_ref.shape[:2]
     last = days - 1
@@ -229,11 +239,8 @@
 
     @pl.when(pl.program_id(0) == 0)
     def _():
-        before, ahead = outside_ref[0], ahead_ref[last]
-        scale_ref[0] = before / outside_ref[1]
-        scale_ref[1] = ahead / outside_ref[2]
-        scale_ref[2] = before * dinv_ref[0]
-        scale_ref[3] = ahead * dinv_ref[last]
+        scale_ref[0] = before_ref[...] * dinv_ref[0]
+        scale_ref[1] = ahead_ref[last] * dinv_ref[last]
 
     def probe(k, carry):
         zero = jnp.zeros((8, 128), F32)
@@ -242,8 +249,8 @@
             bits = bits_ref[k, d]
             w1 = w1e_ref[k, side]
             arrived = chosen(odd, off_ref[k], on_ref[k]) if side == 0 else chosen(odd, on_ref[k], off_ref[k])
-            neighbour = arrived + scale_ref[side] * signed(bits, dinv_ref[d])
-            w2 = w2e_ref[k, side] + scale_ref[2 + side] * neighbour
+            neighbour = arrived + ratio_ref[side] * signed(bits, dinv_ref[d])
+            w2 = w2e_ref[k, side] + scale_ref[side] * neighbour
             p1 = signed(bits, w1)
             p1_ref[k, side] = p1
             p2_ref[k, side] = signed(bits, w2)
@@ -256,9 +263,9 @@
             product = half_product(w2, planes_ref, d)
             product = product + ahead_ref[min(d, inner)] * w2 * inner_w2
             if side == 0:
-                cross = outside_ref[0] * w2
+                cross = before_ref[...] * w2
                 cross_ref[k] = cross
-                product = product + cross * (scale_ref[0] * w1)
+                product = product + cross * (ratio_ref[0] * w1)
             n5 = n5 + folded(product)
         sums_ref[k] = sums_in_ref[k] + stacked([zero, n1, n2, n3, n4, 2.0 * n5])
         return carry
@@ -326,6 +333,10 @@
     return pl.BlockSpec((per,) + tuple(shape[1:]), lambda i: (i,) + (0,) * (len(shape) - 1))
 
 
+def hbm(value):
+    return pltpu.with_memory_space_constraint(value, pltpu.HBM)
+
+
 def whole(shape):
     return pl.BlockSpec(tuple(shape), lambda i: (0,) * len(shape))
 
@@ -350,6 +361,9 @@
         def spec(shape, kind):
             if kind == "hbm":
                 return pl.BlockSpec(memory_space=pltpu.HBM)
+            if kind == "last":
+                index = shape[0] - 1
+                return pl.BlockSpec((1,) + tuple(shape[1:]), lambda i: (index,) + (0,) * (len(shape) - 1))
             if kind == "smem":
                 return pl.BlockSpec(memory_space=pltpu.SMEM)
             return split(shape, per) if kind == "split" else whole(shape)
@@ -368,63 +382,58 @@
         )(*[value for value, _ in ins])
 
     odd = (lax.axis_index("day") % 2).astype(jnp.int32).reshape(1)
-    planes, part, ahead, small_off, small_on = call(
+    own = couplings[5, days - 1]
+    before = moved(own, "next")
+    sent = (probes + 1,) + plane
+    planes, part, ahead, bits, off_signs, on_signs = call(
         planes_kernel, (1,),
-        [(odd, "smem"), (couplings, "whole"), (land_mask, "whole")],
+        [(odd, "smem"), (hbm(couplings), "hbm"), (hbm(probe_bits), "hbm"), (hbm(land_mask), "hbm"),
+         (own, "whole")],
         [(weights, "whole", F32), (dplanes, "whole", F32), (dplanes, "whole", F32),
-         ((2,) + plane, "whole", F32), ((2,) + plane, "whole", F32)],
-        cost=(0.5, 1), mib=20,
-    )
-    small_off = moved(small_off, "off")
-    small_on = moved(small_on, "on")
-    off_bits, on_bits = call(
-        edges_kernel, (1,),
-        [(odd, "smem"), (probe_bits, "hbm")],
-        [(edge, "whole", jnp.int32), (edge, "whole", jnp.int32)],
-        scratch=[pltpu.SemaphoreType.DMA((2,))], cost=(0, 0.5), mib=4,
-    )
-    off_bits, on_bits, small_off, small_on = lax.optimization_barrier(
-        (off_bits, on_bits, small_off, small_on)
-    )
-    off_bits = moved(off_bits, "off")
-    on_bits = moved(on_bits, "on")
-
-    w1, off, on, diag, dinv, outside = call(
+         (field, "whole", jnp.int32), (sent, "whole", F32), (sent, "whole", F32)],
+        scratch=[pltpu.VMEM(couplings.shape, F32), pltpu.VMEM(plane, jnp.int32),
+                 pltpu.SemaphoreType.DMA((6,))],
+        cost=(0.5, 1), mib=32,
+    )
+    off_signs, on_signs, before = lax.optimization_barrier((off_signs, on_signs, before))
+    off_signs = moved(off_signs, "off")
+    on_signs = moved(on_signs, "on")
+
+    w1, off, on, diag, dinv = call(
         first_kernel, grid,
-        [(odd, "smem"), (probe_bits, "split"), (planes, "whole"), (ahead, "whole"),
-         (small_off, "whole"), (small_on, "whole"), (part, "whole")],
+        [(odd, "smem"), (bits, "split"), (planes, "whole"), (ahead, "whole"),
+         (before, "whole"), (part, "whole")],
         [(field, "split", F32), (edge, "split", F32), (edge, "split", F32),
-         (dplanes, "whole", F32), (dplanes, "whole", F32), ((3,) + plane, "whole", F32)],
+         (dplanes, "whole", F32), (dplanes, "whole", F32)],
         scratch=[pltpu.VMEM(dplanes, F32)], cost=(1, 2),
     )
     on = moved(on, "on")
-    token, off_bits, on_bits = lax.optimization_barrier((dinv[0, :8, :128], off_bits, on_bits))
+    off, off_signs = lax.optimization_barrier((off, off_signs))
+    off = moved(off, "off")
+
+    p1m, p2m, w1e, w2e, high2, sums, ratio = call(
+        second_kernel, grid,
+        [(odd, "smem"), (bits, "split"), (w1, "split"), (off_signs, "split"), (on_signs, "split"),
+         (off_signs, "last"), (on_signs, "last"), (planes, "whole"), (ahead, "whole"),
+         (before, "whole"), (diag, "whole"), (dinv, "whole")],
+        [(middle, "split", F32), (middle, "split", F32), (pair, "split", F32),
+         (pair, "split", F32), (edge, "split", F32), (sums_shape, "split", F32),
+         ((2,) + plane, "whole", F32)],
+        scratch=[pltpu.VMEM((2,) + plane, F32), pltpu.VMEM(dplanes, F32)], cost=(1.5, 4), mib=20,
+    )
+    token, off, high2 = lax.optimization_barrier((sums[0], off, high2))
     token = moved(token, "on")
-    off, outside, token = lax.optimization_barrier((off, outside, token))
-    off = moved(off, "off")
-
-    p1m, p2m, w1e, w2e, high2, sums = call(
-        second_kernel, grid,
-        [(odd, "smem"), (token, "whole"), (probe_bits, "split"), (w1, "split"), (off_bits, "split"),
-         (on_bits, "split"), (planes, "whole"), (ahead, "whole"), (outside, "whole"),
-         (diag, "whole"), (dinv, "whole")],
-        [(middle, "split", F32), (middle, "split", F32), (pair, "split", F32),
-         (pair, "split", F32), (edge, "split", F32), (sums_shape, "split", F32)],
-        scratch=[pltpu.VMEM((2,) + plane, F32), pltpu.VMEM(dplanes, F32)], cost=(1.5, 4), mib=20,
-    )
-    token, off, high2 = lax.optimization_barrier((token, off, high2))
-    token = moved(token, "on")
-    high2, outside, token = lax.optimization_barrier((high2, outside, token))
+    high2, ratio, token = lax.optimization_barrier((high2, ratio, token))
     high2_prev = moved(high2, "next")
 
     p1e, p2e, cross, sums = call(
         third_kernel, grid,
-        [(odd, "smem"), (token, "whole"), (probe_bits, "split"), (p2m, "split"), (w1e, "split"), (w2e, "split"),
-         (off, "split"), (on, "split"), (sums, "split"), (planes, "whole"),
-         (ahead, "whole"), (outside, "whole"), (diag, "whole"), (dinv, "whole")],
+        [(odd, "smem"), (token, "whole"), (bits, "split"), (p2m, "split"), (w1e, "split"),
+         (w2e, "split"), (off, "split"), (on, "split"), (sums, "split"), (planes, "whole"),
+         (ahead, "whole"), (before, "whole"), (ratio, "whole"), (diag, "whole"), (dinv, "whole")],
         [(pair, "split", F32), (pair, "split", F32), (edge, "split", F32),
          (sums_shape, "split", F32)],
-        scratch=[pltpu.VMEM((4,) + plane, F32)], cost=(0.7, 4), mib=20,
+        scratch=[pltpu.VMEM((2,) + plane, F32)], cost=(0.7, 4), mib=20,
     )
     (moments,) = call(
         fourth_kernel, (1,),

time: 96 us -> 92.1 us (0.959)
  starting transfers between devices: 30 us -> 20.5 us
  waiting for transfers between devices: 38.2 us -> 45.8 us
  local copies, waits for them, and re-layouts: 4.44 us -> 0.85 us
  Pallas kernels: 23.1 us -> 24.6 us
    ppermute x9 -> x7, starting transfers between devices: 29.9 us -> 19.7 us  [moved(): return lax.ppermute(value, 'day', [(i, target(i)) for i in range(count)])]
    ppermute x9 -> x7, waiting for transfers between devices: 25.4 us -> 33.7 us  [moved(): return lax.ppermute(value, 'day', [(i, target(i)) for i in range(count)])]
    unnamed x8 -> x0, local copies, waits for them, and re-layouts: 4.44 us -> none
    pallas_call x7 -> x6, Pallas kernels: 23.1 us -> 24.6 us  [call(): pl.pallas_call(kernel, grid=grid, in_specs=[spec(value.shape, kind) for v...]
  transfers between devices with their start and end apart: 13 -> 11, of which waited for: 11 -> 10; matrix products, arithmetic and copies ran while one was open for 0% -> 0% of each run, Pallas kernels for 22% -> 25%
where the time goes in v4:
time: 92.1 us; the launch traced here: 91.9 us
  waiting for transfers between devices  45.8 us (50%)
  Pallas kernels  24.6 us (27%)
  starting transfers between devices  20.5 us (22%)
    ppermute x7, waiting for transfers between devices, moved(): return lax.ppermute(value, 'day', [(i, target(i)) for i in range(count)])  33.7 us
    pallas_call x6, Pallas kernels, call(): pl.pallas_call(kernel, grid=grid, in_specs=[spec(value.shape, kind) for v...  24.6 us
    ppermute x7, starting transfers between devices, moved(): return lax.ppermute(value, 'day', [(i, target(i)) for i in range(count)])  19.7 us
    ppermute x4, waiting for transfers between devices, body(): lax.ppermute(moments, 'day', [(i, i ^ step) for i in range(count)])  12.1 us
  transfers between devices with their start and end apart: 11, of which 10 were waited for; matrix products, arithmetic and copies ran while one was open for 0% of the time, Pallas kernels for 25%

profile of v4, /device:TPU:0, one launch (start us, length us, event | category | flops | bytes accessed | tf_op | source)
XLA Modules:
  0.0 91.9 jit_solution(9108304155085397475)
XLA Ops:
  0.0 0.8 slice_bitcast_fusion.own_ref
  0.8 0.5 collective-permute-start
  1.3 3.1 %shard_map.37 = (f32[8,4,32,512]{3,2,1,0:T(8,128)S(1)}, f32[4,32,512]{2,1,0:T(8,128)S(1)}, f32[4,32,512]{2,1,0:T(8,128)S(1)}, s32[16,4,32,512]{3,2,1,0:T(8,128)S...) custom-call(s32[1]{0:T(128)} %bitcast.odd_ref, f32[6,4,32,512]{3,2,1,0:T(8,128)} %coup_hbm.1, ...), custom_call_target="tpu_custom_call" | custom-call | flops 12582912 | bytes 4194304 | tf_op jit(solution)/shard_map/pallas_call | solution.py:371
  4.4 3.8 %collective-permute-done.before_ref = f32[32,512]{1,0:T(8,128)S(1)} collective-permute-done((f32[32,512]{1,0:T(8,128)S(1)}, f32[32,512]{1,0:T(8,128)S(1)}, u32[]{:S(2)}, u32[]{:S(2)}) %collective-permute-start) | collective-permute-done | bytes 65568 | tf_op jit(solution)/shard_map/ppermute | solution.py:22
  8.2 1.2 %collective-permute-start.1 = (f32[17,32,512]{2,1,0:T(8,128)S(1)}, f32[17,32,512]{2,1,0:T(8,128)S(1)}, u32[]{:S(2)}, u32[]{:S(2)}) collective-permute-start(f32[17,32,512]{2,1,0:T(8,128)S(1)} %get-tuple-element.47), channel_id=1, source_target_pairs={{0,15},{1,2},{2,1},{3,4},{4,3},{5,6},{6,5},{7,8},{8,7},{9,10},{10,... | collective-permute-start | bytes 3342344 | tf_op jit(solution)/shard_map/ppermute | solution.py:22
  9.5 0.0 collective-permute-start.2
  9.5 5.9 %shard_map.38 = (f32[16,4,32,512]{3,2,1,0:T(8,128)S(1)}, f32[16,32,512]{2,1,0:T(8,128)S(1)}, f32[16,32,512]{2,1,0:T(8,128)S(1)}, f32[4,32,512]{2,1,0:T(8,128)S(1)}, f32[4,32,512]{2,1,0:T(8,128)S(1)}) custom-call(s32[1]{0:T(128)} %bitcast.odd_ref, s32[16,4,32,512]{3,2,1,0:T(8,128)S(1)} %get-tuple-element.38.bits_ref, ...), custom_call_target="tpu_custom_call" | custom-call | flops 25165824 | bytes 8388608 | tf_op jit(solution)/shard_map/pallas_call | solution.py:371
  15.4 10.6 %collective-permute-done.1.off_ref.doff_ref = f32[17,32,512]{2,1,0:T(8,128)S(1)} collective-permute-done((f32[17,32,512]{2,1,0:T(8,128)S(1)}, f32[17,32,512]{2,1,0:T(8,128)S(1)}, u32[]{:S(2)}, u32[]{:S(2)}) %collective-permute-start.1) | collective-permute-done | bytes 1114144 | tf_op jit(solution)/shard_map/ppermute | solution.py:22
  26.0 1.2 %collective-permute-start.3 = (f32[16,32,512]{2,1,0:T(8,128)S(1)}, f32[16,32,512]{2,1,0:T(8,128)S(1)}, u32[]{:S(2)}, u32[]{:S(2)}) collective-permute-start(f32[16,32,512]{2,1,0:T(8,128)S(1)} %get-tuple-element.53), channel_id=1, source_target_pairs={{0,15},{1,2},{2,1},{3,4},{4,3},{5,6},{6,5},{7,8},{8,7},{9,10},{10,... | collective-permute-start | bytes 3145736 | tf_op jit(solution)/shard_map/ppermute | solution.py:22
  27.2 0.0 collective-permute-done.2.on_ref.don_ref
  27.2 9.8 %shard_map.39 = (f32[16,2,32,512]{3,2,1,0:T(8,128)S(1)}, f32[16,2,32,512]{3,2,1,0:T(8,128)S(1)}, f32[16,2,32,512]{3,2,1,0:T(8,128)S(1)}, f32[16,2,32,512]{3,2,1,...) custom-call(s32[1]{0:T(128)} %bitcast.odd_ref, ...), custom_call_target="tpu_custom_call" | custom-call | flops 37748736 | bytes 16777216 | tf_op jit(solution)/shard_map/pallas_call | solution.py:371
  37.0 6.0 %collective-permute-done.3.off_ref = f32[16,32,512]{2,1,0:T(8,128)S(1)} collective-permute-done((f32[16,32,512]{2,1,0:T(8,128)S(1)}, f32[16,32,512]{2,1,0:T(8,128)S(1)}, u32[]{:S(2)}, u32[]{:S(2)}) %collective-permute-start.3) | collective-permute-done | bytes 1048608 | tf_op jit(solution)/shard_map/ppermute | solution.py:22
  43.0 16.4 %collective-permute-start.4 = (f32[8,128]{1,0:T(8,128)S(1)}, f32[8,128]{1,0:T(8,128)S(1)}, u32[]{:S(2)}, u32[]{:S(2)}) collective-permute-start(f32[8,128]{1,0:T(8,128)S(1)} %slice_bitcast_fusion.1), channel_id=1, source_target_pairs={{0,1},{1,0},{2,3},{3,2},{4,5},{5,4},{6,7},{7,6},{8,9},{9,8},{10,11... | collective-permute-start | bytes 12296 | tf_op jit(solution)/shard_map/ppermute | solution.py:22
  59.4 0.0 collective-permute-start.5
  59.4 0.8 collective-permute-done.4.token_ref
  60.3 0.3 collective-permute-start.6
  60.6 1.5 %collective-permute-done.5.on_ref = f32[16,32,512]{2,1,0:T(8,128)S(1)} collective-permute-done((f32[16,32,512]{2,1,0:T(8,128)S(1)}, f32[16,32,512]{2,1,0:T(8,128)S(1)}, u32[]{:S(2)}, u32[]{:S(2)}) %collective-permute-start.5) | collective-permute-done | bytes 1048608 | tf_op jit(solution)/shard_map/ppermute | solution.py:22
  62.1 4.1 %shard_map.40 = (f32[16,2,32,512]{3,2,1,0:T(8,128)S(1)}, f32[16,2,32,512]{3,2,1,0:T(8,128)S(1)}, f32[16,32,512]{2,1,0:T(8,128)S(1)}, f32[16,8,128]{2,1,0:T(8,128)S(1)}) custom-call(s32[1]{0:T(128)} %bitcast.odd_ref, f32[8,128]{1,0:T(8,128)S(1)} %collective-permute-done.4.token_ref, s32[16,4,32,512]{3,2,1,0:T(8,128)S(1)} %get-tuple-element.38.bits_ref, ...), custom_call_target="tpu_custom_call" | custom-call | flops 17616076 | bytes 16777216 | tf_op jit(solution)/shard_map/pallas_call | solution.py:371
  66.2 11.0 %collective-permute-done.6.high_ref = f32[16,32,512]{2,1,0:T(8,128)S(1)} collective-permute-done((f32[16,32,512]{2,1,0:T(8,128)S(1)}, f32[16,32,512]{2,1,0:T(8,128)S(1)}, u32[]{:S(2)}, u32[]{:S(2)}) %collective-permute-start.6) | collective-permute-done | bytes 1048608 | tf_op jit(solution)/shard_map/ppermute | solution.py:22
  77.2 0.2 shard_map.41
  77.4 0.0 collective-permute-start.7
  77.4 1.2 %collective-permute-done.7 = f32[8,128]{1,0:T(8,128)S(1)} collective-permute-done((f32[8,128]{1,0:T(8,128)S(1)}, f32[8,128]{1,0:T(8,128)S(1)}, u32[]{:S(2)}, u32[]{:S(2)}) %collective-permute-start.7) | collective-permute-done | bytes 4128 | tf_op jit(solution)/shard_map/ppermute | solution.py:445
  78.6 0.0 collective-permute-start.8
  78.6 3.6 %collective-permute-done.8 = f32[8,128]{1,0:T(8,128)S(1)} collective-permute-done((f32[8,128]{1,0:T(8,128)S(1)}, f32[8,128]{1,0:T(8,128)S(1)}, u32[]{:S(2)}, u32[]{:S(2)}) %collective-permute-start.8) | collective-permute-done | bytes 4128 | tf_op jit(solution)/shard_map/ppermute | solution.py:445
  82.2 0.0 collective-permute-start.9
  82.2 3.6 %collective-permute-done.9 = f32[8,128]{1,0:T(8,128)S(1)} collective-permute-done((f32[8,128]{1,0:T(8,128)S(1)}, f32[8,128]{1,0:T(8,128)S(1)}, u32[]{:S(2)}, u32[]{:S(2)}) %collective-permute-start.9) | collective-permute-done | bytes 4128 | tf_op jit(solution)/shard_map/ppermute | solution.py:445
  85.8 0.8 collective-permute-start.10
  86.6 3.7 %collective-permute-done.10 = f32[8,128]{1,0:T(8,128)S(1)} collective-permute-done((f32[8,128]{1,0:T(8,128)S(1)}, f32[8,128]{1,0:T(8,128)S(1)}, u32[]{:S(2)}, u32[]{:S(2)}) %collective-permute-start.10) | collective-permute-done | bytes 4128 | tf_op jit(solution)/shard_map/ppermute | solution.py:445
  90.3 1.6 %shard_map.42 = f32[4,32,512]{2,1,0:T(8,128)} custom-call(f32[8,128]{1,0:T(8,128)S(1)} %add.20.moments_ref, f32[16,2,32,512]{3,2,1,0:T(8,128)S(1)} %get-tuple-element.68.p1m_ref, f32[16,2,32,512]{3,2,1,0:T(8,128)S(1)} %get-tuple-element.59.p2m_ref, f32[16,2,32,512]{3,2,1,0:T(8,128)S(1)} %get-tuple-element.69.p1e_ref, ...), custom_call_target="tpu_custom_call" | custom-call | flops 5033164 | bytes 8388608 | tf_op jit(solution)/shard_map/pallas_call | solution.py:371
  (5 shorter events, 0.0 us)
Async XLA Ops:
  0.8 7.4 %collective-permute-start = (f32[32,512]{1,0:T(8,128)S(1)}, f32[32,512]{1,0:T(8,128)S(1)}, u32[]{:S(2)}, u32[]{:S(2)}) collective-permute-start(f32[32,512]{1,0:T(8,128)S(1)} %slice_bitcast_fusion.own_ref), channel_id=1, source_target_pairs={{0,1},{1,2},{2,3},{3,4},{4,5},{5,6},{6,7},{7,8},{8,9},{9,10},{10,1... | collective-permute-start | bytes 196616 | tf_op jit(solution)/shard_map/ppermute | solution.py:22
  8.2 17.7 %collective-permute-start.1 = (f32[17,32,512]{2,1,0:T(8,128)S(1)}, f32[17,32,512]{2,1,0:T(8,128)S(1)}, u32[]{:S(2)}, u32[]{:S(2)}) collective-permute-start(f32[17,32,512]{2,1,0:T(8,128)S(1)} %get-tuple-element.47), channel_id=1, source_target_pairs={{0,15},{1,2},{2,1},{3,4},{4,3},{5,6},{6,5},{7,8},{8,7},{9,10},{10,... | collective-permute-start | bytes 3342344 | tf_op jit(solution)/shard_map/ppermute | solution.py:22
  9.5 17.7 %collective-permute-start.2 = (f32[17,32,512]{2,1,0:T(8,128)S(1)}, f32[17,32,512]{2,1,0:T(8,128)S(1)}, u32[]{:S(2)}, u32[]{:S(2)}) collective-permute-start(f32[17,32,512]{2,1,0:T(8,128)S(1)} %get-tuple-element.49), channel_id=1, source_target_pairs={{0,1},{1,0},{2,3},{3,2},{4,5},{5,4},{6,7},{7,6},{8,9},{9,8},{10,11... | collective-permute-start | bytes 3342344 | tf_op jit(solution)/shard_map/ppermute | solution.py:22
  26.0 17.0 %collective-permute-start.3 = (f32[16,32,512]{2,1,0:T(8,128)S(1)}, f32[16,32,512]{2,1,0:T(8,128)S(1)}, u32[]{:S(2)}, u32[]{:S(2)}) collective-permute-start(f32[16,32,512]{2,1,0:T(8,128)S(1)} %get-tuple-element.53), channel_id=1, source_target_pairs={{0,15},{1,2},{2,1},{3,4},{4,3},{5,6},{6,5},{7,8},{8,7},{9,10},{10,... | collective-permute-start | bytes 3145736 | tf_op jit(solution)/shard_map/ppermute | solution.py:22
  43.0 17.3 %collective-permute-start.4 = (f32[8,128]{1,0:T(8,128)S(1)}, f32[8,128]{1,0:T(8,128)S(1)}, u32[]{:S(2)}, u32[]{:S(2)}) collective-permute-start(f32[8,128]{1,0:T(8,128)S(1)} %slice_bitcast_fusion.1), channel_id=1, source_target_pairs={{0,1},{1,0},{2,3},{3,2},{4,5},{5,4},{6,7},{7,6},{8,9},{9,8},{10,11... | collective-permute-start | bytes 12296 | tf_op jit(solution)/shard_map/ppermute | solution.py:22
  59.4 2.7 %collective-permute-start.5 = (f32[16,32,512]{2,1,0:T(8,128)S(1)}, f32[16,32,512]{2,1,0:T(8,128)S(1)}, u32[]{:S(2)}, u32[]{:S(2)}) collective-permute-start(f32[16,32,512]{2,1,0:T(8,128)S(1)} %get-tuple-element.63), channel_id=1, source_target_pairs={{0,1},{1,0},{2,3},{3,2},{4,5},{5,4},{6,7},{7,6},{8,9},{9,8},{10,11... | collective-permute-start | bytes 3145736 | tf_op jit(solution)/shard_map/ppermute | solution.py:22
  60.3 16.9 %collective-permute-start.6 = (f32[16,32,512]{2,1,0:T(8,128)S(1)}, f32[16,32,512]{2,1,0:T(8,128)S(1)}, u32[]{:S(2)}, u32[]{:S(2)}) collective-permute-start(f32[16,32,512]{2,1,0:T(8,128)S(1)} %get-tuple-element.66), channel_id=1, source_target_pairs={{0,1},{1,2},{2,3},{3,4},{4,5},{5,6},{6,7},{7,8},{8,9},{9,10},{10,1... | collective-permute-start | bytes 3145736 | tf_op jit(solution)/shard_map/ppermute | solution.py:22
  77.4 1.2 %collective-permute-start.7 = (f32[8,128]{1,0:T(8,128)S(1)}, f32[8,128]{1,0:T(8,128)S(1)}, u32[]{:S(2)}, u32[]{:S(2)}) collective-permute-start(f32[8,128]{1,0:T(8,128)S(1)} %shard_map.41), channel_id=1, source_target_pairs={{0,1},{1,0},{2,3},{3,2},{4,5},{5,4},{6,7},{7,6},{8,9},{9,8},{10,11... | collective-permute-start | bytes 12296 | tf_op jit(solution)/shard_map/ppermute | solution.py:445
  78.6 3.6 %collective-permute-start.8 = (f32[8,128]{1,0:T(8,128)S(1)}, f32[8,128]{1,0:T(8,128)S(1)}, u32[]{:S(2)}, u32[]{:S(2)}) collective-permute-start(f32[8,128]{1,0:T(8,128)S(1)} %add.17), channel_id=1, source_target_pairs={{0,2},{1,3},{2,0},{3,1},{4,6},{5,7},{6,4},{7,5},{8,10},{9,11},{10,... | collective-permute-start | bytes 12296 | tf_op jit(solution)/shard_map/ppermute | solution.py:445
  82.2 3.6 %collective-permute-start.9 = (f32[8,128]{1,0:T(8,128)S(1)}, f32[8,128]{1,0:T(8,128)S(1)}, u32[]{:S(2)}, u32[]{:S(2)}) collective-permute-start(f32[8,128]{1,0:T(8,128)S(1)} %add.18), channel_id=1, source_target_pairs={{0,4},{1,5},{2,6},{3,7},{4,0},{5,1},{6,2},{7,3},{8,12},{9,13},{10,... | collective-permute-start | bytes 12296 | tf_op jit(solution)/shard_map/ppermute | solution.py:445
  85.8 4.5 %collective-permute-start.10 = (f32[8,128]{1,0:T(8,128)S(1)}, f32[8,128]{1,0:T(8,128)S(1)}, u32[]{:S(2)}, u32[]{:S(2)}) collective-permute-start(f32[8,128]{1,0:T(8,128)S(1)} %add.19), channel_id=1, source_target_pairs={{0,8},{1,9},{2,10},{3,11},{4,12},{5,13},{6,14},{7,15},{8,0},{9,1},... | collective-permute-start | bytes 12296 | tf_op jit(solution)/shard_map/ppermute | solution.py:445

commit v5 on v4

--- a/solution.py
+++ b/solution.py
@@ -314,10 +314,11 @@
     )
 
 
-def last_kernel(moments_ref, p1m_ref, p2m_ref, p1e_ref, p2e_ref, dinv_ref, out_ref):
+def last_kernel(p1m_ref, p2m_ref, p1e_ref, p2e_ref, dinv_ref, *refs):
+    out_ref = refs[-1]
     probes, inner = p1m_ref.shape[:2]
     days = inner + 2
-    c0, c1, c2 = coefficients(moments_ref[...], probes)
+    c0, c1, c2 = coefficients(functools.reduce(jnp.add, [ref[...] for ref in refs[:-1]]), probes)
     c0 = jnp.sum(c0, axis=1, keepdims=True)
     for d in range(days):
         edge = d in (0, days - 1)
@@ -408,7 +409,6 @@
         scratch=[pltpu.VMEM(dplanes, F32)], cost=(1, 2),
     )
     on = moved(on, "on")
-    off, off_signs = lax.optimization_barrier((off, off_signs))
     off = moved(off, "off")
 
     p1m, p2m, w1e, w2e, high2, sums, ratio = call(
@@ -440,15 +440,21 @@
         [(cross, "whole"), (high2_prev, "whole"), (sums, "whole")],
         [(tile, "whole", F32)], cost=(0.1, 0.5), mib=8,
     )
+    groups = [moments]
     step = 1
     while step < count:
-        moments = moments + lax.ppermute(moments, "day", [(i, i ^ step) for i in range(count)])
-        step *= 2
+        near = min(4, count // step)
+        moments = functools.reduce(jnp.add, groups)
+        groups = [moments] + [
+            lax.ppermute(moments, "day", [(i, i ^ (n * step)) for i in range(count)])
+            for n in range(1, near)
+        ]
+        step *= near
 
     (out,) = call(
         last_kernel, (1,),
-        [(moments, "whole"), (p1m, "whole"), (p2m, "whole"), (p1e, "whole"), (p2e, "whole"),
-         (dinv, "whole")],
+        [(p1m, "whole"), (p2m, "whole"), (p1e, "whole"), (p2e, "whole"), (dinv, "whole")]
+        + [(moments, "whole") for moments in groups],
         [(dplanes, "whole", F32)], cost=(0.2, 2), mib=24,
     )
     return out

time: 92.1 us -> 86.2 us (0.936)
  waiting for transfers between devices: 45.8 us -> 29.7 us
  starting transfers between devices: 20.5 us -> 30.9 us
    ppermute x4 -> x6, waiting for transfers between devices: 12.1 us -> 3.74 us  [body(): lax.ppermute(moments, 'day', [(i, i ^ n * step) for i in range(count)])]
    ppermute x7, waiting for transfers between devices: 33.7 us -> 25.9 us  [moved(): return lax.ppermute(value, 'day', [(i, target(i)) for i in range(count)])]
    ppermute x4 -> x6, starting transfers between devices: 0.82 us -> 6.32 us  [body(): lax.ppermute(moments, 'day', [(i, i ^ n * step) for i in range(count)])]
    ppermute x7, starting transfers between devices: 19.7 us -> 24.5 us  [moved(): return lax.ppermute(value, 'day', [(i, target(i)) for i in range(count)])]
  transfers between devices with their start and end apart: 11 -> 13, of which waited for: 10 -> 10; matrix products, arithmetic and copies ran while one was open for 0% -> 0% of each run, Pallas kernels for 25% -> 27%
where the time goes in v5:
time: 86.2 us; the launch traced here: 86.1 us
  starting transfers between devices  30.9 us (36%)
  waiting for transfers between devices  29.7 us (34%)
  Pallas kernels  24.6 us (29%)
    ppermute x7, waiting for transfers between devices, moved(): return lax.ppermute(value, 'day', [(i, target(i)) for i in range(count)])  25.9 us
    pallas_call x6, Pallas kernels, call(): pl.pallas_call(kernel, grid=grid, in_specs=[spec(value.shape, kind) for v...  24.6 us
    ppermute x7, starting transfers between devices, moved(): return lax.ppermute(value, 'day', [(i, target(i)) for i in range(count)])  24.5 us
    ppermute x6, starting transfers between devices, body(): lax.ppermute(moments, 'day', [(i, i ^ n * step) for i in range(count)])  6.32 us
    ppermute x6, waiting for transfers between devices, body(): lax.ppermute(moments, 'day', [(i, i ^ n * step) for i in range(count)])  3.74 us
  transfers between devices with their start and end apart: 13, of which 10 were waited for; matrix products, arithmetic and copies ran while one was open for 0% of the time, Pallas kernels for 27%

profile of v5, /device:TPU:0, one launch (start us, length us, event | category | flops | bytes accessed | tf_op | source)
XLA Modules:
  0.0 86.1 jit_solution(5271906777433347988)
XLA Ops:
  0.0 0.8 slice_bitcast_fusion.own_ref
  0.8 0.5 collective-permute-start
  1.3 3.1 %shard_map.37 = (f32[8,4,32,512]{3,2,1,0:T(8,128)S(1)}, f32[4,32,512]{2,1,0:T(8,128)S(1)}, f32[4,32,512]{2,1,0:T(8,128)S(1)}, s32[16,4,32,512]{3,2,1,0:T(8,128)S...) custom-call(s32[1]{0:T(128)} %bitcast.odd_ref, f32[6,4,32,512]{3,2,1,0:T(8,128)} %coup_hbm.1, ...), custom_call_target="tpu_custom_call" | custom-call | flops 12582912 | bytes 4194304 | tf_op jit(solution)/shard_map/pallas_call | solution.py:372
  4.4 3.8 %collective-permute-done.before_ref = f32[32,512]{1,0:T(8,128)S(1)} collective-permute-done((f32[32,512]{1,0:T(8,128)S(1)}, f32[32,512]{1,0:T(8,128)S(1)}, u32[]{:S(2)}, u32[]{:S(2)}) %collective-permute-start) | collective-permute-done | bytes 65568 | tf_op jit(solution)/shard_map/ppermute | solution.py:22
  8.2 1.2 %collective-permute-start.1 = (f32[17,32,512]{2,1,0:T(8,128)S(1)}, f32[17,32,512]{2,1,0:T(8,128)S(1)}, u32[]{:S(2)}, u32[]{:S(2)}) collective-permute-start(f32[17,32,512]{2,1,0:T(8,128)S(1)} %get-tuple-element.44), channel_id=1, source_target_pairs={{0,15},{1,2},{2,1},{3,4},{4,3},{5,6},{6,5},{7,8},{8,7},{9,10},{10,... | collective-permute-start | bytes 3342344 | tf_op jit(solution)/shard_map/ppermute | solution.py:22
  9.5 0.0 collective-permute-start.2
  9.5 5.9 %shard_map.38 = (f32[16,4,32,512]{3,2,1,0:T(8,128)S(1)}, f32[16,32,512]{2,1,0:T(8,128)S(1)}, f32[16,32,512]{2,1,0:T(8,128)S(1)}, f32[4,32,512]{2,1,0:T(8,128)S(1)}, f32[4,32,512]{2,1,0:T(8,128)S(1)}) custom-call(s32[1]{0:T(128)} %bitcast.odd_ref, s32[16,4,32,512]{3,2,1,0:T(8,128)S(1)} %get-tuple-element.36.bits_ref, ...), custom_call_target="tpu_custom_call" | custom-call | flops 25165824 | bytes 8388608 | tf_op jit(solution)/shard_map/pallas_call | solution.py:372
  15.4 3.3 %collective-permute-start.3 = (f32[16,32,512]{2,1,0:T(8,128)S(1)}, f32[16,32,512]{2,1,0:T(8,128)S(1)}, u32[]{:S(2)}, u32[]{:S(2)}) collective-permute-start(f32[16,32,512]{2,1,0:T(8,128)S(1)} %get-tuple-element.51), channel_id=1, source_target_pairs={{0,15},{1,2},{2,1},{3,4},{4,3},{5,6},{6,5},{7,8},{8,7},{9,10},{10,... | collective-permute-start | bytes 3145736 | tf_op jit(solution)/shard_map/ppermute | solution.py:22
  18.6 7.3 %collective-permute-done.1.off_ref.doff_ref = f32[17,32,512]{2,1,0:T(8,128)S(1)} collective-permute-done((f32[17,32,512]{2,1,0:T(8,128)S(1)}, f32[17,32,512]{2,1,0:T(8,128)S(1)}, u32[]{:S(2)}, u32[]{:S(2)}) %collective-permute-start.1) | collective-permute-done | bytes 1114144 | tf_op jit(solution)/shard_map/ppermute | solution.py:22
  26.0 0.0 collective-permute-done.2.on_ref.don_ref
  26.0 9.8 %shard_map.39 = (f32[16,2,32,512]{3,2,1,0:T(8,128)S(1)}, f32[16,2,32,512]{3,2,1,0:T(8,128)S(1)}, f32[16,2,32,512]{3,2,1,0:T(8,128)S(1)}, f32[16,2,32,512]{3,2,1,...) custom-call(s32[1]{0:T(128)} %bitcast.odd_ref, ...), custom_call_target="tpu_custom_call" | custom-call | flops 37748736 | bytes 16777216 | tf_op jit(solution)/shard_map/pallas_call | solution.py:372
  35.8 1.4 %collective-permute-done.3.off_ref = f32[16,32,512]{2,1,0:T(8,128)S(1)} collective-permute-done((f32[16,32,512]{2,1,0:T(8,128)S(1)}, f32[16,32,512]{2,1,0:T(8,128)S(1)}, u32[]{:S(2)}, u32[]{:S(2)}) %collective-permute-start.3) | collective-permute-done | bytes 1048608 | tf_op jit(solution)/shard_map/ppermute | solution.py:22
  37.2 19.2 %collective-permute-start.4 = (f32[8,128]{1,0:T(8,128)S(1)}, f32[8,128]{1,0:T(8,128)S(1)}, u32[]{:S(2)}, u32[]{:S(2)}) collective-permute-start(f32[8,128]{1,0:T(8,128)S(1)} %slice_bitcast_fusion.1), channel_id=1, source_target_pairs={{0,1},{1,0},{2,3},{3,2},{4,5},{5,4},{6,7},{7,6},{8,9},{9,8},{10,11... | collective-permute-start | bytes 12296 | tf_op jit(solution)/shard_map/ppermute | solution.py:22
  56.4 0.0 collective-permute-start.5
  56.4 0.8 collective-permute-done.4.token_ref
  57.3 0.3 collective-permute-start.6
  57.6 1.5 %collective-permute-done.5.on_ref = f32[16,32,512]{2,1,0:T(8,128)S(1)} collective-permute-done((f32[16,32,512]{2,1,0:T(8,128)S(1)}, f32[16,32,512]{2,1,0:T(8,128)S(1)}, u32[]{:S(2)}, u32[]{:S(2)}) %collective-permute-start.5) | collective-permute-done | bytes 1048608 | tf_op jit(solution)/shard_map/ppermute | solution.py:22
  59.1 4.1 %shard_map.40 = (f32[16,2,32,512]{3,2,1,0:T(8,128)S(1)}, f32[16,2,32,512]{3,2,1,0:T(8,128)S(1)}, f32[16,32,512]{2,1,0:T(8,128)S(1)}, f32[16,8,128]{2,1,0:T(8,128)S(1)}) custom-call(s32[1]{0:T(128)} %bitcast.odd_ref, f32[8,128]{1,0:T(8,128)S(1)} %collective-permute-done.4.token_ref, s32[16,4,32,512]{3,2,1,0:T(8,128)S(1)} %get-tuple-element.36.bits_ref, ...), custom_call_target="tpu_custom_call" | custom-call | flops 17616076 | bytes 16777216 | tf_op jit(solution)/shard_map/pallas_call | solution.py:372
  63.2 11.0 %collective-permute-done.6.high_ref = f32[16,32,512]{2,1,0:T(8,128)S(1)} collective-permute-done((f32[16,32,512]{2,1,0:T(8,128)S(1)}, f32[16,32,512]{2,1,0:T(8,128)S(1)}, u32[]{:S(2)}, u32[]{:S(2)}) %collective-permute-start.6) | collective-permute-done | bytes 1048608 | tf_op jit(solution)/shard_map/ppermute | solution.py:22
  74.2 0.2 shard_map.41
  74.4 0.0 collective-permute-start.9
  74.5 0.1 collective-permute-start.8
  74.5 1.8 %collective-permute-start.7 = (f32[8,128]{1,0:T(8,128)S(1)}, f32[8,128]{1,0:T(8,128)S(1)}, u32[]{:S(2)}, u32[]{:S(2)}) collective-permute-start(f32[8,128]{1,0:T(8,128)S(1)} %shard_map.41), channel_id=1, source_target_pairs={{0,1},{1,0},{2,3},{3,2},{4,5},{5,4},{6,7},{7,6},{8,9},{9,8},{10,11... | collective-permute-start | bytes 12296 | tf_op jit(solution)/shard_map/ppermute | solution.py:449
  76.3 1.2 %collective-permute-done.9 = f32[8,128]{1,0:T(8,128)S(1)} collective-permute-done((f32[8,128]{1,0:T(8,128)S(1)}, f32[8,128]{1,0:T(8,128)S(1)}, u32[]{:S(2)}, u32[]{:S(2)}) %collective-permute-start.9) | collective-permute-done | bytes 4128 | tf_op jit(solution)/shard_map/ppermute | solution.py:449
  77.5 0.7 collective-permute-done.8
  78.1 0.0 collective-permute-done.7
  78.2 1.9 %collective-permute-start.12 = (f32[8,128]{1,0:T(8,128)S(1)}, f32[8,128]{1,0:T(8,128)S(1)}, u32[]{:S(2)}, u32[]{:S(2)}) collective-permute-start(f32[8,128]{1,0:T(8,128)S(1)} %add_add_fusion.refs_0_), channel_id=1, source_target_pairs={{0,12},{1,13},{2,14},{3,15},{4,8},{5,9},{6,10},{7,11},{8,4},{9,5},... | collective-permute-start | bytes 12296 | tf_op jit(solution)/shard_map/ppermute | solution.py:449
  80.0 0.0 collective-permute-start.11
  80.0 2.6 %collective-permute-start.10 = (f32[8,128]{1,0:T(8,128)S(1)}, f32[8,128]{1,0:T(8,128)S(1)}, u32[]{:S(2)}, u32[]{:S(2)}) collective-permute-start(f32[8,128]{1,0:T(8,128)S(1)} %add_add_fusion.refs_0_), channel_id=1, source_target_pairs={{0,4},{1,5},{2,6},{3,7},{4,0},{5,1},{6,2},{7,3},{8,12},{9,13},{10,... | collective-permute-start | bytes 12296 | tf_op jit(solution)/shard_map/ppermute | solution.py:449
  82.6 1.0 %collective-permute-done.12.refs_3_ = f32[8,128]{1,0:T(8,128)S(1)} collective-permute-done((f32[8,128]{1,0:T(8,128)S(1)}, f32[8,128]{1,0:T(8,128)S(1)}, u32[]{:S(2)}, u32[]{:S(2)}) %collective-permute-start.12) | collective-permute-done | bytes 4128 | tf_op jit(solution)/shard_map/ppermute | solution.py:449
  83.6 0.9 %collective-permute-done.11.refs_2_ = f32[8,128]{1,0:T(8,128)S(1)} collective-permute-done((f32[8,128]{1,0:T(8,128)S(1)}, f32[8,128]{1,0:T(8,128)S(1)}, u32[]{:S(2)}, u32[]{:S(2)}) %collective-permute-start.11) | collective-permute-done | bytes 4128 | tf_op jit(solution)/shard_map/ppermute | solution.py:449
  84.5 0.0 collective-permute-done.10.refs_1_
  84.5 1.6 %shard_map.42 = f32[4,32,512]{2,1,0:T(8,128)} custom-call(f32[16,2,32,512]{3,2,1,0:T(8,128)S(1)} %get-tuple-element.48.p1m_ref, f32[16,2,32,512]{3,2,1,0:T(8,128)S(1)} %get-tuple-element.49.p2m_ref, f32[16,2,32,512]{3,2,1,0:T(8,128)S(1)} %get-tuple-element.62.p1e_ref, f32[16,2,32,512]{3,2,1,0:T(8,128)S(1)} %get-tuple-element.63.p2e_ref, ...), custom_call_target="tpu_custom_call" | custom-call | flops 5033164 | bytes 8388608 | tf_op jit(solution)/shard_map/pallas_call | solution.py:372
  (2 shorter events, 0.0 us)
Async XLA Ops:
  0.8 7.4 %collective-permute-start = (f32[32,512]{1,0:T(8,128)S(1)}, f32[32,512]{1,0:T(8,128)S(1)}, u32[]{:S(2)}, u32[]{:S(2)}) collective-permute-start(f32[32,512]{1,0:T(8,128)S(1)} %slice_bitcast_fusion.own_ref), channel_id=1, source_target_pairs={{0,1},{1,2},{2,3},{3,4},{4,5},{5,6},{6,7},{7,8},{8,9},{9,10},{10,1... | collective-permute-start | bytes 196616 | tf_op jit(solution)/shard_map/ppermute | solution.py:22
  8.2 17.7 %collective-permute-start.1 = (f32[17,32,512]{2,1,0:T(8,128)S(1)}, f32[17,32,512]{2,1,0:T(8,128)S(1)}, u32[]{:S(2)}, u32[]{:S(2)}) collective-permute-start(f32[17,32,512]{2,1,0:T(8,128)S(1)} %get-tuple-element.44), channel_id=1, source_target_pairs={{0,15},{1,2},{2,1},{3,4},{4,3},{5,6},{6,5},{7,8},{8,7},{9,10},{10,... | collective-permute-start | bytes 3342344 | tf_op jit(solution)/shard_map/ppermute | solution.py:22
  9.5 16.5 %collective-permute-start.2 = (f32[17,32,512]{2,1,0:T(8,128)S(1)}, f32[17,32,512]{2,1,0:T(8,128)S(1)}, u32[]{:S(2)}, u32[]{:S(2)}) collective-permute-start(f32[17,32,512]{2,1,0:T(8,128)S(1)} %get-tuple-element.45), channel_id=1, source_target_pairs={{0,1},{1,0},{2,3},{3,2},{4,5},{5,4},{6,7},{7,6},{8,9},{9,8},{10,11... | collective-permute-start | bytes 3342344 | tf_op jit(solution)/shard_map/ppermute | solution.py:22
  15.4 21.8 %collective-permute-start.3 = (f32[16,32,512]{2,1,0:T(8,128)S(1)}, f32[16,32,512]{2,1,0:T(8,128)S(1)}, u32[]{:S(2)}, u32[]{:S(2)}) collective-permute-start(f32[16,32,512]{2,1,0:T(8,128)S(1)} %get-tuple-element.51), channel_id=1, source_target_pairs={{0,15},{1,2},{2,1},{3,4},{4,3},{5,6},{6,5},{7,8},{8,7},{9,10},{10,... | collective-permute-start | bytes 3145736 | tf_op jit(solution)/shard_map/ppermute | solution.py:22
  37.2 20.1 %collective-permute-start.4 = (f32[8,128]{1,0:T(8,128)S(1)}, f32[8,128]{1,0:T(8,128)S(1)}, u32[]{:S(2)}, u32[]{:S(2)}) collective-permute-start(f32[8,128]{1,0:T(8,128)S(1)} %slice_bitcast_fusion.1), channel_id=1, source_target_pairs={{0,1},{1,0},{2,3},{3,2},{4,5},{5,4},{6,7},{7,6},{8,9},{9,8},{10,11... | collective-permute-start | bytes 12296 | tf_op jit(solution)/shard_map/ppermute | solution.py:22
  56.4 2.7 %collective-permute-start.5 = (f32[16,32,512]{2,1,0:T(8,128)S(1)}, f32[16,32,512]{2,1,0:T(8,128)S(1)}, u32[]{:S(2)}, u32[]{:S(2)}) collective-permute-start(f32[16,32,512]{2,1,0:T(8,128)S(1)} %get-tuple-element.60), channel_id=1, source_target_pairs={{0,1},{1,0},{2,3},{3,2},{4,5},{5,4},{6,7},{7,6},{8,9},{9,8},{10,11... | collective-permute-start | bytes 3145736 | tf_op jit(solution)/shard_map/ppermute | solution.py:22
  57.3 16.9 %collective-permute-start.6 = (f32[16,32,512]{2,1,0:T(8,128)S(1)}, f32[16,32,512]{2,1,0:T(8,128)S(1)}, u32[]{:S(2)}, u32[]{:S(2)}) collective-permute-start(f32[16,32,512]{2,1,0:T(8,128)S(1)} %get-tuple-element.65), channel_id=1, source_target_pairs={{0,1},{1,2},{2,3},{3,4},{4,5},{5,6},{6,7},{7,8},{8,9},{9,10},{10,1... | collective-permute-start | bytes 3145736 | tf_op jit(solution)/shard_map/ppermute | solution.py:22
  74.4 3.1 %collective-permute-start.9 = (f32[8,128]{1,0:T(8,128)S(1)}, f32[8,128]{1,0:T(8,128)S(1)}, u32[]{:S(2)}, u32[]{:S(2)}) collective-permute-start(f32[8,128]{1,0:T(8,128)S(1)} %shard_map.41), channel_id=1, source_target_pairs={{0,3},{1,2},{2,1},{3,0},{4,7},{5,6},{6,5},{7,4},{8,11},{9,10},{10,... | collective-permute-start | bytes 12296 | tf_op jit(solution)/shard_map/ppermute | solution.py:449
  74.5 3.7 %collective-permute-start.8 = (f32[8,128]{1,0:T(8,128)S(1)}, f32[8,128]{1,0:T(8,128)S(1)}, u32[]{:S(2)}, u32[]{:S(2)}) collective-permute-start(f32[8,128]{1,0:T(8,128)S(1)} %shard_map.41), channel_id=1, source_target_pairs={{0,2},{1,3},{2,0},{3,1},{4,6},{5,7},{6,4},{7,5},{8,10},{9,11},{10,... | collective-permute-start | bytes 12296 | tf_op jit(solution)/shard_map/ppermute | solution.py:449
  74.5 3.6 %collective-permute-start.7 = (f32[8,128]{1,0:T(8,128)S(1)}, f32[8,128]{1,0:T(8,128)S(1)}, u32[]{:S(2)}, u32[]{:S(2)}) collective-permute-start(f32[8,128]{1,0:T(8,128)S(1)} %shard_map.41), channel_id=1, source_target_pairs={{0,1},{1,0},{2,3},{3,2},{4,5},{5,4},{6,7},{7,6},{8,9},{9,8},{10,11... | collective-permute-start | bytes 12296 | tf_op jit(solution)/shard_map/ppermute | solution.py:449
  78.2 5.5 %collective-permute-start.12 = (f32[8,128]{1,0:T(8,128)S(1)}, f32[8,128]{1,0:T(8,128)S(1)}, u32[]{:S(2)}, u32[]{:S(2)}) collective-permute-start(f32[8,128]{1,0:T(8,128)S(1)} %add_add_fusion.refs_0_), channel_id=1, source_target_pairs={{0,12},{1,13},{2,14},{3,15},{4,8},{5,9},{6,10},{7,11},{8,4},{9,5},... | collective-permute-start | bytes 12296 | tf_op jit(solution)/shard_map/ppermute | solution.py:449
  80.0 4.5 %collective-permute-start.11 = (f32[8,128]{1,0:T(8,128)S(1)}, f32[8,128]{1,0:T(8,128)S(1)}, u32[]{:S(2)}, u32[]{:S(2)}) collective-permute-start(f32[8,128]{1,0:T(8,128)S(1)} %add_add_fusion.refs_0_), channel_id=1, source_target_pairs={{0,8},{1,9},{2,10},{3,11},{4,12},{5,13},{6,14},{7,15},{8,0},{9,1},... | collective-permute-start | bytes 12296 | tf_op jit(solution)/shard_map/ppermute | solution.py:449
  80.0 4.5 %collective-permute-start.10 = (f32[8,128]{1,0:T(8,128)S(1)}, f32[8,128]{1,0:T(8,128)S(1)}, u32[]{:S(2)}, u32[]{:S(2)}) collective-permute-start(f32[8,128]{1,0:T(8,128)S(1)} %add_add_fusion.refs_0_), channel_id=1, source_target_pairs={{0,4},{1,5},{2,6},{3,7},{4,0},{5,1},{6,2},{7,3},{8,12},{9,13},{10,... | collective-permute-start | bytes 12296 | tf_op jit(solution)/shard_map/ppermute | solution.py:449

commit v6 on v4

--- a/solution.py
+++ b/solution.py
@@ -1,5 +1,3 @@
-import functools
-
 import jax
 import jax.numpy as jnp
 from jax import lax
@@ -34,17 +32,78 @@
 PLANES = 8
 
 
-def planes_kernel(odd_ref, coup_hbm, bits_hbm, mask_hbm, own_ref, planes_ref, part_ref, ahead_ref,
-                  bits_ref, off_ref, on_ref, coup_ref, mask_ref, sems):
-    days, rows, cols = coup_ref.shape[1:]
-    probes = bits_ref.shape[0]
+def link_factors(mask):
+    rows, cols = mask.shape
+    row = lax.broadcasted_iota(jnp.int32, (rows, cols), 0)
+    col = lax.broadcasted_iota(jnp.int32, (rows, cols), 1)
+    factors = []
+    for step_row, step_col in LINK_OFFSETS:
+        same = mask == turned(mask, -step_row, -step_col)
+        inside = (row + step_row < rows) & (col + step_col < cols) & (col + step_col >= 0)
+        factors.append(jnp.where(inside, jnp.where(same, 1.0, COASTAL_FACTOR), 0.0))
+    return factors
+
+
+def day_planes(coup_ref, factors, d):
+    east, south, se, sw = (coup_ref[n + 1, d] * factors[n] for n in range(4))
+    west = turned(east, 0, 1)
+    se_w = turned(se, 0, 1)
+    sw_e = turned(sw, 0, -1)
+    above = turned(south, 1, 0)
+    diag = coup_ref[0, d] + coup_ref[5, d]
+    if d:
+        diag = diag + coup_ref[5, d - 1]
+    diag = diag + east + west + south + above
+    diag = diag + se + turned(se_w, 1, 0) + sw + turned(sw_e, 1, 0)
+    return (east, west, south, se_w, sw_e, above, turned(se, 1, 0), turned(sw, 1, 0)), diag
+
+
+def edges_kernel(odd_ref, coup_hbm, bits_hbm, mask_hbm, own_ref, off_ref, on_ref,
+                 coup_ref, mask_ref, bits_ref, sems):
+    probes, days = bits_hbm.shape[:2]
     last = days - 1
     odd = odd_ref[0]
+    half = probes // 2
+    copies = [
+        pltpu.make_async_copy(mask_hbm, mask_ref, sems.at[0]),
+        pltpu.make_async_copy(coup_hbm, coup_ref, sems.at[1]),
+    ]
+    for side, day in enumerate((odd * last, last - odd * last)):
+        for n in range(2):
+            part = pl.ds(n * half, half)
+            copies.append(
+                pltpu.make_async_copy(
+                    bits_hbm.at[part, day], bits_ref.at[side, part], sems.at[2 + 2 * side + n]
+                )
+            )
+    for copy in copies:
+        copy.start()
+    for copy in copies[:2]:
+        copy.wait()
+    factors = link_factors(mask_ref[...])
+    first = day_planes(coup_ref, factors, 0)[1]
+    final = day_planes(coup_ref, factors, last)[1]
+    off_ref[probes] = chosen(odd, first, final)
+    on_ref[probes] = chosen(odd, final, first)
+    for copy in copies[2:]:
+        copy.wait()
+    for side, out_ref in enumerate((off_ref, on_ref)):
+
+        def probe(k, carry):
+            out_ref[k] = jnp.where(bits_ref[side, k] == 1, 1.0, -1.0)
+            return carry
+
+        lax.fori_loop(0, probes, probe, 0, unroll=4)
+
+
+def planes_kernel(coup_hbm, bits_hbm, mask_hbm, before_ref, planes_ref, diag_ref, dinv_ref,
+                  ahead_ref, bits_ref, coup_ref, mask_ref, sems):
+    days = coup_ref.shape[1]
+    chunk = bits_ref.shape[0] // 4
     small = [
         pltpu.make_async_copy(mask_hbm, mask_ref, sems.at[0]),
         pltpu.make_async_copy(coup_hbm, coup_ref, sems.at[1]),
     ]
-    chunk = probes // 4
     large = [
         pltpu.make_async_copy(
             bits_hbm.at[pl.ds(n * chunk, chunk)], bits_ref.at[pl.ds(n * chunk, chunk)], sems.at[2 + n]
@@ -55,42 +114,18 @@
         copy.start()
     for copy in small:
         copy.wait()
-    mask = mask_ref[...]
-    row = lax.broadcasted_iota(jnp.int32, (rows, cols), 0)
-    col = lax.broadcasted_iota(jnp.int32, (rows, cols), 1)
-    factors = []
-    for step_row, step_col in LINK_OFFSETS:
-        same = mask == turned(mask, -step_row, -step_col)
-        inside = (row + step_row < rows) & (col + step_col < cols) & (col + step_col >= 0)
-        factors.append(jnp.where(inside, jnp.where(same, 1.0, COASTAL_FACTOR), 0.0))
+    factors = link_factors(mask_ref[...])
     for d in range(days):
-        east, south, se, sw = (coup_ref[n + 1, d] * factors[n] for n in range(4))
-        west = turned(east, 0, 1)
-        se_w = turned(se, 0, 1)
-        sw_e = turned(sw, 0, -1)
-        above = turned(south, 1, 0)
-        ahead = coup_ref[5, d]
-        part = coup_ref[0, d] + ahead
-        if d:
-            part = part + coup_ref[5, d - 1]
-        part = part + east + west + south + above
-        part = part + se + turned(se_w, 1, 0) + sw + turned(sw_e, 1, 0)
-        part_ref[d] = part
-        ahead_ref[d] = ahead
-        for n, plane in enumerate(
-            (east, west, south, se_w, sw_e, above, turned(se, 1, 0), turned(sw, 1, 0))
-        ):
+        planes, diag = day_planes(coup_ref, factors, d)
+        if d == 0:
+            diag = diag + before_ref[...]
+        diag_ref[d] = diag
+        dinv_ref[d] = 1.0 / diag
+        ahead_ref[d] = coup_ref[5, d]
+        for n, plane in enumerate(planes):
             planes_ref[n, d] = plane
     for copy in large:
         copy.wait()
-    for out_ref, d in ((off_ref, odd * last), (on_ref, last - odd * last)):
-        out_ref[probes] = part_ref[d]
-
-        def probe(k, carry):
-            out_ref[k] = jnp.where(bits_ref[k, d] == 1, 1.0, -1.0)
-            return carry
-
-        lax.fori_loop(0, probes, probe, 0)
 
 
 def chosen(odd, even_value, odd_value):
@@ -143,19 +178,10 @@
     return jnp.concatenate(rows, axis=0)
 
 
-def first_kernel(odd_ref, bits_ref, planes_ref, ahead_ref, before_ref, part_ref,
-                 w1_ref, off_ref, on_ref, diag_ref, dinv_ref, w0_ref):
+def first_kernel(odd_ref, bits_ref, planes_ref, ahead_ref, dinv_ref,
+                 w1_ref, off_ref, on_ref, w0_ref):
     per, days = bits_ref.shape[:2]
     odd = odd_ref[0]
-
-    @pl.when(pl.program_id(0) == 0)
-    def _():
-        for d in range(days):
-            diag = part_ref[d]
-            if d == 0:
-                diag = diag + before_ref[...]
-            diag_ref[d] = diag
-            dinv_ref[d] = 1.0 / diag
 
     def probe(k, carry):
         for d in range(days):
@@ -174,7 +200,8 @@
 
 def second_kernel(odd_ref, bits_ref, w1_ref, off_ref, on_ref, doff_ref, don_ref, planes_ref,
                   ahead_ref, before_ref, diag_ref, dinv_ref,
-                  p1_ref, p2_ref, w1e_ref, w2e_ref, high_ref, sums_ref, ratio_ref, scale_ref, w1c_ref):
+                  p1_ref, p2_ref, w1e_ref, w2e_ref, high_ref, sums_ref, ratio_ref, scale_ref,
+                  w1c_ref):
     per, days = w1_ref.shape[:2]
     last = days - 1
     odd = odd_ref[0]
@@ -248,7 +275,8 @@
         for side, (d, inner) in enumerate(((0, 1), (last, last - 1))):
             bits = bits_ref[k, d]
             w1 = w1e_ref[k, side]
-            arrived = chosen(odd, off_ref[k], on_ref[k]) if side == 0 else chosen(odd, on_ref[k], off_ref[k])
+            off = off_ref[k]
+            arrived = chosen(odd, off, on_ref[k]) if side == 0 else chosen(odd, on_ref[k], off)
             neighbour = arrived + ratio_ref[side] * signed(bits, dinv_ref[d])
             w2 = w2e_ref[k, side] + scale_ref[side] * neighbour
             p1 = signed(bits, w1)
@@ -282,7 +310,8 @@
         extra = jnp.sum(2.0 * folded(cross_ref[k] * high_ref[k]), axis=0, keepdims=True)
         sums = sums_ref[k] + jnp.where(row == 5, extra, 0.0)
         result = jnp.where(lane == k, jnp.sum(sums, axis=1, keepdims=True), result)
-    moments_ref[...] = result
+    for n in range(moments_ref.shape[0]):
+        moments_ref[n] = result
 
 
 def coefficients(moments, probes):
@@ -317,7 +346,7 @@
 def last_kernel(moments_ref, p1m_ref, p2m_ref, p1e_ref, p2e_ref, dinv_ref, out_ref):
     probes, inner = p1m_ref.shape[:2]
     days = inner + 2
-    c0, c1, c2 = coefficients(moments_ref[...], probes)
+    c0, c1, c2 = coefficients(jnp.sum(moments_ref[...], axis=0), probes)
     c0 = jnp.sum(c0, axis=1, keepdims=True)
     for d in range(days):
         edge = d in (0, days - 1)
@@ -385,31 +414,39 @@
     own = couplings[5, days - 1]
     before = moved(own, "next")
     sent = (probes + 1,) + plane
-    planes, part, ahead, bits, off_signs, on_signs = call(
-        planes_kernel, (1,),
+    off_signs, on_signs = call(
+        edges_kernel, (1,),
         [(odd, "smem"), (hbm(couplings), "hbm"), (hbm(probe_bits), "hbm"), (hbm(land_mask), "hbm"),
          (own, "whole")],
+        [(sent, "whole", F32), (sent, "whole", F32)],
+        scratch=[pltpu.VMEM(couplings.shape, F32), pltpu.VMEM(plane, jnp.int32),
+                 pltpu.VMEM((2,) + edge, jnp.int32), pltpu.SemaphoreType.DMA((6,))],
+        cost=(0.1, 0.5), mib=16,
+    )
+    off_signs, on_signs, before = lax.optimization_barrier((off_signs, on_signs, before))
+    off_signs = moved(off_signs, "off")
+    on_signs = moved(on_signs, "on")
+    planes, diag, dinv, ahead, bits = call(
+        planes_kernel, (1,),
+        [(hbm(couplings), "hbm"), (hbm(probe_bits), "hbm"), (hbm(land_mask), "hbm"),
+         (before, "whole")],
         [(weights, "whole", F32), (dplanes, "whole", F32), (dplanes, "whole", F32),
-         (field, "whole", jnp.int32), (sent, "whole", F32), (sent, "whole", F32)],
+         (dplanes, "whole", F32), (field, "whole", jnp.int32)],
         scratch=[pltpu.VMEM(couplings.shape, F32), pltpu.VMEM(plane, jnp.int32),
                  pltpu.SemaphoreType.DMA((6,))],
         cost=(0.5, 1), mib=32,
     )
-    off_signs, on_signs, before = lax.optimization_barrier((off_signs, on_signs, before))
-    off_signs = moved(off_signs, "off")
-    on_signs = moved(on_signs, "on")
-
-    w1, off, on, diag, dinv = call(
+
+    w1, off, on = call(
         first_kernel, grid,
-        [(odd, "smem"), (bits, "split"), (planes, "whole"), (ahead, "whole"),
-         (before, "whole"), (part, "whole")],
-        [(field, "split", F32), (edge, "split", F32), (edge, "split", F32),
-         (dplanes, "whole", F32), (dplanes, "whole", F32)],
+        [(odd, "smem"), (bits, "split"), (planes, "whole"), (ahead, "whole"), (dinv, "whole")],
+        [(field, "split", F32), (edge, "split", F32), (edge, "split", F32)],
         scratch=[pltpu.VMEM(dplanes, F32)], cost=(1, 2),
     )
+    off = moved(off, "off")
     on = moved(on, "on")
-    off, off_signs = lax.optimization_barrier((off, off_signs))
-    off = moved(off, "off")
+    token, off_signs, on_signs = lax.optimization_barrier((dinv[0, :8, :128], off_signs, on_signs))
+    token = moved(token, "on")
 
     p1m, p2m, w1e, w2e, high2, sums, ratio = call(
         second_kernel, grid,
@@ -421,9 +458,7 @@
          ((2,) + plane, "whole", F32)],
         scratch=[pltpu.VMEM((2,) + plane, F32), pltpu.VMEM(dplanes, F32)], cost=(1.5, 4), mib=20,
     )
-    token, off, high2 = lax.optimization_barrier((sums[0], off, high2))
-    token = moved(token, "on")
-    high2, ratio, token = lax.optimization_barrier((high2, ratio, token))
+    high2, ratio, token, off = lax.optimization_barrier((high2, ratio, token, off))
     high2_prev = moved(high2, "next")
 
     p1e, p2e, cross, sums = call(
@@ -438,13 +473,9 @@
     (moments,) = call(
         fourth_kernel, (1,),
         [(cross, "whole"), (high2_prev, "whole"), (sums, "whole")],
-        [(tile, "whole", F32)], cost=(0.1, 0.5), mib=8,
-    )
-    step = 1
-    while step < count:
-        moments = moments + lax.ppermute(moments, "day", [(i, i ^ step) for i in range(count)])
-        step *= 2
-
+        [((count,) + tile, "whole", F32)], cost=(0.1, 0.5), mib=8,
+    )
+    moments = lax.all_to_all(moments, "day", 0, 0)
     (out,) = call(
         last_kernel, (1,),
         [(moments, "whole"), (p1m, "whole"), (p2m, "whole"), (p1e, "whole"), (p2e, "whole"),

time: 92.1 us -> 84.2 us (0.914)
  waiting for transfers between devices: 45.8 us -> 20.8 us
  blocking collectives: 0 us -> 10.9 us
  starting transfers between devices: 20.5 us -> 24.8 us
  Pallas kernels: 24.6 us -> 26.5 us
    ppermute x7, waiting for transfers between devices: 33.7 us -> 20.8 us  [moved(): return lax.ppermute(value, 'day', [(i, target(i)) for i in range(count)])]
    ppermute x4 -> x0, waiting for transfers between devices: 12.1 us -> none  [body(): lax.ppermute(moments, 'day', [(i, i ^ step) for i in range(count)])]
    all_to_all x0 -> x1, blocking collectives: none -> 10.9 us  [body(): moments = lax.all_to_all(moments, 'day', 0, 0)]
    ppermute x7, starting transfers between devices: 19.7 us -> 24.8 us  [moved(): return lax.ppermute(value, 'day', [(i, target(i)) for i in range(count)])]
    pallas_call x6 -> x7, Pallas kernels: 24.6 us -> 26.5 us  [call(): pl.pallas_call(kernel, grid=grid, in_specs=[spec(value.shape, kind) for v...]
  transfers between devices with their start and end apart: 11 -> 7, of which waited for: 10 -> 3; matrix products, arithmetic and copies ran while one was open for 0% -> 0% of each run, Pallas kernels for 25% -> 29%
where the time goes in v6:
time: 84.2 us; the launch traced here: 84 us
  Pallas kernels  26.5 us (31%)
  starting transfers between devices  24.8 us (29%)
  waiting for transfers between devices  20.8 us (25%)
  blocking collectives  10.9 us (13%)
  local copies, waits for them, and re-layouts  0.85 us (1%)
    pallas_call x7, Pallas kernels, call(): pl.pallas_call(kernel, grid=grid, in_specs=[spec(value.shape, kind) for v...  26.5 us
    ppermute x7, starting transfers between devices, moved(): return lax.ppermute(value, 'day', [(i, target(i)) for i in range(count)])  24.8 us
    ppermute x7, waiting for transfers between devices, moved(): return lax.ppermute(value, 'day', [(i, target(i)) for i in range(count)])  20.8 us
    all_to_all x1, blocking collectives, body(): moments = lax.all_to_all(moments, 'day', 0, 0)  10.9 us
  transfers between devices with their start and end apart: 7, of which 3 were waited for; matrix products, arithmetic and copies ran while one was open for 0% of the time, Pallas kernels for 29%

profile of v6, /device:TPU:0, one launch (start us, length us, event | category | flops | bytes accessed | tf_op | source)
XLA Modules:
  0.0 84.0 jit_solution(6889754209593234575)
XLA Ops:
  0.0 0.8 %slice_bitcast_fusion.own_ref = f32[32,512]{1,0:T(8,128)S(1)} fusion(f32[6,4,32,512]{3,2,1,0:T(8,128)} %coup_hbm.3), kind=kLoop, calls=%fused_computation | loop fusion | bytes 131072 | tf_op jit(solution)/shard_map/squeeze | solution.py:414
  0.8 0.5 collective-permute-start
  1.3 2.3 %shard_map.37 = (f32[17,32,512]{2,1,0:T(8,128)S(1)}, f32[17,32,512]{2,1,0:T(8,128)S(1)}) custom-call(s32[1]{0:T(128)} %bitcast.odd_ref, f32[6,4,32,512]{3,2,1,0:T(8,128)} %coup_hbm.3, s32[16,4,32,512]{3,2,1,0:T(8,128)} %bits_hbm.3, s32[32,512]{1,0:T(8,128)} %mask_hbm.3, f32[32,512]{1,0:T(8,128)S(1)} %slice_bitcast_fusion.own_ref), custom_call_target="tpu_custom_call" | custom-call | flops 2516582 | bytes 2097152 | tf_op jit(solution)/shard_map/pallas_call | solution.py:400
  3.6 4.6 %collective-permute-done.before_ref = f32[32,512]{1,0:T(8,128)S(1)} collective-permute-done((f32[32,512]{1,0:T(8,128)S(1)}, f32[32,512]{1,0:T(8,128)S(1)}, u32[]{:S(2)}, u32[]{:S(2)}) %collective-permute-start) | collective-permute-done | bytes 65568 | tf_op jit(solution)/shard_map/ppermute | solution.py:20
  8.2 0.4 collective-permute-start.1
  8.7 0.0 collective-permute-start.2
  8.7 2.7 %shard_map.38 = (f32[8,4,32,512]{3,2,1,0:T(8,128)S(1)}, f32[4,32,512]{2,1,0:T(8,128)S(1)}, f32[4,32,512]{2,1,0:T(8,128)S(1)}, f32[4,32,512]{2,1,0:T(8,128)S(1)}, s32[16,4,32,512]{3,2,1,0:T(8,128)S(1)}) custom-call(f32[6,4,32,512]{3,2,1,0:T(8,128)} %coup_hbm.3, s32[16,4,32,512]{3,2,1,0:T(8,128)} %bits_hbm.3, s32[32,512]{1,0:T(8,128)} %mask_hbm.3, ...), custom_call_target="tpu_custom_call" | custom-call | flops 12582912 | bytes 4194304 | tf_op jit(solution)/shard_map/pallas_call | solution.py:400
  11.4 5.9 %shard_map.39 = (f32[16,4,32,512]{3,2,1,0:T(8,128)S(1)}, f32[16,32,512]{2,1,0:T(8,128)S(1)}, f32[16,32,512]{2,1,0:T(8,128)S(1)}) custom-call(s32[1]{0:T(128)} %bitcast.odd_ref, s32[16,4,32,512]{3,2,1,0:T(8,128)S(1)} %get-tuple-element.39.bits_ref, f32[8,4,32,512]{3,2,1,0:T(8,128)S(1)} %get-tuple-element.40.planes_ref, ...), custom_call_target="tpu_custom_call" | custom-call | flops 25165824 | bytes 8388608 | tf_op jit(solution)/shard_map/pallas_call | solution.py:400
  17.3 4.1 %collective-permute-start.4 = (f32[16,32,512]{2,1,0:T(8,128)S(1)}, f32[16,32,512]{2,1,0:T(8,128)S(1)}, u32[]{:S(2)}, u32[]{:S(2)}) collective-permute-start(f32[16,32,512]{2,1,0:T(8,128)S(1)} %get-tuple-element.52), channel_id=1, source_target_pairs={{0,15},{1,2},{2,1},{3,4},{4,3},{5,6},{6,5},{7,8},{8,7},{9,10},{10,... | collective-permute-start | bytes 3145736 | tf_op jit(solution)/shard_map/ppermute | solution.py:20
  21.4 4.6 %collective-permute-done.1.off_ref.doff_ref = f32[17,32,512]{2,1,0:T(8,128)S(1)} collective-permute-done((f32[17,32,512]{2,1,0:T(8,128)S(1)}, f32[17,32,512]{2,1,0:T(8,128)S(1)}, u32[]{:S(2)}, u32[]{:S(2)}) %collective-permute-start.1) | collective-permute-done | bytes 1114144 | tf_op jit(solution)/shard_map/ppermute | solution.py:20
  26.0 0.0 collective-permute-done.2.on_ref.don_ref
  26.0 18.4 %collective-permute-start.3 = (f32[8,128]{1,0:T(8,128)S(1)}, f32[8,128]{1,0:T(8,128)S(1)}, u32[]{:S(2)}, u32[]{:S(2)}) collective-permute-start(f32[8,128]{1,0:T(8,128)S(1)} %slice_bitcast_fusion.1), channel_id=1, source_target_pairs={{0,1},{1,0},{2,3},{3,2},{4,5},{5,4},{6,7},{7,6},{8,9},{9,8},{10,11... | collective-permute-start | bytes 12296 | tf_op jit(solution)/shard_map/ppermute | solution.py:20
  44.4 0.0 collective-permute-start.5
  44.4 9.8 %shard_map.40 = (f32[16,2,32,512]{3,2,1,0:T(8,128)S(1)}, f32[16,2,32,512]{3,2,1,0:T(8,128)S(1)}, f32[16,2,32,512]{3,2,1,0:T(8,128)S(1)}, f32[16,2,32,512]{3,2,1,...) custom-call(s32[1]{0:T(128)} %bitcast.odd_ref, ...), custom_call_target="tpu_custom_call" | custom-call | flops 37748736 | bytes 16777216 | tf_op jit(solution)/shard_map/pallas_call | solution.py:400
  54.2 0.0 collective-permute-done.4.off_ref
  54.3 0.0 collective-permute-done.3.token_ref
  54.3 1.4 %collective-permute-start.6 = (f32[16,32,512]{2,1,0:T(8,128)S(1)}, f32[16,32,512]{2,1,0:T(8,128)S(1)}, u32[]{:S(2)}, u32[]{:S(2)}) collective-permute-start(f32[16,32,512]{2,1,0:T(8,128)S(1)} %get-tuple-element.62), channel_id=1, source_target_pairs={{0,1},{1,2},{2,3},{3,4},{4,5},{5,6},{6,7},{7,8},{8,9},{9,10},{10,1... | collective-permute-start | bytes 3145736 | tf_op jit(solution)/shard_map/ppermute | solution.py:20
  55.6 0.0 collective-permute-done.5.on_ref
  55.6 4.1 %shard_map.41 = (f32[16,2,32,512]{3,2,1,0:T(8,128)S(1)}, f32[16,2,32,512]{3,2,1,0:T(8,128)S(1)}, f32[16,32,512]{2,1,0:T(8,128)S(1)}, f32[16,8,128]{2,1,0:T(8,128)S(1)}) custom-call(s32[1]{0:T(128)} %bitcast.odd_ref, f32[8,128]{1,0:T(8,128)S(1)} %collective-permute-done.3.token_ref, s32[16,4,32,512]{3,2,1,0:T(8,128)S(1)} %get-tuple-element.39.bits_ref, ...), custom_call_target="tpu_custom_call" | custom-call | flops 17616076 | bytes 16777216 | tf_op jit(solution)/shard_map/pallas_call | solution.py:400
  59.7 11.5 %collective-permute-done.6.high_ref = f32[16,32,512]{2,1,0:T(8,128)S(1)} collective-permute-done((f32[16,32,512]{2,1,0:T(8,128)S(1)}, f32[16,32,512]{2,1,0:T(8,128)S(1)}, u32[]{:S(2)}, u32[]{:S(2)}) %collective-permute-start.6) | collective-permute-done | bytes 1048608 | tf_op jit(solution)/shard_map/ppermute | solution.py:20
  71.2 0.2 shard_map.42
  71.4 10.9 %all_to_all.5.moments_ref = f32[16,8,128]{2,1,0:T(8,128)S(1)} all-to-all(f32[16,8,128]{2,1,0:T(8,128)S(1)} %shard_map.42), channel_id=1, replica_groups=mesh['groups'=2,'day'=16] {'day'}, dimensions={0} | all-to-all | bytes 131072 | tf_op jit(solution)/shard_map/all_to_all | solution.py:478
  82.4 1.6 %shard_map.43 = f32[4,32,512]{2,1,0:T(8,128)} custom-call(f32[16,8,128]{2,1,0:T(8,128)S(1)} %all_to_all.5.moments_ref, f32[16,2,32,512]{3,2,1,0:T(8,128)S(1)} %get-tuple-element.64.p1m_ref, f32[16,2,32,512]{3,2,1,0:T(8,128)S(1)} %get-tuple-element.54.p2m_ref, f32[16,2,32,512]{3,2,1,0:T(8,128)S(1)} %get-tuple-element.65.p1e_ref, ...), custom_call_target="tpu_custom_call" | custom-call | flops 5033164 | bytes 8388608 | tf_op jit(solution)/shard_map/pallas_call | solution.py:400
  (1 shorter events, 0.0 us)
Async XLA Ops:
  0.8 7.4 %collective-permute-start = (f32[32,512]{1,0:T(8,128)S(1)}, f32[32,512]{1,0:T(8,128)S(1)}, u32[]{:S(2)}, u32[]{:S(2)}) collective-permute-start(f32[32,512]{1,0:T(8,128)S(1)} %slice_bitcast_fusion.own_ref), channel_id=1, source_target_pairs={{0,1},{1,2},{2,3},{3,4},{4,5},{5,6},{6,7},{7,8},{8,9},{9,10},{10,1... | collective-permute-start | bytes 196616 | tf_op jit(solution)/shard_map/ppermute | solution.py:20
  8.2 17.7 %collective-permute-start.1 = (f32[17,32,512]{2,1,0:T(8,128)S(1)}, f32[17,32,512]{2,1,0:T(8,128)S(1)}, u32[]{:S(2)}, u32[]{:S(2)}) collective-permute-start(f32[17,32,512]{2,1,0:T(8,128)S(1)} %get-tuple-element.44), channel_id=1, source_target_pairs={{0,15},{1,2},{2,1},{3,4},{4,3},{5,6},{6,5},{7,8},{8,7},{9,10},{10,... | collective-permute-start | bytes 3342344 | tf_op jit(solution)/shard_map/ppermute | solution.py:20
  8.7 17.3 %collective-permute-start.2 = (f32[17,32,512]{2,1,0:T(8,128)S(1)}, f32[17,32,512]{2,1,0:T(8,128)S(1)}, u32[]{:S(2)}, u32[]{:S(2)}) collective-permute-start(f32[17,32,512]{2,1,0:T(8,128)S(1)} %get-tuple-element.45), channel_id=1, source_target_pairs={{0,1},{1,0},{2,3},{3,2},{4,5},{5,4},{6,7},{7,6},{8,9},{9,8},{10,11... | collective-permute-start | bytes 3342344 | tf_op jit(solution)/shard_map/ppermute | solution.py:20
  17.3 37.0 %collective-permute-start.4 = (f32[16,32,512]{2,1,0:T(8,128)S(1)}, f32[16,32,512]{2,1,0:T(8,128)S(1)}, u32[]{:S(2)}, u32[]{:S(2)}) collective-permute-start(f32[16,32,512]{2,1,0:T(8,128)S(1)} %get-tuple-element.52), channel_id=1, source_target_pairs={{0,15},{1,2},{2,1},{3,4},{4,3},{5,6},{6,5},{7,8},{8,7},{9,10},{10,... | collective-permute-start | bytes 3145736 | tf_op jit(solution)/shard_map/ppermute | solution.py:20
  26.0 28.3 %collective-permute-start.3 = (f32[8,128]{1,0:T(8,128)S(1)}, f32[8,128]{1,0:T(8,128)S(1)}, u32[]{:S(2)}, u32[]{:S(2)}) collective-permute-start(f32[8,128]{1,0:T(8,128)S(1)} %slice_bitcast_fusion.1), channel_id=1, source_target_pairs={{0,1},{1,0},{2,3},{3,2},{4,5},{5,4},{6,7},{7,6},{8,9},{9,8},{10,11... | collective-permute-start | bytes 12296 | tf_op jit(solution)/shard_map/ppermute | solution.py:20
  44.4 11.2 %collective-permute-start.5 = (f32[16,32,512]{2,1,0:T(8,128)S(1)}, f32[16,32,512]{2,1,0:T(8,128)S(1)}, u32[]{:S(2)}, u32[]{:S(2)}) collective-permute-start(f32[16,32,512]{2,1,0:T(8,128)S(1)} %get-tuple-element.58), channel_id=1, source_target_pairs={{0,1},{1,0},{2,3},{3,2},{4,5},{5,4},{6,7},{7,6},{8,9},{9,8},{10,11... | collective-permute-start | bytes 3145736 | tf_op jit(solution)/shard_map/ppermute | solution.py:20
  54.3 17.0 %collective-permute-start.6 = (f32[16,32,512]{2,1,0:T(8,128)S(1)}, f32[16,32,512]{2,1,0:T(8,128)S(1)}, u32[]{:S(2)}, u32[]{:S(2)}) collective-permute-start(f32[16,32,512]{2,1,0:T(8,128)S(1)} %get-tuple-element.62), channel_id=1, source_target_pairs={{0,1},{1,2},{2,3},{3,4},{4,5},{5,6},{6,7},{7,8},{8,9},{9,10},{10,1... | collective-permute-start | bytes 3145736 | tf_op jit(solution)/shard_map/ppermute | solution.py:20

commit v7 on v6

--- a/solution.py
+++ b/solution.py
@@ -7,6 +7,7 @@
 
 LINK_OFFSETS = ((0, 1), (1, 0), (1, 1), (1, -1))
 COASTAL_FACTOR = 0.2
+ITERS = 3
 F32 = jnp.float32
 
 
@@ -310,43 +311,53 @@
         extra = jnp.sum(2.0 * folded(cross_ref[k] * high_ref[k]), axis=0, keepdims=True)
         sums = sums_ref[k] + jnp.where(row == 5, extra, 0.0)
         result = jnp.where(lane == k, jnp.sum(sums, axis=1, keepdims=True), result)
-    for n in range(moments_ref.shape[0]):
-        moments_ref[n] = result
+    moments_ref[...] = result
 
 
 def coefficients(moments, probes):
     lane = lax.broadcasted_iota(jnp.int32, (1, 128), 1)
     live = lane < probes
-    n0, n1, n2, n3, n4, n5 = (jnp.where(live, moments[j : j + 1], 1.0) for j in range(6))
+    n0, n1, n2, n3, n4, n5 = (jnp.where(live, moments[j : j + 1], float(j == 0)) for j in range(6))
     a0 = n1 / n0
-    s11 = jnp.maximum(n2 - a0 * n1, 1e-7 * n2 + 1e-30)
+    s11 = n2 - a0 * n1
     s12 = n3 - a0 * n2
     s13 = n4 - a0 * n3
     s14 = n5 - a0 * n4
-    a1 = jnp.clip(s12 / s11 - a0, -1.0, 0.999)
+    sound = s11 > 0.01 * n2
+    s11 = jnp.where(sound, s11, 1.0)
+    a1 = s12 / s11 - a0
     b1 = s11 / n0
-    s22 = jnp.maximum(s13 - a1 * s12 - b1 * n2, 1e-7 * n4 + 1e-30)
+    s22 = s13 - a1 * s12 - b1 * n2
     s23 = s14 - a1 * s13 - b1 * n3
-    a2 = jnp.clip(s23 / s22 - s12 / s11, -1.0, 0.999)
+    sound = sound & (s22 > 0.001 * n4)
+    s22 = jnp.where(sound, s22, 1.0)
+    a2 = s23 / s22 - s12 / s11
     b2 = s22 / s11
     e2 = 1.0 - a2
     e1 = (1.0 - a1) - b2 / e2
     e0 = (1.0 - a0) - b1 / e1
+    sound = sound & (e2 > 0.01) & (e1 > 0.01) & (e0 > 0.01)
     y0 = 1.0 / e0
     y1 = y0 / e1
     y2 = y1 / e2
-    scale = jnp.where(live, 1.0 / probes, 0.0)
-    return (
-        scale * (y0 - a0 * y1 + (a0 * a1 - b1) * y2),
-        scale * (y1 - (a0 + a1) * y2),
-        scale * y2,
-    )
-
-
-def last_kernel(moments_ref, p1m_ref, p2m_ref, p1e_ref, p2e_ref, dinv_ref, out_ref):
+    weights = (y0 - a0 * y1 + (a0 * a1 - b1) * y2, y1 - (a0 + a1) * y2, y2)
+    return tuple(jnp.where(live, weight / probes, 0.0) for weight in weights) + (
+        jnp.max(jnp.where(live & jnp.logical_not(sound), 1, 0)),
+    )
+
+
+def paired_sum(values):
+    while len(values) > 1:
+        values = [first + second for first, second in zip(values[::2], values[1::2])]
+    return values[0]
+
+
+def last_kernel(p1m_ref, p2m_ref, p1e_ref, p2e_ref, dinv_ref, *refs):
+    share_refs, out_ref, unsound_ref = refs[:-2], refs[-2], refs[-1]
     probes, inner = p1m_ref.shape[:2]
     days = inner + 2
-    c0, c1, c2 = coefficients(jnp.sum(moments_ref[...], axis=0), probes)
+    c0, c1, c2, unsound = coefficients(paired_sum([ref[...] for ref in share_refs]), probes)
+    unsound_ref[0] = unsound
     c0 = jnp.sum(c0, axis=1, keepdims=True)
     for d in range(days):
         edge = d in (0, days - 1)
@@ -356,6 +367,18 @@
         for k in range(probes):
             total = total + (c1[:, k : k + 1] * p1_ref[k, spot] + c2[:, k : k + 1] * p2_ref[k, spot])
         out_ref[d] = total
+
+
+def copies_kernel(*refs):
+    sems = refs[-1]
+    half = len(refs) // 2
+    copies = [
+        pltpu.make_async_copy(refs[n], refs[half + n], sems.at[n]) for n in range(half)
+    ]
+    for copy in copies:
+        copy.start()
+    for copy in copies:
+        copy.wait()
 
 
 def split(shape, per):
@@ -473,16 +496,143 @@
     (moments,) = call(
         fourth_kernel, (1,),
         [(cross, "whole"), (high2_prev, "whole"), (sums, "whole")],
-        [((count,) + tile, "whole", F32)], cost=(0.1, 0.5), mib=8,
-    )
-    moments = lax.all_to_all(moments, "day", 0, 0)
-    (out,) = call(
+        [(tile, "whole", F32)], cost=(0.1, 0.5), mib=8,
+    )
+    shares = [moments]
+    step = 1
+    while step < count:
+        near = min(4, count // step)
+        moments = paired_sum(shares)
+        shares = [moments] + [
+            lax.ppermute(moments, "day", [(i, i ^ (n * step)) for i in range(count)])
+            for n in range(1, near)
+        ]
+        step *= near
+    out, unsound = call(
         last_kernel, (1,),
-        [(moments, "whole"), (p1m, "whole"), (p2m, "whole"), (p1e, "whole"), (p2e, "whole"),
-         (dinv, "whole")],
-        [(dplanes, "whole", F32)], cost=(0.2, 2), mib=24,
-    )
-    return out
+        [(p1m, "whole"), (p2m, "whole"), (p1e, "whole"), (p2e, "whole"), (dinv, "whole")]
+        + [(share, "whole") for share in shares],
+        [(dplanes, "whole", F32), ((1,), "smem", jnp.int32)], cost=(0.2, 2), mib=24,
+    )
+
+    def stepwise(*inputs):
+        return direct(*call(
+            copies_kernel, (1,),
+            [(hbm(value), "hbm") for value in inputs[:3]],
+            [(value.shape, "hbm", value.dtype) for value in inputs[:3]],
+            scratch=[pltpu.SemaphoreType.DMA((3,))], cost=(0, 1), mib=4,
+        ))
+
+    return lax.cond(
+        unsound[0] > 0, stepwise, lambda *inputs: inputs[3], couplings, probe_bits, land_mask, out
+    )
+
+
+def passed_along(value, axis, steps):
+    count = lax.axis_size(axis)
+    pairs = [(source, (source + steps) % count) for source in range(count)]
+    return lax.ppermute(value, axis, pairs)
+
+
+def extended(block, sides, width):
+    for axis, dim in sides:
+        count = lax.axis_size(axis)
+        forward = [(i, i + 1) for i in range(count - 1)]
+        forward.append((count - 1, 0))
+        backward = [(target, source) for source, target in forward]
+        low = lax.ppermute(
+            lax.slice_in_dim(block, block.shape[dim] - width, None, axis=dim), axis, forward
+        )
+        high = lax.ppermute(lax.slice_in_dim(block, 0, width, axis=dim), axis, backward)
+        block = jnp.concatenate([low, block, high], axis=dim)
+    return block
+
+
+def shift_plane(values, step_row, step_col):
+    lat_size, lon_size = (values.shape[-2], values.shape[-1])
+    margins = [(0, 0)] * (values.ndim - 2) + [
+        (max(step_row, 0), max(-step_row, 0)),
+        (max(step_col, 0), max(-step_col, 0)),
+    ]
+    padded = jnp.pad(values, margins)
+    row_start = max(-step_row, 0)
+    col_start = max(-step_col, 0)
+    return padded[..., row_start : row_start + lat_size, col_start : col_start + lon_size]
+
+
+def prepare(couplings, land_mask):
+    ones_field = jnp.ones(land_mask.shape, jnp.float32)
+    result = [couplings[0]]
+    for slot_n, (step_row, step_col) in enumerate(LINK_OFFSETS):
+        target = shift_plane(land_mask, -step_row, -step_col)
+        inside = shift_plane(ones_field, -step_row, -step_col)
+        factor = (
+            jnp.where(land_mask == target, jnp.float32(1.0), jnp.float32(COASTAL_FACTOR)) * inside
+        )
+        result.append(couplings[slot_n + 1] * factor)
+    result.append(couplings[5])
+    return jnp.stack(result)
+
+
+def stencil(padded, coef_block, link_prev):
+    field = padded[..., 1:-1, :, :]
+    next_day = padded[..., 2:, :, :]
+    prev_day = padded[..., :-2, :, :]
+    result = (
+        coef_block[0] * field + coef_block[5] * (field - next_day) + link_prev * (field - prev_day)
+    )
+    for slot_n, (step_row, step_col) in enumerate(LINK_OFFSETS):
+        link_coef = coef_block[slot_n + 1]
+        link_back = shift_plane(link_coef, step_row, step_col)
+        result = result + link_coef * (field - shift_plane(field, -step_row, -step_col))
+        result = result + link_back * (field - shift_plane(field, step_row, step_col))
+    return result
+
+
+def diagonal(coef_block, link_prev):
+    result = coef_block[0] + coef_block[5] + link_prev
+    for slot_n, (step_row, step_col) in enumerate(LINK_OFFSETS):
+        link_coef = coef_block[slot_n + 1]
+        result = result + link_coef + shift_plane(link_coef, step_row, step_col)
+    return result
+
+
+def spread(vector):
+    return vector[:, None, None, None]
+
+
+def summed(first, second):
+    return jnp.sum(first * second, axis=(1, 2, 3))
+
+
+def norm_sum(residual, scaled):
+    return lax.psum(summed(residual, scaled), "day")
+
+
+def direct(couplings, probe_bits, land_mask):
+    probes_n, days_n = (probe_bits.shape[0], probe_bits.shape[1])
+    links_eff = prepare(couplings, land_mask)
+    signs = (2 * probe_bits - 1).astype(jnp.float32)
+    prev_plane = passed_along(links_eff[5, days_n - 1 : days_n], "day", 1)
+    link_prev = jnp.concatenate([prev_plane, links_eff[5, : days_n - 1]], axis=0)
+    diag_own = diagonal(links_eff, link_prev)
+    residual = signs
+    scaled = signs / diag_own
+    estimate = jnp.zeros_like(signs)
+    norm_now = norm_sum(residual, scaled)
+    direction = scaled
+    for turn in range(ITERS):
+        padded = extended(direction, (("day", 1),), 1)
+        image = stencil(padded, links_eff, link_prev)
+        step_len = norm_now / lax.psum(summed(direction, image), "day")
+        estimate = estimate + spread(step_len) * direction
+        if turn + 1 < ITERS:
+            residual = residual - spread(step_len) * image
+            scaled = residual / diag_own
+            norm_next = norm_sum(residual, scaled)
+            direction = scaled + spread(norm_next / norm_now) * direction
+            norm_now = norm_next
+    return jnp.sum(signs * estimate, axis=0) / probes_n
 
 
 def solution(mesh):

time: 84.2 us -> 84 us (level)
  blocking collectives: 10.9 us -> 0 us
  starting transfers between devices: 24.8 us -> 32.1 us
  waiting for transfers between devices: 20.8 us -> 25.3 us
  Pallas kernels: 26.5 us -> 23.9 us
    all_to_all x1 -> x0, blocking collectives: 10.9 us -> none  [body(): moments = lax.all_to_all(moments, 'day', 0, 0)]
    ppermute x0 -> x6, starting transfers between devices: none -> 6.33 us  [body(): lax.ppermute(moments, 'day', [(i, i ^ n * step) for i in range(count)])]
    ppermute x0 -> x6, waiting for transfers between devices: none -> 4.33 us  [body(): lax.ppermute(moments, 'day', [(i, i ^ n * step) for i in range(count)])]
    pallas_call x7, Pallas kernels: 26.5 us -> 23.9 us  [call(): pl.pallas_call(kernel, grid=grid, in_specs=[spec(value.shape, kind) for v...]
    ppermute x7, starting transfers between devices: 24.8 us -> 25.7 us  [moved(): return lax.ppermute(value, 'day', [(i, target(i)) for i in range(count)])]
  transfers between devices with their start and end apart: 7 -> 13, of which waited for: 3 -> 7; matrix products, arithmetic and copies ran while one was open for 0% -> 0% of each run, Pallas kernels for 29% -> 27%
where the time goes in v7:
time: 84 us; the launch traced here: 83.8 us
  starting transfers between devices  32.1 us (38%)
  waiting for transfers between devices  25.3 us (30%)
  Pallas kernels  23.9 us (28%)
  local copies, waits for them, and re-layouts  1.54 us (2%)
    ppermute x7, starting transfers between devices, moved(): return lax.ppermute(value, 'day', [(i, target(i)) for i in range(count)])  25.7 us
    pallas_call x7, Pallas kernels, call(): pl.pallas_call(kernel, grid=grid, in_specs=[spec(value.shape, kind) for v...  23.9 us
    ppermute x7, waiting for transfers between devices, moved(): return lax.ppermute(value, 'day', [(i, target(i)) for i in range(count)])  21 us
    ppermute x6, starting transfers between devices, body(): lax.ppermute(moments, 'day', [(i, i ^ n * step) for i in range(count)])  6.33 us
    ppermute x6, waiting for transfers between devices, body(): lax.ppermute(moments, 'day', [(i, i ^ n * step) for i in range(count)])  4.33 us
  transfers between devices with their start and end apart: 13, of which 7 were waited for; matrix products, arithmetic and copies ran while one was open for 0% of the time, Pallas kernels for 27%

profile of v7, /device:TPU:0, one launch (start us, length us, event | category | flops | bytes accessed | tf_op | source)
XLA Modules:
  0.0 83.8 jit_solution(12441304190587469127)
XLA Ops:
  0.0 0.8 %slice_bitcast_fusion.4.own_ref = f32[32,512]{1,0:T(8,128)S(1)} fusion(f32[6,4,32,512]{3,2,1,0:T(8,128)} %coup_hbm.3), kind=kLoop, calls=%fused_computation.169 | loop fusion | bytes 131072 | tf_op jit(solution)/shard_map/squeeze | solution.py:437
  0.8 0.5 collective-permute-start.7
  1.3 2.3 %shard_map.39 = (f32[17,32,512]{2,1,0:T(8,128)S(1)}, f32[17,32,512]{2,1,0:T(8,128)S(1)}) custom-call(s32[1]{0:T(128)} %bitcast.12.odd_ref, f32[6,4,32,512]{3,2,1,0:T(8,128)} %coup_hbm.3, s32[16,4,32,512]{3,2,1,0:T(8,128)} %bits_hbm.3, s32[32,512]{1,0:T(8,128)} %mask_hbm.3, f32[32,512]{1,0:T(8,128)S(1)} %slice_bitcast_fusion.4.own_ref), custom_call_target="tpu_custom_call" | custom-call | flops 2516582 | bytes 2097152 | tf_op jit(solution)/shard_map/pallas_call | solution.py:423
  3.6 4.6 %collective-permute-done.7.before_ref = f32[32,512]{1,0:T(8,128)S(1)} collective-permute-done((f32[32,512]{1,0:T(8,128)S(1)}, f32[32,512]{1,0:T(8,128)S(1)}, u32[]{:S(2)}, u32[]{:S(2)}) %collective-permute-start.7) | collective-permute-done | bytes 65568 | tf_op jit(solution)/shard_map/ppermute | solution.py:21
  8.2 0.4 collective-permute-start.8
  8.7 0.0 collective-permute-start.9
  8.7 2.7 %shard_map.40 = (f32[8,4,32,512]{3,2,1,0:T(8,128)S(1)}, f32[4,32,512]{2,1,0:T(8,128)S(1)}, f32[4,32,512]{2,1,0:T(8,128)S(1)}, f32[4,32,512]{2,1,0:T(8,128)S(1)}, s32[16,4,32,512]{3,2,1,0:T(8,128)S(1)}) custom-call(f32[6,4,32,512]{3,2,1,0:T(8,128)} %coup_hbm.3, s32[16,4,32,512]{3,2,1,0:T(8,128)} %bits_hbm.3, s32[32,512]{1,0:T(8,128)} %mask_hbm.3, ...), custom_call_target="tpu_custom_call" | custom-call | flops 12582912 | bytes 4194304 | tf_op jit(solution)/shard_map/pallas_call | solution.py:423
  11.4 5.1 %shard_map.41 = (f32[16,4,32,512]{3,2,1,0:T(8,128)S(1)}, f32[16,32,512]{2,1,0:T(8,128)S(1)}, f32[16,32,512]{2,1,0:T(8,128)S(1)}) custom-call(s32[1]{0:T(128)} %bitcast.12.odd_ref, s32[16,4,32,512]{3,2,1,0:T(8,128)S(1)} %get-tuple-element.57.bits_ref, f32[8,4,32,512]{3,2,1,0:T(8,128)S(1)} %get-tuple-element.58.planes_ref, ...), custom_call_target="tpu_custom_call" | custom-call | flops 25165824 | bytes 8388608 | tf_op jit(solution)/shard_map/pallas_call | solution.py:423
  16.5 4.1 %collective-permute-start.11 = (f32[16,32,512]{2,1,0:T(8,128)S(1)}, f32[16,32,512]{2,1,0:T(8,128)S(1)}, u32[]{:S(2)}, u32[]{:S(2)}) collective-permute-start(f32[16,32,512]{2,1,0:T(8,128)S(1)} %get-tuple-element.72), channel_id=1, source_target_pairs={{0,15},{1,2},{2,1},{3,4},{4,3},{5,6},{6,5},{7,8},{8,7},{9,10},{10,... | collective-permute-start | bytes 3145736 | tf_op jit(solution)/shard_map/ppermute | solution.py:21
  20.6 5.4 %collective-permute-done.8.off_ref.doff_ref = f32[17,32,512]{2,1,0:T(8,128)S(1)} collective-permute-done((f32[17,32,512]{2,1,0:T(8,128)S(1)}, f32[17,32,512]{2,1,0:T(8,128)S(1)}, u32[]{:S(2)}, u32[]{:S(2)}) %collective-permute-start.8) | collective-permute-done | bytes 1114144 | tf_op jit(solution)/shard_map/ppermute | solution.py:21
  26.0 0.0 collective-permute-done.9.on_ref.don_ref
  26.0 18.4 %collective-permute-start.10 = (f32[8,128]{1,0:T(8,128)S(1)}, f32[8,128]{1,0:T(8,128)S(1)}, u32[]{:S(2)}, u32[]{:S(2)}) collective-permute-start(f32[8,128]{1,0:T(8,128)S(1)} %slice_bitcast_fusion.5), channel_id=1, source_target_pairs={{0,1},{1,0},{2,3},{3,2},{4,5},{5,4},{6,7},{7,6},{8,9},{9,8},{10,11... | collective-permute-start | bytes 12296 | tf_op jit(solution)/shard_map/ppermute | solution.py:21
  44.4 0.0 collective-permute-start.12
  44.4 8.9 %shard_map.42 = (f32[16,2,32,512]{3,2,1,0:T(8,128)S(1)}, f32[16,2,32,512]{3,2,1,0:T(8,128)S(1)}, f32[16,2,32,512]{3,2,1,0:T(8,128)S(1)}, f32[16,2,32,512]{3,2,1,...) custom-call(s32[1]{0:T(128)} %bitcast.12.odd_ref, ...), custom_call_target="tpu_custom_call" | custom-call | flops 37748736 | bytes 16777216 | tf_op jit(solution)/shard_map/pallas_call | solution.py:423
  53.3 0.0 collective-permute-done.11.off_ref
  53.3 0.0 collective-permute-done.10.token_ref
  53.3 2.3 %collective-permute-start.13 = (f32[16,32,512]{2,1,0:T(8,128)S(1)}, f32[16,32,512]{2,1,0:T(8,128)S(1)}, u32[]{:S(2)}, u32[]{:S(2)}) collective-permute-start(f32[16,32,512]{2,1,0:T(8,128)S(1)} %get-tuple-element.83), channel_id=1, source_target_pairs={{0,1},{1,2},{2,3},{3,4},{4,5},{5,6},{6,7},{7,8},{8,9},{9,10},{10,1... | collective-permute-start | bytes 3145736 | tf_op jit(solution)/shard_map/ppermute | solution.py:21
  55.6 0.0 collective-permute-done.12.on_ref
  55.6 3.7 %shard_map.43 = (f32[16,2,32,512]{3,2,1,0:T(8,128)S(1)}, f32[16,2,32,512]{3,2,1,0:T(8,128)S(1)}, f32[16,32,512]{2,1,0:T(8,128)S(1)}, f32[16,8,128]{2,1,0:T(8,128)S(1)}) custom-call(s32[1]{0:T(128)} %bitcast.12.odd_ref, f32[8,128]{1,0:T(8,128)S(1)} %collective-permute-done.10.token_ref, s32[16,4,32,512]{3,2,1,0:T(8,128)S(1)} %get-tuple-element.57.bits_ref, ...), custom_call_target="tpu_custom_call" | custom-call | flops 17616076 | bytes 16777216 | tf_op jit(solution)/shard_map/pallas_call | solution.py:423
  59.3 11.0 %collective-permute-done.13.high_ref = f32[16,32,512]{2,1,0:T(8,128)S(1)} collective-permute-done((f32[16,32,512]{2,1,0:T(8,128)S(1)}, f32[16,32,512]{2,1,0:T(8,128)S(1)}, u32[]{:S(2)}, u32[]{:S(2)}) %collective-permute-start.13) | collective-permute-done | bytes 1048608 | tf_op jit(solution)/shard_map/ppermute | solution.py:21
  70.3 0.2 shard_map.44
  70.5 0.0 collective-permute-start.16
  70.5 0.9 %collective-permute-start.15 = (f32[8,128]{1,0:T(8,128)S(1)}, f32[8,128]{1,0:T(8,128)S(1)}, u32[]{:S(2)}, u32[]{:S(2)}) collective-permute-start(f32[8,128]{1,0:T(8,128)S(1)} %shard_map.44), channel_id=1, source_target_pairs={{0,2},{1,3},{2,0},{3,1},{4,6},{5,7},{6,4},{7,5},{8,10},{9,11},{10,... | collective-permute-start | bytes 12296 | tf_op jit(solution)/shard_map/ppermute | solution.py:507
  71.4 1.0 %collective-permute-start.14 = (f32[8,128]{1,0:T(8,128)S(1)}, f32[8,128]{1,0:T(8,128)S(1)}, u32[]{:S(2)}, u32[]{:S(2)}) collective-permute-start(f32[8,128]{1,0:T(8,128)S(1)} %shard_map.44), channel_id=1, source_target_pairs={{0,1},{1,0},{2,3},{3,2},{4,5},{5,4},{6,7},{7,6},{8,9},{9,8},{10,11... | collective-permute-start | bytes 12296 | tf_op jit(solution)/shard_map/ppermute | solution.py:507
  72.4 1.2 %collective-permute-done.16 = f32[8,128]{1,0:T(8,128)S(1)} collective-permute-done((f32[8,128]{1,0:T(8,128)S(1)}, f32[8,128]{1,0:T(8,128)S(1)}, u32[]{:S(2)}, u32[]{:S(2)}) %collective-permute-start.16) | collective-permute-done | bytes 4128 | tf_op jit(solution)/shard_map/ppermute | solution.py:507
  73.5 0.7 collective-permute-done.15
  74.2 0.0 collective-permute-done.14
  74.2 2.4 %collective-permute-start.19 = (f32[8,128]{1,0:T(8,128)S(1)}, f32[8,128]{1,0:T(8,128)S(1)}, u32[]{:S(2)}, u32[]{:S(2)}) collective-permute-start(f32[8,128]{1,0:T(8,128)S(1)} %add_add_fusion.1.refs_0_), channel_id=1, source_target_pairs={{0,12},{1,13},{2,14},{3,15},{4,8},{5,9},{6,10},{7,11},{8,4},{9,5},... | collective-permute-start | bytes 12296 | tf_op jit(solution)/shard_map/ppermute | solution.py:507
  76.6 0.0 collective-permute-start.18
  76.6 2.0 %collective-permute-start.17 = (f32[8,128]{1,0:T(8,128)S(1)}, f32[8,128]{1,0:T(8,128)S(1)}, u32[]{:S(2)}, u32[]{:S(2)}) collective-permute-start(f32[8,128]{1,0:T(8,128)S(1)} %add_add_fusion.1.refs_0_), channel_id=1, source_target_pairs={{0,4},{1,5},{2,6},{3,7},{4,0},{5,1},{6,2},{7,3},{8,12},{9,13},{10,... | collective-permute-start | bytes 12296 | tf_op jit(solution)/shard_map/ppermute | solution.py:507
  78.6 1.0 %collective-permute-done.19.refs_3_ = f32[8,128]{1,0:T(8,128)S(1)} collective-permute-done((f32[8,128]{1,0:T(8,128)S(1)}, f32[8,128]{1,0:T(8,128)S(1)}, u32[]{:S(2)}, u32[]{:S(2)}) %collective-permute-start.19) | collective-permute-done | bytes 4128 | tf_op jit(solution)/shard_map/ppermute | solution.py:507
  79.7 1.5 %collective-permute-done.18.refs_2_ = f32[8,128]{1,0:T(8,128)S(1)} collective-permute-done((f32[8,128]{1,0:T(8,128)S(1)}, f32[8,128]{1,0:T(8,128)S(1)}, u32[]{:S(2)}, u32[]{:S(2)}) %collective-permute-start.18) | collective-permute-done | bytes 4128 | tf_op jit(solution)/shard_map/ppermute | solution.py:507
  81.1 0.0 collective-permute-done.17.refs_1_
  81.1 1.1 %shard_map.45 = (f32[4,32,512]{2,1,0:T(8,128)S(1)}, s32[1]{0:T(128)}) custom-call(f32[16,2,32,512]{3,2,1,0:T(8,128)S(1)} %get-tuple-element.67.p1m_ref, f32[16,2,32,512]{3,2,1,0:T(8,128)S(1)} %get-tuple-element.68.p2m_ref, f32[16,2,32,512]{3,2,1,0:T(8,128)S(1)} %get-tuple-element.80.p1e_ref, f32[16,2,32,512]{3,2,1,0:T(8,128)S(1)} %get-tuple-element.81.p2e_ref, ...), custom_call_target="tpu_custom_call" | custom-call | flops 5033164 | bytes 8388608 | tf_op jit(solution)/shard_map/pallas_call | solution.py:423
  82.9 0.2 conditional.1
  83.1 0.0 copy-start.3
  83.1 0.7 copy-done.3
  (2 shorter events, 0.0 us)
Async XLA Ops:
  0.8 7.4 %collective-permute-start.7 = (f32[32,512]{1,0:T(8,128)S(1)}, f32[32,512]{1,0:T(8,128)S(1)}, u32[]{:S(2)}, u32[]{:S(2)}) collective-permute-start(f32[32,512]{1,0:T(8,128)S(1)} %slice_bitcast_fusion.4.own_ref), channel_id=1, source_target_pairs={{0,1},{1,2},{2,3},{3,4},{4,5},{5,6},{6,7},{7,8},{8,9},{9,10},{10,1... | collective-permute-start | bytes 196616 | tf_op jit(solution)/shard_map/ppermute | solution.py:21
  8.2 17.7 %collective-permute-start.8 = (f32[17,32,512]{2,1,0:T(8,128)S(1)}, f32[17,32,512]{2,1,0:T(8,128)S(1)}, u32[]{:S(2)}, u32[]{:S(2)}) collective-permute-start(f32[17,32,512]{2,1,0:T(8,128)S(1)} %get-tuple-element.62), channel_id=1, source_target_pairs={{0,15},{1,2},{2,1},{3,4},{4,3},{5,6},{6,5},{7,8},{8,7},{9,10},{10,... | collective-permute-start | bytes 3342344 | tf_op jit(solution)/shard_map/ppermute | solution.py:21
  8.7 17.3 %collective-permute-start.9 = (f32[17,32,512]{2,1,0:T(8,128)S(1)}, f32[17,32,512]{2,1,0:T(8,128)S(1)}, u32[]{:S(2)}, u32[]{:S(2)}) collective-permute-start(f32[17,32,512]{2,1,0:T(8,128)S(1)} %get-tuple-element.63), channel_id=1, source_target_pairs={{0,1},{1,0},{2,3},{3,2},{4,5},{5,4},{6,7},{7,6},{8,9},{9,8},{10,11... | collective-permute-start | bytes 3342344 | tf_op jit(solution)/shard_map/ppermute | solution.py:21
  16.5 36.8 %collective-permute-start.11 = (f32[16,32,512]{2,1,0:T(8,128)S(1)}, f32[16,32,512]{2,1,0:T(8,128)S(1)}, u32[]{:S(2)}, u32[]{:S(2)}) collective-permute-start(f32[16,32,512]{2,1,0:T(8,128)S(1)} %get-tuple-element.72), channel_id=1, source_target_pairs={{0,15},{1,2},{2,1},{3,4},{4,3},{5,6},{6,5},{7,8},{8,7},{9,10},{10,... | collective-permute-start | bytes 3145736 | tf_op jit(solution)/shard_map/ppermute | solution.py:21
  26.0 27.3 %collective-permute-start.10 = (f32[8,128]{1,0:T(8,128)S(1)}, f32[8,128]{1,0:T(8,128)S(1)}, u32[]{:S(2)}, u32[]{:S(2)}) collective-permute-start(f32[8,128]{1,0:T(8,128)S(1)} %slice_bitcast_fusion.5), channel_id=1, source_target_pairs={{0,1},{1,0},{2,3},{3,2},{4,5},{5,4},{6,7},{7,6},{8,9},{9,8},{10,11... | collective-permute-start | bytes 12296 | tf_op jit(solution)/shard_map/ppermute | solution.py:21
  44.4 11.2 %collective-permute-start.12 = (f32[16,32,512]{2,1,0:T(8,128)S(1)}, f32[16,32,512]{2,1,0:T(8,128)S(1)}, u32[]{:S(2)}, u32[]{:S(2)}) collective-permute-start(f32[16,32,512]{2,1,0:T(8,128)S(1)} %get-tuple-element.77), channel_id=1, source_target_pairs={{0,1},{1,0},{2,3},{3,2},{4,5},{5,4},{6,7},{7,6},{8,9},{9,8},{10,11... | collective-permute-start | bytes 3145736 | tf_op jit(solution)/shard_map/ppermute | solution.py:21
  53.3 17.0 %collective-permute-start.13 = (f32[16,32,512]{2,1,0:T(8,128)S(1)}, f32[16,32,512]{2,1,0:T(8,128)S(1)}, u32[]{:S(2)}, u32[]{:S(2)}) collective-permute-start(f32[16,32,512]{2,1,0:T(8,128)S(1)} %get-tuple-element.83), channel_id=1, source_target_pairs={{0,1},{1,2},{2,3},{3,4},{4,5},{5,6},{6,7},{7,8},{8,9},{9,10},{10,1... | collective-permute-start | bytes 3145736 | tf_op jit(solution)/shard_map/ppermute | solution.py:21
  70.5 3.1 %collective-permute-start.16 = (f32[8,128]{1,0:T(8,128)S(1)}, f32[8,128]{1,0:T(8,128)S(1)}, u32[]{:S(2)}, u32[]{:S(2)}) collective-permute-start(f32[8,128]{1,0:T(8,128)S(1)} %shard_map.44), channel_id=1, source_target_pairs={{0,3},{1,2},{2,1},{3,0},{4,7},{5,6},{6,5},{7,4},{8,11},{9,10},{10,... | collective-permute-start | bytes 12296 | tf_op jit(solution)/shard_map/ppermute | solution.py:507
  70.5 3.7 %collective-permute-start.15 = (f32[8,128]{1,0:T(8,128)S(1)}, f32[8,128]{1,0:T(8,128)S(1)}, u32[]{:S(2)}, u32[]{:S(2)}) collective-permute-start(f32[8,128]{1,0:T(8,128)S(1)} %shard_map.44), channel_id=1, source_target_pairs={{0,2},{1,3},{2,0},{3,1},{4,6},{5,7},{6,4},{7,5},{8,10},{9,11},{10,... | collective-permute-start | bytes 12296 | tf_op jit(solution)/shard_map/ppermute | solution.py:507
  71.4 2.8 %collective-permute-start.14 = (f32[8,128]{1,0:T(8,128)S(1)}, f32[8,128]{1,0:T(8,128)S(1)}, u32[]{:S(2)}, u32[]{:S(2)}) collective-permute-start(f32[8,128]{1,0:T(8,128)S(1)} %shard_map.44), channel_id=1, source_target_pairs={{0,1},{1,0},{2,3},{3,2},{4,5},{5,4},{6,7},{7,6},{8,9},{9,8},{10,11... | collective-permute-start | bytes 12296 | tf_op jit(solution)/shard_map/ppermute | solution.py:507
  74.2 5.5 %collective-permute-start.19 = (f32[8,128]{1,0:T(8,128)S(1)}, f32[8,128]{1,0:T(8,128)S(1)}, u32[]{:S(2)}, u32[]{:S(2)}) collective-permute-start(f32[8,128]{1,0:T(8,128)S(1)} %add_add_fusion.1.refs_0_), channel_id=1, source_target_pairs={{0,12},{1,13},{2,14},{3,15},{4,8},{5,9},{6,10},{7,11},{8,4},{9,5},... | collective-permute-start | bytes 12296 | tf_op jit(solution)/shard_map/ppermute | solution.py:507
  76.6 4.5 %collective-permute-start.18 = (f32[8,128]{1,0:T(8,128)S(1)}, f32[8,128]{1,0:T(8,128)S(1)}, u32[]{:S(2)}, u32[]{:S(2)}) collective-permute-start(f32[8,128]{1,0:T(8,128)S(1)} %add_add_fusion.1.refs_0_), channel_id=1, source_target_pairs={{0,8},{1,9},{2,10},{3,11},{4,12},{5,13},{6,14},{7,15},{8,0},{9,1},... | collective-permute-start | bytes 12296 | tf_op jit(solution)/shard_map/ppermute | solution.py:507
  76.6 4.5 %collective-permute-start.17 = (f32[8,128]{1,0:T(8,128)S(1)}, f32[8,128]{1,0:T(8,128)S(1)}, u32[]{:S(2)}, u32[]{:S(2)}) collective-permute-start(f32[8,128]{1,0:T(8,128)S(1)} %add_add_fusion.1.refs_0_), channel_id=1, source_target_pairs={{0,4},{1,5},{2,6},{3,7},{4,0},{5,1},{6,2},{7,3},{8,12},{9,13},{10,... | collective-permute-start | bytes 12296 | tf_op jit(solution)/shard_map/ppermute | solution.py:507
  83.1 0.7 copy-start.3

commit v8 on v7

--- a/solution.py
+++ b/solution.py
@@ -498,16 +498,18 @@
         [(cross, "whole"), (high2_prev, "whole"), (sums, "whole")],
         [(tile, "whole", F32)], cost=(0.1, 0.5), mib=8,
     )
-    shares = [moments]
-    step = 1
-    while step < count:
-        near = min(4, count // step)
-        moments = paired_sum(shares)
-        shares = [moments] + [
-            lax.ppermute(moments, "day", [(i, i ^ (n * step)) for i in range(count)])
-            for n in range(1, near)
+    moments = moments + moved(moments, "on")
+    half = max(count // 4, 1)
+    shares = []
+    for n in range(half if count > 2 else 0):
+        pairs = [
+            (i ^ (2 * (n + half * (i % 2))), i) for i in range(count) if n or i % 2
         ]
-        step *= near
+        share = lax.ppermute(moments, "day", pairs)
+        shares.append(share if n else jnp.where(odd == 1, share, moments))
+    moments = paired_sum(shares) if shares else moments
+    shares = [moments] + ([moved(moments, "on")] if count > 2 else [])
+
     out, unsound = call(
         last_kernel, (1,),
         [(p1m, "whole"), (p2m, "whole"), (p1e, "whole"), (p2e, "whole"), (dinv, "whole")]

time: 84 us -> 88.5 us (1.054)
  starting transfers between devices: 32.1 us -> 35.6 us
  waiting for transfers between devices: 25.3 us -> 26.4 us
    ppermute x7 -> x9, starting transfers between devices: 25.7 us -> 31.4 us  [moved(): return lax.ppermute(value, 'day', [(i, target(i)) for i in range(count)])]
    ppermute x6 -> x4, starting transfers between devices: 6.33 us -> 4.2 us  [body(): share = lax.ppermute(moments, 'day', pairs)]
    ppermute x7 -> x9, waiting for transfers between devices: 21 us -> 23 us  [moved(): return lax.ppermute(value, 'day', [(i, target(i)) for i in range(count)])]
    ppermute x6 -> x4, waiting for transfers between devices: 4.33 us -> 3.39 us  [body(): share = lax.ppermute(moments, 'day', pairs)]
  transfers between devices with their start and end apart: 13 -> 13, of which waited for: 7 -> 8; matrix products, arithmetic and copies ran while one was open for 0% -> 0% of each run, Pallas kernels for 27% -> 26%
where the time goes in v8:
time: 88.5 us; the launch traced here: 88.4 us
  starting transfers between devices  35.6 us (40%)
  waiting for transfers between devices  26.4 us (30%)
  Pallas kernels  23.9 us (27%)
  local copies, waits for them, and re-layouts  1.54 us (2%)
    ppermute x9, starting transfers between devices, moved(): return lax.ppermute(value, 'day', [(i, target(i)) for i in range(count)])  31.4 us
    pallas_call x7, Pallas kernels, call(): pl.pallas_call(kernel, grid=grid, in_specs=[spec(value.shape, kind) for v...  23.9 us
    ppermute x9, waiting for transfers between devices, moved(): return lax.ppermute(value, 'day', [(i, target(i)) for i in range(count)])  23 us
    ppermute x4, starting transfers between devices, body(): share = lax.ppermute(moments, 'day', pairs)  4.2 us
    ppermute x4, waiting for transfers between devices, body(): share = lax.ppermute(moments, 'day', pairs)  3.39 us
  transfers between devices with their start and end apart: 13, of which 8 were waited for; matrix products, arithmetic and copies ran while one was open for 0% of the time, Pallas kernels for 26%

profile of v8, /device:TPU:0, one launch (start us, length us, event | category | flops | bytes accessed | tf_op | source)
XLA Modules:
  0.0 88.4 jit_solution(8015743483498595557)
XLA Ops:
  0.0 0.8 slice_bitcast_fusion.4.own_ref
  0.8 0.5 collective-permute-start.7
  1.3 2.3 %shard_map.39 = (f32[17,32,512]{2,1,0:T(8,128)S(1)}, f32[17,32,512]{2,1,0:T(8,128)S(1)}) custom-call(s32[1]{0:T(128)} %bitcast.12.odd_ref, f32[6,4,32,512]{3,2,1,0:T(8,128)} %coup_hbm.3, s32[16,4,32,512]{3,2,1,0:T(8,128)} %bits_hbm.3, s32[32,512]{1,0:T(8,128)} %mask_hbm.3, f32[32,512]{1,0:T(8,128)S(1)} %slice_bitcast_fusion.4.own_ref), custom_call_target="tpu_custom_call" | custom-call | flops 2516582 | bytes 2097152 | tf_op jit(solution)/shard_map/pallas_call | solution.py:423
  3.6 4.6 %collective-permute-done.7.before_ref = f32[32,512]{1,0:T(8,128)S(1)} collective-permute-done((f32[32,512]{1,0:T(8,128)S(1)}, f32[32,512]{1,0:T(8,128)S(1)}, u32[]{:S(2)}, u32[]{:S(2)}) %collective-permute-start.7) | collective-permute-done | bytes 65568 | tf_op jit(solution)/shard_map/ppermute | solution.py:21
  8.2 0.4 collective-permute-start.8
  8.7 0.0 collective-permute-start.9
  8.7 2.7 %shard_map.40 = (f32[8,4,32,512]{3,2,1,0:T(8,128)S(1)}, f32[4,32,512]{2,1,0:T(8,128)S(1)}, f32[4,32,512]{2,1,0:T(8,128)S(1)}, f32[4,32,512]{2,1,0:T(8,128)S(1)}, s32[16,4,32,512]{3,2,1,0:T(8,128)S(1)}) custom-call(f32[6,4,32,512]{3,2,1,0:T(8,128)} %coup_hbm.3, s32[16,4,32,512]{3,2,1,0:T(8,128)} %bits_hbm.3, s32[32,512]{1,0:T(8,128)} %mask_hbm.3, ...), custom_call_target="tpu_custom_call" | custom-call | flops 12582912 | bytes 4194304 | tf_op jit(solution)/shard_map/pallas_call | solution.py:423
  11.4 5.1 %shard_map.41 = (f32[16,4,32,512]{3,2,1,0:T(8,128)S(1)}, f32[16,32,512]{2,1,0:T(8,128)S(1)}, f32[16,32,512]{2,1,0:T(8,128)S(1)}) custom-call(s32[1]{0:T(128)} %bitcast.12.odd_ref, s32[16,4,32,512]{3,2,1,0:T(8,128)S(1)} %get-tuple-element.57.bits_ref, f32[8,4,32,512]{3,2,1,0:T(8,128)S(1)} %get-tuple-element.58.planes_ref, ...), custom_call_target="tpu_custom_call" | custom-call | flops 25165824 | bytes 8388608 | tf_op jit(solution)/shard_map/pallas_call | solution.py:423
  16.5 4.1 %collective-permute-start.11 = (f32[16,32,512]{2,1,0:T(8,128)S(1)}, f32[16,32,512]{2,1,0:T(8,128)S(1)}, u32[]{:S(2)}, u32[]{:S(2)}) collective-permute-start(f32[16,32,512]{2,1,0:T(8,128)S(1)} %get-tuple-element.72), channel_id=1, source_target_pairs={{0,15},{1,2},{2,1},{3,4},{4,3},{5,6},{6,5},{7,8},{8,7},{9,10},{10,... | collective-permute-start | bytes 3145736 | tf_op jit(solution)/shard_map/ppermute | solution.py:21
  20.6 5.4 %collective-permute-done.8.off_ref.doff_ref = f32[17,32,512]{2,1,0:T(8,128)S(1)} collective-permute-done((f32[17,32,512]{2,1,0:T(8,128)S(1)}, f32[17,32,512]{2,1,0:T(8,128)S(1)}, u32[]{:S(2)}, u32[]{:S(2)}) %collective-permute-start.8) | collective-permute-done | bytes 1114144 | tf_op jit(solution)/shard_map/ppermute | solution.py:21
  26.0 0.0 collective-permute-done.9.on_ref.don_ref
  26.0 18.4 %collective-permute-start.10 = (f32[8,128]{1,0:T(8,128)S(1)}, f32[8,128]{1,0:T(8,128)S(1)}, u32[]{:S(2)}, u32[]{:S(2)}) collective-permute-start(f32[8,128]{1,0:T(8,128)S(1)} %slice_bitcast_fusion.5), channel_id=1, source_target_pairs={{0,1},{1,0},{2,3},{3,2},{4,5},{5,4},{6,7},{7,6},{8,9},{9,8},{10,11... | collective-permute-start | bytes 12296 | tf_op jit(solution)/shard_map/ppermute | solution.py:21
  44.4 0.0 collective-permute-start.12
  44.4 8.9 %shard_map.42 = (f32[16,2,32,512]{3,2,1,0:T(8,128)S(1)}, f32[16,2,32,512]{3,2,1,0:T(8,128)S(1)}, f32[16,2,32,512]{3,2,1,0:T(8,128)S(1)}, f32[16,2,32,512]{3,2,1,...) custom-call(s32[1]{0:T(128)} %bitcast.12.odd_ref, ...), custom_call_target="tpu_custom_call" | custom-call | flops 37748736 | bytes 16777216 | tf_op jit(solution)/shard_map/pallas_call | solution.py:423
  53.3 0.0 collective-permute-done.11.off_ref
  53.3 0.0 collective-permute-done.10.token_ref
  53.3 2.3 %collective-permute-start.13 = (f32[16,32,512]{2,1,0:T(8,128)S(1)}, f32[16,32,512]{2,1,0:T(8,128)S(1)}, u32[]{:S(2)}, u32[]{:S(2)}) collective-permute-start(f32[16,32,512]{2,1,0:T(8,128)S(1)} %get-tuple-element.83), channel_id=1, source_target_pairs={{0,1},{1,2},{2,3},{3,4},{4,5},{5,6},{6,7},{7,8},{8,9},{9,10},{10,1... | collective-permute-start | bytes 3145736 | tf_op jit(solution)/shard_map/ppermute | solution.py:21
  55.6 0.0 collective-permute-done.12.on_ref
  55.6 3.7 %shard_map.43 = (f32[16,2,32,512]{3,2,1,0:T(8,128)S(1)}, f32[16,2,32,512]{3,2,1,0:T(8,128)S(1)}, f32[16,32,512]{2,1,0:T(8,128)S(1)}, f32[16,8,128]{2,1,0:T(8,128)S(1)}) custom-call(s32[1]{0:T(128)} %bitcast.12.odd_ref, f32[8,128]{1,0:T(8,128)S(1)} %collective-permute-done.10.token_ref, s32[16,4,32,512]{3,2,1,0:T(8,128)S(1)} %get-tuple-element.57.bits_ref, ...), custom_call_target="tpu_custom_call" | custom-call | flops 17616076 | bytes 16777216 | tf_op jit(solution)/shard_map/pallas_call | solution.py:423
  59.3 11.0 %collective-permute-done.13.high_ref = f32[16,32,512]{2,1,0:T(8,128)S(1)} collective-permute-done((f32[16,32,512]{2,1,0:T(8,128)S(1)}, f32[16,32,512]{2,1,0:T(8,128)S(1)}, u32[]{:S(2)}, u32[]{:S(2)}) %collective-permute-start.13) | collective-permute-done | bytes 1048608 | tf_op jit(solution)/shard_map/ppermute | solution.py:21
  70.3 0.2 shard_map.44
  70.5 0.0 collective-permute-start.14
  70.5 1.2 %collective-permute-done.14 = f32[8,128]{1,0:T(8,128)S(1)} collective-permute-done((f32[8,128]{1,0:T(8,128)S(1)}, f32[8,128]{1,0:T(8,128)S(1)}, u32[]{:S(2)}, u32[]{:S(2)}) %collective-permute-start.14) | collective-permute-done | bytes 4128 | tf_op jit(solution)/shard_map/ppermute | solution.py:21
  71.7 0.7 collective-permute-start.15
  72.3 0.9 collective-permute-start.16
  73.2 1.6 %collective-permute-start.17 = (f32[8,128]{1,0:T(8,128)S(1)}, f32[8,128]{1,0:T(8,128)S(1)}, u32[]{:S(2)}, u32[]{:S(2)}) collective-permute-start(f32[8,128]{1,0:T(8,128)S(1)} %add.234), channel_id=1, source_target_pairs={{4,0},{13,1},{6,2},{15,3},{0,4},{9,5},{2,6},{11,7},{12,8},{5,9},{1... | collective-permute-start | bytes 12296 | tf_op jit(solution)/shard_map/ppermute | solution.py:508
  74.8 1.1 %collective-permute-start.18 = (f32[8,128]{1,0:T(8,128)S(1)}, f32[8,128]{1,0:T(8,128)S(1)}, u32[]{:S(2)}, u32[]{:S(2)}) collective-permute-start(f32[8,128]{1,0:T(8,128)S(1)} %add.234), channel_id=1, source_target_pairs={{6,0},{15,1},{4,2},{13,3},{2,4},{11,5},{0,6},{9,7},{14,8},{7,9},{1... | collective-permute-start | bytes 12296 | tf_op jit(solution)/shard_map/ppermute | solution.py:508
  75.9 0.0 collective-permute-done.15
  75.9 0.1 collective-permute-done.16
  76.0 0.8 collective-permute-done.17
  76.8 2.5 %collective-permute-done.18 = f32[8,128]{1,0:T(8,128)S(1)} collective-permute-done((f32[8,128]{1,0:T(8,128)S(1)}, f32[8,128]{1,0:T(8,128)S(1)}, u32[]{:S(2)}, u32[]{:S(2)}) %collective-permute-start.18) | collective-permute-done | bytes 4128 | tf_op jit(solution)/shard_map/ppermute | solution.py:508
  79.3 5.6 %collective-permute-start.19 = (f32[8,128]{1,0:T(8,128)S(1)}, f32[8,128]{1,0:T(8,128)S(1)}, u32[]{:S(2)}, u32[]{:S(2)}) collective-permute-start(f32[8,128]{1,0:T(8,128)S(1)} %add_add_fusion.1.refs_0_), channel_id=1, source_target_pairs={{0,1},{1,0},{2,3},{3,2},{4,5},{5,4},{6,7},{7,6},{8,9},{9,8},{10,11... | collective-permute-start | bytes 12296 | tf_op jit(solution)/shard_map/ppermute | solution.py:21
  84.9 0.8 collective-permute-done.19.refs_1_
  85.7 1.1 %shard_map.45 = (f32[4,32,512]{2,1,0:T(8,128)S(1)}, s32[1]{0:T(128)}) custom-call(f32[16,2,32,512]{3,2,1,0:T(8,128)S(1)} %get-tuple-element.67.p1m_ref, f32[16,2,32,512]{3,2,1,0:T(8,128)S(1)} %get-tuple-element.68.p2m_ref, f32[16,2,32,512]{3,2,1,0:T(8,128)S(1)} %get-tuple-element.80.p1e_ref, f32[16,2,32,512]{3,2,1,0:T(8,128)S(1)} %get-tuple-element.81.p2e_ref, ...), custom_call_target="tpu_custom_call" | custom-call | flops 5033164 | bytes 8388608 | tf_op jit(solution)/shard_map/pallas_call | solution.py:423
  87.4 0.2 conditional.1
  87.6 0.0 copy-start.3
  87.7 0.7 copy-done.3
  (3 shorter events, 0.0 us)
Async XLA Ops:
  0.8 7.4 %collective-permute-start.7 = (f32[32,512]{1,0:T(8,128)S(1)}, f32[32,512]{1,0:T(8,128)S(1)}, u32[]{:S(2)}, u32[]{:S(2)}) collective-permute-start(f32[32,512]{1,0:T(8,128)S(1)} %slice_bitcast_fusion.4.own_ref), channel_id=1, source_target_pairs={{0,1},{1,2},{2,3},{3,4},{4,5},{5,6},{6,7},{7,8},{8,9},{9,10},{10,1... | collective-permute-start | bytes 196616 | tf_op jit(solution)/shard_map/ppermute | solution.py:21
  8.2 17.7 %collective-permute-start.8 = (f32[17,32,512]{2,1,0:T(8,128)S(1)}, f32[17,32,512]{2,1,0:T(8,128)S(1)}, u32[]{:S(2)}, u32[]{:S(2)}) collective-permute-start(f32[17,32,512]{2,1,0:T(8,128)S(1)} %get-tuple-element.62), channel_id=1, source_target_pairs={{0,15},{1,2},{2,1},{3,4},{4,3},{5,6},{6,5},{7,8},{8,7},{9,10},{10,... | collective-permute-start | bytes 3342344 | tf_op jit(solution)/shard_map/ppermute | solution.py:21
  8.7 17.3 %collective-permute-start.9 = (f32[17,32,512]{2,1,0:T(8,128)S(1)}, f32[17,32,512]{2,1,0:T(8,128)S(1)}, u32[]{:S(2)}, u32[]{:S(2)}) collective-permute-start(f32[17,32,512]{2,1,0:T(8,128)S(1)} %get-tuple-element.63), channel_id=1, source_target_pairs={{0,1},{1,0},{2,3},{3,2},{4,5},{5,4},{6,7},{7,6},{8,9},{9,8},{10,11... | collective-permute-start | bytes 3342344 | tf_op jit(solution)/shard_map/ppermute | solution.py:21
  16.5 36.8 %collective-permute-start.11 = (f32[16,32,512]{2,1,0:T(8,128)S(1)}, f32[16,32,512]{2,1,0:T(8,128)S(1)}, u32[]{:S(2)}, u32[]{:S(2)}) collective-permute-start(f32[16,32,512]{2,1,0:T(8,128)S(1)} %get-tuple-element.72), channel_id=1, source_target_pairs={{0,15},{1,2},{2,1},{3,4},{4,3},{5,6},{6,5},{7,8},{8,7},{9,10},{10,... | collective-permute-start | bytes 3145736 | tf_op jit(solution)/shard_map/ppermute | solution.py:21
  26.0 27.3 %collective-permute-start.10 = (f32[8,128]{1,0:T(8,128)S(1)}, f32[8,128]{1,0:T(8,128)S(1)}, u32[]{:S(2)}, u32[]{:S(2)}) collective-permute-start(f32[8,128]{1,0:T(8,128)S(1)} %slice_bitcast_fusion.5), channel_id=1, source_target_pairs={{0,1},{1,0},{2,3},{3,2},{4,5},{5,4},{6,7},{7,6},{8,9},{9,8},{10,11... | collective-permute-start | bytes 12296 | tf_op jit(solution)/shard_map/ppermute | solution.py:21
  44.4 11.2 %collective-permute-start.12 = (f32[16,32,512]{2,1,0:T(8,128)S(1)}, f32[16,32,512]{2,1,0:T(8,128)S(1)}, u32[]{:S(2)}, u32[]{:S(2)}) collective-permute-start(f32[16,32,512]{2,1,0:T(8,128)S(1)} %get-tuple-element.77), channel_id=1, source_target_pairs={{0,1},{1,0},{2,3},{3,2},{4,5},{5,4},{6,7},{7,6},{8,9},{9,8},{10,11... | collective-permute-start | bytes 3145736 | tf_op jit(solution)/shard_map/ppermute | solution.py:21
  53.3 17.0 %collective-permute-start.13 = (f32[16,32,512]{2,1,0:T(8,128)S(1)}, f32[16,32,512]{2,1,0:T(8,128)S(1)}, u32[]{:S(2)}, u32[]{:S(2)}) collective-permute-start(f32[16,32,512]{2,1,0:T(8,128)S(1)} %get-tuple-element.83), channel_id=1, source_target_pairs={{0,1},{1,2},{2,3},{3,4},{4,5},{5,6},{6,7},{7,8},{8,9},{9,10},{10,1... | collective-permute-start | bytes 3145736 | tf_op jit(solution)/shard_map/ppermute | solution.py:21
  70.5 1.2 %collective-permute-start.14 = (f32[8,128]{1,0:T(8,128)S(1)}, f32[8,128]{1,0:T(8,128)S(1)}, u32[]{:S(2)}, u32[]{:S(2)}) collective-permute-start(f32[8,128]{1,0:T(8,128)S(1)} %shard_map.44), channel_id=1, source_target_pairs={{0,1},{1,0},{2,3},{3,2},{4,5},{5,4},{6,7},{7,6},{8,9},{9,8},{10,11... | collective-permute-start | bytes 12296 | tf_op jit(solution)/shard_map/ppermute | solution.py:21
  71.7 4.2 %collective-permute-start.15 = (f32[8,128]{1,0:T(8,128)S(1)}, f32[8,128]{1,0:T(8,128)S(1)}, u32[]{:S(2)}, u32[]{:S(2)}) collective-permute-start(f32[8,128]{1,0:T(8,128)S(1)} %add.234), channel_id=1, source_target_pairs={{9,1},{11,3},{13,5},{15,7},{1,9},{3,11},{5,13},{7,15},{25,17},{27,... | collective-permute-start | bytes 12296 | tf_op jit(solution)/shard_map/ppermute | solution.py:508
  72.3 3.7 %collective-permute-start.16 = (f32[8,128]{1,0:T(8,128)S(1)}, f32[8,128]{1,0:T(8,128)S(1)}, u32[]{:S(2)}, u32[]{:S(2)}) collective-permute-start(f32[8,128]{1,0:T(8,128)S(1)} %add.234), channel_id=1, source_target_pairs={{2,0},{11,1},{0,2},{9,3},{6,4},{15,5},{4,6},{13,7},{10,8},{3,9},{8... | collective-permute-start | bytes 12296 | tf_op jit(solution)/shard_map/ppermute | solution.py:508
  73.2 3.6 %collective-permute-start.17 = (f32[8,128]{1,0:T(8,128)S(1)}, f32[8,128]{1,0:T(8,128)S(1)}, u32[]{:S(2)}, u32[]{:S(2)}) collective-permute-start(f32[8,128]{1,0:T(8,128)S(1)} %add.234), channel_id=1, source_target_pairs={{4,0},{13,1},{6,2},{15,3},{0,4},{9,5},{2,6},{11,7},{12,8},{5,9},{1... | collective-permute-start | bytes 12296 | tf_op jit(solution)/shard_map/ppermute | solution.py:508
  74.8 4.5 %collective-permute-start.18 = (f32[8,128]{1,0:T(8,128)S(1)}, f32[8,128]{1,0:T(8,128)S(1)}, u32[]{:S(2)}, u32[]{:S(2)}) collective-permute-start(f32[8,128]{1,0:T(8,128)S(1)} %add.234), channel_id=1, source_target_pairs={{6,0},{15,1},{4,2},{13,3},{2,4},{11,5},{0,6},{9,7},{14,8},{7,9},{1... | collective-permute-start | bytes 12296 | tf_op jit(solution)/shard_map/ppermute | solution.py:508
  79.3 6.4 %collective-permute-start.19 = (f32[8,128]{1,0:T(8,128)S(1)}, f32[8,128]{1,0:T(8,128)S(1)}, u32[]{:S(2)}, u32[]{:S(2)}) collective-permute-start(f32[8,128]{1,0:T(8,128)S(1)} %add_add_fusion.1.refs_0_), channel_id=1, source_target_pairs={{0,1},{1,0},{2,3},{3,2},{4,5},{5,4},{6,7},{7,6},{8,9},{9,8},{10,11... | collective-permute-start | bytes 12296 | tf_op jit(solution)/shard_map/ppermute | solution.py:21
  87.6 0.7 copy-start.3

commit v9 on v7

--- a/solution.py
+++ b/solution.py
@@ -1,3 +1,5 @@
+import functools
+
 import jax
 import jax.numpy as jnp
 from jax import lax
@@ -59,22 +61,39 @@
     return (east, west, south, se_w, sw_e, above, turned(se, 1, 0), turned(sw, 1, 0)), diag
 
 
+def lead_kernel(odd_ref, coup_hbm, bits_hbm, own_ref, lead_ref, sems):
+    last = bits_hbm.shape[1] - 1
+    copies = [
+        pltpu.make_async_copy(coup_hbm.at[5, last], own_ref, sems.at[0]),
+        pltpu.make_async_copy(
+            bits_hbm.at[pl.ds(0, lead_ref.shape[0]), odd_ref[0] * last], lead_ref, sems.at[1]
+        ),
+    ]
+    for copy in copies:
+        copy.start()
+    for copy in copies:
+        copy.wait()
+
+
 def edges_kernel(odd_ref, coup_hbm, bits_hbm, mask_hbm, own_ref, off_ref, on_ref,
                  coup_ref, mask_ref, bits_ref, sems):
     probes, days = bits_hbm.shape[:2]
     last = days - 1
     odd = odd_ref[0]
-    half = probes // 2
+    rest = off_ref.shape[0] - 1
     copies = [
         pltpu.make_async_copy(mask_hbm, mask_ref, sems.at[0]),
         pltpu.make_async_copy(coup_hbm, coup_ref, sems.at[1]),
     ]
-    for side, day in enumerate((odd * last, last - odd * last)):
+    for side, (day, size) in enumerate(((odd * last, rest), (last - odd * last, probes))):
+        half = size // 2
         for n in range(2):
-            part = pl.ds(n * half, half)
+            source = pl.ds(probes - size + n * half, half)
             copies.append(
                 pltpu.make_async_copy(
-                    bits_hbm.at[part, day], bits_ref.at[side, part], sems.at[2 + 2 * side + n]
+                    bits_hbm.at[source, day],
+                    bits_ref.at[side, pl.ds(n * half, half)],
+                    sems.at[2 + 2 * side + n],
                 )
             )
     for copy in copies:
@@ -84,7 +103,7 @@
     factors = link_factors(mask_ref[...])
     first = day_planes(coup_ref, factors, 0)[1]
     final = day_planes(coup_ref, factors, last)[1]
-    off_ref[probes] = chosen(odd, first, final)
+    off_ref[rest] = chosen(odd, first, final)
     on_ref[probes] = chosen(odd, final, first)
     for copy in copies[2:]:
         copy.wait()
@@ -94,7 +113,7 @@
             out_ref[k] = jnp.where(bits_ref[side, k] == 1, 1.0, -1.0)
             return carry
 
-        lax.fori_loop(0, probes, probe, 0, unroll=4)
+        lax.fori_loop(0, out_ref.shape[0] - 1, probe, 0, unroll=2)
 
 
 def planes_kernel(coup_hbm, bits_hbm, mask_hbm, before_ref, planes_ref, diag_ref, dinv_ref,
@@ -180,9 +199,10 @@
 
 
 def first_kernel(odd_ref, bits_ref, planes_ref, ahead_ref, dinv_ref,
-                 w1_ref, off_ref, on_ref, w0_ref):
+                 w1_ref, fore_ref, aft_ref, on_ref, w0_ref):
     per, days = bits_ref.shape[:2]
     odd = odd_ref[0]
+    in_fore = pl.program_id(0) < pl.num_programs(0) // 2
 
     def probe(k, carry):
         for d in range(days):
@@ -192,20 +212,30 @@
             w1_ref[k, d] = w1
             if d == 0:
                 w1_low = w1
-        off_ref[k] = chosen(odd, w1_low, w1)
+        off = chosen(odd, w1_low, w1)
+
+        @pl.when(in_fore)
+        def _():
+            fore_ref[k] = off
+
+        @pl.when(jnp.logical_not(in_fore))
+        def _():
+            aft_ref[k] = off
+
         on_ref[k] = chosen(odd, w1, w1_low)
         return carry
 
     lax.fori_loop(0, per, probe, 0)
 
 
-def second_kernel(odd_ref, bits_ref, w1_ref, off_ref, on_ref, doff_ref, don_ref, planes_ref,
+def second_kernel(leads, odd_ref, bits_ref, w1_ref, lead_ref, off_ref, on_ref, doff_ref, don_ref, planes_ref,
                   ahead_ref, before_ref, diag_ref, dinv_ref,
                   p1_ref, p2_ref, w1e_ref, w2e_ref, high_ref, sums_ref, ratio_ref, scale_ref,
                   w1c_ref):
     per, days = w1_ref.shape[:2]
     last = days - 1
     odd = odd_ref[0]
+    leading = (pl.program_id(0) < leads).astype(jnp.int32)
 
     @pl.when(pl.program_id(0) == 0)
     def _():
@@ -216,12 +246,14 @@
         scale_ref[1] = ratio_ref[1] * dinv_ref[last]
 
     def probe(k, carry):
+        lead_sign = (2 * lead_ref[k] - 1).astype(F32)
+        off_sign = chosen(leading, off_ref[k], lead_sign)
         for d in range(days):
             w1 = w1_ref[k, d]
             if d == 0:
-                w1 = w1 + chosen(odd, off_ref[k], on_ref[k]) * scale_ref[0]
+                w1 = w1 + chosen(odd, off_sign, on_ref[k]) * scale_ref[0]
             if d == last:
-                w1 = w1 + chosen(odd, on_ref[k], off_ref[k]) * scale_ref[1]
+                w1 = w1 + chosen(odd, on_ref[k], off_sign) * scale_ref[1]
             w1c_ref[d] = w1
         w1e_ref[k, 0] = w1c_ref[0]
         w1e_ref[k, 1] = w1c_ref[last]
@@ -258,12 +290,14 @@
     lax.fori_loop(0, per, probe, 0)
 
 
-def third_kernel(odd_ref, token_ref, bits_ref, p2m_ref, w1e_ref, w2e_ref, off_ref, on_ref, sums_in_ref,
+def third_kernel(odd_ref, token_ref, bits_ref, p2m_ref, w1e_ref, w2e_ref, fore_ref, aft_ref, on_ref,
+                 sums_in_ref,
                  planes_ref, ahead_ref, before_ref, ratio_ref, diag_ref, dinv_ref,
                  p1_ref, p2_ref, cross_ref, sums_ref, scale_ref):
     per, days = bits_ref.shape[:2]
     last = days - 1
     odd = odd_ref[0]
+    in_fore = (pl.program_id(0) < pl.num_programs(0) // 2).astype(jnp.int32)
 
     @pl.when(pl.program_id(0) == 0)
     def _():
@@ -276,7 +310,7 @@
         for side, (d, inner) in enumerate(((0, 1), (last, last - 1))):
             bits = bits_ref[k, d]
             w1 = w1e_ref[k, side]
-            off = off_ref[k]
+            off = chosen(in_fore, aft_ref[k], fore_ref[k])
             arrived = chosen(odd, off, on_ref[k]) if side == 0 else chosen(odd, on_ref[k], off)
             neighbour = arrived + ratio_ref[side] * signed(bits, dinv_ref[d])
             w2 = w2e_ref[k, side] + scale_ref[side] * neighbour
@@ -407,6 +441,7 @@
     weights = (PLANES,) + dplanes
     per = 2
     grid = (probes // per,)
+    leads = 2 // per
     size = probes * days * rows * cols
 
     def call(kernel, grid, ins, outs, scratch=(), cost=(1, 1), mib=16):
@@ -416,6 +451,24 @@
             if kind == "last":
                 index = shape[0] - 1
                 return pl.BlockSpec((1,) + tuple(shape[1:]), lambda i: (index,) + (0,) * (len(shape) - 1))
+            if kind == "fore":
+                return pl.BlockSpec(
+                    (per,) + tuple(shape[1:]),
+                    lambda i: (jnp.minimum(i, grid[0] // 2 - 1),) + (0,) * (len(shape) - 1),
+                )
+            if kind == "aft":
+                return pl.BlockSpec(
+                    (per,) + tuple(shape[1:]),
+                    lambda i: (jnp.maximum(i - grid[0] // 2, 0),) + (0,) * (len(shape) - 1),
+                )
+            if kind == "lead":
+                return pl.BlockSpec(
+                    (per,) + tuple(shape[1:]), lambda i: (jnp.minimum(i, leads - 1),) + (0,) * (len(shape) - 1)
+                )
+            if kind == "rest":
+                return pl.BlockSpec(
+                    (per,) + tuple(shape[1:]), lambda i: (jnp.maximum(i - leads, 0),) + (0,) * (len(shape) - 1)
+                )
             if kind == "smem":
                 return pl.BlockSpec(memory_space=pltpu.SMEM)
             return split(shape, per) if kind == "split" else whole(shape)
@@ -434,19 +487,26 @@
         )(*[value for value, _ in ins])
 
     odd = (lax.axis_index("day") % 2).astype(jnp.int32).reshape(1)
-    own = couplings[5, days - 1]
+    own, lead = call(
+        lead_kernel, (1,),
+        [(odd, "smem"), (hbm(couplings), "hbm"), (hbm(probe_bits), "hbm")],
+        [(plane, "whole", F32), ((leads * per,) + plane, "whole", jnp.int32)],
+        scratch=[pltpu.SemaphoreType.DMA((2,))], cost=(0, 0.1), mib=4,
+    )
     before = moved(own, "next")
+    lead = moved(lead, "off")
     sent = (probes + 1,) + plane
+    rest = (probes - leads * per + 1,) + plane
     off_signs, on_signs = call(
         edges_kernel, (1,),
         [(odd, "smem"), (hbm(couplings), "hbm"), (hbm(probe_bits), "hbm"), (hbm(land_mask), "hbm"),
          (own, "whole")],
-        [(sent, "whole", F32), (sent, "whole", F32)],
+        [(rest, "whole", F32), (sent, "whole", F32)],
         scratch=[pltpu.VMEM(couplings.shape, F32), pltpu.VMEM(plane, jnp.int32),
                  pltpu.VMEM((2,) + edge, jnp.int32), pltpu.SemaphoreType.DMA((6,))],
         cost=(0.1, 0.5), mib=16,
     )
-    off_signs, on_signs, before = lax.optimization_barrier((off_signs, on_signs, before))
+    off_signs, on_signs, before, lead = lax.optimization_barrier((off_signs, on_signs, before, lead))
     off_signs = moved(off_signs, "off")
     on_signs = moved(on_signs, "on")
     planes, diag, dinv, ahead, bits = call(
@@ -460,20 +520,22 @@
         cost=(0.5, 1), mib=32,
     )
 
-    w1, off, on = call(
+    half = (probes // 2,) + plane
+    w1, fore, aft, on = call(
         first_kernel, grid,
         [(odd, "smem"), (bits, "split"), (planes, "whole"), (ahead, "whole"), (dinv, "whole")],
-        [(field, "split", F32), (edge, "split", F32), (edge, "split", F32)],
+        [(field, "split", F32), (half, "fore", F32), (half, "aft", F32), (edge, "split", F32)],
         scratch=[pltpu.VMEM(dplanes, F32)], cost=(1, 2),
     )
-    off = moved(off, "off")
+    fore = moved(fore, "off")
+    aft = moved(aft, "off")
     on = moved(on, "on")
     token, off_signs, on_signs = lax.optimization_barrier((dinv[0, :8, :128], off_signs, on_signs))
     token = moved(token, "on")
 
     p1m, p2m, w1e, w2e, high2, sums, ratio = call(
-        second_kernel, grid,
-        [(odd, "smem"), (bits, "split"), (w1, "split"), (off_signs, "split"), (on_signs, "split"),
+        functools.partial(second_kernel, leads), grid,
+        [(odd, "smem"), (bits, "split"), (w1, "split"), (lead, "lead"), (off_signs, "rest"), (on_signs, "split"),
          (off_signs, "last"), (on_signs, "last"), (planes, "whole"), (ahead, "whole"),
          (before, "whole"), (diag, "whole"), (dinv, "whole")],
         [(middle, "split", F32), (middle, "split", F32), (pair, "split", F32),
@@ -481,13 +543,15 @@
          ((2,) + plane, "whole", F32)],
         scratch=[pltpu.VMEM((2,) + plane, F32), pltpu.VMEM(dplanes, F32)], cost=(1.5, 4), mib=20,
     )
-    high2, ratio, token, off = lax.optimization_barrier((high2, ratio, token, off))
+    high2, ratio, token, fore, aft = lax.optimization_barrier(
+        (high2, ratio, token, fore, aft)
+    )
     high2_prev = moved(high2, "next")
 
     p1e, p2e, cross, sums = call(
         third_kernel, grid,
         [(odd, "smem"), (token, "whole"), (bits, "split"), (p2m, "split"), (w1e, "split"),
-         (w2e, "split"), (off, "split"), (on, "split"), (sums, "split"), (planes, "whole"),
+         (w2e, "split"), (fore, "fore"), (aft, "aft"), (on, "split"), (sums, "split"), (planes, "whole"),
          (ahead, "whole"), (before, "whole"), (ratio, "whole"), (diag, "whole"), (dinv, "whole")],
         [(pair, "split", F32), (pair, "split", F32), (edge, "split", F32),
          (sums_shape, "split", F32)],

time: 84 us -> 87.4 us (1.040)
  starting transfers between devices: 32.1 us -> 38.7 us
  waiting for transfers between devices: 25.3 us -> 21.8 us
  Pallas kernels: 23.9 us -> 25 us
    ppermute x7 -> x9, starting transfers between devices: 25.7 us -> 32.4 us  [moved(): return lax.ppermute(value, 'day', [(i, target(i)) for i in range(count)])]
    ppermute x7 -> x9, waiting for transfers between devices: 21 us -> 18.4 us  [moved(): return lax.ppermute(value, 'day', [(i, target(i)) for i in range(count)])]
    pallas_call x7 -> x8, Pallas kernels: 23.9 us -> 25 us  [call(): pl.pallas_call(kernel, grid=grid, in_specs=[spec(value.shape, kind) for v...]
    ppermute x6, waiting for transfers between devices: 4.33 us -> 3.41 us  [body(): lax.ppermute(moments, 'day', [(i, i ^ n * step) for i in range(count)])]
  transfers between devices with their start and end apart: 13 -> 15, of which waited for: 7 -> 7; matrix products, arithmetic and copies ran while one was open for 0% -> 0% of each run, Pallas kernels for 27% -> 26%
where the time goes in v9:
time: 87.4 us; the launch traced here: 87.3 us
  starting transfers between devices  38.7 us (44%)
  Pallas kernels  25 us (29%)
  waiting for transfers between devices  21.8 us (25%)
    ppermute x9, starting transfers between devices, moved(): return lax.ppermute(value, 'day', [(i, target(i)) for i in range(count)])  32.4 us
    pallas_call x8, Pallas kernels, call(): pl.pallas_call(kernel, grid=grid, in_specs=[spec(value.shape, kind) for v...  25 us
    ppermute x9, waiting for transfers between devices, moved(): return lax.ppermute(value, 'day', [(i, target(i)) for i in range(count)])  18.4 us
    ppermute x6, starting transfers between devices, body(): lax.ppermute(moments, 'day', [(i, i ^ n * step) for i in range(count)])  6.31 us
    ppermute x6, waiting for transfers between devices, body(): lax.ppermute(moments, 'day', [(i, i ^ n * step) for i in range(count)])  3.41 us
  transfers between devices with their start and end apart: 15, of which 7 were waited for; matrix products, arithmetic and copies ran while one was open for 0% of the time, Pallas kernels for 26%

profile of v9, /device:TPU:0, one launch (start us, length us, event | category | flops | bytes accessed | tf_op | source)
XLA Modules:
  0.0 87.3 jit_solution(6928752655052466071)
XLA Ops:
  0.0 1.0 %shard_map.39 = (f32[32,512]{1,0:T(8,128)S(1)}, s32[2,32,512]{2,1,0:T(8,128)S(1)}) custom-call(s32[1]{0:T(128)} %bitcast.12.odd_ref, f32[6,4,32,512]{3,2,1,0:T(8,128)} %coup_hbm.5, s32[16,4,32,512]{3,2,1,0:T(8,128)} %bits_hbm.5), custom_call_target="tpu_custom_call" | custom-call | bytes 419430 | tf_op jit(solution)/shard_map/pallas_call | solution.py:476
  1.0 5.5 %collective-permute-start.8 = (s32[2,32,512]{2,1,0:T(8,128)S(1)}, s32[2,32,512]{2,1,0:T(8,128)S(1)}, u32[]{:S(2)}, u32[]{:S(2)}) collective-permute-start(s32[2,32,512]{2,1,0:T(8,128)S(1)} %get-tuple-element.62), channel_id=1, source_target_pairs={{0,15},{1,2},{2,1},{3,4},{4,3},{5,6},{6,5},{7,8},{8,7},{9,10},{10,... | collective-permute-start | bytes 393224 | tf_op jit(solution)/shard_map/ppermute | solution.py:23
  6.5 0.0 collective-permute-start.7
  6.5 2.3 %shard_map.40 = (f32[15,32,512]{2,1,0:T(8,128)S(1)}, f32[17,32,512]{2,1,0:T(8,128)S(1)}) custom-call(s32[1]{0:T(128)} %bitcast.12.odd_ref, f32[6,4,32,512]{3,2,1,0:T(8,128)} %coup_hbm.5, s32[16,4,32,512]{3,2,1,0:T(8,128)} %bits_hbm.5, s32[32,512]{1,0:T(8,128)} %mask_hbm.3, f32[32,512]{1,0:T(8,128)S(1)} %get-tuple-element.59.own_ref), custom_call_target="tpu_custom_call" | custom-call | flops 2516582 | bytes 2097152 | tf_op jit(solution)/shard_map/pallas_call | solution.py:476
  8.7 4.1 %collective-permute-done.7.before_ref = f32[32,512]{1,0:T(8,128)S(1)} collective-permute-done((f32[32,512]{1,0:T(8,128)S(1)}, f32[32,512]{1,0:T(8,128)S(1)}, u32[]{:S(2)}, u32[]{:S(2)}) %collective-permute-start.7) | collective-permute-done | bytes 65568 | tf_op jit(solution)/shard_map/ppermute | solution.py:23
  12.9 0.0 collective-permute-done.8.lead_ref
  12.9 0.0 collective-permute-start.10
  12.9 0.7 collective-permute-start.9
  13.6 2.7 %shard_map.41 = (f32[8,4,32,512]{3,2,1,0:T(8,128)S(1)}, f32[4,32,512]{2,1,0:T(8,128)S(1)}, f32[4,32,512]{2,1,0:T(8,128)S(1)}, f32[4,32,512]{2,1,0:T(8,128)S(1)}, s32[16,4,32,512]{3,2,1,0:T(8,128)S(1)}) custom-call(f32[6,4,32,512]{3,2,1,0:T(8,128)} %coup_hbm.5, s32[16,4,32,512]{3,2,1,0:T(8,128)} %bits_hbm.5, s32[32,512]{1,0:T(8,128)} %mask_hbm.3, ...), custom_call_target="tpu_custom_call" | custom-call | flops 12582912 | bytes 4194304 | tf_op jit(solution)/shard_map/pallas_call | solution.py:476
  16.3 5.3 %shard_map.42 = (f32[16,4,32,512]{3,2,1,0:T(8,128)S(1)}, f32[8,32,512]{2,1,0:T(8,128)S(1)}, f32[8,32,512]{2,1,0:T(8,128)S(1)}, f32[16,32,512]{2,1,0:T(8,128)S(1)}) custom-call(s32[1]{0:T(128)} %bitcast.12.odd_ref, s32[16,4,32,512]{3,2,1,0:T(8,128)S(1)} %get-tuple-element.64.bits_ref, f32[8,4,32,512]{3,2,1,0:T(8,128)S(1)} %get-tuple-element.65.planes_ref, ...), custom_call_target="tpu_custom_call" | custom-call | flops 25165824 | bytes 8388608 | tf_op jit(solution)/shard_map/pallas_call | solution.py:476
  21.6 3.8 %collective-permute-start.12 = (f32[8,32,512]{2,1,0:T(8,128)S(1)}, f32[8,32,512]{2,1,0:T(8,128)S(1)}, u32[]{:S(2)}, u32[]{:S(2)}) collective-permute-start(f32[8,32,512]{2,1,0:T(8,128)S(1)} %get-tuple-element.80), channel_id=1, source_target_pairs={{0,15},{1,2},{2,1},{3,4},{4,3},{5,6},{6,5},{7,8},{8,7},{9,10},{10,... | collective-permute-start | bytes 1572872 | tf_op jit(solution)/shard_map/ppermute | solution.py:23
  25.4 0.7 collective-permute-start.13
  26.1 3.1 %collective-permute-done.9.off_ref.doff_ref = f32[15,32,512]{2,1,0:T(8,128)S(1)} collective-permute-done((f32[15,32,512]{2,1,0:T(8,128)S(1)}, f32[15,32,512]{2,1,0:T(8,128)S(1)}, u32[]{:S(2)}, u32[]{:S(2)}) %collective-permute-start.9) | collective-permute-done | bytes 983072 | tf_op jit(solution)/shard_map/ppermute | solution.py:23
  29.2 0.0 collective-permute-done.10.on_ref.don_ref
  29.2 19.5 %collective-permute-start.11 = (f32[8,128]{1,0:T(8,128)S(1)}, f32[8,128]{1,0:T(8,128)S(1)}, u32[]{:S(2)}, u32[]{:S(2)}) collective-permute-start(f32[8,128]{1,0:T(8,128)S(1)} %slice_bitcast_fusion.4), channel_id=1, source_target_pairs={{0,1},{1,0},{2,3},{3,2},{4,5},{5,4},{6,7},{7,6},{8,9},{9,8},{10,11... | collective-permute-start | bytes 12296 | tf_op jit(solution)/shard_map/ppermute | solution.py:23
  48.7 0.0 collective-permute-start.14
  48.7 9.0 %shard_map.43 = (f32[16,2,32,512]{3,2,1,0:T(8,128)S(1)}, f32[16,2,32,512]{3,2,1,0:T(8,128)S(1)}, f32[16,2,32,512]{3,2,1,0:T(8,128)S(1)}, f32[16,2,32,512]{3,2,1,...) custom-call(s32[1]{0:T(128)} %bitcast.12.odd_ref, ...), custom_call_target="tpu_custom_call" | custom-call | flops 37748736 | bytes 16777216 | tf_op jit(solution)/shard_map/pallas_call | solution.py:476
  57.6 0.0 collective-permute-done.12.fore_ref
  57.7 0.0 collective-permute-done.13.aft_ref
  57.7 0.0 collective-permute-done.11.token_ref
  57.7 2.2 %collective-permute-start.15 = (f32[16,32,512]{2,1,0:T(8,128)S(1)}, f32[16,32,512]{2,1,0:T(8,128)S(1)}, u32[]{:S(2)}, u32[]{:S(2)}) collective-permute-start(f32[16,32,512]{2,1,0:T(8,128)S(1)} %get-tuple-element.93), channel_id=1, source_target_pairs={{0,1},{1,2},{2,3},{3,4},{4,5},{5,6},{6,7},{7,8},{8,9},{9,10},{10,1... | collective-permute-start | bytes 3145736 | tf_op jit(solution)/shard_map/ppermute | solution.py:23
  59.9 0.0 collective-permute-done.14.on_ref
  59.9 3.6 %shard_map.44 = (f32[16,2,32,512]{3,2,1,0:T(8,128)S(1)}, f32[16,2,32,512]{3,2,1,0:T(8,128)S(1)}, f32[16,32,512]{2,1,0:T(8,128)S(1)}, f32[16,8,128]{2,1,0:T(8,128)S(1)}) custom-call(s32[1]{0:T(128)} %bitcast.12.odd_ref, f32[8,128]{1,0:T(8,128)S(1)} %collective-permute-done.11.token_ref, s32[16,4,32,512]{3,2,1,0:T(8,128)S(1)} %get-tuple-element.64.bits_ref, ...), custom_call_target="tpu_custom_call" | custom-call | flops 17616076 | bytes 16777216 | tf_op jit(solution)/shard_map/pallas_call | solution.py:476
  63.5 11.1 %collective-permute-done.15.high_ref = f32[16,32,512]{2,1,0:T(8,128)S(1)} collective-permute-done((f32[16,32,512]{2,1,0:T(8,128)S(1)}, f32[16,32,512]{2,1,0:T(8,128)S(1)}, u32[]{:S(2)}, u32[]{:S(2)}) %collective-permute-start.15) | collective-permute-done | bytes 1048608 | tf_op jit(solution)/shard_map/ppermute | solution.py:23
  74.7 0.2 shard_map.45
  74.8 0.0 collective-permute-start.18
  74.9 0.1 collective-permute-start.17
  75.0 1.8 %collective-permute-start.16 = (f32[8,128]{1,0:T(8,128)S(1)}, f32[8,128]{1,0:T(8,128)S(1)}, u32[]{:S(2)}, u32[]{:S(2)}) collective-permute-start(f32[8,128]{1,0:T(8,128)S(1)} %shard_map.45), channel_id=1, source_target_pairs={{0,1},{1,0},{2,3},{3,2},{4,5},{5,4},{6,7},{7,6},{8,9},{9,8},{10,11... | collective-permute-start | bytes 12296 | tf_op jit(solution)/shard_map/ppermute | solution.py:571
  76.7 1.2 %collective-permute-done.18 = f32[8,128]{1,0:T(8,128)S(1)} collective-permute-done((f32[8,128]{1,0:T(8,128)S(1)}, f32[8,128]{1,0:T(8,128)S(1)}, u32[]{:S(2)}, u32[]{:S(2)}) %collective-permute-start.18) | collective-permute-done | bytes 4128 | tf_op jit(solution)/shard_map/ppermute | solution.py:571
  77.9 0.7 collective-permute-done.17
  78.6 0.0 collective-permute-done.16
  78.6 0.1 collective-permute-start.21
  78.6 0.1 collective-permute-start.20
  78.7 4.3 %collective-permute-start.19 = (f32[8,128]{1,0:T(8,128)S(1)}, f32[8,128]{1,0:T(8,128)S(1)}, u32[]{:S(2)}, u32[]{:S(2)}) collective-permute-start(f32[8,128]{1,0:T(8,128)S(1)} %add_add_fusion.1.refs_0_), channel_id=1, source_target_pairs={{0,4},{1,5},{2,6},{3,7},{4,0},{5,1},{6,2},{7,3},{8,12},{9,13},{10,... | collective-permute-start | bytes 12296 | tf_op jit(solution)/shard_map/ppermute | solution.py:571
  83.0 1.0 %collective-permute-done.21.refs_3_ = f32[8,128]{1,0:T(8,128)S(1)} collective-permute-done((f32[8,128]{1,0:T(8,128)S(1)}, f32[8,128]{1,0:T(8,128)S(1)}, u32[]{:S(2)}, u32[]{:S(2)}) %collective-permute-start.21) | collective-permute-done | bytes 4128 | tf_op jit(solution)/shard_map/ppermute | solution.py:571
  84.0 0.0 collective-permute-done.20.refs_2_
  84.0 0.6 collective-permute-done.19.refs_1_
  84.6 1.1 %shard_map.46 = (f32[4,32,512]{2,1,0:T(8,128)S(1)}, s32[1]{0:T(128)}) custom-call(f32[16,2,32,512]{3,2,1,0:T(8,128)S(1)} %get-tuple-element.75.p1m_ref, f32[16,2,32,512]{3,2,1,0:T(8,128)S(1)} %get-tuple-element.76.p2m_ref, f32[16,2,32,512]{3,2,1,0:T(8,128)S(1)} %get-tuple-element.90.p1e_ref, f32[16,2,32,512]{3,2,1,0:T(8,128)S(1)} %get-tuple-element.91.p2e_ref, ...), custom_call_target="tpu_custom_call" | custom-call | flops 5033164 | bytes 8388608 | tf_op jit(solution)/shard_map/pallas_call | solution.py:476
  86.3 0.2 conditional.1
  86.6 0.0 copy-start.3
  86.6 0.7 copy-done.3
  (2 shorter events, 0.0 us)
Async XLA Ops:
  1.0 11.9 %collective-permute-start.8 = (s32[2,32,512]{2,1,0:T(8,128)S(1)}, s32[2,32,512]{2,1,0:T(8,128)S(1)}, u32[]{:S(2)}, u32[]{:S(2)}) collective-permute-start(s32[2,32,512]{2,1,0:T(8,128)S(1)} %get-tuple-element.62), channel_id=1, source_target_pairs={{0,15},{1,2},{2,1},{3,4},{4,3},{5,6},{6,5},{7,8},{8,7},{9,10},{10,... | collective-permute-start | bytes 393224 | tf_op jit(solution)/shard_map/ppermute | solution.py:23
  6.5 6.4 %collective-permute-start.7 = (f32[32,512]{1,0:T(8,128)S(1)}, f32[32,512]{1,0:T(8,128)S(1)}, u32[]{:S(2)}, u32[]{:S(2)}) collective-permute-start(f32[32,512]{1,0:T(8,128)S(1)} %get-tuple-element.59.own_ref), channel_id=1, source_target_pairs={{0,1},{1,2},{2,3},{3,4},{4,5},{5,6},{6,7},{7,8},{8,9},{9,10},{10,1... | collective-permute-start | bytes 196616 | tf_op jit(solution)/shard_map/ppermute | solution.py:23
  12.9 16.3 %collective-permute-start.10 = (f32[17,32,512]{2,1,0:T(8,128)S(1)}, f32[17,32,512]{2,1,0:T(8,128)S(1)}, u32[]{:S(2)}, u32[]{:S(2)}) collective-permute-start(f32[17,32,512]{2,1,0:T(8,128)S(1)} %get-tuple-element.71), channel_id=1, source_target_pairs={{0,1},{1,0},{2,3},{3,2},{4,5},{5,4},{6,7},{7,6},{8,9},{9,8},{10,11... | collective-permute-start | bytes 3342344 | tf_op jit(solution)/shard_map/ppermute | solution.py:23
  12.9 16.3 %collective-permute-start.9 = (f32[15,32,512]{2,1,0:T(8,128)S(1)}, f32[15,32,512]{2,1,0:T(8,128)S(1)}, u32[]{:S(2)}, u32[]{:S(2)}) collective-permute-start(f32[15,32,512]{2,1,0:T(8,128)S(1)} %get-tuple-element.70), channel_id=1, source_target_pairs={{0,15},{1,2},{2,1},{3,4},{4,3},{5,6},{6,5},{7,8},{8,7},{9,10},{10,... | collective-permute-start | bytes 2949128 | tf_op jit(solution)/shard_map/ppermute | solution.py:23
  21.6 36.1 %collective-permute-start.12 = (f32[8,32,512]{2,1,0:T(8,128)S(1)}, f32[8,32,512]{2,1,0:T(8,128)S(1)}, u32[]{:S(2)}, u32[]{:S(2)}) collective-permute-start(f32[8,32,512]{2,1,0:T(8,128)S(1)} %get-tuple-element.80), channel_id=1, source_target_pairs={{0,15},{1,2},{2,1},{3,4},{4,3},{5,6},{6,5},{7,8},{8,7},{9,10},{10,... | collective-permute-start | bytes 1572872 | tf_op jit(solution)/shard_map/ppermute | solution.py:23
  25.4 32.3 %collective-permute-start.13 = (f32[8,32,512]{2,1,0:T(8,128)S(1)}, f32[8,32,512]{2,1,0:T(8,128)S(1)}, u32[]{:S(2)}, u32[]{:S(2)}) collective-permute-start(f32[8,32,512]{2,1,0:T(8,128)S(1)} %get-tuple-element.81), channel_id=1, source_target_pairs={{0,15},{1,2},{2,1},{3,4},{4,3},{5,6},{6,5},{7,8},{8,7},{9,10},{10,... | collective-permute-start | bytes 1572872 | tf_op jit(solution)/shard_map/ppermute | solution.py:23
  29.2 28.5 %collective-permute-start.11 = (f32[8,128]{1,0:T(8,128)S(1)}, f32[8,128]{1,0:T(8,128)S(1)}, u32[]{:S(2)}, u32[]{:S(2)}) collective-permute-start(f32[8,128]{1,0:T(8,128)S(1)} %slice_bitcast_fusion.4), channel_id=1, source_target_pairs={{0,1},{1,0},{2,3},{3,2},{4,5},{5,4},{6,7},{7,6},{8,9},{9,8},{10,11... | collective-permute-start | bytes 12296 | tf_op jit(solution)/shard_map/ppermute | solution.py:23
  48.7 11.2 %collective-permute-start.14 = (f32[16,32,512]{2,1,0:T(8,128)S(1)}, f32[16,32,512]{2,1,0:T(8,128)S(1)}, u32[]{:S(2)}, u32[]{:S(2)}) collective-permute-start(f32[16,32,512]{2,1,0:T(8,128)S(1)} %get-tuple-element.87), channel_id=1, source_target_pairs={{0,1},{1,0},{2,3},{3,2},{4,5},{5,4},{6,7},{7,6},{8,9},{9,8},{10,11... | collective-permute-start | bytes 3145736 | tf_op jit(solution)/shard_map/ppermute | solution.py:23
  57.7 17.0 %collective-permute-start.15 = (f32[16,32,512]{2,1,0:T(8,128)S(1)}, f32[16,32,512]{2,1,0:T(8,128)S(1)}, u32[]{:S(2)}, u32[]{:S(2)}) collective-permute-start(f32[16,32,512]{2,1,0:T(8,128)S(1)} %get-tuple-element.93), channel_id=1, source_target_pairs={{0,1},{1,2},{2,3},{3,4},{4,5},{5,6},{6,7},{7,8},{8,9},{9,10},{10,1... | collective-permute-start | bytes 3145736 | tf_op jit(solution)/shard_map/ppermute | solution.py:23
  74.8 3.1 %collective-permute-start.18 = (f32[8,128]{1,0:T(8,128)S(1)}, f32[8,128]{1,0:T(8,128)S(1)}, u32[]{:S(2)}, u32[]{:S(2)}) collective-permute-start(f32[8,128]{1,0:T(8,128)S(1)} %shard_map.45), channel_id=1, source_target_pairs={{0,3},{1,2},{2,1},{3,0},{4,7},{5,6},{6,5},{7,4},{8,11},{9,10},{10,... | collective-permute-start | bytes 12296 | tf_op jit(solution)/shard_map/ppermute | solution.py:571
  74.9 3.7 %collective-permute-start.17 = (f32[8,128]{1,0:T(8,128)S(1)}, f32[8,128]{1,0:T(8,128)S(1)}, u32[]{:S(2)}, u32[]{:S(2)}) collective-permute-start(f32[8,128]{1,0:T(8,128)S(1)} %shard_map.45), channel_id=1, source_target_pairs={{0,2},{1,3},{2,0},{3,1},{4,6},{5,7},{6,4},{7,5},{8,10},{9,11},{10,... | collective-permute-start | bytes 12296 | tf_op jit(solution)/shard_map/ppermute | solution.py:571
  75.0 3.6 %collective-permute-start.16 = (f32[8,128]{1,0:T(8,128)S(1)}, f32[8,128]{1,0:T(8,128)S(1)}, u32[]{:S(2)}, u32[]{:S(2)}) collective-permute-start(f32[8,128]{1,0:T(8,128)S(1)} %shard_map.45), channel_id=1, source_target_pairs={{0,1},{1,0},{2,3},{3,2},{4,5},{5,4},{6,7},{7,6},{8,9},{9,8},{10,11... | collective-permute-start | bytes 12296 | tf_op jit(solution)/shard_map/ppermute | solution.py:571
  78.6 5.5 %collective-permute-start.21 = (f32[8,128]{1,0:T(8,128)S(1)}, f32[8,128]{1,0:T(8,128)S(1)}, u32[]{:S(2)}, u32[]{:S(2)}) collective-permute-start(f32[8,128]{1,0:T(8,128)S(1)} %add_add_fusion.1.refs_0_), channel_id=1, source_target_pairs={{0,12},{1,13},{2,14},{3,15},{4,8},{5,9},{6,10},{7,11},{8,4},{9,5},... | collective-permute-start | bytes 12296 | tf_op jit(solution)/shard_map/ppermute | solution.py:571
  78.6 5.4 %collective-permute-start.20 = (f32[8,128]{1,0:T(8,128)S(1)}, f32[8,128]{1,0:T(8,128)S(1)}, u32[]{:S(2)}, u32[]{:S(2)}) collective-permute-start(f32[8,128]{1,0:T(8,128)S(1)} %add_add_fusion.1.refs_0_), channel_id=1, source_target_pairs={{0,8},{1,9},{2,10},{3,11},{4,12},{5,13},{6,14},{7,15},{8,0},{9,1},... | collective-permute-start | bytes 12296 | tf_op jit(solution)/shard_map/ppermute | solution.py:571
  78.7 5.9 %collective-permute-start.19 = (f32[8,128]{1,0:T(8,128)S(1)}, f32[8,128]{1,0:T(8,128)S(1)}, u32[]{:S(2)}, u32[]{:S(2)}) collective-permute-start(f32[8,128]{1,0:T(8,128)S(1)} %add_add_fusion.1.refs_0_), channel_id=1, source_target_pairs={{0,4},{1,5},{2,6},{3,7},{4,0},{5,1},{6,2},{7,3},{8,12},{9,13},{10,... | collective-permute-start | bytes 12296 | tf_op jit(solution)/shard_map/ppermute | solution.py:571
  86.6 0.7 copy-start.3

commit v10 on v7

--- a/solution.py
+++ b/solution.py
@@ -180,9 +180,10 @@
 
 
 def first_kernel(odd_ref, bits_ref, planes_ref, ahead_ref, dinv_ref,
-                 w1_ref, off_ref, on_ref, w0_ref):
+                 w1_ref, off_ref, on_ref, mark_ref, w0_ref):
     per, days = bits_ref.shape[:2]
     odd = odd_ref[0]
+    mark_ref[...] = jnp.zeros_like(mark_ref)
 
     def probe(k, carry):
         for d in range(days):
@@ -460,15 +461,15 @@
         cost=(0.5, 1), mib=32,
     )
 
-    w1, off, on = call(
+    w1, off, on, mark = call(
         first_kernel, grid,
         [(odd, "smem"), (bits, "split"), (planes, "whole"), (ahead, "whole"), (dinv, "whole")],
-        [(field, "split", F32), (edge, "split", F32), (edge, "split", F32)],
+        [(field, "split", F32), (edge, "split", F32), (edge, "split", F32), (tile, "whole", F32)],
         scratch=[pltpu.VMEM(dplanes, F32)], cost=(1, 2),
     )
     off = moved(off, "off")
     on = moved(on, "on")
-    token, off_signs, on_signs = lax.optimization_barrier((dinv[0, :8, :128], off_signs, on_signs))
+    token, off_signs, on_signs = lax.optimization_barrier((mark, off_signs, on_signs))
     token = moved(token, "on")
 
     p1m, p2m, w1e, w2e, high2, sums, ratio = call(
@@ -479,9 +480,9 @@
         [(middle, "split", F32), (middle, "split", F32), (pair, "split", F32),
          (pair, "split", F32), (edge, "split", F32), (sums_shape, "split", F32),
          ((2,) + plane, "whole", F32)],
-        scratch=[pltpu.VMEM((2,) + plane, F32), pltpu.VMEM(dplanes, F32)], cost=(1.5, 4), mib=20,
-    )
-    high2, ratio, token, off = lax.optimization_barrier((high2, ratio, token, off))
+        scratch=[pltpu.VMEM((2,) + plane, F32), pltpu.VMEM(dplanes, F32)], cost=(10, 60), mib=20,
+    )
+    high2, ratio, token = lax.optimization_barrier((high2, ratio, token))
     high2_prev = moved(high2, "next")
 
     p1e, p2e, cross, sums = call(
@@ -491,7 +492,7 @@
          (ahead, "whole"), (before, "whole"), (ratio, "whole"), (diag, "whole"), (dinv, "whole")],
         [(pair, "split", F32), (pair, "split", F32), (edge, "split", F32),
          (sums_shape, "split", F32)],
-        scratch=[pltpu.VMEM((2,) + plane, F32)], cost=(0.7, 4), mib=20,
+        scratch=[pltpu.VMEM((2,) + plane, F32)], cost=(10, 60), mib=20,
     )
     (moments,) = call(
         fourth_kernel, (1,),

time: 84 us -> 83.4 us (level)
  starting transfers between devices: 32.1 us -> 29.8 us
  waiting for transfers between devices: 25.3 us -> 27 us
    ppermute x7, starting transfers between devices: 25.7 us -> 23.5 us  [moved(): return lax.ppermute(value, 'day', [(i, target(i)) for i in range(count)])]
    ppermute x7, waiting for transfers between devices: 21 us -> 23.2 us  [moved(): return lax.ppermute(value, 'day', [(i, target(i)) for i in range(count)])]
where the time goes in v10:
time: 83.4 us; the launch traced here: 83.2 us
  starting transfers between devices  29.8 us (36%)
  waiting for transfers between devices  27 us (32%)
  Pallas kernels  23.9 us (29%)
  local copies, waits for them, and re-layouts  1.54 us (2%)
    pallas_call x7, Pallas kernels, call(): pl.pallas_call(kernel, grid=grid, in_specs=[spec(value.shape, kind) for v...  23.9 us
    ppermute x7, starting transfers between devices, moved(): return lax.ppermute(value, 'day', [(i, target(i)) for i in range(count)])  23.5 us
    ppermute x7, waiting for transfers between devices, moved(): return lax.ppermute(value, 'day', [(i, target(i)) for i in range(count)])  23.2 us
    ppermute x6, starting transfers between devices, body(): lax.ppermute(moments, 'day', [(i, i ^ n * step) for i in range(count)])  6.33 us
    ppermute x6, waiting for transfers between devices, body(): lax.ppermute(moments, 'day', [(i, i ^ n * step) for i in range(count)])  3.75 us
  transfers between devices with their start and end apart: 13, of which 7 were waited for; matrix products, arithmetic and copies ran while one was open for 0% of the time, Pallas kernels for 27%

profile of v10, /device:TPU:0, one launch (start us, length us, event | category | flops | bytes accessed | tf_op | source)
XLA Modules:
  0.0 83.2 jit_solution(2769599582100590860)
XLA Ops:
  0.0 0.8 %slice_bitcast_fusion.4.own_ref = f32[32,512]{1,0:T(8,128)S(1)} fusion(f32[6,4,32,512]{3,2,1,0:T(8,128)} %coup_hbm.3), kind=kLoop, calls=%fused_computation.169 | loop fusion | bytes 131072 | tf_op jit(solution)/shard_map/squeeze | solution.py:438
  0.8 0.5 collective-permute-start.7
  1.3 2.3 %shard_map.39 = (f32[17,32,512]{2,1,0:T(8,128)S(1)}, f32[17,32,512]{2,1,0:T(8,128)S(1)}) custom-call(s32[1]{0:T(128)} %bitcast.12.odd_ref, f32[6,4,32,512]{3,2,1,0:T(8,128)} %coup_hbm.3, s32[16,4,32,512]{3,2,1,0:T(8,128)} %bits_hbm.3, s32[32,512]{1,0:T(8,128)} %mask_hbm.3, f32[32,512]{1,0:T(8,128)S(1)} %slice_bitcast_fusion.4.own_ref), custom_call_target="tpu_custom_call" | custom-call | flops 2516582 | bytes 2097152 | tf_op jit(solution)/shard_map/pallas_call | solution.py:424
  3.6 4.6 %collective-permute-done.7.before_ref = f32[32,512]{1,0:T(8,128)S(1)} collective-permute-done((f32[32,512]{1,0:T(8,128)S(1)}, f32[32,512]{1,0:T(8,128)S(1)}, u32[]{:S(2)}, u32[]{:S(2)}) %collective-permute-start.7) | collective-permute-done | bytes 65568 | tf_op jit(solution)/shard_map/ppermute | solution.py:21
  8.2 0.4 collective-permute-start.8
  8.7 0.0 collective-permute-start.9
  8.7 2.7 %shard_map.40 = (f32[8,4,32,512]{3,2,1,0:T(8,128)S(1)}, f32[4,32,512]{2,1,0:T(8,128)S(1)}, f32[4,32,512]{2,1,0:T(8,128)S(1)}, f32[4,32,512]{2,1,0:T(8,128)S(1)}, s32[16,4,32,512]{3,2,1,0:T(8,128)S(1)}) custom-call(f32[6,4,32,512]{3,2,1,0:T(8,128)} %coup_hbm.3, s32[16,4,32,512]{3,2,1,0:T(8,128)} %bits_hbm.3, s32[32,512]{1,0:T(8,128)} %mask_hbm.3, ...), custom_call_target="tpu_custom_call" | custom-call | flops 12582912 | bytes 4194304 | tf_op jit(solution)/shard_map/pallas_call | solution.py:424
  11.4 5.1 %shard_map.41 = (f32[16,4,32,512]{3,2,1,0:T(8,128)S(1)}, f32[16,32,512]{2,1,0:T(8,128)S(1)}, f32[16,32,512]{2,1,0:T(8,128)S(1)}, f32[8,128]{1,0:T(8,128)S(1)}) custom-call(s32[1]{0:T(128)} %bitcast.12.odd_ref, s32[16,4,32,512]{3,2,1,0:T(8,128)S(1)} %get-tuple-element.57.bits_ref, f32[8,4,32,512]{3,2,1,0:T(8,128)S(1)} %get-tuple-element.58.planes_ref, ...), custom_call_target="tpu_custom_call" | custom-call | flops 25165824 | bytes 8388608 | tf_op jit(solution)/shard_map/pallas_call | solution.py:424
  16.5 4.1 %collective-permute-start.11 = (f32[16,32,512]{2,1,0:T(8,128)S(1)}, f32[16,32,512]{2,1,0:T(8,128)S(1)}, u32[]{:S(2)}, u32[]{:S(2)}) collective-permute-start(f32[16,32,512]{2,1,0:T(8,128)S(1)} %get-tuple-element.76), channel_id=1, source_target_pairs={{0,15},{1,2},{2,1},{3,4},{4,3},{5,6},{6,5},{7,8},{8,7},{9,10},{10,... | collective-permute-start | bytes 3145736 | tf_op jit(solution)/shard_map/ppermute | solution.py:21
  20.6 0.0 collective-permute-start.12
  20.6 5.4 %collective-permute-done.8.off_ref.doff_ref = f32[17,32,512]{2,1,0:T(8,128)S(1)} collective-permute-done((f32[17,32,512]{2,1,0:T(8,128)S(1)}, f32[17,32,512]{2,1,0:T(8,128)S(1)}, u32[]{:S(2)}, u32[]{:S(2)}) %collective-permute-start.8) | collective-permute-done | bytes 1114144 | tf_op jit(solution)/shard_map/ppermute | solution.py:21
  26.0 0.0 collective-permute-done.9.on_ref.don_ref
  26.0 18.4 %collective-permute-start.10 = (f32[8,128]{1,0:T(8,128)S(1)}, f32[8,128]{1,0:T(8,128)S(1)}, u32[]{:S(2)}, u32[]{:S(2)}) collective-permute-start(f32[8,128]{1,0:T(8,128)S(1)} %get-tuple-element.72), channel_id=1, source_target_pairs={{0,1},{1,0},{2,3},{3,2},{4,5},{5,4},{6,7},{7,6},{8,9},{9,8},{10,11... | collective-permute-start | bytes 12296 | tf_op jit(solution)/shard_map/ppermute | solution.py:21
  44.4 8.9 %shard_map.42 = (f32[16,2,32,512]{3,2,1,0:T(8,128)S(1)}, f32[16,2,32,512]{3,2,1,0:T(8,128)S(1)}, f32[16,2,32,512]{3,2,1,0:T(8,128)S(1)}, f32[16,2,32,512]{3,2,1,...) custom-call(s32[1]{0:T(128)} %bitcast.12.odd_ref, ...), custom_call_target="tpu_custom_call" | custom-call | flops 251658240 | bytes 251658240 | tf_op jit(solution)/shard_map/pallas_call | solution.py:424
  53.3 0.0 collective-permute-done.10.token_ref
  53.3 0.1 collective-permute-start.13
  53.3 0.0 collective-permute-done.11.off_ref
  53.4 0.0 collective-permute-done.12.on_ref
  53.4 3.7 %shard_map.43 = (f32[16,2,32,512]{3,2,1,0:T(8,128)S(1)}, f32[16,2,32,512]{3,2,1,0:T(8,128)S(1)}, f32[16,32,512]{2,1,0:T(8,128)S(1)}, f32[16,8,128]{2,1,0:T(8,128)S(1)}) custom-call(s32[1]{0:T(128)} %bitcast.12.odd_ref, f32[8,128]{1,0:T(8,128)S(1)} %collective-permute-done.10.token_ref, s32[16,4,32,512]{3,2,1,0:T(8,128)S(1)} %get-tuple-element.57.bits_ref, ...), custom_call_target="tpu_custom_call" | custom-call | flops 251658240 | bytes 251658240 | tf_op jit(solution)/shard_map/pallas_call | solution.py:424
  57.0 13.2 %collective-permute-done.13.high_ref = f32[16,32,512]{2,1,0:T(8,128)S(1)} collective-permute-done((f32[16,32,512]{2,1,0:T(8,128)S(1)}, f32[16,32,512]{2,1,0:T(8,128)S(1)}, u32[]{:S(2)}, u32[]{:S(2)}) %collective-permute-start.13) | collective-permute-done | bytes 1048608 | tf_op jit(solution)/shard_map/ppermute | solution.py:21
  70.3 0.2 shard_map.44
  70.4 0.0 collective-permute-start.16
  70.5 0.1 collective-permute-start.15
  70.6 1.8 %collective-permute-start.14 = (f32[8,128]{1,0:T(8,128)S(1)}, f32[8,128]{1,0:T(8,128)S(1)}, u32[]{:S(2)}, u32[]{:S(2)}) collective-permute-start(f32[8,128]{1,0:T(8,128)S(1)} %shard_map.44), channel_id=1, source_target_pairs={{0,1},{1,0},{2,3},{3,2},{4,5},{5,4},{6,7},{7,6},{8,9},{9,8},{10,11... | collective-permute-start | bytes 12296 | tf_op jit(solution)/shard_map/ppermute | solution.py:508
  72.3 1.2 %collective-permute-done.16 = f32[8,128]{1,0:T(8,128)S(1)} collective-permute-done((f32[8,128]{1,0:T(8,128)S(1)}, f32[8,128]{1,0:T(8,128)S(1)}, u32[]{:S(2)}, u32[]{:S(2)}) %collective-permute-start.16) | collective-permute-done | bytes 4128 | tf_op jit(solution)/shard_map/ppermute | solution.py:508
  73.5 0.7 collective-permute-done.15
  74.2 0.0 collective-permute-done.14
  74.2 1.9 %collective-permute-start.19 = (f32[8,128]{1,0:T(8,128)S(1)}, f32[8,128]{1,0:T(8,128)S(1)}, u32[]{:S(2)}, u32[]{:S(2)}) collective-permute-start(f32[8,128]{1,0:T(8,128)S(1)} %add_add_fusion.1.refs_0_), channel_id=1, source_target_pairs={{0,12},{1,13},{2,14},{3,15},{4,8},{5,9},{6,10},{7,11},{8,4},{9,5},... | collective-permute-start | bytes 12296 | tf_op jit(solution)/shard_map/ppermute | solution.py:508
  76.0 0.0 collective-permute-start.18
  76.0 2.6 %collective-permute-start.17 = (f32[8,128]{1,0:T(8,128)S(1)}, f32[8,128]{1,0:T(8,128)S(1)}, u32[]{:S(2)}, u32[]{:S(2)}) collective-permute-start(f32[8,128]{1,0:T(8,128)S(1)} %add_add_fusion.1.refs_0_), channel_id=1, source_target_pairs={{0,4},{1,5},{2,6},{3,7},{4,0},{5,1},{6,2},{7,3},{8,12},{9,13},{10,... | collective-permute-start | bytes 12296 | tf_op jit(solution)/shard_map/ppermute | solution.py:508
  78.6 1.0 %collective-permute-done.19.refs_3_ = f32[8,128]{1,0:T(8,128)S(1)} collective-permute-done((f32[8,128]{1,0:T(8,128)S(1)}, f32[8,128]{1,0:T(8,128)S(1)}, u32[]{:S(2)}, u32[]{:S(2)}) %collective-permute-start.19) | collective-permute-done | bytes 4128 | tf_op jit(solution)/shard_map/ppermute | solution.py:508
  79.6 0.9 %collective-permute-done.18.refs_2_ = f32[8,128]{1,0:T(8,128)S(1)} collective-permute-done((f32[8,128]{1,0:T(8,128)S(1)}, f32[8,128]{1,0:T(8,128)S(1)}, u32[]{:S(2)}, u32[]{:S(2)}) %collective-permute-start.18) | collective-permute-done | bytes 4128 | tf_op jit(solution)/shard_map/ppermute | solution.py:508
  80.5 0.0 collective-permute-done.17.refs_1_
  80.6 1.1 %shard_map.45 = (f32[4,32,512]{2,1,0:T(8,128)S(1)}, s32[1]{0:T(128)}) custom-call(f32[16,2,32,512]{3,2,1,0:T(8,128)S(1)} %get-tuple-element.68.p1m_ref, f32[16,2,32,512]{3,2,1,0:T(8,128)S(1)} %get-tuple-element.69.p2m_ref, f32[16,2,32,512]{3,2,1,0:T(8,128)S(1)} %get-tuple-element.80.p1e_ref, f32[16,2,32,512]{3,2,1,0:T(8,128)S(1)} %get-tuple-element.81.p2e_ref, ...), custom_call_target="tpu_custom_call" | custom-call | flops 5033164 | bytes 8388608 | tf_op jit(solution)/shard_map/pallas_call | solution.py:424
  82.3 0.2 conditional.1
  82.5 0.0 copy-start.3
  82.5 0.7 copy-done.3
  (1 shorter events, 0.0 us)
Async XLA Ops:
  0.8 7.4 %collective-permute-start.7 = (f32[32,512]{1,0:T(8,128)S(1)}, f32[32,512]{1,0:T(8,128)S(1)}, u32[]{:S(2)}, u32[]{:S(2)}) collective-permute-start(f32[32,512]{1,0:T(8,128)S(1)} %slice_bitcast_fusion.4.own_ref), channel_id=1, source_target_pairs={{0,1},{1,2},{2,3},{3,4},{4,5},{5,6},{6,7},{7,8},{8,9},{9,10},{10,1... | collective-permute-start | bytes 196616 | tf_op jit(solution)/shard_map/ppermute | solution.py:21
  8.2 17.7 %collective-permute-start.8 = (f32[17,32,512]{2,1,0:T(8,128)S(1)}, f32[17,32,512]{2,1,0:T(8,128)S(1)}, u32[]{:S(2)}, u32[]{:S(2)}) collective-permute-start(f32[17,32,512]{2,1,0:T(8,128)S(1)} %get-tuple-element.63), channel_id=1, source_target_pairs={{0,15},{1,2},{2,1},{3,4},{4,3},{5,6},{6,5},{7,8},{8,7},{9,10},{10,... | collective-permute-start | bytes 3342344 | tf_op jit(solution)/shard_map/ppermute | solution.py:21
  8.7 17.3 %collective-permute-start.9 = (f32[17,32,512]{2,1,0:T(8,128)S(1)}, f32[17,32,512]{2,1,0:T(8,128)S(1)}, u32[]{:S(2)}, u32[]{:S(2)}) collective-permute-start(f32[17,32,512]{2,1,0:T(8,128)S(1)} %get-tuple-element.64), channel_id=1, source_target_pairs={{0,1},{1,0},{2,3},{3,2},{4,5},{5,4},{6,7},{7,6},{8,9},{9,8},{10,11... | collective-permute-start | bytes 3342344 | tf_op jit(solution)/shard_map/ppermute | solution.py:21
  16.5 36.8 %collective-permute-start.11 = (f32[16,32,512]{2,1,0:T(8,128)S(1)}, f32[16,32,512]{2,1,0:T(8,128)S(1)}, u32[]{:S(2)}, u32[]{:S(2)}) collective-permute-start(f32[16,32,512]{2,1,0:T(8,128)S(1)} %get-tuple-element.76), channel_id=1, source_target_pairs={{0,15},{1,2},{2,1},{3,4},{4,3},{5,6},{6,5},{7,8},{8,7},{9,10},{10,... | collective-permute-start | bytes 3145736 | tf_op jit(solution)/shard_map/ppermute | solution.py:21
  20.6 32.8 %collective-permute-start.12 = (f32[16,32,512]{2,1,0:T(8,128)S(1)}, f32[16,32,512]{2,1,0:T(8,128)S(1)}, u32[]{:S(2)}, u32[]{:S(2)}) collective-permute-start(f32[16,32,512]{2,1,0:T(8,128)S(1)} %get-tuple-element.77), channel_id=1, source_target_pairs={{0,1},{1,0},{2,3},{3,2},{4,5},{5,4},{6,7},{7,6},{8,9},{9,8},{10,11... | collective-permute-start | bytes 3145736 | tf_op jit(solution)/shard_map/ppermute | solution.py:21
  26.0 27.3 %collective-permute-start.10 = (f32[8,128]{1,0:T(8,128)S(1)}, f32[8,128]{1,0:T(8,128)S(1)}, u32[]{:S(2)}, u32[]{:S(2)}) collective-permute-start(f32[8,128]{1,0:T(8,128)S(1)} %get-tuple-element.72), channel_id=1, source_target_pairs={{0,1},{1,0},{2,3},{3,2},{4,5},{5,4},{6,7},{7,6},{8,9},{9,8},{10,11... | collective-permute-start | bytes 12296 | tf_op jit(solution)/shard_map/ppermute | solution.py:21
  53.3 17.0 %collective-permute-start.13 = (f32[16,32,512]{2,1,0:T(8,128)S(1)}, f32[16,32,512]{2,1,0:T(8,128)S(1)}, u32[]{:S(2)}, u32[]{:S(2)}) collective-permute-start(f32[16,32,512]{2,1,0:T(8,128)S(1)} %get-tuple-element.83), channel_id=1, source_target_pairs={{0,1},{1,2},{2,3},{3,4},{4,5},{5,6},{6,7},{7,8},{8,9},{9,10},{10,1... | collective-permute-start | bytes 3145736 | tf_op jit(solution)/shard_map/ppermute | solution.py:21
  70.4 3.1 %collective-permute-start.16 = (f32[8,128]{1,0:T(8,128)S(1)}, f32[8,128]{1,0:T(8,128)S(1)}, u32[]{:S(2)}, u32[]{:S(2)}) collective-permute-start(f32[8,128]{1,0:T(8,128)S(1)} %shard_map.44), channel_id=1, source_target_pairs={{0,3},{1,2},{2,1},{3,0},{4,7},{5,6},{6,5},{7,4},{8,11},{9,10},{10,... | collective-permute-start | bytes 12296 | tf_op jit(solution)/shard_map/ppermute | solution.py:508
  70.5 3.7 %collective-permute-start.15 = (f32[8,128]{1,0:T(8,128)S(1)}, f32[8,128]{1,0:T(8,128)S(1)}, u32[]{:S(2)}, u32[]{:S(2)}) collective-permute-start(f32[8,128]{1,0:T(8,128)S(1)} %shard_map.44), channel_id=1, source_target_pairs={{0,2},{1,3},{2,0},{3,1},{4,6},{5,7},{6,4},{7,5},{8,10},{9,11},{10,... | collective-permute-start | bytes 12296 | tf_op jit(solution)/shard_map/ppermute | solution.py:508
  70.6 3.6 %collective-permute-start.14 = (f32[8,128]{1,0:T(8,128)S(1)}, f32[8,128]{1,0:T(8,128)S(1)}, u32[]{:S(2)}, u32[]{:S(2)}) collective-permute-start(f32[8,128]{1,0:T(8,128)S(1)} %shard_map.44), channel_id=1, source_target_pairs={{0,1},{1,0},{2,3},{3,2},{4,5},{5,4},{6,7},{7,6},{8,9},{9,8},{10,11... | collective-permute-start | bytes 12296 | tf_op jit(solution)/shard_map/ppermute | solution.py:508
  74.2 5.5 %collective-permute-start.19 = (f32[8,128]{1,0:T(8,128)S(1)}, f32[8,128]{1,0:T(8,128)S(1)}, u32[]{:S(2)}, u32[]{:S(2)}) collective-permute-start(f32[8,128]{1,0:T(8,128)S(1)} %add_add_fusion.1.refs_0_), channel_id=1, source_target_pairs={{0,12},{1,13},{2,14},{3,15},{4,8},{5,9},{6,10},{7,11},{8,4},{9,5},... | collective-permute-start | bytes 12296 | tf_op jit(solution)/shard_map/ppermute | solution.py:508
  76.0 4.5 %collective-permute-start.18 = (f32[8,128]{1,0:T(8,128)S(1)}, f32[8,128]{1,0:T(8,128)S(1)}, u32[]{:S(2)}, u32[]{:S(2)}) collective-permute-start(f32[8,128]{1,0:T(8,128)S(1)} %add_add_fusion.1.refs_0_), channel_id=1, source_target_pairs={{0,8},{1,9},{2,10},{3,11},{4,12},{5,13},{6,14},{7,15},{8,0},{9,1},... | collective-permute-start | bytes 12296 | tf_op jit(solution)/shard_map/ppermute | solution.py:508
  76.0 4.5 %collective-permute-start.17 = (f32[8,128]{1,0:T(8,128)S(1)}, f32[8,128]{1,0:T(8,128)S(1)}, u32[]{:S(2)}, u32[]{:S(2)}) collective-permute-start(f32[8,128]{1,0:T(8,128)S(1)} %add_add_fusion.1.refs_0_), channel_id=1, source_target_pairs={{0,4},{1,5},{2,6},{3,7},{4,0},{5,1},{6,2},{7,3},{8,12},{9,13},{10,... | collective-permute-start | bytes 12296 | tf_op jit(solution)/shard_map/ppermute | solution.py:508
  82.5 0.7 copy-start.3

commit v11 on v10

--- a/solution.py
+++ b/solution.py
@@ -447,7 +447,6 @@
                  pltpu.VMEM((2,) + edge, jnp.int32), pltpu.SemaphoreType.DMA((6,))],
         cost=(0.1, 0.5), mib=16,
     )
-    off_signs, on_signs, before = lax.optimization_barrier((off_signs, on_signs, before))
     off_signs = moved(off_signs, "off")
     on_signs = moved(on_signs, "on")
     planes, diag, dinv, ahead, bits = call(
@@ -458,14 +457,14 @@
          (dplanes, "whole", F32), (field, "whole", jnp.int32)],
         scratch=[pltpu.VMEM(couplings.shape, F32), pltpu.VMEM(plane, jnp.int32),
                  pltpu.SemaphoreType.DMA((6,))],
-        cost=(0.5, 1), mib=32,
+        cost=(3, 20), mib=32,
     )
 
     w1, off, on, mark = call(
         first_kernel, grid,
         [(odd, "smem"), (bits, "split"), (planes, "whole"), (ahead, "whole"), (dinv, "whole")],
         [(field, "split", F32), (edge, "split", F32), (edge, "split", F32), (tile, "whole", F32)],
-        scratch=[pltpu.VMEM(dplanes, F32)], cost=(1, 2),
+        scratch=[pltpu.VMEM(dplanes, F32)], cost=(600, 4000),
     )
     off = moved(off, "off")
     on = moved(on, "on")

time: 83.4 us -> 83.1 us (level)
  waiting for transfers between devices: 27 us -> 19.6 us
  starting transfers between devices: 29.8 us -> 36.8 us
    ppermute x7, starting transfers between devices: 23.5 us -> 30.5 us  [moved(): return lax.ppermute(value, 'day', [(i, target(i)) for i in range(count)])]
    ppermute x7, waiting for transfers between devices: 23.2 us -> 16.2 us  [moved(): return lax.ppermute(value, 'day', [(i, target(i)) for i in range(count)])]
  transfers between devices with their start and end apart: 13 -> 13, of which waited for: 7 -> 6; matrix products, arithmetic and copies ran while one was open for 0% -> 0% of each run, Pallas kernels for 27% -> 27%
where the time goes in v11:
time: 83.1 us; the launch traced here: 82.9 us
  starting transfers between devices  36.8 us (44%)
  Pallas kernels  23.9 us (29%)
  waiting for transfers between devices  19.6 us (24%)
  local copies, waits for them, and re-layouts  1.54 us (2%)
    ppermute x7, starting transfers between devices, moved(): return lax.ppermute(value, 'day', [(i, target(i)) for i in range(count)])  30.5 us
    pallas_call x7, Pallas kernels, call(): pl.pallas_call(kernel, grid=grid, in_specs=[spec(value.shape, kind) for v...  23.9 us
    ppermute x7, waiting for transfers between devices, moved(): return lax.ppermute(value, 'day', [(i, target(i)) for i in range(count)])  16.2 us
    ppermute x6, starting transfers between devices, body(): lax.ppermute(moments, 'day', [(i, i ^ n * step) for i in range(count)])  6.33 us
    ppermute x6, waiting for transfers between devices, body(): lax.ppermute(moments, 'day', [(i, i ^ n * step) for i in range(count)])  3.41 us
  transfers between devices with their start and end apart: 13, of which 6 were waited for; matrix products, arithmetic and copies ran while one was open for 0% of the time, Pallas kernels for 27%

profile of v11, /device:TPU:0, one launch (start us, length us, event | category | flops | bytes accessed | tf_op | source)
XLA Modules:
  0.0 82.9 jit_solution(17355359591951455182)
XLA Ops:
  0.0 0.8 %slice_bitcast_fusion.4.own_ref = f32[32,512]{1,0:T(8,128)S(1)} fusion(f32[6,4,32,512]{3,2,1,0:T(8,128)} %coup_hbm.3), kind=kLoop, calls=%fused_computation.169 | loop fusion | bytes 131072 | tf_op jit(solution)/shard_map/squeeze | solution.py:438
  0.8 0.5 collective-permute-start.7
  1.3 2.3 %shard_map.41 = (f32[17,32,512]{2,1,0:T(8,128)S(1)}, f32[17,32,512]{2,1,0:T(8,128)S(1)}) custom-call(s32[1]{0:T(128)} %bitcast.12.odd_ref, f32[6,4,32,512]{3,2,1,0:T(8,128)} %coup_hbm.3, s32[16,4,32,512]{3,2,1,0:T(8,128)} %bits_hbm.3, s32[32,512]{1,0:T(8,128)} %mask_hbm.3, f32[32,512]{1,0:T(8,128)S(1)} %slice_bitcast_fusion.4.own_ref), custom_call_target="tpu_custom_call" | custom-call | flops 2516582 | bytes 2097152 | tf_op jit(solution)/shard_map/pallas_call | solution.py:424
  3.6 5.1 %collective-permute-start.8 = (f32[17,32,512]{2,1,0:T(8,128)S(1)}, f32[17,32,512]{2,1,0:T(8,128)S(1)}, u32[]{:S(2)}, u32[]{:S(2)}) collective-permute-start(f32[17,32,512]{2,1,0:T(8,128)S(1)} %get-tuple-element.57), channel_id=1, source_target_pairs={{0,15},{1,2},{2,1},{3,4},{4,3},{5,6},{6,5},{7,8},{8,7},{9,10},{10,... | collective-permute-start | bytes 3342344 | tf_op jit(solution)/shard_map/ppermute | solution.py:21
  8.6 0.0 collective-permute-start.9
  8.7 0.0 collective-permute-done.7.before_ref
  8.7 2.7 %shard_map.39 = (f32[8,4,32,512]{3,2,1,0:T(8,128)S(1)}, f32[4,32,512]{2,1,0:T(8,128)S(1)}, f32[4,32,512]{2,1,0:T(8,128)S(1)}, f32[4,32,512]{2,1,0:T(8,128)S(1)}, s32[16,4,32,512]{3,2,1,0:T(8,128)S(1)}) custom-call(f32[6,4,32,512]{3,2,1,0:T(8,128)} %coup_hbm.3, s32[16,4,32,512]{3,2,1,0:T(8,128)} %bits_hbm.3, s32[32,512]{1,0:T(8,128)} %mask_hbm.3, ...), custom_call_target="tpu_custom_call" | custom-call | flops 75497472 | bytes 83886080 | tf_op jit(solution)/shard_map/pallas_call | solution.py:424
  11.4 5.1 %shard_map.40 = (f32[16,4,32,512]{3,2,1,0:T(8,128)S(1)}, f32[16,32,512]{2,1,0:T(8,128)S(1)}, f32[16,32,512]{2,1,0:T(8,128)S(1)}, f32[8,128]{1,0:T(8,128)S(1)}) custom-call(s32[1]{0:T(128)} %bitcast.12.odd_ref, s32[16,4,32,512]{3,2,1,0:T(8,128)S(1)} %get-tuple-element.51.bits_ref, f32[8,4,32,512]{3,2,1,0:T(8,128)S(1)} %get-tuple-element.52.planes_ref, ...), custom_call_target="tpu_custom_call" | custom-call | flops 15099494400 | bytes 16777216000 | tf_op jit(solution)/shard_map/pallas_call | solution.py:424
  16.5 2.5 %collective-permute-start.11 = (f32[16,32,512]{2,1,0:T(8,128)S(1)}, f32[16,32,512]{2,1,0:T(8,128)S(1)}, u32[]{:S(2)}, u32[]{:S(2)}) collective-permute-start(f32[16,32,512]{2,1,0:T(8,128)S(1)} %get-tuple-element.70), channel_id=1, source_target_pairs={{0,15},{1,2},{2,1},{3,4},{4,3},{5,6},{6,5},{7,8},{8,7},{9,10},{10,... | collective-permute-start | bytes 3145736 | tf_op jit(solution)/shard_map/ppermute | solution.py:21
  19.0 0.0 collective-permute-start.12
  19.0 3.0 %collective-permute-done.8.off_ref.doff_ref = f32[17,32,512]{2,1,0:T(8,128)S(1)} collective-permute-done((f32[17,32,512]{2,1,0:T(8,128)S(1)}, f32[17,32,512]{2,1,0:T(8,128)S(1)}, u32[]{:S(2)}, u32[]{:S(2)}) %collective-permute-start.8) | collective-permute-done | bytes 1114144 | tf_op jit(solution)/shard_map/ppermute | solution.py:21
  21.9 0.0 collective-permute-done.9.on_ref.don_ref
  21.9 22.4 %collective-permute-start.10 = (f32[8,128]{1,0:T(8,128)S(1)}, f32[8,128]{1,0:T(8,128)S(1)}, u32[]{:S(2)}, u32[]{:S(2)}) collective-permute-start(f32[8,128]{1,0:T(8,128)S(1)} %get-tuple-element.66), channel_id=1, source_target_pairs={{0,1},{1,0},{2,3},{3,2},{4,5},{5,4},{6,7},{7,6},{8,9},{9,8},{10,11... | collective-permute-start | bytes 12296 | tf_op jit(solution)/shard_map/ppermute | solution.py:21
  44.4 8.9 %shard_map.42 = (f32[16,2,32,512]{3,2,1,0:T(8,128)S(1)}, f32[16,2,32,512]{3,2,1,0:T(8,128)S(1)}, f32[16,2,32,512]{3,2,1,0:T(8,128)S(1)}, f32[16,2,32,512]{3,2,1,...) custom-call(s32[1]{0:T(128)} %bitcast.12.odd_ref, ...), custom_call_target="tpu_custom_call" | custom-call | flops 251658240 | bytes 251658240 | tf_op jit(solution)/shard_map/pallas_call | solution.py:424
  53.3 0.0 collective-permute-done.10.token_ref
  53.3 0.1 collective-permute-start.13
  53.3 0.0 collective-permute-done.11.off_ref
  53.3 0.0 collective-permute-done.12.on_ref
  53.4 3.7 %shard_map.43 = (f32[16,2,32,512]{3,2,1,0:T(8,128)S(1)}, f32[16,2,32,512]{3,2,1,0:T(8,128)S(1)}, f32[16,32,512]{2,1,0:T(8,128)S(1)}, f32[16,8,128]{2,1,0:T(8,128)S(1)}) custom-call(s32[1]{0:T(128)} %bitcast.12.odd_ref, f32[8,128]{1,0:T(8,128)S(1)} %collective-permute-done.10.token_ref, s32[16,4,32,512]{3,2,1,0:T(8,128)S(1)} %get-tuple-element.51.bits_ref, ...), custom_call_target="tpu_custom_call" | custom-call | flops 251658240 | bytes 251658240 | tf_op jit(solution)/shard_map/pallas_call | solution.py:424
  57.0 13.3 %collective-permute-done.13.high_ref = f32[16,32,512]{2,1,0:T(8,128)S(1)} collective-permute-done((f32[16,32,512]{2,1,0:T(8,128)S(1)}, f32[16,32,512]{2,1,0:T(8,128)S(1)}, u32[]{:S(2)}, u32[]{:S(2)}) %collective-permute-start.13) | collective-permute-done | bytes 1048608 | tf_op jit(solution)/shard_map/ppermute | solution.py:21
  70.3 0.2 shard_map.44
  70.5 0.0 collective-permute-start.16
  70.5 0.1 collective-permute-start.15
  70.6 1.8 %collective-permute-start.14 = (f32[8,128]{1,0:T(8,128)S(1)}, f32[8,128]{1,0:T(8,128)S(1)}, u32[]{:S(2)}, u32[]{:S(2)}) collective-permute-start(f32[8,128]{1,0:T(8,128)S(1)} %shard_map.44), channel_id=1, source_target_pairs={{0,1},{1,0},{2,3},{3,2},{4,5},{5,4},{6,7},{7,6},{8,9},{9,8},{10,11... | collective-permute-start | bytes 12296 | tf_op jit(solution)/shard_map/ppermute | solution.py:507
  72.4 1.2 %collective-permute-done.16 = f32[8,128]{1,0:T(8,128)S(1)} collective-permute-done((f32[8,128]{1,0:T(8,128)S(1)}, f32[8,128]{1,0:T(8,128)S(1)}, u32[]{:S(2)}, u32[]{:S(2)}) %collective-permute-start.16) | collective-permute-done | bytes 4128 | tf_op jit(solution)/shard_map/ppermute | solution.py:507
  73.5 0.7 collective-permute-done.15
  74.2 0.0 collective-permute-done.14
  74.2 0.9 %collective-permute-start.19 = (f32[8,128]{1,0:T(8,128)S(1)}, f32[8,128]{1,0:T(8,128)S(1)}, u32[]{:S(2)}, u32[]{:S(2)}) collective-permute-start(f32[8,128]{1,0:T(8,128)S(1)} %add_add_fusion.1.refs_0_), channel_id=1, source_target_pairs={{0,12},{1,13},{2,14},{3,15},{4,8},{5,9},{6,10},{7,11},{8,4},{9,5},... | collective-permute-start | bytes 12296 | tf_op jit(solution)/shard_map/ppermute | solution.py:507
  75.1 0.0 collective-permute-start.18
  75.1 3.5 %collective-permute-start.17 = (f32[8,128]{1,0:T(8,128)S(1)}, f32[8,128]{1,0:T(8,128)S(1)}, u32[]{:S(2)}, u32[]{:S(2)}) collective-permute-start(f32[8,128]{1,0:T(8,128)S(1)} %add_add_fusion.1.refs_0_), channel_id=1, source_target_pairs={{0,4},{1,5},{2,6},{3,7},{4,0},{5,1},{6,2},{7,3},{8,12},{9,13},{10,... | collective-permute-start | bytes 12296 | tf_op jit(solution)/shard_map/ppermute | solution.py:507
  78.7 1.0 %collective-permute-done.19.refs_3_ = f32[8,128]{1,0:T(8,128)S(1)} collective-permute-done((f32[8,128]{1,0:T(8,128)S(1)}, f32[8,128]{1,0:T(8,128)S(1)}, u32[]{:S(2)}, u32[]{:S(2)}) %collective-permute-start.19) | collective-permute-done | bytes 4128 | tf_op jit(solution)/shard_map/ppermute | solution.py:507
  79.7 0.0 collective-permute-done.18.refs_2_
  79.7 0.6 collective-permute-done.17.refs_1_
  80.2 1.1 %shard_map.45 = (f32[4,32,512]{2,1,0:T(8,128)S(1)}, s32[1]{0:T(128)}) custom-call(f32[16,2,32,512]{3,2,1,0:T(8,128)S(1)} %get-tuple-element.62.p1m_ref, f32[16,2,32,512]{3,2,1,0:T(8,128)S(1)} %get-tuple-element.63.p2m_ref, f32[16,2,32,512]{3,2,1,0:T(8,128)S(1)} %get-tuple-element.74.p1e_ref, f32[16,2,32,512]{3,2,1,0:T(8,128)S(1)} %get-tuple-element.75.p2e_ref, ...), custom_call_target="tpu_custom_call" | custom-call | flops 5033164 | bytes 8388608 | tf_op jit(solution)/shard_map/pallas_call | solution.py:424
  82.0 0.2 conditional.1
  82.2 0.0 copy-start.3
  82.2 0.7 copy-done.3
  (1 shorter events, 0.0 us)
Async XLA Ops:
  0.8 7.8 %collective-permute-start.7 = (f32[32,512]{1,0:T(8,128)S(1)}, f32[32,512]{1,0:T(8,128)S(1)}, u32[]{:S(2)}, u32[]{:S(2)}) collective-permute-start(f32[32,512]{1,0:T(8,128)S(1)} %slice_bitcast_fusion.4.own_ref), channel_id=1, source_target_pairs={{0,1},{1,2},{2,3},{3,4},{4,5},{5,6},{6,7},{7,8},{8,9},{9,10},{10,1... | collective-permute-start | bytes 196616 | tf_op jit(solution)/shard_map/ppermute | solution.py:21
  3.6 18.4 %collective-permute-start.8 = (f32[17,32,512]{2,1,0:T(8,128)S(1)}, f32[17,32,512]{2,1,0:T(8,128)S(1)}, u32[]{:S(2)}, u32[]{:S(2)}) collective-permute-start(f32[17,32,512]{2,1,0:T(8,128)S(1)} %get-tuple-element.57), channel_id=1, source_target_pairs={{0,15},{1,2},{2,1},{3,4},{4,3},{5,6},{6,5},{7,8},{8,7},{9,10},{10,... | collective-permute-start | bytes 3342344 | tf_op jit(solution)/shard_map/ppermute | solution.py:21
  8.6 13.3 %collective-permute-start.9 = (f32[17,32,512]{2,1,0:T(8,128)S(1)}, f32[17,32,512]{2,1,0:T(8,128)S(1)}, u32[]{:S(2)}, u32[]{:S(2)}) collective-permute-start(f32[17,32,512]{2,1,0:T(8,128)S(1)} %get-tuple-element.58), channel_id=1, source_target_pairs={{0,1},{1,0},{2,3},{3,2},{4,5},{5,4},{6,7},{7,6},{8,9},{9,8},{10,11... | collective-permute-start | bytes 3342344 | tf_op jit(solution)/shard_map/ppermute | solution.py:21
  16.5 36.8 %collective-permute-start.11 = (f32[16,32,512]{2,1,0:T(8,128)S(1)}, f32[16,32,512]{2,1,0:T(8,128)S(1)}, u32[]{:S(2)}, u32[]{:S(2)}) collective-permute-start(f32[16,32,512]{2,1,0:T(8,128)S(1)} %get-tuple-element.70), channel_id=1, source_target_pairs={{0,15},{1,2},{2,1},{3,4},{4,3},{5,6},{6,5},{7,8},{8,7},{9,10},{10,... | collective-permute-start | bytes 3145736 | tf_op jit(solution)/shard_map/ppermute | solution.py:21
  19.0 34.4 %collective-permute-start.12 = (f32[16,32,512]{2,1,0:T(8,128)S(1)}, f32[16,32,512]{2,1,0:T(8,128)S(1)}, u32[]{:S(2)}, u32[]{:S(2)}) collective-permute-start(f32[16,32,512]{2,1,0:T(8,128)S(1)} %get-tuple-element.71), channel_id=1, source_target_pairs={{0,1},{1,0},{2,3},{3,2},{4,5},{5,4},{6,7},{7,6},{8,9},{9,8},{10,11... | collective-permute-start | bytes 3145736 | tf_op jit(solution)/shard_map/ppermute | solution.py:21
  21.9 31.3 %collective-permute-start.10 = (f32[8,128]{1,0:T(8,128)S(1)}, f32[8,128]{1,0:T(8,128)S(1)}, u32[]{:S(2)}, u32[]{:S(2)}) collective-permute-start(f32[8,128]{1,0:T(8,128)S(1)} %get-tuple-element.66), channel_id=1, source_target_pairs={{0,1},{1,0},{2,3},{3,2},{4,5},{5,4},{6,7},{7,6},{8,9},{9,8},{10,11... | collective-permute-start | bytes 12296 | tf_op jit(solution)/shard_map/ppermute | solution.py:21
  53.3 17.0 %collective-permute-start.13 = (f32[16,32,512]{2,1,0:T(8,128)S(1)}, f32[16,32,512]{2,1,0:T(8,128)S(1)}, u32[]{:S(2)}, u32[]{:S(2)}) collective-permute-start(f32[16,32,512]{2,1,0:T(8,128)S(1)} %get-tuple-element.77), channel_id=1, source_target_pairs={{0,1},{1,2},{2,3},{3,4},{4,5},{5,6},{6,7},{7,8},{8,9},{9,10},{10,1... | collective-permute-start | bytes 3145736 | tf_op jit(solution)/shard_map/ppermute | solution.py:21
  70.5 3.1 %collective-permute-start.16 = (f32[8,128]{1,0:T(8,128)S(1)}, f32[8,128]{1,0:T(8,128)S(1)}, u32[]{:S(2)}, u32[]{:S(2)}) collective-permute-start(f32[8,128]{1,0:T(8,128)S(1)} %shard_map.44), channel_id=1, source_target_pairs={{0,3},{1,2},{2,1},{3,0},{4,7},{5,6},{6,5},{7,4},{8,11},{9,10},{10,... | collective-permute-start | bytes 12296 | tf_op jit(solution)/shard_map/ppermute | solution.py:507
  70.5 3.7 %collective-permute-start.15 = (f32[8,128]{1,0:T(8,128)S(1)}, f32[8,128]{1,0:T(8,128)S(1)}, u32[]{:S(2)}, u32[]{:S(2)}) collective-permute-start(f32[8,128]{1,0:T(8,128)S(1)} %shard_map.44), channel_id=1, source_target_pairs={{0,2},{1,3},{2,0},{3,1},{4,6},{5,7},{6,4},{7,5},{8,10},{9,11},{10,... | collective-permute-start | bytes 12296 | tf_op jit(solution)/shard_map/ppermute | solution.py:507
  70.6 3.6 %collective-permute-start.14 = (f32[8,128]{1,0:T(8,128)S(1)}, f32[8,128]{1,0:T(8,128)S(1)}, u32[]{:S(2)}, u32[]{:S(2)}) collective-permute-start(f32[8,128]{1,0:T(8,128)S(1)} %shard_map.44), channel_id=1, source_target_pairs={{0,1},{1,0},{2,3},{3,2},{4,5},{5,4},{6,7},{7,6},{8,9},{9,8},{10,11... | collective-permute-start | bytes 12296 | tf_op jit(solution)/shard_map/ppermute | solution.py:507
  74.2 5.5 %collective-permute-start.19 = (f32[8,128]{1,0:T(8,128)S(1)}, f32[8,128]{1,0:T(8,128)S(1)}, u32[]{:S(2)}, u32[]{:S(2)}) collective-permute-start(f32[8,128]{1,0:T(8,128)S(1)} %add_add_fusion.1.refs_0_), channel_id=1, source_target_pairs={{0,12},{1,13},{2,14},{3,15},{4,8},{5,9},{6,10},{7,11},{8,4},{9,5},... | collective-permute-start | bytes 12296 | tf_op jit(solution)/shard_map/ppermute | solution.py:507
  75.1 4.6 %collective-permute-start.18 = (f32[8,128]{1,0:T(8,128)S(1)}, f32[8,128]{1,0:T(8,128)S(1)}, u32[]{:S(2)}, u32[]{:S(2)}) collective-permute-start(f32[8,128]{1,0:T(8,128)S(1)} %add_add_fusion.1.refs_0_), channel_id=1, source_target_pairs={{0,8},{1,9},{2,10},{3,11},{4,12},{5,13},{6,14},{7,15},{8,0},{9,1},... | collective-permute-start | bytes 12296 | tf_op jit(solution)/shard_map/ppermute | solution.py:507
  75.1 5.1 %collective-permute-start.17 = (f32[8,128]{1,0:T(8,128)S(1)}, f32[8,128]{1,0:T(8,128)S(1)}, u32[]{:S(2)}, u32[]{:S(2)}) collective-permute-start(f32[8,128]{1,0:T(8,128)S(1)} %add_add_fusion.1.refs_0_), channel_id=1, source_target_pairs={{0,4},{1,5},{2,6},{3,7},{4,0},{5,1},{6,2},{7,3},{8,12},{9,13},{10,... | collective-permute-start | bytes 12296 | tf_op jit(solution)/shard_map/ppermute | solution.py:507
  82.2 0.7 copy-start.3

commit v12 on v11

--- a/solution.py
+++ b/solution.py
@@ -67,8 +67,11 @@
     half = probes // 2
     copies = [
         pltpu.make_async_copy(mask_hbm, mask_ref, sems.at[0]),
-        pltpu.make_async_copy(coup_hbm, coup_ref, sems.at[1]),
+        pltpu.make_async_copy(coup_hbm.at[:, 0], coup_ref.at[:, 0], sems.at[1]),
+        pltpu.make_async_copy(coup_hbm.at[:, last], coup_ref.at[:, last], sems.at[6]),
+        pltpu.make_async_copy(coup_hbm.at[5, last - 1], coup_ref.at[5, last - 1], sems.at[7]),
     ]
+    small = len(copies)
     for side, day in enumerate((odd * last, last - odd * last)):
         for n in range(2):
             part = pl.ds(n * half, half)
@@ -79,14 +82,15 @@
             )
     for copy in copies:
         copy.start()
-    for copy in copies[:2]:
+    for copy in copies[:small]:
         copy.wait()
+    own_ref[...] = coup_ref[5, last]
     factors = link_factors(mask_ref[...])
     first = day_planes(coup_ref, factors, 0)[1]
     final = day_planes(coup_ref, factors, last)[1]
     off_ref[probes] = chosen(odd, first, final)
     on_ref[probes] = chosen(odd, final, first)
-    for copy in copies[2:]:
+    for copy in copies[small:]:
         copy.wait()
     for side, out_ref in enumerate((off_ref, on_ref)):
 
@@ -435,18 +439,16 @@
         )(*[value for value, _ in ins])
 
     odd = (lax.axis_index("day") % 2).astype(jnp.int32).reshape(1)
-    own = couplings[5, days - 1]
+    sent = (probes + 1,) + plane
+    own, off_signs, on_signs = call(
+        edges_kernel, (1,),
+        [(odd, "smem"), (hbm(couplings), "hbm"), (hbm(probe_bits), "hbm"), (hbm(land_mask), "hbm")],
+        [(plane, "whole", F32), (sent, "whole", F32), (sent, "whole", F32)],
+        scratch=[pltpu.VMEM(couplings.shape, F32), pltpu.VMEM(plane, jnp.int32),
+                 pltpu.VMEM((2,) + edge, jnp.int32), pltpu.SemaphoreType.DMA((8,))],
+        cost=(0.1, 0.5), mib=16,
+    )
     before = moved(own, "next")
-    sent = (probes + 1,) + plane
-    off_signs, on_signs = call(
-        edges_kernel, (1,),
-        [(odd, "smem"), (hbm(couplings), "hbm"), (hbm(probe_bits), "hbm"), (hbm(land_mask), "hbm"),
-         (own, "whole")],
-        [(sent, "whole", F32), (sent, "whole", F32)],
-        scratch=[pltpu.VMEM(couplings.shape, F32), pltpu.VMEM(plane, jnp.int32),
-                 pltpu.VMEM((2,) + edge, jnp.int32), pltpu.SemaphoreType.DMA((6,))],
-        cost=(0.1, 0.5), mib=16,
-    )
     off_signs = moved(off_signs, "off")
     on_signs = moved(on_signs, "on")
     planes, diag, dinv, ahead, bits = call(

time: 83.1 us -> 82.7 us (level)
  waiting for transfers between devices: 19.6 us -> 22.4 us
  starting transfers between devices: 36.8 us -> 34.8 us
  local copies, waits for them, and re-layouts: 1.54 us -> 0.7 us
    ppermute x7, waiting for transfers between devices: 16.2 us -> 19 us  [moved(): return lax.ppermute(value, 'day', [(i, target(i)) for i in range(count)])]
    ppermute x7, starting transfers between devices: 30.5 us -> 28.5 us  [moved(): return lax.ppermute(value, 'day', [(i, target(i)) for i in range(count)])]
    squeeze x1 -> x0, local copies, waits for them, and re-layouts: 0.84 us -> none  [body(): own = couplings[5, days - 1]]
  transfers between devices with their start and end apart: 13 -> 13, of which waited for: 6 -> 7; matrix products, arithmetic and copies ran while one was open for 0% -> 0% of each run, Pallas kernels for 27% -> 24%
where the time goes in v12:
time: 82.7 us; the launch traced here: 82.6 us
  starting transfers between devices  34.8 us (42%)
  Pallas kernels  23.6 us (29%)
  waiting for transfers between devices  22.4 us (27%)
    ppermute x7, starting transfers between devices, moved(): return lax.ppermute(value, 'day', [(i, target(i)) for i in range(count)])  28.5 us
    pallas_call x7, Pallas kernels, call(): pl.pallas_call(kernel, grid=grid, in_specs=[spec(value.shape, kind) for v...  23.6 us
    ppermute x7, waiting for transfers between devices, moved(): return lax.ppermute(value, 'day', [(i, target(i)) for i in range(count)])  19 us
    ppermute x6, starting transfers between devices, body(): lax.ppermute(moments, 'day', [(i, i ^ n * step) for i in range(count)])  6.32 us
    ppermute x6, waiting for transfers between devices, body(): lax.ppermute(moments, 'day', [(i, i ^ n * step) for i in range(count)])  3.41 us
  transfers between devices with their start and end apart: 13, of which 7 were waited for; matrix products, arithmetic and copies ran while one was open for 0% of the time, Pallas kernels for 24%

profile of v12, /device:TPU:0, one launch (start us, length us, event | category | flops | bytes accessed | tf_op | source)
XLA Modules:
  0.0 82.6 jit_solution(7282138517542801224)
XLA Ops:
  0.0 2.1 %shard_map.39 = (f32[32,512]{1,0:T(8,128)S(1)}, f32[17,32,512]{2,1,0:T(8,128)S(1)}, f32[17,32,512]{2,1,0:T(8,128)S(1)}) custom-call(s32[1]{0:T(128)} %bitcast.12.odd_ref, f32[6,4,32,512]{3,2,1,0:T(8,128)} %coup_hbm.3, s32[16,4,32,512]{3,2,1,0:T(8,128)} %bits_hbm.3, s32[32,512]{1,0:T(8,128)} %mask_hbm.3), custom_call_target="tpu_custom_call" | custom-call | flops 2516582 | bytes 2097152 | tf_op jit(solution)/shard_map/pallas_call | solution.py:428
  2.1 0.5 collective-permute-start.7
  2.6 5.1 %collective-permute-start.8 = (f32[17,32,512]{2,1,0:T(8,128)S(1)}, f32[17,32,512]{2,1,0:T(8,128)S(1)}, u32[]{:S(2)}, u32[]{:S(2)}) collective-permute-start(f32[17,32,512]{2,1,0:T(8,128)S(1)} %get-tuple-element.59), channel_id=1, source_target_pairs={{0,15},{1,2},{2,1},{3,4},{4,3},{5,6},{6,5},{7,8},{8,7},{9,10},{10,... | collective-permute-start | bytes 3342344 | tf_op jit(solution)/shard_map/ppermute | solution.py:21
  7.7 0.0 collective-permute-start.9
  7.7 2.0 %collective-permute-done.7.before_ref = f32[32,512]{1,0:T(8,128)S(1)} collective-permute-done((f32[32,512]{1,0:T(8,128)S(1)}, f32[32,512]{1,0:T(8,128)S(1)}, u32[]{:S(2)}, u32[]{:S(2)}) %collective-permute-start.7) | collective-permute-done | bytes 65568 | tf_op jit(solution)/shard_map/ppermute | solution.py:21
  9.6 2.7 %shard_map.40 = (f32[8,4,32,512]{3,2,1,0:T(8,128)S(1)}, f32[4,32,512]{2,1,0:T(8,128)S(1)}, f32[4,32,512]{2,1,0:T(8,128)S(1)}, f32[4,32,512]{2,1,0:T(8,128)S(1)}, s32[16,4,32,512]{3,2,1,0:T(8,128)S(1)}) custom-call(f32[6,4,32,512]{3,2,1,0:T(8,128)} %coup_hbm.3, s32[16,4,32,512]{3,2,1,0:T(8,128)} %bits_hbm.3, s32[32,512]{1,0:T(8,128)} %mask_hbm.3, ...), custom_call_target="tpu_custom_call" | custom-call | flops 75497472 | bytes 83886080 | tf_op jit(solution)/shard_map/pallas_call | solution.py:428
  12.4 5.1 %shard_map.41 = (f32[16,4,32,512]{3,2,1,0:T(8,128)S(1)}, f32[16,32,512]{2,1,0:T(8,128)S(1)}, f32[16,32,512]{2,1,0:T(8,128)S(1)}, f32[8,128]{1,0:T(8,128)S(1)}) custom-call(s32[1]{0:T(128)} %bitcast.12.odd_ref, s32[16,4,32,512]{3,2,1,0:T(8,128)S(1)} %get-tuple-element.53.bits_ref, f32[8,4,32,512]{3,2,1,0:T(8,128)S(1)} %get-tuple-element.54.planes_ref, ...), custom_call_target="tpu_custom_call" | custom-call | flops 15099494400 | bytes 16777216000 | tf_op jit(solution)/shard_map/pallas_call | solution.py:428
  17.5 0.4 collective-permute-start.11
  17.9 0.0 collective-permute-start.12
  17.9 3.7 %collective-permute-done.8.off_ref.doff_ref = f32[17,32,512]{2,1,0:T(8,128)S(1)} collective-permute-done((f32[17,32,512]{2,1,0:T(8,128)S(1)}, f32[17,32,512]{2,1,0:T(8,128)S(1)}, u32[]{:S(2)}, u32[]{:S(2)}) %collective-permute-start.8) | collective-permute-done | bytes 1114144 | tf_op jit(solution)/shard_map/ppermute | solution.py:21
  21.6 0.0 collective-permute-done.9.on_ref.don_ref
  21.6 22.4 %collective-permute-start.10 = (f32[8,128]{1,0:T(8,128)S(1)}, f32[8,128]{1,0:T(8,128)S(1)}, u32[]{:S(2)}, u32[]{:S(2)}) collective-permute-start(f32[8,128]{1,0:T(8,128)S(1)} %get-tuple-element.68), channel_id=1, source_target_pairs={{0,1},{1,0},{2,3},{3,2},{4,5},{5,4},{6,7},{7,6},{8,9},{9,8},{10,11... | collective-permute-start | bytes 12296 | tf_op jit(solution)/shard_map/ppermute | solution.py:21
  44.0 8.9 %shard_map.42 = (f32[16,2,32,512]{3,2,1,0:T(8,128)S(1)}, f32[16,2,32,512]{3,2,1,0:T(8,128)S(1)}, f32[16,2,32,512]{3,2,1,0:T(8,128)S(1)}, f32[16,2,32,512]{3,2,1,...) custom-call(s32[1]{0:T(128)} %bitcast.12.odd_ref, ...), custom_call_target="tpu_custom_call" | custom-call | flops 251658240 | bytes 251658240 | tf_op jit(solution)/shard_map/pallas_call | solution.py:428
  52.9 0.0 collective-permute-done.10.token_ref
  52.9 0.1 collective-permute-start.13
  53.0 0.0 collective-permute-done.11.off_ref
  53.0 0.0 collective-permute-done.12.on_ref
  53.0 3.5 %shard_map.43 = (f32[16,2,32,512]{3,2,1,0:T(8,128)S(1)}, f32[16,2,32,512]{3,2,1,0:T(8,128)S(1)}, f32[16,32,512]{2,1,0:T(8,128)S(1)}, f32[16,8,128]{2,1,0:T(8,128)S(1)}) custom-call(s32[1]{0:T(128)} %bitcast.12.odd_ref, f32[8,128]{1,0:T(8,128)S(1)} %collective-permute-done.10.token_ref, s32[16,4,32,512]{3,2,1,0:T(8,128)S(1)} %get-tuple-element.53.bits_ref, ...), custom_call_target="tpu_custom_call" | custom-call | flops 251658240 | bytes 251658240 | tf_op jit(solution)/shard_map/pallas_call | solution.py:428
  56.5 13.4 %collective-permute-done.13.high_ref = f32[16,32,512]{2,1,0:T(8,128)S(1)} collective-permute-done((f32[16,32,512]{2,1,0:T(8,128)S(1)}, f32[16,32,512]{2,1,0:T(8,128)S(1)}, u32[]{:S(2)}, u32[]{:S(2)}) %collective-permute-start.13) | collective-permute-done | bytes 1048608 | tf_op jit(solution)/shard_map/ppermute | solution.py:21
  69.9 0.2 shard_map.44
  70.2 0.0 collective-permute-start.16
  70.2 0.1 collective-permute-start.15
  70.3 1.8 %collective-permute-start.14 = (f32[8,128]{1,0:T(8,128)S(1)}, f32[8,128]{1,0:T(8,128)S(1)}, u32[]{:S(2)}, u32[]{:S(2)}) collective-permute-start(f32[8,128]{1,0:T(8,128)S(1)} %shard_map.44), channel_id=1, source_target_pairs={{0,1},{1,0},{2,3},{3,2},{4,5},{5,4},{6,7},{7,6},{8,9},{9,8},{10,11... | collective-permute-start | bytes 12296 | tf_op jit(solution)/shard_map/ppermute | solution.py:509
  72.1 1.2 %collective-permute-done.16 = f32[8,128]{1,0:T(8,128)S(1)} collective-permute-done((f32[8,128]{1,0:T(8,128)S(1)}, f32[8,128]{1,0:T(8,128)S(1)}, u32[]{:S(2)}, u32[]{:S(2)}) %collective-permute-start.16) | collective-permute-done | bytes 4128 | tf_op jit(solution)/shard_map/ppermute | solution.py:509
  73.2 0.7 collective-permute-done.15
  73.9 0.0 collective-permute-done.14
  73.9 0.9 %collective-permute-start.19 = (f32[8,128]{1,0:T(8,128)S(1)}, f32[8,128]{1,0:T(8,128)S(1)}, u32[]{:S(2)}, u32[]{:S(2)}) collective-permute-start(f32[8,128]{1,0:T(8,128)S(1)} %add_add_fusion.1.refs_0_), channel_id=1, source_target_pairs={{0,12},{1,13},{2,14},{3,15},{4,8},{5,9},{6,10},{7,11},{8,4},{9,5},... | collective-permute-start | bytes 12296 | tf_op jit(solution)/shard_map/ppermute | solution.py:509
  74.8 0.0 collective-permute-start.18
  74.8 3.5 %collective-permute-start.17 = (f32[8,128]{1,0:T(8,128)S(1)}, f32[8,128]{1,0:T(8,128)S(1)}, u32[]{:S(2)}, u32[]{:S(2)}) collective-permute-start(f32[8,128]{1,0:T(8,128)S(1)} %add_add_fusion.1.refs_0_), channel_id=1, source_target_pairs={{0,4},{1,5},{2,6},{3,7},{4,0},{5,1},{6,2},{7,3},{8,12},{9,13},{10,... | collective-permute-start | bytes 12296 | tf_op jit(solution)/shard_map/ppermute | solution.py:509
  78.3 1.0 %collective-permute-done.19.refs_3_ = f32[8,128]{1,0:T(8,128)S(1)} collective-permute-done((f32[8,128]{1,0:T(8,128)S(1)}, f32[8,128]{1,0:T(8,128)S(1)}, u32[]{:S(2)}, u32[]{:S(2)}) %collective-permute-start.19) | collective-permute-done | bytes 4128 | tf_op jit(solution)/shard_map/ppermute | solution.py:509
  79.4 0.0 collective-permute-done.18.refs_2_
  79.4 0.6 collective-permute-done.17.refs_1_
  79.9 1.1 %shard_map.45 = (f32[4,32,512]{2,1,0:T(8,128)S(1)}, s32[1]{0:T(128)}) custom-call(f32[16,2,32,512]{3,2,1,0:T(8,128)S(1)} %get-tuple-element.64.p1m_ref, f32[16,2,32,512]{3,2,1,0:T(8,128)S(1)} %get-tuple-element.65.p2m_ref, f32[16,2,32,512]{3,2,1,0:T(8,128)S(1)} %get-tuple-element.76.p1e_ref, f32[16,2,32,512]{3,2,1,0:T(8,128)S(1)} %get-tuple-element.77.p2e_ref, ...), custom_call_target="tpu_custom_call" | custom-call | flops 5033164 | bytes 8388608 | tf_op jit(solution)/shard_map/pallas_call | solution.py:428
  81.6 0.2 conditional.1
  81.9 0.0 copy-start.3
  81.9 0.7 copy-done.3
  (1 shorter events, 0.0 us)
Async XLA Ops:
  2.1 7.5 %collective-permute-start.7 = (f32[32,512]{1,0:T(8,128)S(1)}, f32[32,512]{1,0:T(8,128)S(1)}, u32[]{:S(2)}, u32[]{:S(2)}) collective-permute-start(f32[32,512]{1,0:T(8,128)S(1)} %get-tuple-element.52), channel_id=1, source_target_pairs={{0,1},{1,2},{2,3},{3,4},{4,5},{5,6},{6,7},{7,8},{8,9},{9,10},{10,1... | collective-permute-start | bytes 196616 | tf_op jit(solution)/shard_map/ppermute | solution.py:21
  2.6 19.0 %collective-permute-start.8 = (f32[17,32,512]{2,1,0:T(8,128)S(1)}, f32[17,32,512]{2,1,0:T(8,128)S(1)}, u32[]{:S(2)}, u32[]{:S(2)}) collective-permute-start(f32[17,32,512]{2,1,0:T(8,128)S(1)} %get-tuple-element.59), channel_id=1, source_target_pairs={{0,15},{1,2},{2,1},{3,4},{4,3},{5,6},{6,5},{7,8},{8,7},{9,10},{10,... | collective-permute-start | bytes 3342344 | tf_op jit(solution)/shard_map/ppermute | solution.py:21
  7.7 13.9 %collective-permute-start.9 = (f32[17,32,512]{2,1,0:T(8,128)S(1)}, f32[17,32,512]{2,1,0:T(8,128)S(1)}, u32[]{:S(2)}, u32[]{:S(2)}) collective-permute-start(f32[17,32,512]{2,1,0:T(8,128)S(1)} %get-tuple-element.60), channel_id=1, source_target_pairs={{0,1},{1,0},{2,3},{3,2},{4,5},{5,4},{6,7},{7,6},{8,9},{9,8},{10,11... | collective-permute-start | bytes 3342344 | tf_op jit(solution)/shard_map/ppermute | solution.py:21
  17.5 35.5 %collective-permute-start.11 = (f32[16,32,512]{2,1,0:T(8,128)S(1)}, f32[16,32,512]{2,1,0:T(8,128)S(1)}, u32[]{:S(2)}, u32[]{:S(2)}) collective-permute-start(f32[16,32,512]{2,1,0:T(8,128)S(1)} %get-tuple-element.72), channel_id=1, source_target_pairs={{0,15},{1,2},{2,1},{3,4},{4,3},{5,6},{6,5},{7,8},{8,7},{9,10},{10,... | collective-permute-start | bytes 3145736 | tf_op jit(solution)/shard_map/ppermute | solution.py:21
  17.9 35.1 %collective-permute-start.12 = (f32[16,32,512]{2,1,0:T(8,128)S(1)}, f32[16,32,512]{2,1,0:T(8,128)S(1)}, u32[]{:S(2)}, u32[]{:S(2)}) collective-permute-start(f32[16,32,512]{2,1,0:T(8,128)S(1)} %get-tuple-element.73), channel_id=1, source_target_pairs={{0,1},{1,0},{2,3},{3,2},{4,5},{5,4},{6,7},{7,6},{8,9},{9,8},{10,11... | collective-permute-start | bytes 3145736 | tf_op jit(solution)/shard_map/ppermute | solution.py:21
  21.6 31.3 %collective-permute-start.10 = (f32[8,128]{1,0:T(8,128)S(1)}, f32[8,128]{1,0:T(8,128)S(1)}, u32[]{:S(2)}, u32[]{:S(2)}) collective-permute-start(f32[8,128]{1,0:T(8,128)S(1)} %get-tuple-element.68), channel_id=1, source_target_pairs={{0,1},{1,0},{2,3},{3,2},{4,5},{5,4},{6,7},{7,6},{8,9},{9,8},{10,11... | collective-permute-start | bytes 12296 | tf_op jit(solution)/shard_map/ppermute | solution.py:21
  52.9 17.0 %collective-permute-start.13 = (f32[16,32,512]{2,1,0:T(8,128)S(1)}, f32[16,32,512]{2,1,0:T(8,128)S(1)}, u32[]{:S(2)}, u32[]{:S(2)}) collective-permute-start(f32[16,32,512]{2,1,0:T(8,128)S(1)} %get-tuple-element.79), channel_id=1, source_target_pairs={{0,1},{1,2},{2,3},{3,4},{4,5},{5,6},{6,7},{7,8},{8,9},{9,10},{10,1... | collective-permute-start | bytes 3145736 | tf_op jit(solution)/shard_map/ppermute | solution.py:21
  70.2 3.1 %collective-permute-start.16 = (f32[8,128]{1,0:T(8,128)S(1)}, f32[8,128]{1,0:T(8,128)S(1)}, u32[]{:S(2)}, u32[]{:S(2)}) collective-permute-start(f32[8,128]{1,0:T(8,128)S(1)} %shard_map.44), channel_id=1, source_target_pairs={{0,3},{1,2},{2,1},{3,0},{4,7},{5,6},{6,5},{7,4},{8,11},{9,10},{10,... | collective-permute-start | bytes 12296 | tf_op jit(solution)/shard_map/ppermute | solution.py:509
  70.2 3.7 %collective-permute-start.15 = (f32[8,128]{1,0:T(8,128)S(1)}, f32[8,128]{1,0:T(8,128)S(1)}, u32[]{:S(2)}, u32[]{:S(2)}) collective-permute-start(f32[8,128]{1,0:T(8,128)S(1)} %shard_map.44), channel_id=1, source_target_pairs={{0,2},{1,3},{2,0},{3,1},{4,6},{5,7},{6,4},{7,5},{8,10},{9,11},{10,... | collective-permute-start | bytes 12296 | tf_op jit(solution)/shard_map/ppermute | solution.py:509
  70.3 3.6 %collective-permute-start.14 = (f32[8,128]{1,0:T(8,128)S(1)}, f32[8,128]{1,0:T(8,128)S(1)}, u32[]{:S(2)}, u32[]{:S(2)}) collective-permute-start(f32[8,128]{1,0:T(8,128)S(1)} %shard_map.44), channel_id=1, source_target_pairs={{0,1},{1,0},{2,3},{3,2},{4,5},{5,4},{6,7},{7,6},{8,9},{9,8},{10,11... | collective-permute-start | bytes 12296 | tf_op jit(solution)/shard_map/ppermute | solution.py:509
  73.9 5.5 %collective-permute-start.19 = (f32[8,128]{1,0:T(8,128)S(1)}, f32[8,128]{1,0:T(8,128)S(1)}, u32[]{:S(2)}, u32[]{:S(2)}) collective-permute-start(f32[8,128]{1,0:T(8,128)S(1)} %add_add_fusion.1.refs_0_), channel_id=1, source_target_pairs={{0,12},{1,13},{2,14},{3,15},{4,8},{5,9},{6,10},{7,11},{8,4},{9,5},... | collective-permute-start | bytes 12296 | tf_op jit(solution)/shard_map/ppermute | solution.py:509
  74.8 4.6 %collective-permute-start.18 = (f32[8,128]{1,0:T(8,128)S(1)}, f32[8,128]{1,0:T(8,128)S(1)}, u32[]{:S(2)}, u32[]{:S(2)}) collective-permute-start(f32[8,128]{1,0:T(8,128)S(1)} %add_add_fusion.1.refs_0_), channel_id=1, source_target_pairs={{0,8},{1,9},{2,10},{3,11},{4,12},{5,13},{6,14},{7,15},{8,0},{9,1},... | collective-permute-start | bytes 12296 | tf_op jit(solution)/shard_map/ppermute | solution.py:509
  74.8 5.1 %collective-permute-start.17 = (f32[8,128]{1,0:T(8,128)S(1)}, f32[8,128]{1,0:T(8,128)S(1)}, u32[]{:S(2)}, u32[]{:S(2)}) collective-permute-start(f32[8,128]{1,0:T(8,128)S(1)} %add_add_fusion.1.refs_0_), channel_id=1, source_target_pairs={{0,4},{1,5},{2,6},{3,7},{4,0},{5,1},{6,2},{7,3},{8,12},{9,13},{10,... | collective-permute-start | bytes 12296 | tf_op jit(solution)/shard_map/ppermute | solution.py:509
  81.9 0.7 copy-start.3

commit v13 on v12

--- a/solution.py
+++ b/solution.py
@@ -206,7 +206,7 @@
 
 def second_kernel(odd_ref, bits_ref, w1_ref, off_ref, on_ref, doff_ref, don_ref, planes_ref,
                   ahead_ref, before_ref, diag_ref, dinv_ref,
-                  p1_ref, p2_ref, w1e_ref, w2e_ref, high_ref, sums_ref, ratio_ref, scale_ref,
+                  p1_ref, p2_ref, w1e_ref, w2e_ref, high_ref, ratio_ref, scale_ref,
                   w1c_ref):
     per, days = w1_ref.shape[:2]
     last = days - 1
@@ -230,11 +230,8 @@
             w1c_ref[d] = w1
         w1e_ref[k, 0] = w1c_ref[0]
         w1e_ref[k, 1] = w1c_ref[last]
-        zero = jnp.zeros((8, 128), F32)
-        n0 = n1 = n2 = n3 = n4 = n5 = zero
         for d in range(days):
             w2 = local_apply(lambda t: w1c_ref[t], ahead_ref, dinv_ref, planes_ref, d)
-            n0 = n0 + folded(dinv_ref[d])
             if d == 0:
                 w2e_ref[k, 0] = w2
                 continue
@@ -242,28 +239,15 @@
                 w2e_ref[k, 1] = w2
                 high_ref[k] = w2
                 continue
-            w1 = w1c_ref[d]
             bits = bits_ref[k, d]
-            p1 = signed(bits, w1)
-            p1_ref[k, d - 1] = p1
+            p1_ref[k, d - 1] = signed(bits, w1c_ref[d])
             p2_ref[k, d - 1] = signed(bits, w2)
-            scaled = diag_ref[d] * w2
-            n1 = n1 + folded(p1)
-            n2 = n2 + folded(diag_ref[d] * w1 * w1)
-            n3 = n3 + folded(scaled * w1)
-            n4 = n4 + folded(scaled * w2)
-            product = half_product(w2, planes_ref, d)
-            if d > 1:
-                product = product + ahead_ref[d - 1] * w2_before * w2
-            n5 = n5 + folded(product)
-            w2_before = w2
-        sums_ref[k] = stacked([n0, n1, n2, n3, n4, 2.0 * n5])
         return carry
 
     lax.fori_loop(0, per, probe, 0)
 
 
-def third_kernel(odd_ref, token_ref, bits_ref, p2m_ref, w1e_ref, w2e_ref, off_ref, on_ref, sums_in_ref,
+def third_kernel(odd_ref, token_ref, bits_ref, p1m_ref, p2m_ref, w1e_ref, w2e_ref, off_ref, on_ref,
                  planes_ref, ahead_ref, before_ref, ratio_ref, diag_ref, dinv_ref,
                  p1_ref, p2_ref, cross_ref, sums_ref, scale_ref):
     per, days = bits_ref.shape[:2]
@@ -277,7 +261,22 @@
 
     def probe(k, carry):
         zero = jnp.zeros((8, 128), F32)
-        n1 = n2 = n3 = n4 = n5 = zero
+        n0 = n1 = n2 = n3 = n4 = n5 = zero
+        inner_w2 = {}
+        for d in range(1, last):
+            p1, p2 = p1m_ref[k, d - 1], p2m_ref[k, d - 1]
+            w2 = signed(bits_ref[k, d], p2)
+            scaled = diag_ref[d] * p2
+            n0 = n0 + folded(dinv_ref[d])
+            n1 = n1 + folded(p1)
+            n2 = n2 + folded(diag_ref[d] * p1 * p1)
+            n3 = n3 + folded(scaled * p1)
+            n4 = n4 + folded(scaled * p2)
+            product = half_product(w2, planes_ref, d)
+            if d > 1:
+                product = product + ahead_ref[d - 1] * inner_w2[d - 1] * w2
+            n5 = n5 + folded(product)
+            inner_w2[d] = w2
         for side, (d, inner) in enumerate(((0, 1), (last, last - 1))):
             bits = bits_ref[k, d]
             w1 = w1e_ref[k, side]
@@ -289,19 +288,19 @@
             p1_ref[k, side] = p1
             p2_ref[k, side] = signed(bits, w2)
             scaled = diag_ref[d] * w2
+            n0 = n0 + folded(dinv_ref[d])
             n1 = n1 + folded(p1)
             n2 = n2 + folded(diag_ref[d] * w1 * w1)
             n3 = n3 + folded(scaled * w1)
             n4 = n4 + folded(scaled * w2)
-            inner_w2 = signed(bits_ref[k, inner], p2m_ref[k, inner - 1])
             product = half_product(w2, planes_ref, d)
-            product = product + ahead_ref[min(d, inner)] * w2 * inner_w2
+            product = product + ahead_ref[min(d, inner)] * w2 * inner_w2[inner]
             if side == 0:
                 cross = before_ref[...] * w2
                 cross_ref[k] = cross
                 product = product + cross * (ratio_ref[0] * w1)
             n5 = n5 + folded(product)
-        sums_ref[k] = sums_in_ref[k] + stacked([zero, n1, n2, n3, n4, 2.0 * n5])
+        sums_ref[k] = stacked([n0, n1, n2, n3, n4, 2.0 * n5])
         return carry
 
     lax.fori_loop(0, per, probe, 0)
@@ -473,14 +472,13 @@
     token, off_signs, on_signs = lax.optimization_barrier((mark, off_signs, on_signs))
     token = moved(token, "on")
 
-    p1m, p2m, w1e, w2e, high2, sums, ratio = call(
+    p1m, p2m, w1e, w2e, high2, ratio = call(
         second_kernel, grid,
         [(odd, "smem"), (bits, "split"), (w1, "split"), (off_signs, "split"), (on_signs, "split"),
          (off_signs, "last"), (on_signs, "last"), (planes, "whole"), (ahead, "whole"),
          (before, "whole"), (diag, "whole"), (dinv, "whole")],
         [(middle, "split", F32), (middle, "split", F32), (pair, "split", F32),
-         (pair, "split", F32), (edge, "split", F32), (sums_shape, "split", F32),
-         ((2,) + plane, "whole", F32)],
+         (pair, "split", F32), (edge, "split", F32), ((2,) + plane, "whole", F32)],
         scratch=[pltpu.VMEM((2,) + plane, F32), pltpu.VMEM(dplanes, F32)], cost=(10, 60), mib=20,
     )
     high2, ratio, token = lax.optimization_barrier((high2, ratio, token))
@@ -488,8 +486,8 @@
 
     p1e, p2e, cross, sums = call(
         third_kernel, grid,
-        [(odd, "smem"), (token, "whole"), (bits, "split"), (p2m, "split"), (w1e, "split"),
-         (w2e, "split"), (off, "split"), (on, "split"), (sums, "split"), (planes, "whole"),
+        [(odd, "smem"), (token, "whole"), (bits, "split"), (p1m, "split"), (p2m, "split"), (w1e, "split"),
+         (w2e, "split"), (off, "split"), (on, "split"), (planes, "whole"),
          (ahead, "whole"), (before, "whole"), (ratio, "whole"), (diag, "whole"), (dinv, "whole")],
         [(pair, "split", F32), (pair, "split", F32), (edge, "split", F32),
          (sums_shape, "split", F32)],

time: 82.7 us -> 85.7 us (1.036)
  starting transfers between devices: 34.8 us -> 38.6 us
    ppermute x6, starting transfers between devices: 6.32 us -> 10.1 us  [body(): lax.ppermute(moments, 'day', [(i, i ^ n * step) for i in range(count)])]
    ppermute x6, waiting for transfers between devices: 3.41 us -> 5.69 us  [body(): lax.ppermute(moments, 'day', [(i, i ^ n * step) for i in range(count)])]
    ppermute x7, waiting for transfers between devices: 19 us -> 16.9 us  [moved(): return lax.ppermute(value, 'day', [(i, target(i)) for i in range(count)])]
  transfers between devices with their start and end apart: 13 -> 13, of which waited for: 7 -> 7; matrix products, arithmetic and copies ran while one was open for 0% -> 0% of each run, Pallas kernels for 24% -> 23%
where the time goes in v13:
time: 85.7 us; the launch traced here: 85.6 us
  starting transfers between devices  38.6 us (45%)
  Pallas kernels  22.8 us (27%)
  waiting for transfers between devices  22.5 us (26%)
    ppermute x7, starting transfers between devices, moved(): return lax.ppermute(value, 'day', [(i, target(i)) for i in range(count)])  28.5 us
    pallas_call x7, Pallas kernels, call(): pl.pallas_call(kernel, grid=grid, in_specs=[spec(value.shape, kind) for v...  22.8 us
    ppermute x7, waiting for transfers between devices, moved(): return lax.ppermute(value, 'day', [(i, target(i)) for i in range(count)])  16.9 us
    ppermute x6, starting transfers between devices, body(): lax.ppermute(moments, 'day', [(i, i ^ n * step) for i in range(count)])  10.1 us
    ppermute x6, waiting for transfers between devices, body(): lax.ppermute(moments, 'day', [(i, i ^ n * step) for i in range(count)])  5.69 us
  transfers between devices with their start and end apart: 13, of which 7 were waited for; matrix products, arithmetic and copies ran while one was open for 0% of the time, Pallas kernels for 23%

profile of v13, /device:TPU:0, one launch (start us, length us, event | category | flops | bytes accessed | tf_op | source)
XLA Modules:
  0.0 85.6 jit_solution(10178710539690380976)
XLA Ops:
  0.0 2.1 %shard_map.39 = (f32[32,512]{1,0:T(8,128)S(1)}, f32[17,32,512]{2,1,0:T(8,128)S(1)}, f32[17,32,512]{2,1,0:T(8,128)S(1)}) custom-call(s32[1]{0:T(128)} %bitcast.12.odd_ref, f32[6,4,32,512]{3,2,1,0:T(8,128)} %coup_hbm.3, s32[16,4,32,512]{3,2,1,0:T(8,128)} %bits_hbm.3, s32[32,512]{1,0:T(8,128)} %mask_hbm.3), custom_call_target="tpu_custom_call" | custom-call | flops 2516582 | bytes 2097152 | tf_op jit(solution)/shard_map/pallas_call | solution.py:427
  2.1 0.5 collective-permute-start.7
  2.6 5.1 %collective-permute-start.8 = (f32[17,32,512]{2,1,0:T(8,128)S(1)}, f32[17,32,512]{2,1,0:T(8,128)S(1)}, u32[]{:S(2)}, u32[]{:S(2)}) collective-permute-start(f32[17,32,512]{2,1,0:T(8,128)S(1)} %get-tuple-element.58), channel_id=1, source_target_pairs={{0,15},{1,2},{2,1},{3,4},{4,3},{5,6},{6,5},{7,8},{8,7},{9,10},{10,... | collective-permute-start | bytes 3342344 | tf_op jit(solution)/shard_map/ppermute | solution.py:21
  7.7 0.0 collective-permute-start.9
  7.7 2.0 %collective-permute-done.7.before_ref = f32[32,512]{1,0:T(8,128)S(1)} collective-permute-done((f32[32,512]{1,0:T(8,128)S(1)}, f32[32,512]{1,0:T(8,128)S(1)}, u32[]{:S(2)}, u32[]{:S(2)}) %collective-permute-start.7) | collective-permute-done | bytes 65568 | tf_op jit(solution)/shard_map/ppermute | solution.py:21
  9.6 2.7 %shard_map.40 = (f32[8,4,32,512]{3,2,1,0:T(8,128)S(1)}, f32[4,32,512]{2,1,0:T(8,128)S(1)}, f32[4,32,512]{2,1,0:T(8,128)S(1)}, f32[4,32,512]{2,1,0:T(8,128)S(1)}, s32[16,4,32,512]{3,2,1,0:T(8,128)S(1)}) custom-call(f32[6,4,32,512]{3,2,1,0:T(8,128)} %coup_hbm.3, s32[16,4,32,512]{3,2,1,0:T(8,128)} %bits_hbm.3, s32[32,512]{1,0:T(8,128)} %mask_hbm.3, ...), custom_call_target="tpu_custom_call" | custom-call | flops 75497472 | bytes 83886080 | tf_op jit(solution)/shard_map/pallas_call | solution.py:427
  12.4 5.1 %shard_map.41 = (f32[16,4,32,512]{3,2,1,0:T(8,128)S(1)}, f32[16,32,512]{2,1,0:T(8,128)S(1)}, f32[16,32,512]{2,1,0:T(8,128)S(1)}, f32[8,128]{1,0:T(8,128)S(1)}) custom-call(s32[1]{0:T(128)} %bitcast.12.odd_ref, s32[16,4,32,512]{3,2,1,0:T(8,128)S(1)} %get-tuple-element.52.bits_ref, f32[8,4,32,512]{3,2,1,0:T(8,128)S(1)} %get-tuple-element.53.planes_ref, ...), custom_call_target="tpu_custom_call" | custom-call | flops 15099494400 | bytes 16777216000 | tf_op jit(solution)/shard_map/pallas_call | solution.py:427
  17.5 0.4 collective-permute-start.11
  17.9 0.0 collective-permute-start.12
  17.9 3.7 %collective-permute-done.8.off_ref.doff_ref = f32[17,32,512]{2,1,0:T(8,128)S(1)} collective-permute-done((f32[17,32,512]{2,1,0:T(8,128)S(1)}, f32[17,32,512]{2,1,0:T(8,128)S(1)}, u32[]{:S(2)}, u32[]{:S(2)}) %collective-permute-start.8) | collective-permute-done | bytes 1114144 | tf_op jit(solution)/shard_map/ppermute | solution.py:21
  21.6 0.0 collective-permute-done.9.on_ref.don_ref
  21.6 22.4 %collective-permute-start.10 = (f32[8,128]{1,0:T(8,128)S(1)}, f32[8,128]{1,0:T(8,128)S(1)}, u32[]{:S(2)}, u32[]{:S(2)}) collective-permute-start(f32[8,128]{1,0:T(8,128)S(1)} %get-tuple-element.67), channel_id=1, source_target_pairs={{0,1},{1,0},{2,3},{3,2},{4,5},{5,4},{6,7},{7,6},{8,9},{9,8},{10,11... | collective-permute-start | bytes 12296 | tf_op jit(solution)/shard_map/ppermute | solution.py:21
  44.0 5.9 %shard_map.42 = (f32[16,2,32,512]{3,2,1,0:T(8,128)S(1)}, f32[16,2,32,512]{3,2,1,0:T(8,128)S(1)}, f32[16,2,32,512]{3,2,1,0:T(8,128)S(1)}, f32[16,2,32,512]{3,2,1,...) custom-call(s32[1]{0:T(128)} %bitcast.12.odd_ref, ...), custom_call_target="tpu_custom_call" | custom-call | flops 251658240 | bytes 251658240 | tf_op jit(solution)/shard_map/pallas_call | solution.py:427
  49.9 0.0 collective-permute-done.10.token_ref
  49.9 0.1 collective-permute-start.13
  50.0 0.0 collective-permute-done.11.off_ref
  50.0 0.0 collective-permute-done.12.on_ref
  50.0 5.7 %shard_map.43 = (f32[16,2,32,512]{3,2,1,0:T(8,128)S(1)}, f32[16,2,32,512]{3,2,1,0:T(8,128)S(1)}, f32[16,32,512]{2,1,0:T(8,128)S(1)}, f32[16,8,128]{2,1,0:T(8,128)S(1)}) custom-call(s32[1]{0:T(128)} %bitcast.12.odd_ref, f32[8,128]{1,0:T(8,128)S(1)} %collective-permute-done.10.token_ref, s32[16,4,32,512]{3,2,1,0:T(8,128)S(1)} %get-tuple-element.52.bits_ref, ...), custom_call_target="tpu_custom_call" | custom-call | flops 251658240 | bytes 251658240 | tf_op jit(solution)/shard_map/pallas_call | solution.py:427
  55.7 11.2 %collective-permute-done.13.high_ref = f32[16,32,512]{2,1,0:T(8,128)S(1)} collective-permute-done((f32[16,32,512]{2,1,0:T(8,128)S(1)}, f32[16,32,512]{2,1,0:T(8,128)S(1)}, u32[]{:S(2)}, u32[]{:S(2)}) %collective-permute-start.13) | collective-permute-done | bytes 1048608 | tf_op jit(solution)/shard_map/ppermute | solution.py:21
  66.9 0.2 shard_map.44
  67.2 0.0 collective-permute-start.16
  67.2 0.1 collective-permute-start.15
  67.3 1.8 %collective-permute-start.14 = (f32[8,128]{1,0:T(8,128)S(1)}, f32[8,128]{1,0:T(8,128)S(1)}, u32[]{:S(2)}, u32[]{:S(2)}) collective-permute-start(f32[8,128]{1,0:T(8,128)S(1)} %shard_map.44), channel_id=1, source_target_pairs={{0,1},{1,0},{2,3},{3,2},{4,5},{5,4},{6,7},{7,6},{8,9},{9,8},{10,11... | collective-permute-start | bytes 12296 | tf_op jit(solution)/shard_map/ppermute | solution.py:507
  69.0 1.2 %collective-permute-done.16 = f32[8,128]{1,0:T(8,128)S(1)} collective-permute-done((f32[8,128]{1,0:T(8,128)S(1)}, f32[8,128]{1,0:T(8,128)S(1)}, u32[]{:S(2)}, u32[]{:S(2)}) %collective-permute-start.16) | collective-permute-done | bytes 4128 | tf_op jit(solution)/shard_map/ppermute | solution.py:507
  70.2 0.7 collective-permute-done.15
  70.9 0.0 collective-permute-done.14
  70.9 7.5 %collective-permute-start.19 = (f32[8,128]{1,0:T(8,128)S(1)}, f32[8,128]{1,0:T(8,128)S(1)}, u32[]{:S(2)}, u32[]{:S(2)}) collective-permute-start(f32[8,128]{1,0:T(8,128)S(1)} %add_add_fusion.1.refs_0_), channel_id=1, source_target_pairs={{0,12},{1,13},{2,14},{3,15},{4,8},{5,9},{6,10},{7,11},{8,4},{9,5},... | collective-permute-start | bytes 12296 | tf_op jit(solution)/shard_map/ppermute | solution.py:507
  78.4 0.0 collective-permute-start.18
  78.4 0.6 collective-permute-start.17
  79.1 0.9 %collective-permute-done.19.refs_3_ = f32[8,128]{1,0:T(8,128)S(1)} collective-permute-done((f32[8,128]{1,0:T(8,128)S(1)}, f32[8,128]{1,0:T(8,128)S(1)}, u32[]{:S(2)}, u32[]{:S(2)}) %collective-permute-start.19) | collective-permute-done | bytes 4128 | tf_op jit(solution)/shard_map/ppermute | solution.py:507
  80.0 2.9 %collective-permute-done.18.refs_2_ = f32[8,128]{1,0:T(8,128)S(1)} collective-permute-done((f32[8,128]{1,0:T(8,128)S(1)}, f32[8,128]{1,0:T(8,128)S(1)}, u32[]{:S(2)}, u32[]{:S(2)}) %collective-permute-start.18) | collective-permute-done | bytes 4128 | tf_op jit(solution)/shard_map/ppermute | solution.py:507
  82.9 0.0 collective-permute-done.17.refs_1_
  82.9 1.1 %shard_map.45 = (f32[4,32,512]{2,1,0:T(8,128)S(1)}, s32[1]{0:T(128)}) custom-call(f32[16,2,32,512]{3,2,1,0:T(8,128)S(1)} %get-tuple-element.63.p1m_ref, f32[16,2,32,512]{3,2,1,0:T(8,128)S(1)} %get-tuple-element.64.p2m_ref, f32[16,2,32,512]{3,2,1,0:T(8,128)S(1)} %get-tuple-element.74.p1e_ref, f32[16,2,32,512]{3,2,1,0:T(8,128)S(1)} %get-tuple-element.75.p2e_ref, ...), custom_call_target="tpu_custom_call" | custom-call | flops 5033164 | bytes 8388608 | tf_op jit(solution)/shard_map/pallas_call | solution.py:427
  84.6 0.2 conditional.1
  84.9 0.0 copy-start.3
  84.9 0.7 copy-done.3
  (1 shorter events, 0.0 us)
Async XLA Ops:
  2.1 7.5 %collective-permute-start.7 = (f32[32,512]{1,0:T(8,128)S(1)}, f32[32,512]{1,0:T(8,128)S(1)}, u32[]{:S(2)}, u32[]{:S(2)}) collective-permute-start(f32[32,512]{1,0:T(8,128)S(1)} %get-tuple-element.51), channel_id=1, source_target_pairs={{0,1},{1,2},{2,3},{3,4},{4,5},{5,6},{6,7},{7,8},{8,9},{9,10},{10,1... | collective-permute-start | bytes 196616 | tf_op jit(solution)/shard_map/ppermute | solution.py:21
  2.6 19.0 %collective-permute-start.8 = (f32[17,32,512]{2,1,0:T(8,128)S(1)}, f32[17,32,512]{2,1,0:T(8,128)S(1)}, u32[]{:S(2)}, u32[]{:S(2)}) collective-permute-start(f32[17,32,512]{2,1,0:T(8,128)S(1)} %get-tuple-element.58), channel_id=1, source_target_pairs={{0,15},{1,2},{2,1},{3,4},{4,3},{5,6},{6,5},{7,8},{8,7},{9,10},{10,... | collective-permute-start | bytes 3342344 | tf_op jit(solution)/shard_map/ppermute | solution.py:21
  7.7 13.9 %collective-permute-start.9 = (f32[17,32,512]{2,1,0:T(8,128)S(1)}, f32[17,32,512]{2,1,0:T(8,128)S(1)}, u32[]{:S(2)}, u32[]{:S(2)}) collective-permute-start(f32[17,32,512]{2,1,0:T(8,128)S(1)} %get-tuple-element.59), channel_id=1, source_target_pairs={{0,1},{1,0},{2,3},{3,2},{4,5},{5,4},{6,7},{7,6},{8,9},{9,8},{10,11... | collective-permute-start | bytes 3342344 | tf_op jit(solution)/shard_map/ppermute | solution.py:21
  17.5 32.5 %collective-permute-start.11 = (f32[16,32,512]{2,1,0:T(8,128)S(1)}, f32[16,32,512]{2,1,0:T(8,128)S(1)}, u32[]{:S(2)}, u32[]{:S(2)}) collective-permute-start(f32[16,32,512]{2,1,0:T(8,128)S(1)} %get-tuple-element.71), channel_id=1, source_target_pairs={{0,15},{1,2},{2,1},{3,4},{4,3},{5,6},{6,5},{7,8},{8,7},{9,10},{10,... | collective-permute-start | bytes 3145736 | tf_op jit(solution)/shard_map/ppermute | solution.py:21
  17.9 32.1 %collective-permute-start.12 = (f32[16,32,512]{2,1,0:T(8,128)S(1)}, f32[16,32,512]{2,1,0:T(8,128)S(1)}, u32[]{:S(2)}, u32[]{:S(2)}) collective-permute-start(f32[16,32,512]{2,1,0:T(8,128)S(1)} %get-tuple-element.72), channel_id=1, source_target_pairs={{0,1},{1,0},{2,3},{3,2},{4,5},{5,4},{6,7},{7,6},{8,9},{9,8},{10,11... | collective-permute-start | bytes 3145736 | tf_op jit(solution)/shard_map/ppermute | solution.py:21
  21.6 28.4 %collective-permute-start.10 = (f32[8,128]{1,0:T(8,128)S(1)}, f32[8,128]{1,0:T(8,128)S(1)}, u32[]{:S(2)}, u32[]{:S(2)}) collective-permute-start(f32[8,128]{1,0:T(8,128)S(1)} %get-tuple-element.67), channel_id=1, source_target_pairs={{0,1},{1,0},{2,3},{3,2},{4,5},{5,4},{6,7},{7,6},{8,9},{9,8},{10,11... | collective-permute-start | bytes 12296 | tf_op jit(solution)/shard_map/ppermute | solution.py:21
  49.9 17.0 %collective-permute-start.13 = (f32[16,32,512]{2,1,0:T(8,128)S(1)}, f32[16,32,512]{2,1,0:T(8,128)S(1)}, u32[]{:S(2)}, u32[]{:S(2)}) collective-permute-start(f32[16,32,512]{2,1,0:T(8,128)S(1)} %get-tuple-element.77), channel_id=1, source_target_pairs={{0,1},{1,2},{2,3},{3,4},{4,5},{5,6},{6,7},{7,8},{8,9},{9,10},{10,1... | collective-permute-start | bytes 3145736 | tf_op jit(solution)/shard_map/ppermute | solution.py:21
  67.2 3.1 %collective-permute-start.16 = (f32[8,128]{1,0:T(8,128)S(1)}, f32[8,128]{1,0:T(8,128)S(1)}, u32[]{:S(2)}, u32[]{:S(2)}) collective-permute-start(f32[8,128]{1,0:T(8,128)S(1)} %shard_map.44), channel_id=1, source_target_pairs={{0,3},{1,2},{2,1},{3,0},{4,7},{5,6},{6,5},{7,4},{8,11},{9,10},{10,... | collective-permute-start | bytes 12296 | tf_op jit(solution)/shard_map/ppermute | solution.py:507
  67.2 3.7 %collective-permute-start.15 = (f32[8,128]{1,0:T(8,128)S(1)}, f32[8,128]{1,0:T(8,128)S(1)}, u32[]{:S(2)}, u32[]{:S(2)}) collective-permute-start(f32[8,128]{1,0:T(8,128)S(1)} %shard_map.44), channel_id=1, source_target_pairs={{0,2},{1,3},{2,0},{3,1},{4,6},{5,7},{6,4},{7,5},{8,10},{9,11},{10,... | collective-permute-start | bytes 12296 | tf_op jit(solution)/shard_map/ppermute | solution.py:507
  67.3 3.6 %collective-permute-start.14 = (f32[8,128]{1,0:T(8,128)S(1)}, f32[8,128]{1,0:T(8,128)S(1)}, u32[]{:S(2)}, u32[]{:S(2)}) collective-permute-start(f32[8,128]{1,0:T(8,128)S(1)} %shard_map.44), channel_id=1, source_target_pairs={{0,1},{1,0},{2,3},{3,2},{4,5},{5,4},{6,7},{7,6},{8,9},{9,8},{10,11... | collective-permute-start | bytes 12296 | tf_op jit(solution)/shard_map/ppermute | solution.py:507
  70.9 9.1 %collective-permute-start.19 = (f32[8,128]{1,0:T(8,128)S(1)}, f32[8,128]{1,0:T(8,128)S(1)}, u32[]{:S(2)}, u32[]{:S(2)}) collective-permute-start(f32[8,128]{1,0:T(8,128)S(1)} %add_add_fusion.1.refs_0_), channel_id=1, source_target_pairs={{0,12},{1,13},{2,14},{3,15},{4,8},{5,9},{6,10},{7,11},{8,4},{9,5},... | collective-permute-start | bytes 12296 | tf_op jit(solution)/shard_map/ppermute | solution.py:507
  78.4 4.5 %collective-permute-start.18 = (f32[8,128]{1,0:T(8,128)S(1)}, f32[8,128]{1,0:T(8,128)S(1)}, u32[]{:S(2)}, u32[]{:S(2)}) collective-permute-start(f32[8,128]{1,0:T(8,128)S(1)} %add_add_fusion.1.refs_0_), channel_id=1, source_target_pairs={{0,8},{1,9},{2,10},{3,11},{4,12},{5,13},{6,14},{7,15},{8,0},{9,1},... | collective-permute-start | bytes 12296 | tf_op jit(solution)/shard_map/ppermute | solution.py:507
  78.4 4.5 %collective-permute-start.17 = (f32[8,128]{1,0:T(8,128)S(1)}, f32[8,128]{1,0:T(8,128)S(1)}, u32[]{:S(2)}, u32[]{:S(2)}) collective-permute-start(f32[8,128]{1,0:T(8,128)S(1)} %add_add_fusion.1.refs_0_), channel_id=1, source_target_pairs={{0,4},{1,5},{2,6},{3,7},{4,0},{5,1},{6,2},{7,3},{8,12},{9,13},{10,... | collective-permute-start | bytes 12296 | tf_op jit(solution)/shard_map/ppermute | solution.py:507
  84.9 0.7 copy-start.3

commit v14 on v12

--- a/solution.py
+++ b/solution.py
@@ -505,10 +505,11 @@
     while step < count:
         near = min(4, count // step)
         moments = paired_sum(shares)
-        shares = [moments] + [
+        shares = [
             lax.ppermute(moments, "day", [(i, i ^ (n * step)) for i in range(count)])
-            for n in range(1, near)
+            for n in range(near - 1, 0, -1)
         ]
+        shares = shares + [moments]
         step *= near
     out, unsound = call(
         last_kernel, (1,),

time: 82.7 us -> 83.6 us (1.011)
  waiting for transfers between devices: 22.4 us -> 23.3 us
    ppermute x6, waiting for transfers between devices: 3.41 us -> 4.28 us  [body(): lax.ppermute(moments, 'day', [(i, i ^ n * step) for i in range(count)])]
  transfers between devices with their start and end apart: 13 -> 13, of which waited for: 7 -> 6; matrix products, arithmetic and copies ran while one was open for 0% -> 0% of each run, Pallas kernels for 24% -> 24%
where the time goes in v14:
time: 83.6 us; the launch traced here: 83.4 us
  starting transfers between devices  34.8 us (42%)
  Pallas kernels  23.6 us (28%)
  waiting for transfers between devices  23.3 us (28%)
    ppermute x7, starting transfers between devices, moved(): return lax.ppermute(value, 'day', [(i, target(i)) for i in range(count)])  28.5 us
    pallas_call x7, Pallas kernels, call(): pl.pallas_call(kernel, grid=grid, in_specs=[spec(value.shape, kind) for v...  23.6 us
    ppermute x7, waiting for transfers between devices, moved(): return lax.ppermute(value, 'day', [(i, target(i)) for i in range(count)])  19 us
    ppermute x6, starting transfers between devices, body(): lax.ppermute(moments, 'day', [(i, i ^ n * step) for i in range(count)])  6.32 us
    ppermute x6, waiting for transfers between devices, body(): lax.ppermute(moments, 'day', [(i, i ^ n * step) for i in range(count)])  4.28 us
  transfers between devices with their start and end apart: 13, of which 6 were waited for; matrix products, arithmetic and copies ran while one was open for 0% of the time, Pallas kernels for 24%

profile of v14, /device:TPU:0, one launch (start us, length us, event | category | flops | bytes accessed | tf_op | source)
XLA Modules:
  0.0 83.4 jit_solution(17921518425291543208)
XLA Ops:
  0.0 2.1 %shard_map.39 = (f32[32,512]{1,0:T(8,128)S(1)}, f32[17,32,512]{2,1,0:T(8,128)S(1)}, f32[17,32,512]{2,1,0:T(8,128)S(1)}) custom-call(s32[1]{0:T(128)} %bitcast.12.odd_ref, f32[6,4,32,512]{3,2,1,0:T(8,128)} %coup_hbm.3, s32[16,4,32,512]{3,2,1,0:T(8,128)} %bits_hbm.3, s32[32,512]{1,0:T(8,128)} %mask_hbm.3), custom_call_target="tpu_custom_call" | custom-call | flops 2516582 | bytes 2097152 | tf_op jit(solution)/shard_map/pallas_call | solution.py:428
  2.1 0.5 collective-permute-start.7
  2.6 5.1 %collective-permute-start.8 = (f32[17,32,512]{2,1,0:T(8,128)S(1)}, f32[17,32,512]{2,1,0:T(8,128)S(1)}, u32[]{:S(2)}, u32[]{:S(2)}) collective-permute-start(f32[17,32,512]{2,1,0:T(8,128)S(1)} %get-tuple-element.59), channel_id=1, source_target_pairs={{0,15},{1,2},{2,1},{3,4},{4,3},{5,6},{6,5},{7,8},{8,7},{9,10},{10,... | collective-permute-start | bytes 3342344 | tf_op jit(solution)/shard_map/ppermute | solution.py:21
  7.7 0.0 collective-permute-start.9
  7.7 2.0 %collective-permute-done.7.before_ref = f32[32,512]{1,0:T(8,128)S(1)} collective-permute-done((f32[32,512]{1,0:T(8,128)S(1)}, f32[32,512]{1,0:T(8,128)S(1)}, u32[]{:S(2)}, u32[]{:S(2)}) %collective-permute-start.7) | collective-permute-done | bytes 65568 | tf_op jit(solution)/shard_map/ppermute | solution.py:21
  9.6 2.7 %shard_map.40 = (f32[8,4,32,512]{3,2,1,0:T(8,128)S(1)}, f32[4,32,512]{2,1,0:T(8,128)S(1)}, f32[4,32,512]{2,1,0:T(8,128)S(1)}, f32[4,32,512]{2,1,0:T(8,128)S(1)}, s32[16,4,32,512]{3,2,1,0:T(8,128)S(1)}) custom-call(f32[6,4,32,512]{3,2,1,0:T(8,128)} %coup_hbm.3, s32[16,4,32,512]{3,2,1,0:T(8,128)} %bits_hbm.3, s32[32,512]{1,0:T(8,128)} %mask_hbm.3, ...), custom_call_target="tpu_custom_call" | custom-call | flops 75497472 | bytes 83886080 | tf_op jit(solution)/shard_map/pallas_call | solution.py:428
  12.4 5.1 %shard_map.41 = (f32[16,4,32,512]{3,2,1,0:T(8,128)S(1)}, f32[16,32,512]{2,1,0:T(8,128)S(1)}, f32[16,32,512]{2,1,0:T(8,128)S(1)}, f32[8,128]{1,0:T(8,128)S(1)}) custom-call(s32[1]{0:T(128)} %bitcast.12.odd_ref, s32[16,4,32,512]{3,2,1,0:T(8,128)S(1)} %get-tuple-element.53.bits_ref, f32[8,4,32,512]{3,2,1,0:T(8,128)S(1)} %get-tuple-element.54.planes_ref, ...), custom_call_target="tpu_custom_call" | custom-call | flops 15099494400 | bytes 16777216000 | tf_op jit(solution)/shard_map/pallas_call | solution.py:428
  17.5 0.4 collective-permute-start.11
  17.9 0.0 collective-permute-start.12
  17.9 3.7 %collective-permute-done.8.off_ref.doff_ref = f32[17,32,512]{2,1,0:T(8,128)S(1)} collective-permute-done((f32[17,32,512]{2,1,0:T(8,128)S(1)}, f32[17,32,512]{2,1,0:T(8,128)S(1)}, u32[]{:S(2)}, u32[]{:S(2)}) %collective-permute-start.8) | collective-permute-done | bytes 1114144 | tf_op jit(solution)/shard_map/ppermute | solution.py:21
  21.6 0.0 collective-permute-done.9.on_ref.don_ref
  21.6 22.4 %collective-permute-start.10 = (f32[8,128]{1,0:T(8,128)S(1)}, f32[8,128]{1,0:T(8,128)S(1)}, u32[]{:S(2)}, u32[]{:S(2)}) collective-permute-start(f32[8,128]{1,0:T(8,128)S(1)} %get-tuple-element.68), channel_id=1, source_target_pairs={{0,1},{1,0},{2,3},{3,2},{4,5},{5,4},{6,7},{7,6},{8,9},{9,8},{10,11... | collective-permute-start | bytes 12296 | tf_op jit(solution)/shard_map/ppermute | solution.py:21
  44.0 8.9 %shard_map.42 = (f32[16,2,32,512]{3,2,1,0:T(8,128)S(1)}, f32[16,2,32,512]{3,2,1,0:T(8,128)S(1)}, f32[16,2,32,512]{3,2,1,0:T(8,128)S(1)}, f32[16,2,32,512]{3,2,1,...) custom-call(s32[1]{0:T(128)} %bitcast.12.odd_ref, ...), custom_call_target="tpu_custom_call" | custom-call | flops 251658240 | bytes 251658240 | tf_op jit(solution)/shard_map/pallas_call | solution.py:428
  52.9 0.0 collective-permute-done.10.token_ref
  52.9 0.1 collective-permute-start.13
  53.0 0.0 collective-permute-done.11.off_ref
  53.0 0.0 collective-permute-done.12.on_ref
  53.0 3.5 %shard_map.43 = (f32[16,2,32,512]{3,2,1,0:T(8,128)S(1)}, f32[16,2,32,512]{3,2,1,0:T(8,128)S(1)}, f32[16,32,512]{2,1,0:T(8,128)S(1)}, f32[16,8,128]{2,1,0:T(8,128)S(1)}) custom-call(s32[1]{0:T(128)} %bitcast.12.odd_ref, f32[8,128]{1,0:T(8,128)S(1)} %collective-permute-done.10.token_ref, s32[16,4,32,512]{3,2,1,0:T(8,128)S(1)} %get-tuple-element.53.bits_ref, ...), custom_call_target="tpu_custom_call" | custom-call | flops 251658240 | bytes 251658240 | tf_op jit(solution)/shard_map/pallas_call | solution.py:428
  56.5 13.4 %collective-permute-done.13.high_ref = f32[16,32,512]{2,1,0:T(8,128)S(1)} collective-permute-done((f32[16,32,512]{2,1,0:T(8,128)S(1)}, f32[16,32,512]{2,1,0:T(8,128)S(1)}, u32[]{:S(2)}, u32[]{:S(2)}) %collective-permute-start.13) | collective-permute-done | bytes 1048608 | tf_op jit(solution)/shard_map/ppermute | solution.py:21
  69.9 0.2 shard_map.44
  70.1 0.0 collective-permute-start.16
  70.2 0.1 collective-permute-start.15
  70.2 1.8 %collective-permute-start.14 = (f32[8,128]{1,0:T(8,128)S(1)}, f32[8,128]{1,0:T(8,128)S(1)}, u32[]{:S(2)}, u32[]{:S(2)}) collective-permute-start(f32[8,128]{1,0:T(8,128)S(1)} %shard_map.44), channel_id=1, source_target_pairs={{0,3},{1,2},{2,1},{3,0},{4,7},{5,6},{6,5},{7,4},{8,11},{9,10},{10,... | collective-permute-start | bytes 12296 | tf_op jit(solution)/shard_map/ppermute | solution.py:509
  72.0 0.0 collective-permute-done.16
  72.0 1.8 %collective-permute-done.15 = f32[8,128]{1,0:T(8,128)S(1)} collective-permute-done((f32[8,128]{1,0:T(8,128)S(1)}, f32[8,128]{1,0:T(8,128)S(1)}, u32[]{:S(2)}, u32[]{:S(2)}) %collective-permute-start.15) | collective-permute-done | bytes 4128 | tf_op jit(solution)/shard_map/ppermute | solution.py:509
  73.8 0.0 collective-permute-done.14
  73.8 0.1 collective-permute-start.19
  73.9 1.4 %collective-permute-start.18 = (f32[8,128]{1,0:T(8,128)S(1)}, f32[8,128]{1,0:T(8,128)S(1)}, u32[]{:S(2)}, u32[]{:S(2)}) collective-permute-start(f32[8,128]{1,0:T(8,128)S(1)} %add_add_fusion.1.refs_3_), channel_id=1, source_target_pairs={{0,8},{1,9},{2,10},{3,11},{4,12},{5,13},{6,14},{7,15},{8,0},{9,1},... | collective-permute-start | bytes 12296 | tf_op jit(solution)/shard_map/ppermute | solution.py:509
  75.4 2.9 %collective-permute-start.17 = (f32[8,128]{1,0:T(8,128)S(1)}, f32[8,128]{1,0:T(8,128)S(1)}, u32[]{:S(2)}, u32[]{:S(2)}) collective-permute-start(f32[8,128]{1,0:T(8,128)S(1)} %add_add_fusion.1.refs_3_), channel_id=1, source_target_pairs={{0,12},{1,13},{2,14},{3,15},{4,8},{5,9},{6,10},{7,11},{8,4},{9,5},... | collective-permute-start | bytes 12296 | tf_op jit(solution)/shard_map/ppermute | solution.py:509
  78.3 0.0 collective-permute-done.19.refs_2_
  78.3 0.2 collective-permute-done.18.refs_1_
  78.5 2.3 %collective-permute-done.17.refs_0_ = f32[8,128]{1,0:T(8,128)S(1)} collective-permute-done((f32[8,128]{1,0:T(8,128)S(1)}, f32[8,128]{1,0:T(8,128)S(1)}, u32[]{:S(2)}, u32[]{:S(2)}) %collective-permute-start.17) | collective-permute-done | bytes 4128 | tf_op jit(solution)/shard_map/ppermute | solution.py:509
  80.8 1.1 %shard_map.45 = (f32[4,32,512]{2,1,0:T(8,128)S(1)}, s32[1]{0:T(128)}) custom-call(f32[16,2,32,512]{3,2,1,0:T(8,128)S(1)} %get-tuple-element.64.p1m_ref, f32[16,2,32,512]{3,2,1,0:T(8,128)S(1)} %get-tuple-element.65.p2m_ref, f32[16,2,32,512]{3,2,1,0:T(8,128)S(1)} %get-tuple-element.76.p1e_ref, f32[16,2,32,512]{3,2,1,0:T(8,128)S(1)} %get-tuple-element.77.p2e_ref, ...), custom_call_target="tpu_custom_call" | custom-call | flops 5033164 | bytes 8388608 | tf_op jit(solution)/shard_map/pallas_call | solution.py:428
  82.5 0.2 conditional.1
  82.7 0.0 copy-start.3
  82.7 0.7 copy-done.3
  (1 shorter events, 0.0 us)
Async XLA Ops:
  2.1 7.5 %collective-permute-start.7 = (f32[32,512]{1,0:T(8,128)S(1)}, f32[32,512]{1,0:T(8,128)S(1)}, u32[]{:S(2)}, u32[]{:S(2)}) collective-permute-start(f32[32,512]{1,0:T(8,128)S(1)} %get-tuple-element.52), channel_id=1, source_target_pairs={{0,1},{1,2},{2,3},{3,4},{4,5},{5,6},{6,7},{7,8},{8,9},{9,10},{10,1... | collective-permute-start | bytes 196616 | tf_op jit(solution)/shard_map/ppermute | solution.py:21
  2.6 19.0 %collective-permute-start.8 = (f32[17,32,512]{2,1,0:T(8,128)S(1)}, f32[17,32,512]{2,1,0:T(8,128)S(1)}, u32[]{:S(2)}, u32[]{:S(2)}) collective-permute-start(f32[17,32,512]{2,1,0:T(8,128)S(1)} %get-tuple-element.59), channel_id=1, source_target_pairs={{0,15},{1,2},{2,1},{3,4},{4,3},{5,6},{6,5},{7,8},{8,7},{9,10},{10,... | collective-permute-start | bytes 3342344 | tf_op jit(solution)/shard_map/ppermute | solution.py:21
  7.7 13.9 %collective-permute-start.9 = (f32[17,32,512]{2,1,0:T(8,128)S(1)}, f32[17,32,512]{2,1,0:T(8,128)S(1)}, u32[]{:S(2)}, u32[]{:S(2)}) collective-permute-start(f32[17,32,512]{2,1,0:T(8,128)S(1)} %get-tuple-element.60), channel_id=1, source_target_pairs={{0,1},{1,0},{2,3},{3,2},{4,5},{5,4},{6,7},{7,6},{8,9},{9,8},{10,11... | collective-permute-start | bytes 3342344 | tf_op jit(solution)/shard_map/ppermute | solution.py:21
  17.5 35.5 %collective-permute-start.11 = (f32[16,32,512]{2,1,0:T(8,128)S(1)}, f32[16,32,512]{2,1,0:T(8,128)S(1)}, u32[]{:S(2)}, u32[]{:S(2)}) collective-permute-start(f32[16,32,512]{2,1,0:T(8,128)S(1)} %get-tuple-element.72), channel_id=1, source_target_pairs={{0,15},{1,2},{2,1},{3,4},{4,3},{5,6},{6,5},{7,8},{8,7},{9,10},{10,... | collective-permute-start | bytes 3145736 | tf_op jit(solution)/shard_map/ppermute | solution.py:21
  17.9 35.1 %collective-permute-start.12 = (f32[16,32,512]{2,1,0:T(8,128)S(1)}, f32[16,32,512]{2,1,0:T(8,128)S(1)}, u32[]{:S(2)}, u32[]{:S(2)}) collective-permute-start(f32[16,32,512]{2,1,0:T(8,128)S(1)} %get-tuple-element.73), channel_id=1, source_target_pairs={{0,1},{1,0},{2,3},{3,2},{4,5},{5,4},{6,7},{7,6},{8,9},{9,8},{10,11... | collective-permute-start | bytes 3145736 | tf_op jit(solution)/shard_map/ppermute | solution.py:21
  21.6 31.3 %collective-permute-start.10 = (f32[8,128]{1,0:T(8,128)S(1)}, f32[8,128]{1,0:T(8,128)S(1)}, u32[]{:S(2)}, u32[]{:S(2)}) collective-permute-start(f32[8,128]{1,0:T(8,128)S(1)} %get-tuple-element.68), channel_id=1, source_target_pairs={{0,1},{1,0},{2,3},{3,2},{4,5},{5,4},{6,7},{7,6},{8,9},{9,8},{10,11... | collective-permute-start | bytes 12296 | tf_op jit(solution)/shard_map/ppermute | solution.py:21
  52.9 17.0 %collective-permute-start.13 = (f32[16,32,512]{2,1,0:T(8,128)S(1)}, f32[16,32,512]{2,1,0:T(8,128)S(1)}, u32[]{:S(2)}, u32[]{:S(2)}) collective-permute-start(f32[16,32,512]{2,1,0:T(8,128)S(1)} %get-tuple-element.79), channel_id=1, source_target_pairs={{0,1},{1,2},{2,3},{3,4},{4,5},{5,6},{6,7},{7,8},{8,9},{9,10},{10,1... | collective-permute-start | bytes 3145736 | tf_op jit(solution)/shard_map/ppermute | solution.py:21
  70.1 1.9 %collective-permute-start.16 = (f32[8,128]{1,0:T(8,128)S(1)}, f32[8,128]{1,0:T(8,128)S(1)}, u32[]{:S(2)}, u32[]{:S(2)}) collective-permute-start(f32[8,128]{1,0:T(8,128)S(1)} %shard_map.44), channel_id=1, source_target_pairs={{0,1},{1,0},{2,3},{3,2},{4,5},{5,4},{6,7},{7,6},{8,9},{9,8},{10,11... | collective-permute-start | bytes 12296 | tf_op jit(solution)/shard_map/ppermute | solution.py:509
  70.2 3.7 %collective-permute-start.15 = (f32[8,128]{1,0:T(8,128)S(1)}, f32[8,128]{1,0:T(8,128)S(1)}, u32[]{:S(2)}, u32[]{:S(2)}) collective-permute-start(f32[8,128]{1,0:T(8,128)S(1)} %shard_map.44), channel_id=1, source_target_pairs={{0,2},{1,3},{2,0},{3,1},{4,6},{5,7},{6,4},{7,5},{8,10},{9,11},{10,... | collective-permute-start | bytes 12296 | tf_op jit(solution)/shard_map/ppermute | solution.py:509
  70.2 3.6 %collective-permute-start.14 = (f32[8,128]{1,0:T(8,128)S(1)}, f32[8,128]{1,0:T(8,128)S(1)}, u32[]{:S(2)}, u32[]{:S(2)}) collective-permute-start(f32[8,128]{1,0:T(8,128)S(1)} %shard_map.44), channel_id=1, source_target_pairs={{0,3},{1,2},{2,1},{3,0},{4,7},{5,6},{6,5},{7,4},{8,11},{9,10},{10,... | collective-permute-start | bytes 12296 | tf_op jit(solution)/shard_map/ppermute | solution.py:509
  73.8 4.5 %collective-permute-start.19 = (f32[8,128]{1,0:T(8,128)S(1)}, f32[8,128]{1,0:T(8,128)S(1)}, u32[]{:S(2)}, u32[]{:S(2)}) collective-permute-start(f32[8,128]{1,0:T(8,128)S(1)} %add_add_fusion.1.refs_3_), channel_id=1, source_target_pairs={{0,4},{1,5},{2,6},{3,7},{4,0},{5,1},{6,2},{7,3},{8,12},{9,13},{10,... | collective-permute-start | bytes 12296 | tf_op jit(solution)/shard_map/ppermute | solution.py:509
  73.9 4.6 %collective-permute-start.18 = (f32[8,128]{1,0:T(8,128)S(1)}, f32[8,128]{1,0:T(8,128)S(1)}, u32[]{:S(2)}, u32[]{:S(2)}) collective-permute-start(f32[8,128]{1,0:T(8,128)S(1)} %add_add_fusion.1.refs_3_), channel_id=1, source_target_pairs={{0,8},{1,9},{2,10},{3,11},{4,12},{5,13},{6,14},{7,15},{8,0},{9,1},... | collective-permute-start | bytes 12296 | tf_op jit(solution)/shard_map/ppermute | solution.py:509
  75.4 5.4 %collective-permute-start.17 = (f32[8,128]{1,0:T(8,128)S(1)}, f32[8,128]{1,0:T(8,128)S(1)}, u32[]{:S(2)}, u32[]{:S(2)}) collective-permute-start(f32[8,128]{1,0:T(8,128)S(1)} %add_add_fusion.1.refs_3_), channel_id=1, source_target_pairs={{0,12},{1,13},{2,14},{3,15},{4,8},{5,9},{6,10},{7,11},{8,4},{9,5},... | collective-permute-start | bytes 12296 | tf_op jit(solution)/shard_map/ppermute | solution.py:509
  82.7 0.7 copy-start.3

commit v15 on v12

--- a/solution.py
+++ b/solution.py
@@ -509,6 +509,8 @@
             lax.ppermute(moments, "day", [(i, i ^ (n * step)) for i in range(count)])
             for n in range(1, near)
         ]
+        if step > 1 and near == 4:
+            shares = shares[:2] + shares[:1:-1]
         step *= near
     out, unsound = call(
         last_kernel, (1,),

time: 82.7 us -> 82.2 us (level)
  starting transfers between devices: 34.8 us -> 33.9 us
    ppermute x6, starting transfers between devices: 6.32 us -> 5.41 us  [body(): lax.ppermute(moments, 'day', [(i, i ^ n * step) for i in range(count)])]
  transfers between devices with their start and end apart: 13 -> 13, of which waited for: 7 -> 7; matrix products, arithmetic and copies ran while one was open for 0% -> 0% of each run, Pallas kernels for 24% -> 25%
where the time goes in v15:
time: 82.2 us; the launch traced here: 82.1 us
  starting transfers between devices  33.9 us (41%)
  Pallas kernels  23.6 us (29%)
  waiting for transfers between devices  22.9 us (28%)
    ppermute x7, starting transfers between devices, moved(): return lax.ppermute(value, 'day', [(i, target(i)) for i in range(count)])  28.5 us
    pallas_call x7, Pallas kernels, call(): pl.pallas_call(kernel, grid=grid, in_specs=[spec(value.shape, kind) for v...  23.6 us
    ppermute x7, waiting for transfers between devices, moved(): return lax.ppermute(value, 'day', [(i, target(i)) for i in range(count)])  19 us
    ppermute x6, starting transfers between devices, body(): lax.ppermute(moments, 'day', [(i, i ^ n * step) for i in range(count)])  5.41 us
    ppermute x6, waiting for transfers between devices, body(): lax.ppermute(moments, 'day', [(i, i ^ n * step) for i in range(count)])  3.82 us
  transfers between devices with their start and end apart: 13, of which 7 were waited for; matrix products, arithmetic and copies ran while one was open for 0% of the time, Pallas kernels for 25%

profile of v15, /device:TPU:0, one launch (start us, length us, event | category | flops | bytes accessed | tf_op | source)
XLA Modules:
  0.0 82.1 jit_solution(6887267943365693819)
XLA Ops:
  0.0 2.1 %shard_map.39 = (f32[32,512]{1,0:T(8,128)S(1)}, f32[17,32,512]{2,1,0:T(8,128)S(1)}, f32[17,32,512]{2,1,0:T(8,128)S(1)}) custom-call(s32[1]{0:T(128)} %bitcast.12.odd_ref, f32[6,4,32,512]{3,2,1,0:T(8,128)} %coup_hbm.3, s32[16,4,32,512]{3,2,1,0:T(8,128)} %bits_hbm.3, s32[32,512]{1,0:T(8,128)} %mask_hbm.3), custom_call_target="tpu_custom_call" | custom-call | flops 2516582 | bytes 2097152 | tf_op jit(solution)/shard_map/pallas_call | solution.py:428
  2.1 0.5 collective-permute-start.7
  2.6 5.1 %collective-permute-start.8 = (f32[17,32,512]{2,1,0:T(8,128)S(1)}, f32[17,32,512]{2,1,0:T(8,128)S(1)}, u32[]{:S(2)}, u32[]{:S(2)}) collective-permute-start(f32[17,32,512]{2,1,0:T(8,128)S(1)} %get-tuple-element.59), channel_id=1, source_target_pairs={{0,15},{1,2},{2,1},{3,4},{4,3},{5,6},{6,5},{7,8},{8,7},{9,10},{10,... | collective-permute-start | bytes 3342344 | tf_op jit(solution)/shard_map/ppermute | solution.py:21
  7.7 0.0 collective-permute-start.9
  7.7 2.0 %collective-permute-done.7.before_ref = f32[32,512]{1,0:T(8,128)S(1)} collective-permute-done((f32[32,512]{1,0:T(8,128)S(1)}, f32[32,512]{1,0:T(8,128)S(1)}, u32[]{:S(2)}, u32[]{:S(2)}) %collective-permute-start.7) | collective-permute-done | bytes 65568 | tf_op jit(solution)/shard_map/ppermute | solution.py:21
  9.6 2.7 %shard_map.40 = (f32[8,4,32,512]{3,2,1,0:T(8,128)S(1)}, f32[4,32,512]{2,1,0:T(8,128)S(1)}, f32[4,32,512]{2,1,0:T(8,128)S(1)}, f32[4,32,512]{2,1,0:T(8,128)S(1)}, s32[16,4,32,512]{3,2,1,0:T(8,128)S(1)}) custom-call(f32[6,4,32,512]{3,2,1,0:T(8,128)} %coup_hbm.3, s32[16,4,32,512]{3,2,1,0:T(8,128)} %bits_hbm.3, s32[32,512]{1,0:T(8,128)} %mask_hbm.3, ...), custom_call_target="tpu_custom_call" | custom-call | flops 75497472 | bytes 83886080 | tf_op jit(solution)/shard_map/pallas_call | solution.py:428
  12.4 5.1 %shard_map.41 = (f32[16,4,32,512]{3,2,1,0:T(8,128)S(1)}, f32[16,32,512]{2,1,0:T(8,128)S(1)}, f32[16,32,512]{2,1,0:T(8,128)S(1)}, f32[8,128]{1,0:T(8,128)S(1)}) custom-call(s32[1]{0:T(128)} %bitcast.12.odd_ref, s32[16,4,32,512]{3,2,1,0:T(8,128)S(1)} %get-tuple-element.53.bits_ref, f32[8,4,32,512]{3,2,1,0:T(8,128)S(1)} %get-tuple-element.54.planes_ref, ...), custom_call_target="tpu_custom_call" | custom-call | flops 15099494400 | bytes 16777216000 | tf_op jit(solution)/shard_map/pallas_call | solution.py:428
  17.5 0.4 collective-permute-start.11
  17.9 0.0 collective-permute-start.12
  17.9 3.7 %collective-permute-done.8.off_ref.doff_ref = f32[17,32,512]{2,1,0:T(8,128)S(1)} collective-permute-done((f32[17,32,512]{2,1,0:T(8,128)S(1)}, f32[17,32,512]{2,1,0:T(8,128)S(1)}, u32[]{:S(2)}, u32[]{:S(2)}) %collective-permute-start.8) | collective-permute-done | bytes 1114144 | tf_op jit(solution)/shard_map/ppermute | solution.py:21
  21.6 0.0 collective-permute-done.9.on_ref.don_ref
  21.6 22.4 %collective-permute-start.10 = (f32[8,128]{1,0:T(8,128)S(1)}, f32[8,128]{1,0:T(8,128)S(1)}, u32[]{:S(2)}, u32[]{:S(2)}) collective-permute-start(f32[8,128]{1,0:T(8,128)S(1)} %get-tuple-element.68), channel_id=1, source_target_pairs={{0,1},{1,0},{2,3},{3,2},{4,5},{5,4},{6,7},{7,6},{8,9},{9,8},{10,11... | collective-permute-start | bytes 12296 | tf_op jit(solution)/shard_map/ppermute | solution.py:21
  44.0 8.9 %shard_map.42 = (f32[16,2,32,512]{3,2,1,0:T(8,128)S(1)}, f32[16,2,32,512]{3,2,1,0:T(8,128)S(1)}, f32[16,2,32,512]{3,2,1,0:T(8,128)S(1)}, f32[16,2,32,512]{3,2,1,...) custom-call(s32[1]{0:T(128)} %bitcast.12.odd_ref, ...), custom_call_target="tpu_custom_call" | custom-call | flops 251658240 | bytes 251658240 | tf_op jit(solution)/shard_map/pallas_call | solution.py:428
  52.9 0.0 collective-permute-done.10.token_ref
  52.9 0.1 collective-permute-start.13
  53.0 0.0 collective-permute-done.11.off_ref
  53.0 0.0 collective-permute-done.12.on_ref
  53.0 3.5 %shard_map.43 = (f32[16,2,32,512]{3,2,1,0:T(8,128)S(1)}, f32[16,2,32,512]{3,2,1,0:T(8,128)S(1)}, f32[16,32,512]{2,1,0:T(8,128)S(1)}, f32[16,8,128]{2,1,0:T(8,128)S(1)}) custom-call(s32[1]{0:T(128)} %bitcast.12.odd_ref, f32[8,128]{1,0:T(8,128)S(1)} %collective-permute-done.10.token_ref, s32[16,4,32,512]{3,2,1,0:T(8,128)S(1)} %get-tuple-element.53.bits_ref, ...), custom_call_target="tpu_custom_call" | custom-call | flops 251658240 | bytes 251658240 | tf_op jit(solution)/shard_map/pallas_call | solution.py:428
  56.5 13.4 %collective-permute-done.13.high_ref = f32[16,32,512]{2,1,0:T(8,128)S(1)} collective-permute-done((f32[16,32,512]{2,1,0:T(8,128)S(1)}, f32[16,32,512]{2,1,0:T(8,128)S(1)}, u32[]{:S(2)}, u32[]{:S(2)}) %collective-permute-start.13) | collective-permute-done | bytes 1048608 | tf_op jit(solution)/shard_map/ppermute | solution.py:21
  69.9 0.2 shard_map.44
  70.2 0.0 collective-permute-start.16
  70.2 0.1 collective-permute-start.15
  70.3 1.8 %collective-permute-start.14 = (f32[8,128]{1,0:T(8,128)S(1)}, f32[8,128]{1,0:T(8,128)S(1)}, u32[]{:S(2)}, u32[]{:S(2)}) collective-permute-start(f32[8,128]{1,0:T(8,128)S(1)} %shard_map.44), channel_id=1, source_target_pairs={{0,1},{1,0},{2,3},{3,2},{4,5},{5,4},{6,7},{7,6},{8,9},{9,8},{10,11... | collective-permute-start | bytes 12296 | tf_op jit(solution)/shard_map/ppermute | solution.py:509
  72.1 1.2 %collective-permute-done.16 = f32[8,128]{1,0:T(8,128)S(1)} collective-permute-done((f32[8,128]{1,0:T(8,128)S(1)}, f32[8,128]{1,0:T(8,128)S(1)}, u32[]{:S(2)}, u32[]{:S(2)}) %collective-permute-start.16) | collective-permute-done | bytes 4128 | tf_op jit(solution)/shard_map/ppermute | solution.py:509
  73.2 0.7 collective-permute-done.15
  73.9 0.0 collective-permute-done.14
  73.9 0.1 collective-permute-start.19
  74.0 1.2 %collective-permute-start.18 = (f32[8,128]{1,0:T(8,128)S(1)}, f32[8,128]{1,0:T(8,128)S(1)}, u32[]{:S(2)}, u32[]{:S(2)}) collective-permute-start(f32[8,128]{1,0:T(8,128)S(1)} %add_add_fusion.1.refs_0_), channel_id=1, source_target_pairs={{0,12},{1,13},{2,14},{3,15},{4,8},{5,9},{6,10},{7,11},{8,4},{9,5},... | collective-permute-start | bytes 12296 | tf_op jit(solution)/shard_map/ppermute | solution.py:509
  75.1 2.3 %collective-permute-start.17 = (f32[8,128]{1,0:T(8,128)S(1)}, f32[8,128]{1,0:T(8,128)S(1)}, u32[]{:S(2)}, u32[]{:S(2)}) collective-permute-start(f32[8,128]{1,0:T(8,128)S(1)} %add_add_fusion.1.refs_0_), channel_id=1, source_target_pairs={{0,4},{1,5},{2,6},{3,7},{4,0},{5,1},{6,2},{7,3},{8,12},{9,13},{10,... | collective-permute-start | bytes 12296 | tf_op jit(solution)/shard_map/ppermute | solution.py:509
  77.4 1.0 %collective-permute-done.19.refs_3_ = f32[8,128]{1,0:T(8,128)S(1)} collective-permute-done((f32[8,128]{1,0:T(8,128)S(1)}, f32[8,128]{1,0:T(8,128)S(1)}, u32[]{:S(2)}, u32[]{:S(2)}) %collective-permute-start.19) | collective-permute-done | bytes 4128 | tf_op jit(solution)/shard_map/ppermute | solution.py:509
  78.5 1.0 %collective-permute-done.18.refs_2_ = f32[8,128]{1,0:T(8,128)S(1)} collective-permute-done((f32[8,128]{1,0:T(8,128)S(1)}, f32[8,128]{1,0:T(8,128)S(1)}, u32[]{:S(2)}, u32[]{:S(2)}) %collective-permute-start.18) | collective-permute-done | bytes 4128 | tf_op jit(solution)/shard_map/ppermute | solution.py:509
  79.4 0.0 collective-permute-done.17.refs_1_
  79.4 1.1 %shard_map.45 = (f32[4,32,512]{2,1,0:T(8,128)S(1)}, s32[1]{0:T(128)}) custom-call(f32[16,2,32,512]{3,2,1,0:T(8,128)S(1)} %get-tuple-element.64.p1m_ref, f32[16,2,32,512]{3,2,1,0:T(8,128)S(1)} %get-tuple-element.65.p2m_ref, f32[16,2,32,512]{3,2,1,0:T(8,128)S(1)} %get-tuple-element.76.p1e_ref, f32[16,2,32,512]{3,2,1,0:T(8,128)S(1)} %get-tuple-element.77.p2e_ref, ...), custom_call_target="tpu_custom_call" | custom-call | flops 5033164 | bytes 8388608 | tf_op jit(solution)/shard_map/pallas_call | solution.py:428
  81.2 0.2 conditional.1
  81.4 0.0 copy-start.3
  81.4 0.7 copy-done.3
  (1 shorter events, 0.0 us)
Async XLA Ops:
  2.1 7.5 %collective-permute-start.7 = (f32[32,512]{1,0:T(8,128)S(1)}, f32[32,512]{1,0:T(8,128)S(1)}, u32[]{:S(2)}, u32[]{:S(2)}) collective-permute-start(f32[32,512]{1,0:T(8,128)S(1)} %get-tuple-element.52), channel_id=1, source_target_pairs={{0,1},{1,2},{2,3},{3,4},{4,5},{5,6},{6,7},{7,8},{8,9},{9,10},{10,1... | collective-permute-start | bytes 196616 | tf_op jit(solution)/shard_map/ppermute | solution.py:21
  2.6 19.0 %collective-permute-start.8 = (f32[17,32,512]{2,1,0:T(8,128)S(1)}, f32[17,32,512]{2,1,0:T(8,128)S(1)}, u32[]{:S(2)}, u32[]{:S(2)}) collective-permute-start(f32[17,32,512]{2,1,0:T(8,128)S(1)} %get-tuple-element.59), channel_id=1, source_target_pairs={{0,15},{1,2},{2,1},{3,4},{4,3},{5,6},{6,5},{7,8},{8,7},{9,10},{10,... | collective-permute-start | bytes 3342344 | tf_op jit(solution)/shard_map/ppermute | solution.py:21
  7.7 13.9 %collective-permute-start.9 = (f32[17,32,512]{2,1,0:T(8,128)S(1)}, f32[17,32,512]{2,1,0:T(8,128)S(1)}, u32[]{:S(2)}, u32[]{:S(2)}) collective-permute-start(f32[17,32,512]{2,1,0:T(8,128)S(1)} %get-tuple-element.60), channel_id=1, source_target_pairs={{0,1},{1,0},{2,3},{3,2},{4,5},{5,4},{6,7},{7,6},{8,9},{9,8},{10,11... | collective-permute-start | bytes 3342344 | tf_op jit(solution)/shard_map/ppermute | solution.py:21
  17.5 35.5 %collective-permute-start.11 = (f32[16,32,512]{2,1,0:T(8,128)S(1)}, f32[16,32,512]{2,1,0:T(8,128)S(1)}, u32[]{:S(2)}, u32[]{:S(2)}) collective-permute-start(f32[16,32,512]{2,1,0:T(8,128)S(1)} %get-tuple-element.72), channel_id=1, source_target_pairs={{0,15},{1,2},{2,1},{3,4},{4,3},{5,6},{6,5},{7,8},{8,7},{9,10},{10,... | collective-permute-start | bytes 3145736 | tf_op jit(solution)/shard_map/ppermute | solution.py:21
  17.9 35.1 %collective-permute-start.12 = (f32[16,32,512]{2,1,0:T(8,128)S(1)}, f32[16,32,512]{2,1,0:T(8,128)S(1)}, u32[]{:S(2)}, u32[]{:S(2)}) collective-permute-start(f32[16,32,512]{2,1,0:T(8,128)S(1)} %get-tuple-element.73), channel_id=1, source_target_pairs={{0,1},{1,0},{2,3},{3,2},{4,5},{5,4},{6,7},{7,6},{8,9},{9,8},{10,11... | collective-permute-start | bytes 3145736 | tf_op jit(solution)/shard_map/ppermute | solution.py:21
  21.6 31.3 %collective-permute-start.10 = (f32[8,128]{1,0:T(8,128)S(1)}, f32[8,128]{1,0:T(8,128)S(1)}, u32[]{:S(2)}, u32[]{:S(2)}) collective-permute-start(f32[8,128]{1,0:T(8,128)S(1)} %get-tuple-element.68), channel_id=1, source_target_pairs={{0,1},{1,0},{2,3},{3,2},{4,5},{5,4},{6,7},{7,6},{8,9},{9,8},{10,11... | collective-permute-start | bytes 12296 | tf_op jit(solution)/shard_map/ppermute | solution.py:21
  52.9 17.0 %collective-permute-start.13 = (f32[16,32,512]{2,1,0:T(8,128)S(1)}, f32[16,32,512]{2,1,0:T(8,128)S(1)}, u32[]{:S(2)}, u32[]{:S(2)}) collective-permute-start(f32[16,32,512]{2,1,0:T(8,128)S(1)} %get-tuple-element.79), channel_id=1, source_target_pairs={{0,1},{1,2},{2,3},{3,4},{4,5},{5,6},{6,7},{7,8},{8,9},{9,10},{10,1... | collective-permute-start | bytes 3145736 | tf_op jit(solution)/shard_map/ppermute | solution.py:21
  70.2 3.1 %collective-permute-start.16 = (f32[8,128]{1,0:T(8,128)S(1)}, f32[8,128]{1,0:T(8,128)S(1)}, u32[]{:S(2)}, u32[]{:S(2)}) collective-permute-start(f32[8,128]{1,0:T(8,128)S(1)} %shard_map.44), channel_id=1, source_target_pairs={{0,3},{1,2},{2,1},{3,0},{4,7},{5,6},{6,5},{7,4},{8,11},{9,10},{10,... | collective-permute-start | bytes 12296 | tf_op jit(solution)/shard_map/ppermute | solution.py:509
  70.2 3.7 %collective-permute-start.15 = (f32[8,128]{1,0:T(8,128)S(1)}, f32[8,128]{1,0:T(8,128)S(1)}, u32[]{:S(2)}, u32[]{:S(2)}) collective-permute-start(f32[8,128]{1,0:T(8,128)S(1)} %shard_map.44), channel_id=1, source_target_pairs={{0,2},{1,3},{2,0},{3,1},{4,6},{5,7},{6,4},{7,5},{8,10},{9,11},{10,... | collective-permute-start | bytes 12296 | tf_op jit(solution)/shard_map/ppermute | solution.py:509
  70.3 3.6 %collective-permute-start.14 = (f32[8,128]{1,0:T(8,128)S(1)}, f32[8,128]{1,0:T(8,128)S(1)}, u32[]{:S(2)}, u32[]{:S(2)}) collective-permute-start(f32[8,128]{1,0:T(8,128)S(1)} %shard_map.44), channel_id=1, source_target_pairs={{0,1},{1,0},{2,3},{3,2},{4,5},{5,4},{6,7},{7,6},{8,9},{9,8},{10,11... | collective-permute-start | bytes 12296 | tf_op jit(solution)/shard_map/ppermute | solution.py:509
  73.9 4.6 %collective-permute-start.19 = (f32[8,128]{1,0:T(8,128)S(1)}, f32[8,128]{1,0:T(8,128)S(1)}, u32[]{:S(2)}, u32[]{:S(2)}) collective-permute-start(f32[8,128]{1,0:T(8,128)S(1)} %add_add_fusion.1.refs_0_), channel_id=1, source_target_pairs={{0,8},{1,9},{2,10},{3,11},{4,12},{5,13},{6,14},{7,15},{8,0},{9,1},... | collective-permute-start | bytes 12296 | tf_op jit(solution)/shard_map/ppermute | solution.py:509
  74.0 5.5 %collective-permute-start.18 = (f32[8,128]{1,0:T(8,128)S(1)}, f32[8,128]{1,0:T(8,128)S(1)}, u32[]{:S(2)}, u32[]{:S(2)}) collective-permute-start(f32[8,128]{1,0:T(8,128)S(1)} %add_add_fusion.1.refs_0_), channel_id=1, source_target_pairs={{0,12},{1,13},{2,14},{3,15},{4,8},{5,9},{6,10},{7,11},{8,4},{9,5},... | collective-permute-start | bytes 12296 | tf_op jit(solution)/shard_map/ppermute | solution.py:509
  75.1 4.3 %collective-permute-start.17 = (f32[8,128]{1,0:T(8,128)S(1)}, f32[8,128]{1,0:T(8,128)S(1)}, u32[]{:S(2)}, u32[]{:S(2)}) collective-permute-start(f32[8,128]{1,0:T(8,128)S(1)} %add_add_fusion.1.refs_0_), channel_id=1, source_target_pairs={{0,4},{1,5},{2,6},{3,7},{4,0},{5,1},{6,2},{7,3},{8,12},{9,13},{10,... | collective-permute-start | bytes 12296 | tf_op jit(solution)/shard_map/ppermute | solution.py:509
  81.4 0.7 copy-start.3

commit v16 on v15

--- a/solution.py
+++ b/solution.py
@@ -509,7 +509,7 @@
             lax.ppermute(moments, "day", [(i, i ^ (n * step)) for i in range(count)])
             for n in range(1, near)
         ]
-        if step > 1 and near == 4:
+        if near == 4:
             shares = shares[:2] + shares[:1:-1]
         step *= near
     out, unsound = call(

time: 82.2 us -> 82.2 us (level)
  transfers between devices with their start and end apart: 13 -> 13, of which waited for: 7 -> 6; matrix products, arithmetic and copies ran while one was open for 0% -> 0% of each run, Pallas kernels for 25% -> 25%
where the time goes in v16:
time: 82.2 us; the launch traced here: 82 us
  starting transfers between devices  34.2 us (42%)
  Pallas kernels  23.6 us (29%)
  waiting for transfers between devices  22.5 us (27%)
    ppermute x7, starting transfers between devices, moved(): return lax.ppermute(value, 'day', [(i, target(i)) for i in range(count)])  28.5 us
    pallas_call x7, Pallas kernels, call(): pl.pallas_call(kernel, grid=grid, in_specs=[spec(value.shape, kind) for v...  23.6 us
    ppermute x7, waiting for transfers between devices, moved(): return lax.ppermute(value, 'day', [(i, target(i)) for i in range(count)])  19 us
    ppermute x6, starting transfers between devices, body(): lax.ppermute(moments, 'day', [(i, i ^ n * step) for i in range(count)])  5.69 us
    ppermute x6, waiting for transfers between devices, body(): lax.ppermute(moments, 'day', [(i, i ^ n * step) for i in range(count)])  3.47 us
  transfers between devices with their start and end apart: 13, of which 6 were waited for; matrix products, arithmetic and copies ran while one was open for 0% of the time, Pallas kernels for 25%

profile of v16, /device:TPU:0, one launch (start us, length us, event | category | flops | bytes accessed | tf_op | source)
XLA Modules:
  0.0 82.0 jit_solution(9284454026757524608)
XLA Ops:
  0.0 2.1 %shard_map.39 = (f32[32,512]{1,0:T(8,128)S(1)}, f32[17,32,512]{2,1,0:T(8,128)S(1)}, f32[17,32,512]{2,1,0:T(8,128)S(1)}) custom-call(s32[1]{0:T(128)} %bitcast.12.odd_ref, f32[6,4,32,512]{3,2,1,0:T(8,128)} %coup_hbm.3, s32[16,4,32,512]{3,2,1,0:T(8,128)} %bits_hbm.3, s32[32,512]{1,0:T(8,128)} %mask_hbm.3), custom_call_target="tpu_custom_call" | custom-call | flops 2516582 | bytes 2097152 | tf_op jit(solution)/shard_map/pallas_call | solution.py:428
  2.1 0.5 collective-permute-start.7
  2.6 5.1 %collective-permute-start.8 = (f32[17,32,512]{2,1,0:T(8,128)S(1)}, f32[17,32,512]{2,1,0:T(8,128)S(1)}, u32[]{:S(2)}, u32[]{:S(2)}) collective-permute-start(f32[17,32,512]{2,1,0:T(8,128)S(1)} %get-tuple-element.59), channel_id=1, source_target_pairs={{0,15},{1,2},{2,1},{3,4},{4,3},{5,6},{6,5},{7,8},{8,7},{9,10},{10,... | collective-permute-start | bytes 3342344 | tf_op jit(solution)/shard_map/ppermute | solution.py:21
  7.7 0.0 collective-permute-start.9
  7.7 2.0 %collective-permute-done.7.before_ref = f32[32,512]{1,0:T(8,128)S(1)} collective-permute-done((f32[32,512]{1,0:T(8,128)S(1)}, f32[32,512]{1,0:T(8,128)S(1)}, u32[]{:S(2)}, u32[]{:S(2)}) %collective-permute-start.7) | collective-permute-done | bytes 65568 | tf_op jit(solution)/shard_map/ppermute | solution.py:21
  9.6 2.7 %shard_map.40 = (f32[8,4,32,512]{3,2,1,0:T(8,128)S(1)}, f32[4,32,512]{2,1,0:T(8,128)S(1)}, f32[4,32,512]{2,1,0:T(8,128)S(1)}, f32[4,32,512]{2,1,0:T(8,128)S(1)}, s32[16,4,32,512]{3,2,1,0:T(8,128)S(1)}) custom-call(f32[6,4,32,512]{3,2,1,0:T(8,128)} %coup_hbm.3, s32[16,4,32,512]{3,2,1,0:T(8,128)} %bits_hbm.3, s32[32,512]{1,0:T(8,128)} %mask_hbm.3, ...), custom_call_target="tpu_custom_call" | custom-call | flops 75497472 | bytes 83886080 | tf_op jit(solution)/shard_map/pallas_call | solution.py:428
  12.4 5.1 %shard_map.41 = (f32[16,4,32,512]{3,2,1,0:T(8,128)S(1)}, f32[16,32,512]{2,1,0:T(8,128)S(1)}, f32[16,32,512]{2,1,0:T(8,128)S(1)}, f32[8,128]{1,0:T(8,128)S(1)}) custom-call(s32[1]{0:T(128)} %bitcast.12.odd_ref, s32[16,4,32,512]{3,2,1,0:T(8,128)S(1)} %get-tuple-element.53.bits_ref, f32[8,4,32,512]{3,2,1,0:T(8,128)S(1)} %get-tuple-element.54.planes_ref, ...), custom_call_target="tpu_custom_call" | custom-call | flops 15099494400 | bytes 16777216000 | tf_op jit(solution)/shard_map/pallas_call | solution.py:428
  17.5 0.4 collective-permute-start.11
  17.9 0.0 collective-permute-start.12
  17.9 3.7 %collective-permute-done.8.off_ref.doff_ref = f32[17,32,512]{2,1,0:T(8,128)S(1)} collective-permute-done((f32[17,32,512]{2,1,0:T(8,128)S(1)}, f32[17,32,512]{2,1,0:T(8,128)S(1)}, u32[]{:S(2)}, u32[]{:S(2)}) %collective-permute-start.8) | collective-permute-done | bytes 1114144 | tf_op jit(solution)/shard_map/ppermute | solution.py:21
  21.6 0.0 collective-permute-done.9.on_ref.don_ref
  21.6 22.4 %collective-permute-start.10 = (f32[8,128]{1,0:T(8,128)S(1)}, f32[8,128]{1,0:T(8,128)S(1)}, u32[]{:S(2)}, u32[]{:S(2)}) collective-permute-start(f32[8,128]{1,0:T(8,128)S(1)} %get-tuple-element.68), channel_id=1, source_target_pairs={{0,1},{1,0},{2,3},{3,2},{4,5},{5,4},{6,7},{7,6},{8,9},{9,8},{10,11... | collective-permute-start | bytes 12296 | tf_op jit(solution)/shard_map/ppermute | solution.py:21
  44.0 8.9 %shard_map.42 = (f32[16,2,32,512]{3,2,1,0:T(8,128)S(1)}, f32[16,2,32,512]{3,2,1,0:T(8,128)S(1)}, f32[16,2,32,512]{3,2,1,0:T(8,128)S(1)}, f32[16,2,32,512]{3,2,1,...) custom-call(s32[1]{0:T(128)} %bitcast.12.odd_ref, ...), custom_call_target="tpu_custom_call" | custom-call | flops 251658240 | bytes 251658240 | tf_op jit(solution)/shard_map/pallas_call | solution.py:428
  52.9 0.0 collective-permute-done.10.token_ref
  52.9 0.1 collective-permute-start.13
  53.0 0.0 collective-permute-done.11.off_ref
  53.0 0.0 collective-permute-done.12.on_ref
  53.0 3.5 %shard_map.43 = (f32[16,2,32,512]{3,2,1,0:T(8,128)S(1)}, f32[16,2,32,512]{3,2,1,0:T(8,128)S(1)}, f32[16,32,512]{2,1,0:T(8,128)S(1)}, f32[16,8,128]{2,1,0:T(8,128)S(1)}) custom-call(s32[1]{0:T(128)} %bitcast.12.odd_ref, f32[8,128]{1,0:T(8,128)S(1)} %collective-permute-done.10.token_ref, s32[16,4,32,512]{3,2,1,0:T(8,128)S(1)} %get-tuple-element.53.bits_ref, ...), custom_call_target="tpu_custom_call" | custom-call | flops 251658240 | bytes 251658240 | tf_op jit(solution)/shard_map/pallas_call | solution.py:428
  56.5 13.4 %collective-permute-done.13.high_ref = f32[16,32,512]{2,1,0:T(8,128)S(1)} collective-permute-done((f32[16,32,512]{2,1,0:T(8,128)S(1)}, f32[16,32,512]{2,1,0:T(8,128)S(1)}, u32[]{:S(2)}, u32[]{:S(2)}) %collective-permute-start.13) | collective-permute-done | bytes 1048608 | tf_op jit(solution)/shard_map/ppermute | solution.py:21
  69.9 0.2 shard_map.44
  70.2 0.0 collective-permute-start.16
  70.2 0.1 collective-permute-start.15
  70.3 2.0 %collective-permute-start.14 = (f32[8,128]{1,0:T(8,128)S(1)}, f32[8,128]{1,0:T(8,128)S(1)}, u32[]{:S(2)}, u32[]{:S(2)}) collective-permute-start(f32[8,128]{1,0:T(8,128)S(1)} %shard_map.44), channel_id=1, source_target_pairs={{0,1},{1,0},{2,3},{3,2},{4,5},{5,4},{6,7},{7,6},{8,9},{9,8},{10,11... | collective-permute-start | bytes 12296 | tf_op jit(solution)/shard_map/ppermute | solution.py:509
  72.3 1.5 %collective-permute-done.16 = f32[8,128]{1,0:T(8,128)S(1)} collective-permute-done((f32[8,128]{1,0:T(8,128)S(1)}, f32[8,128]{1,0:T(8,128)S(1)}, u32[]{:S(2)}, u32[]{:S(2)}) %collective-permute-start.16) | collective-permute-done | bytes 4128 | tf_op jit(solution)/shard_map/ppermute | solution.py:509
  73.8 0.0 collective-permute-done.15
  73.8 0.0 collective-permute-done.14
  73.8 0.1 collective-permute-start.19
  73.9 1.2 %collective-permute-start.18 = (f32[8,128]{1,0:T(8,128)S(1)}, f32[8,128]{1,0:T(8,128)S(1)}, u32[]{:S(2)}, u32[]{:S(2)}) collective-permute-start(f32[8,128]{1,0:T(8,128)S(1)} %add_add_fusion.1.refs_0_), channel_id=1, source_target_pairs={{0,12},{1,13},{2,14},{3,15},{4,8},{5,9},{6,10},{7,11},{8,4},{9,5},... | collective-permute-start | bytes 12296 | tf_op jit(solution)/shard_map/ppermute | solution.py:509
  75.1 2.3 %collective-permute-start.17 = (f32[8,128]{1,0:T(8,128)S(1)}, f32[8,128]{1,0:T(8,128)S(1)}, u32[]{:S(2)}, u32[]{:S(2)}) collective-permute-start(f32[8,128]{1,0:T(8,128)S(1)} %add_add_fusion.1.refs_0_), channel_id=1, source_target_pairs={{0,4},{1,5},{2,6},{3,7},{4,0},{5,1},{6,2},{7,3},{8,12},{9,13},{10,... | collective-permute-start | bytes 12296 | tf_op jit(solution)/shard_map/ppermute | solution.py:509
  77.4 1.0 %collective-permute-done.19.refs_3_ = f32[8,128]{1,0:T(8,128)S(1)} collective-permute-done((f32[8,128]{1,0:T(8,128)S(1)}, f32[8,128]{1,0:T(8,128)S(1)}, u32[]{:S(2)}, u32[]{:S(2)}) %collective-permute-start.19) | collective-permute-done | bytes 4128 | tf_op jit(solution)/shard_map/ppermute | solution.py:509
  78.4 1.0 %collective-permute-done.18.refs_2_ = f32[8,128]{1,0:T(8,128)S(1)} collective-permute-done((f32[8,128]{1,0:T(8,128)S(1)}, f32[8,128]{1,0:T(8,128)S(1)}, u32[]{:S(2)}, u32[]{:S(2)}) %collective-permute-start.18) | collective-permute-done | bytes 4128 | tf_op jit(solution)/shard_map/ppermute | solution.py:509
  79.4 0.0 collective-permute-done.17.refs_1_
  79.4 1.1 %shard_map.45 = (f32[4,32,512]{2,1,0:T(8,128)S(1)}, s32[1]{0:T(128)}) custom-call(f32[16,2,32,512]{3,2,1,0:T(8,128)S(1)} %get-tuple-element.64.p1m_ref, f32[16,2,32,512]{3,2,1,0:T(8,128)S(1)} %get-tuple-element.65.p2m_ref, f32[16,2,32,512]{3,2,1,0:T(8,128)S(1)} %get-tuple-element.76.p1e_ref, f32[16,2,32,512]{3,2,1,0:T(8,128)S(1)} %get-tuple-element.77.p2e_ref, ...), custom_call_target="tpu_custom_call" | custom-call | flops 5033164 | bytes 8388608 | tf_op jit(solution)/shard_map/pallas_call | solution.py:428
  81.1 0.2 conditional.1
  81.3 0.0 copy-start.3
  81.3 0.7 copy-done.3
  (1 shorter events, 0.0 us)
Async XLA Ops:
  2.1 7.5 %collective-permute-start.7 = (f32[32,512]{1,0:T(8,128)S(1)}, f32[32,512]{1,0:T(8,128)S(1)}, u32[]{:S(2)}, u32[]{:S(2)}) collective-permute-start(f32[32,512]{1,0:T(8,128)S(1)} %get-tuple-element.52), channel_id=1, source_target_pairs={{0,1},{1,2},{2,3},{3,4},{4,5},{5,6},{6,7},{7,8},{8,9},{9,10},{10,1... | collective-permute-start | bytes 196616 | tf_op jit(solution)/shard_map/ppermute | solution.py:21
  2.6 19.0 %collective-permute-start.8 = (f32[17,32,512]{2,1,0:T(8,128)S(1)}, f32[17,32,512]{2,1,0:T(8,128)S(1)}, u32[]{:S(2)}, u32[]{:S(2)}) collective-permute-start(f32[17,32,512]{2,1,0:T(8,128)S(1)} %get-tuple-element.59), channel_id=1, source_target_pairs={{0,15},{1,2},{2,1},{3,4},{4,3},{5,6},{6,5},{7,8},{8,7},{9,10},{10,... | collective-permute-start | bytes 3342344 | tf_op jit(solution)/shard_map/ppermute | solution.py:21
  7.7 13.9 %collective-permute-start.9 = (f32[17,32,512]{2,1,0:T(8,128)S(1)}, f32[17,32,512]{2,1,0:T(8,128)S(1)}, u32[]{:S(2)}, u32[]{:S(2)}) collective-permute-start(f32[17,32,512]{2,1,0:T(8,128)S(1)} %get-tuple-element.60), channel_id=1, source_target_pairs={{0,1},{1,0},{2,3},{3,2},{4,5},{5,4},{6,7},{7,6},{8,9},{9,8},{10,11... | collective-permute-start | bytes 3342344 | tf_op jit(solution)/shard_map/ppermute | solution.py:21
  17.5 35.5 %collective-permute-start.11 = (f32[16,32,512]{2,1,0:T(8,128)S(1)}, f32[16,32,512]{2,1,0:T(8,128)S(1)}, u32[]{:S(2)}, u32[]{:S(2)}) collective-permute-start(f32[16,32,512]{2,1,0:T(8,128)S(1)} %get-tuple-element.72), channel_id=1, source_target_pairs={{0,15},{1,2},{2,1},{3,4},{4,3},{5,6},{6,5},{7,8},{8,7},{9,10},{10,... | collective-permute-start | bytes 3145736 | tf_op jit(solution)/shard_map/ppermute | solution.py:21
  17.9 35.1 %collective-permute-start.12 = (f32[16,32,512]{2,1,0:T(8,128)S(1)}, f32[16,32,512]{2,1,0:T(8,128)S(1)}, u32[]{:S(2)}, u32[]{:S(2)}) collective-permute-start(f32[16,32,512]{2,1,0:T(8,128)S(1)} %get-tuple-element.73), channel_id=1, source_target_pairs={{0,1},{1,0},{2,3},{3,2},{4,5},{5,4},{6,7},{7,6},{8,9},{9,8},{10,11... | collective-permute-start | bytes 3145736 | tf_op jit(solution)/shard_map/ppermute | solution.py:21
  21.6 31.3 %collective-permute-start.10 = (f32[8,128]{1,0:T(8,128)S(1)}, f32[8,128]{1,0:T(8,128)S(1)}, u32[]{:S(2)}, u32[]{:S(2)}) collective-permute-start(f32[8,128]{1,0:T(8,128)S(1)} %get-tuple-element.68), channel_id=1, source_target_pairs={{0,1},{1,0},{2,3},{3,2},{4,5},{5,4},{6,7},{7,6},{8,9},{9,8},{10,11... | collective-permute-start | bytes 12296 | tf_op jit(solution)/shard_map/ppermute | solution.py:21
  52.9 17.0 %collective-permute-start.13 = (f32[16,32,512]{2,1,0:T(8,128)S(1)}, f32[16,32,512]{2,1,0:T(8,128)S(1)}, u32[]{:S(2)}, u32[]{:S(2)}) collective-permute-start(f32[16,32,512]{2,1,0:T(8,128)S(1)} %get-tuple-element.79), channel_id=1, source_target_pairs={{0,1},{1,2},{2,3},{3,4},{4,5},{5,6},{6,7},{7,8},{8,9},{9,10},{10,1... | collective-permute-start | bytes 3145736 | tf_op jit(solution)/shard_map/ppermute | solution.py:21
  70.2 3.6 %collective-permute-start.16 = (f32[8,128]{1,0:T(8,128)S(1)}, f32[8,128]{1,0:T(8,128)S(1)}, u32[]{:S(2)}, u32[]{:S(2)}) collective-permute-start(f32[8,128]{1,0:T(8,128)S(1)} %shard_map.44), channel_id=1, source_target_pairs={{0,2},{1,3},{2,0},{3,1},{4,6},{5,7},{6,4},{7,5},{8,10},{9,11},{10,... | collective-permute-start | bytes 12296 | tf_op jit(solution)/shard_map/ppermute | solution.py:509
  70.2 3.6 %collective-permute-start.15 = (f32[8,128]{1,0:T(8,128)S(1)}, f32[8,128]{1,0:T(8,128)S(1)}, u32[]{:S(2)}, u32[]{:S(2)}) collective-permute-start(f32[8,128]{1,0:T(8,128)S(1)} %shard_map.44), channel_id=1, source_target_pairs={{0,3},{1,2},{2,1},{3,0},{4,7},{5,6},{6,5},{7,4},{8,11},{9,10},{10,... | collective-permute-start | bytes 12296 | tf_op jit(solution)/shard_map/ppermute | solution.py:509
  70.3 3.5 %collective-permute-start.14 = (f32[8,128]{1,0:T(8,128)S(1)}, f32[8,128]{1,0:T(8,128)S(1)}, u32[]{:S(2)}, u32[]{:S(2)}) collective-permute-start(f32[8,128]{1,0:T(8,128)S(1)} %shard_map.44), channel_id=1, source_target_pairs={{0,1},{1,0},{2,3},{3,2},{4,5},{5,4},{6,7},{7,6},{8,9},{9,8},{10,11... | collective-permute-start | bytes 12296 | tf_op jit(solution)/shard_map/ppermute | solution.py:509
  73.8 4.6 %collective-permute-start.19 = (f32[8,128]{1,0:T(8,128)S(1)}, f32[8,128]{1,0:T(8,128)S(1)}, u32[]{:S(2)}, u32[]{:S(2)}) collective-permute-start(f32[8,128]{1,0:T(8,128)S(1)} %add_add_fusion.1.refs_0_), channel_id=1, source_target_pairs={{0,8},{1,9},{2,10},{3,11},{4,12},{5,13},{6,14},{7,15},{8,0},{9,1},... | collective-permute-start | bytes 12296 | tf_op jit(solution)/shard_map/ppermute | solution.py:509
  73.9 5.5 %collective-permute-start.18 = (f32[8,128]{1,0:T(8,128)S(1)}, f32[8,128]{1,0:T(8,128)S(1)}, u32[]{:S(2)}, u32[]{:S(2)}) collective-permute-start(f32[8,128]{1,0:T(8,128)S(1)} %add_add_fusion.1.refs_0_), channel_id=1, source_target_pairs={{0,12},{1,13},{2,14},{3,15},{4,8},{5,9},{6,10},{7,11},{8,4},{9,5},... | collective-permute-start | bytes 12296 | tf_op jit(solution)/shard_map/ppermute | solution.py:509
  75.1 4.3 %collective-permute-start.17 = (f32[8,128]{1,0:T(8,128)S(1)}, f32[8,128]{1,0:T(8,128)S(1)}, u32[]{:S(2)}, u32[]{:S(2)}) collective-permute-start(f32[8,128]{1,0:T(8,128)S(1)} %add_add_fusion.1.refs_0_), channel_id=1, source_target_pairs={{0,4},{1,5},{2,6},{3,7},{4,0},{5,1},{6,2},{7,3},{8,12},{9,13},{10,... | collective-permute-start | bytes 12296 | tf_op jit(solution)/shard_map/ppermute | solution.py:509
  81.3 0.7 copy-start.3
